TPU v7x, 512 devices: a whole 4x8x8 slice. The times are simulated.
512 devices in a mesh: gx: 32 (over x, z), gy: 16 (over y, core).
Axes of the slice: x: 4, y: 8, z: 8, core: 2. Of those that a mesh axis runs over, the one named last changes fastest.
Arguments:
- rhs: float32 [128, 128, 512], P('gx', 'gy'), may hold values from -6 to 6
- alpha: float32 [128, 128, 512], P('gx', 'gy'), may hold values from 0.0001 to 4
- beta_x: float32 [128, 128, 512], P('gx', 'gy'), may hold values from 0.5 to 2
- beta_y: float32 [128, 128, 512], P('gx', 'gy'), may hold values from 0.5 to 2
- beta_z: float32 [128, 128, 512], P('gx', 'gy'), may hold values from 0.5 to 2
Outputs:
- fine_solution: float32 [128, 128, 512], P('gx', 'gy')
- coarse_correction: float32 [32, 32, 128], P('gx', 'gy')
All inputs are finite; a program needn't handle non-finite values.
Results may differ from a plain program's by a relative error of at most 0.00002.
Values sent between devices are 32-bit elements; how exact they have to be, the bound alone decides.
No kernel may reach another device: no remote copies, remote signals or barrier semaphores. Data moves between devices by JAX's collectives and lax.ppermute only.
A program may use at most 64 MiB of HBM per device.

v0:
```python
import jax
import jax.numpy as jnp
from jax import lax
from jax.sharding import PartitionSpec as P

SWEEPS = 4
COARSE_SWEEPS = 8


def extended(value, sides, width):
    for axis, dim in sides:
        count, length = (lax.axis_size(axis), value.shape[dim])
        up = [(i, (i + 1) % count) for i in range(count - 1)]
        down = [(j, i) for i, j in up]
        last = lax.slice_in_dim(value, length - width, length, axis=dim)
        leading = lax.slice_in_dim(value, 0, width, axis=dim)
        before = lax.ppermute(last, axis, up)
        after = lax.ppermute(leading, axis, down)
        value = jnp.concatenate([before, value, after], axis=dim)
    return value


def passed_along(value, axis, steps):
    count = lax.axis_size(axis)
    leading, last = (max(0, -steps), min(count, count - steps))
    return lax.ppermute(value, axis, [(source, source + steps) for source in range(leading, last)])


def upper_faces(beta, axis_pos):
    rest = lax.slice_in_dim(beta, 1, beta.shape[axis_pos], axis=axis_pos)
    zero_layer = jnp.zeros_like(lax.slice_in_dim(beta, 0, 1, axis=axis_pos))
    return jnp.concatenate([rest, zero_layer], axis=axis_pos)


def coarsen_face(faces, axis_pos, upper):
    size_x, size_y, size_z = faces.shape
    blocks = faces.reshape(size_x // 2, 2, size_y // 2, 2, size_z // 2, 2)
    taken = 2 * axis_pos + 1
    picked = jnp.take(blocks, upper, axis=taken)
    others = tuple((pair - 1 if pair > taken else pair for pair in (1, 3, 5) if pair != taken))
    return jnp.mean(picked, axis=others) * 0.25


def coarsen_all(faces):
    return tuple((coarsen_face(faces[number], number // 2, number % 2) for number in range(6)))


def restrict(field):
    size_x, size_y, size_z = field.shape
    return jnp.mean(field.reshape(size_x // 2, 2, size_y // 2, 2, size_z // 2, 2), axis=(1, 3, 5))


def prolong(field):
    return jnp.repeat(jnp.repeat(jnp.repeat(field, 2, 0), 2, 1), 2, 2)


def beside_sum(padded, faces):
    total = faces[0] * padded[:-2, 1:-1, 1:-1] + faces[1] * padded[2:, 1:-1, 1:-1]
    total = total + faces[2] * padded[1:-1, :-2, 1:-1] + faces[3] * padded[1:-1, 2:, 1:-1]
    total = total + faces[4] * padded[1:-1, 1:-1, :-2] + faces[5] * padded[1:-1, 1:-1, 2:]
    return total


def diagonal_of(cell_coef, faces):
    total = cell_coef
    for face in faces:
        total = total + face
    return total


def red_cells(shape, offset_x, offset_y):
    index_x = jnp.arange(shape[0], dtype=jnp.int32) + offset_x
    index_y = jnp.arange(shape[1], dtype=jnp.int32) + offset_y
    index_z = jnp.arange(shape[2], dtype=jnp.int32)
    return (index_x[:, None, None] + index_y[None, :, None] + index_z[None, None, :]) % 2 == 0


def extend_fine(field):
    padded = extended(field, (("gx", 0), ("gy", 1)), 1)
    return jnp.pad(padded, ((0, 0), (0, 0), (1, 1)))


def extend_residual(field):
    padded = extended(field, (("gx", 0), ("gy", 1)), 1)
    return jnp.pad(padded, ((0, 0), (0, 0), (1, 1)))


def extend_grid(field):
    padded = extended(field, (("gx", 0), ("gy", 1)), 1)
    return jnp.pad(padded, ((0, 0), (0, 0), (1, 1)))


def smooth(field, source, inverse, faces, red_mask, count, extend):

    def one_sweep(sweep_index, current):
        for colour in (True, False):
            beside = beside_sum(extend(current), faces)
            current = jnp.where(red_mask == colour, (source + beside) * inverse, current)
        return current

    return lax.fori_loop(0, count, one_sweep, field)


def residual_of(field, source, diagonal, faces):
    return source - (diagonal * field - beside_sum(extend_residual(field), faces))


def local_red(shape):
    return red_cells(shape, lax.axis_index("gx") * shape[0], lax.axis_index("gy") * shape[1])


def smooth_level(source, inverse, faces, count):
    return smooth(
        jnp.zeros_like(source), source, inverse, faces, local_red(source.shape), count, extend_fine
    )


def on_device(rhs, alpha, beta_x, beta_y, beta_z):
    next_x = passed_along(beta_x[0:1], "gx", -1)
    next_y = passed_along(beta_y[:, 0:1], "gy", -1)
    faces_fine = (
        beta_x,
        jnp.concatenate([beta_x[1:], next_x], 0),
        beta_y,
        jnp.concatenate([beta_y[:, 1:], next_y], 1),
        beta_z,
        upper_faces(beta_z, 2),
    )
    diagonal_fine = diagonal_of(alpha, faces_fine)
    smoothed = smooth_level(rhs, 1.0 / diagonal_fine, faces_fine, SWEEPS)
    source_mid = restrict(residual_of(smoothed, rhs, diagonal_fine, faces_fine))
    coef_mid = restrict(alpha)
    faces_mid = coarsen_all(faces_fine)
    diagonal_mid = diagonal_of(coef_mid, faces_mid)
    level_mid = smooth_level(source_mid, 1.0 / diagonal_mid, faces_mid, SWEEPS)
    source_low = restrict(residual_of(level_mid, source_mid, diagonal_mid, faces_mid))
    coef_low = restrict(coef_mid)
    faces_low = coarsen_all(faces_mid)
    inverse_low = 1.0 / diagonal_of(coef_low, faces_low)
    coarse = smooth(
        jnp.zeros_like(source_low),
        source_low,
        inverse_low,
        faces_low,
        local_red(source_low.shape),
        COARSE_SWEEPS,
        extend_grid,
    )
    corrected = level_mid + prolong(coarse)
    return (smoothed + prolong(corrected), coarse)


def solution(mesh):
    placed = (
        P("gx", "gy", None),
        P("gx", "gy", None),
        P("gx", "gy", None),
        P("gx", "gy", None),
        P("gx", "gy", None),
    )
    return jax.shard_map(
        on_device,
        mesh=mesh,
        in_specs=placed,
        out_specs=(P("gx", "gy", None), P("gx", "gy", None)),
        check_vma=False,
    )
```

profile of v0, /device:TPU:38, one launch (start us, length us, event | category | flops | bytes accessed | tf_op | source)
XLA Modules:
  0.0 703.9 jit_solution(13089568681583672517)
XLA Ops:
  1.4 11.2 %collective-permute-start.24 = (f32[1,8,512]{2,1,0:T(8,128)S(1)}, f32[1,8,512]{2,1,0:T(8,128)S(1)}, u32[]{:S(2)}, u32[]{:S(2)}) collective-permute-start(f32[1,8,512]{2,1,0:T(8,128)S(1)} %slice.468), channel_id=1, source_target_pairs={{16,0},{32,16},{48,32},{64,48},{80,64},{96,80},{112,96},{128,112},... | collective-permute-start | bytes 49160 | tf_op jit(solution)/shard_map/ppermute | solution.py:26
  15.4 6.3 reshape.453
  21.7 5.5 reshape.451
  27.2 5.5 reshape.455
  38.9 5.5 reshape.458
  47.1 5.5 reshape.454
  52.6 5.5 reshape.456
  58.1 146.1 %while.54 = (s32[]{:T(128)}, f32[4,8,512]{2,1,0:T(8,128)S(1)}, f32[4,8,512]{2,1,0:T(8,128)S(1)}, f32[4,8,512]{2,1,0:T(8,128)S(1)}, f32[4,8,512]{2,1,0:T(8,128)S(...) while((s32[]{:T(128)}, f32[4,8,512]{2,1,0:T(8,128)S(1)}, ...), condition=%wide.region_1.2_spmd.clone, body=%wide.region_0.1_spmd.clone.sunk | while | flops 1944387 | bytes 3147399 | solution.py:101
  64.0 4.3 collective-permute-done.1
  78.8 3.9 collective-permute-start.5
  97.0 3.9 collective-permute-start.1
  115.2 3.9 collective-permute-start.5
  133.4 3.9 collective-permute-start.1
  151.5 3.9 collective-permute-start.5
  169.8 3.9 collective-permute-start.1
  187.9 3.9 collective-permute-start.5
  206.6 4.5 slice_reduce_fusion
  211.4 5.5 reshape.452
  216.9 6.0 collective-permute-start.27
  226.3 4.9 collective-permute-start.29
  233.8 5.5 reshape.457
  246.4 147.7 %while.55 = (s32[]{:T(128)}, f32[2,4,256]{2,1,0:T(4,128)S(1)}, f32[2,4,256]{2,1,0:T(4,128)S(1)}, f32[2,4,256]{2,1,0:T(4,128)S(1)}, f32[2,4,256]{2,1,0:T(4,128)S(...) while((s32[]{:T(128)}, f32[2,4,256]{2,1,0:T(4,128)S(1)}, ...), condition=%wide.region_11.18_spmd.clone, body=%wide.region_10.17_spmd.clone.sunk | while | flops 304259 | bytes 557959 | solution.py:101
  246.4 6.3 collective-permute-start.8
  254.7 5.7 collective-permute-done.9
  264.7 4.2 collective-permute-done.11
  289.0 3.9 collective-permute-start.9
  306.8 3.9 collective-permute-start.13
  324.7 3.9 collective-permute-start.9
  342.5 3.9 collective-permute-start.13
  360.3 3.9 collective-permute-start.9
  378.2 3.9 collective-permute-start.13
  396.0 6.0 collective-permute-start.31
  407.1 4.9 collective-permute-start.33
  414.2 287.8 %while.56 = (s32[]{:T(128)}, f32[1,2,128]{2,1,0:T(2,128)S(1)}, f32[1,2,128]{2,1,0:T(2,128)S(1)}, f32[1,2,128]{2,1,0:T(2,128)S(1)}, f32[1,2,128]{2,1,0:T(2,128)S(...) while((s32[]{:T(128)}, f32[1,2,128]{2,1,0:T(2,128)S(1)}, ...), condition=%wide.region_23.36_spmd.clone, body=%wide.region_22.35_spmd.clone.sunk | while | flops 57923 | bytes 127639 | solution.py:101
  414.2 4.5 collective-permute-start.16
  420.6 5.6 collective-permute-done.17
  431.6 4.2 collective-permute-done.19
  455.7 3.9 collective-permute-start.17
  473.4 3.9 collective-permute-start.21
  491.1 3.9 collective-permute-start.17
  508.8 3.9 collective-permute-start.21
  526.6 3.9 collective-permute-start.17
  544.3 3.9 collective-permute-start.21
  562.0 3.9 collective-permute-start.17
  579.8 3.9 collective-permute-start.21
  597.5 3.9 collective-permute-start.17
  650.7 3.9 collective-permute-start.21
  668.4 3.9 collective-permute-start.17
  (481 shorter events, 489.3 us)
Async XLA Ops:
  1.4 45.6 %collective-permute-start.24 = (f32[1,8,512]{2,1,0:T(8,128)S(1)}, f32[1,8,512]{2,1,0:T(8,128)S(1)}, u32[]{:S(2)}, u32[]{:S(2)}) collective-permute-start(f32[1,8,512]{2,1,0:T(8,128)S(1)} %slice.468), channel_id=1, source_target_pairs={{16,0},{32,16},{48,32},{64,48},{80,64},{96,80},{112,96},{128,112},... | collective-permute-start | bytes 49160 | tf_op jit(solution)/shard_map/ppermute | solution.py:26
  13.5 33.5 %collective-permute-start.25 = (f32[4,1,512]{2,1,0:T(1,128)S(1)}, f32[4,1,512]{2,1,0:T(1,128)S(1)}, u32[]{:S(2)}, u32[]{:S(2)}) collective-permute-start(f32[4,1,512]{2,1,0:T(1,128)S(1)} %slice.470), channel_id=1, source_target_pairs={{1,0},{2,1},{3,2},{4,3},{5,4},{6,5},{7,6},{8,7},{9,8},{10,9},{11,1... | collective-permute-start | bytes 24584 | tf_op jit(solution)/shard_map/ppermute | solution.py:26
  60.6 7.7 %collective-permute-start.1 = (f32[1,8,512]{2,1,0:T(8,128)S(1)}, f32[1,8,512]{2,1,0:T(8,128)S(1)}, u32[]{:S(2)}, u32[]{:S(2)}) collective-permute-start(f32[1,8,512]{2,1,0:T(8,128)S(1)} %get-tuple-element.989), channel_id=1, source_target_pairs={{0,16},{16,32},{32,48},{48,64},{64,80},{80,96},{96,112},{112,128},... | collective-permute-start | bytes 49160 | tf_op jit(solution)/shard_map/while/body/eval_jaxpr/ppermute | solution.py:17
  70.3 6.2 collective-permute-start.3
  78.8 7.7 %collective-permute-start.5 = (f32[1,8,512]{2,1,0:T(8,128)S(1)}, f32[1,8,512]{2,1,0:T(8,128)S(1)}, u32[]{:S(2)}, u32[]{:S(2)}) collective-permute-start(f32[1,8,512]{2,1,0:T(8,128)S(1)} %get-tuple-element.993), channel_id=1, source_target_pairs={{0,16},{16,32},{32,48},{48,64},{64,80},{80,96},{96,112},{112,128},... | collective-permute-start | bytes 49160 | tf_op jit(solution)/shard_map/while/body/eval_jaxpr/ppermute | solution.py:17
  88.5 6.2 collective-permute-start.7
  97.0 7.7 %collective-permute-start.1 = (f32[1,8,512]{2,1,0:T(8,128)S(1)}, f32[1,8,512]{2,1,0:T(8,128)S(1)}, u32[]{:S(2)}, u32[]{:S(2)}) collective-permute-start(f32[1,8,512]{2,1,0:T(8,128)S(1)} %get-tuple-element.989), channel_id=1, source_target_pairs={{0,16},{16,32},{32,48},{48,64},{64,80},{80,96},{96,112},{112,128},... | collective-permute-start | bytes 49160 | tf_op jit(solution)/shard_map/while/body/eval_jaxpr/ppermute | solution.py:17
  106.7 6.2 collective-permute-start.3
  115.2 7.7 %collective-permute-start.5 = (f32[1,8,512]{2,1,0:T(8,128)S(1)}, f32[1,8,512]{2,1,0:T(8,128)S(1)}, u32[]{:S(2)}, u32[]{:S(2)}) collective-permute-start(f32[1,8,512]{2,1,0:T(8,128)S(1)} %get-tuple-element.993), channel_id=1, source_target_pairs={{0,16},{16,32},{32,48},{48,64},{64,80},{80,96},{96,112},{112,128},... | collective-permute-start | bytes 49160 | tf_op jit(solution)/shard_map/while/body/eval_jaxpr/ppermute | solution.py:17
  124.9 6.2 collective-permute-start.7
  133.4 7.7 %collective-permute-start.1 = (f32[1,8,512]{2,1,0:T(8,128)S(1)}, f32[1,8,512]{2,1,0:T(8,128)S(1)}, u32[]{:S(2)}, u32[]{:S(2)}) collective-permute-start(f32[1,8,512]{2,1,0:T(8,128)S(1)} %get-tuple-element.989), channel_id=1, source_target_pairs={{0,16},{16,32},{32,48},{48,64},{64,80},{80,96},{96,112},{112,128},... | collective-permute-start | bytes 49160 | tf_op jit(solution)/shard_map/while/body/eval_jaxpr/ppermute | solution.py:17
  143.1 6.2 collective-permute-start.3
  151.5 7.7 %collective-permute-start.5 = (f32[1,8,512]{2,1,0:T(8,128)S(1)}, f32[1,8,512]{2,1,0:T(8,128)S(1)}, u32[]{:S(2)}, u32[]{:S(2)}) collective-permute-start(f32[1,8,512]{2,1,0:T(8,128)S(1)} %get-tuple-element.993), channel_id=1, source_target_pairs={{0,16},{16,32},{32,48},{48,64},{64,80},{80,96},{96,112},{112,128},... | collective-permute-start | bytes 49160 | tf_op jit(solution)/shard_map/while/body/eval_jaxpr/ppermute | solution.py:17
  169.8 7.7 %collective-permute-start.1 = (f32[1,8,512]{2,1,0:T(8,128)S(1)}, f32[1,8,512]{2,1,0:T(8,128)S(1)}, u32[]{:S(2)}, u32[]{:S(2)}) collective-permute-start(f32[1,8,512]{2,1,0:T(8,128)S(1)} %get-tuple-element.989), channel_id=1, source_target_pairs={{0,16},{16,32},{32,48},{48,64},{64,80},{80,96},{96,112},{112,128},... | collective-permute-start | bytes 49160 | tf_op jit(solution)/shard_map/while/body/eval_jaxpr/ppermute | solution.py:17
  187.9 7.7 %collective-permute-start.5 = (f32[1,8,512]{2,1,0:T(8,128)S(1)}, f32[1,8,512]{2,1,0:T(8,128)S(1)}, u32[]{:S(2)}, u32[]{:S(2)}) collective-permute-start(f32[1,8,512]{2,1,0:T(8,128)S(1)} %get-tuple-element.993), channel_id=1, source_target_pairs={{0,16},{16,32},{32,48},{48,64},{64,80},{80,96},{96,112},{112,128},... | collective-permute-start | bytes 49160 | tf_op jit(solution)/shard_map/while/body/eval_jaxpr/ppermute | solution.py:17
  204.2 18.7 %collective-permute-start.26 = (f32[1,8,512]{2,1,0:T(8,128)S(1)}, f32[1,8,512]{2,1,0:T(8,128)S(1)}, u32[]{:S(2)}, u32[]{:S(2)}) collective-permute-start(f32[1,8,512]{2,1,0:T(8,128)S(1)} %get-tuple-element.774), channel_id=1, source_target_pairs={{0,16},{16,32},{32,48},{48,64},{64,80},{80,96},{96,112},{112,128},... | collective-permute-start | bytes 49160 | tf_op jit(solution)/shard_map/ppermute | solution.py:17
  216.9 7.4 %collective-permute-start.27 = (f32[1,8,512]{2,1,0:T(8,128)S(1)}, f32[1,8,512]{2,1,0:T(8,128)S(1)}, u32[]{:S(2)}, u32[]{:S(2)}) collective-permute-start(f32[1,8,512]{2,1,0:T(8,128)S(1)} %get-tuple-element.773), channel_id=1, source_target_pairs={{16,0},{32,16},{48,32},{64,48},{80,64},{96,80},{112,96},{128,112},... | collective-permute-start | bytes 49160 | tf_op jit(solution)/shard_map/ppermute | solution.py:18
  224.4 9.1 %collective-permute-start.28 = (f32[6,1,512]{2,1,0:T(1,128)S(1)}, f32[6,1,512]{2,1,0:T(1,128)S(1)}, u32[]{:S(2)}, u32[]{:S(2)}) collective-permute-start(f32[6,1,512]{2,1,0:T(1,128)S(1)} %get-tuple-element.771), channel_id=1, source_target_pairs={{0,1},{1,2},{2,3},{3,4},{4,5},{5,6},{6,7},{7,8},{8,9},{9,10},{10,1... | collective-permute-start | bytes 36872 | tf_op jit(solution)/shard_map/ppermute | solution.py:17
  226.3 7.2 %collective-permute-start.29 = (f32[6,1,512]{2,1,0:T(1,128)S(1)}, f32[6,1,512]{2,1,0:T(1,128)S(1)}, u32[]{:S(2)}, u32[]{:S(2)}) collective-permute-start(f32[6,1,512]{2,1,0:T(1,128)S(1)} %get-tuple-element.772), channel_id=1, source_target_pairs={{1,0},{2,1},{3,2},{4,3},{5,4},{6,5},{7,6},{8,7},{9,8},{10,9},{11,1... | collective-permute-start | bytes 36872 | tf_op jit(solution)/shard_map/ppermute | solution.py:18
  246.4 8.3 %collective-permute-start.8 = (f32[1,4,256]{2,1,0:T(4,128)S(1)}, f32[1,4,256]{2,1,0:T(4,128)S(1)}, u32[]{:S(2)}, u32[]{:S(2)}) collective-permute-start(f32[1,4,256]{2,1,0:T(4,128)S(1)} %get-tuple-element.1007), channel_id=1, source_target_pairs={{16,0},{32,16},{48,32},{64,48},{80,64},{96,80},{112,96},{128,112},... | collective-permute-start | bytes 12296 | tf_op jit(solution)/shard_map/while/body/eval_jaxpr/ppermute | solution.py:18
  252.7 7.6 %collective-permute-start.9 = (f32[1,4,256]{2,1,0:T(4,128)S(1)}, f32[1,4,256]{2,1,0:T(4,128)S(1)}, u32[]{:S(2)}, u32[]{:S(2)}) collective-permute-start(f32[1,4,256]{2,1,0:T(4,128)S(1)} %get-tuple-element.1008), channel_id=1, source_target_pairs={{0,16},{16,32},{32,48},{48,64},{64,80},{80,96},{96,112},{112,128},... | collective-permute-start | bytes 12296 | tf_op jit(solution)/shard_map/while/body/eval_jaxpr/ppermute | solution.py:17
  271.1 7.6 %collective-permute-start.13 = (f32[1,4,256]{2,1,0:T(4,128)S(1)}, f32[1,4,256]{2,1,0:T(4,128)S(1)}, u32[]{:S(2)}, u32[]{:S(2)}) collective-permute-start(f32[1,4,256]{2,1,0:T(4,128)S(1)} %get-tuple-element.1012), channel_id=1, source_target_pairs={{0,16},{16,32},{32,48},{48,64},{64,80},{80,96},{96,112},{112,128},... | collective-permute-start | bytes 12296 | tf_op jit(solution)/shard_map/while/body/eval_jaxpr/ppermute | solution.py:17
  289.0 7.6 %collective-permute-start.9 = (f32[1,4,256]{2,1,0:T(4,128)S(1)}, f32[1,4,256]{2,1,0:T(4,128)S(1)}, u32[]{:S(2)}, u32[]{:S(2)}) collective-permute-start(f32[1,4,256]{2,1,0:T(4,128)S(1)} %get-tuple-element.1008), channel_id=1, source_target_pairs={{0,16},{16,32},{32,48},{48,64},{64,80},{80,96},{96,112},{112,128},... | collective-permute-start | bytes 12296 | tf_op jit(solution)/shard_map/while/body/eval_jaxpr/ppermute | solution.py:17
  306.8 7.6 %collective-permute-start.13 = (f32[1,4,256]{2,1,0:T(4,128)S(1)}, f32[1,4,256]{2,1,0:T(4,128)S(1)}, u32[]{:S(2)}, u32[]{:S(2)}) collective-permute-start(f32[1,4,256]{2,1,0:T(4,128)S(1)} %get-tuple-element.1012), channel_id=1, source_target_pairs={{0,16},{16,32},{32,48},{48,64},{64,80},{80,96},{96,112},{112,128},... | collective-permute-start | bytes 12296 | tf_op jit(solution)/shard_map/while/body/eval_jaxpr/ppermute | solution.py:17
  324.7 7.6 %collective-permute-start.9 = (f32[1,4,256]{2,1,0:T(4,128)S(1)}, f32[1,4,256]{2,1,0:T(4,128)S(1)}, u32[]{:S(2)}, u32[]{:S(2)}) collective-permute-start(f32[1,4,256]{2,1,0:T(4,128)S(1)} %get-tuple-element.1008), channel_id=1, source_target_pairs={{0,16},{16,32},{32,48},{48,64},{64,80},{80,96},{96,112},{112,128},... | collective-permute-start | bytes 12296 | tf_op jit(solution)/shard_map/while/body/eval_jaxpr/ppermute | solution.py:17
  342.5 7.6 %collective-permute-start.13 = (f32[1,4,256]{2,1,0:T(4,128)S(1)}, f32[1,4,256]{2,1,0:T(4,128)S(1)}, u32[]{:S(2)}, u32[]{:S(2)}) collective-permute-start(f32[1,4,256]{2,1,0:T(4,128)S(1)} %get-tuple-element.1012), channel_id=1, source_target_pairs={{0,16},{16,32},{32,48},{48,64},{64,80},{80,96},{96,112},{112,128},... | collective-permute-start | bytes 12296 | tf_op jit(solution)/shard_map/while/body/eval_jaxpr/ppermute | solution.py:17
  360.3 7.6 %collective-permute-start.9 = (f32[1,4,256]{2,1,0:T(4,128)S(1)}, f32[1,4,256]{2,1,0:T(4,128)S(1)}, u32[]{:S(2)}, u32[]{:S(2)}) collective-permute-start(f32[1,4,256]{2,1,0:T(4,128)S(1)} %get-tuple-element.1008), channel_id=1, source_target_pairs={{0,16},{16,32},{32,48},{48,64},{64,80},{80,96},{96,112},{112,128},... | collective-permute-start | bytes 12296 | tf_op jit(solution)/shard_map/while/body/eval_jaxpr/ppermute | solution.py:17
  378.2 7.6 %collective-permute-start.13 = (f32[1,4,256]{2,1,0:T(4,128)S(1)}, f32[1,4,256]{2,1,0:T(4,128)S(1)}, u32[]{:S(2)}, u32[]{:S(2)}) collective-permute-start(f32[1,4,256]{2,1,0:T(4,128)S(1)} %get-tuple-element.1012), channel_id=1, source_target_pairs={{0,16},{16,32},{32,48},{48,64},{64,80},{80,96},{96,112},{112,128},... | collective-permute-start | bytes 12296 | tf_op jit(solution)/shard_map/while/body/eval_jaxpr/ppermute | solution.py:17
  394.1 11.0 %collective-permute-start.30 = (f32[1,4,256]{2,1,0:T(4,128)S(1)}, f32[1,4,256]{2,1,0:T(4,128)S(1)}, u32[]{:S(2)}, u32[]{:S(2)}) collective-permute-start(f32[1,4,256]{2,1,0:T(4,128)S(1)} %get-tuple-element.780), channel_id=1, source_target_pairs={{0,16},{16,32},{32,48},{48,64},{64,80},{80,96},{96,112},{112,128},... | collective-permute-start | bytes 12296 | tf_op jit(solution)/shard_map/ppermute | solution.py:17
  396.0 9.1 %collective-permute-start.31 = (f32[1,4,256]{2,1,0:T(4,128)S(1)}, f32[1,4,256]{2,1,0:T(4,128)S(1)}, u32[]{:S(2)}, u32[]{:S(2)}) collective-permute-start(f32[1,4,256]{2,1,0:T(4,128)S(1)} %get-tuple-element.779), channel_id=1, source_target_pairs={{16,0},{32,16},{48,32},{64,48},{80,64},{96,80},{112,96},{128,112},... | collective-permute-start | bytes 12296 | tf_op jit(solution)/shard_map/ppermute | solution.py:18
  405.2 6.8 collective-permute-start.32
  414.2 6.4 collective-permute-start.16
  418.7 7.6 %collective-permute-start.17 = (f32[1,2,128]{2,1,0:T(2,128)S(1)}, f32[1,2,128]{2,1,0:T(2,128)S(1)}, u32[]{:S(2)}, u32[]{:S(2)}) collective-permute-start(f32[1,2,128]{2,1,0:T(2,128)S(1)} %broadcast_select_fusion.8), channel_id=1, source_target_pairs={{0,16},{16,32},{32,48},{48,64},{64,80},{80,96},{96,112},{112,128},... | collective-permute-start | bytes 3080 | tf_op jit(solution)/shard_map/while/body/eval_jaxpr/ppermute | solution.py:17
  437.9 7.6 %collective-permute-start.21 = (f32[1,2,128]{2,1,0:T(2,128)S(1)}, f32[1,2,128]{2,1,0:T(2,128)S(1)}, u32[]{:S(2)}, u32[]{:S(2)}) collective-permute-start(f32[1,2,128]{2,1,0:T(2,128)S(1)} %fusion.153), channel_id=1, source_target_pairs={{0,16},{16,32},{32,48},{48,64},{64,80},{80,96},{96,112},{112,128},... | collective-permute-start | bytes 3080 | tf_op jit(solution)/shard_map/while/body/eval_jaxpr/ppermute | solution.py:17
  455.7 7.6 %collective-permute-start.17 = (f32[1,2,128]{2,1,0:T(2,128)S(1)}, f32[1,2,128]{2,1,0:T(2,128)S(1)}, u32[]{:S(2)}, u32[]{:S(2)}) collective-permute-start(f32[1,2,128]{2,1,0:T(2,128)S(1)} %broadcast_select_fusion.8), channel_id=1, source_target_pairs={{0,16},{16,32},{32,48},{48,64},{64,80},{80,96},{96,112},{112,128},... | collective-permute-start | bytes 3080 | tf_op jit(solution)/shard_map/while/body/eval_jaxpr/ppermute | solution.py:17
  473.4 7.6 %collective-permute-start.21 = (f32[1,2,128]{2,1,0:T(2,128)S(1)}, f32[1,2,128]{2,1,0:T(2,128)S(1)}, u32[]{:S(2)}, u32[]{:S(2)}) collective-permute-start(f32[1,2,128]{2,1,0:T(2,128)S(1)} %fusion.153), channel_id=1, source_target_pairs={{0,16},{16,32},{32,48},{48,64},{64,80},{80,96},{96,112},{112,128},... | collective-permute-start | bytes 3080 | tf_op jit(solution)/shard_map/while/body/eval_jaxpr/ppermute | solution.py:17
  491.1 7.6 %collective-permute-start.17 = (f32[1,2,128]{2,1,0:T(2,128)S(1)}, f32[1,2,128]{2,1,0:T(2,128)S(1)}, u32[]{:S(2)}, u32[]{:S(2)}) collective-permute-start(f32[1,2,128]{2,1,0:T(2,128)S(1)} %broadcast_select_fusion.8), channel_id=1, source_target_pairs={{0,16},{16,32},{32,48},{48,64},{64,80},{80,96},{96,112},{112,128},... | collective-permute-start | bytes 3080 | tf_op jit(solution)/shard_map/while/body/eval_jaxpr/ppermute | solution.py:17
  508.8 7.6 %collective-permute-start.21 = (f32[1,2,128]{2,1,0:T(2,128)S(1)}, f32[1,2,128]{2,1,0:T(2,128)S(1)}, u32[]{:S(2)}, u32[]{:S(2)}) collective-permute-start(f32[1,2,128]{2,1,0:T(2,128)S(1)} %fusion.153), channel_id=1, source_target_pairs={{0,16},{16,32},{32,48},{48,64},{64,80},{80,96},{96,112},{112,128},... | collective-permute-start | bytes 3080 | tf_op jit(solution)/shard_map/while/body/eval_jaxpr/ppermute | solution.py:17
  526.6 7.6 %collective-permute-start.17 = (f32[1,2,128]{2,1,0:T(2,128)S(1)}, f32[1,2,128]{2,1,0:T(2,128)S(1)}, u32[]{:S(2)}, u32[]{:S(2)}) collective-permute-start(f32[1,2,128]{2,1,0:T(2,128)S(1)} %broadcast_select_fusion.8), channel_id=1, source_target_pairs={{0,16},{16,32},{32,48},{48,64},{64,80},{80,96},{96,112},{112,128},... | collective-permute-start | bytes 3080 | tf_op jit(solution)/shard_map/while/body/eval_jaxpr/ppermute | solution.py:17
  544.3 7.6 %collective-permute-start.21 = (f32[1,2,128]{2,1,0:T(2,128)S(1)}, f32[1,2,128]{2,1,0:T(2,128)S(1)}, u32[]{:S(2)}, u32[]{:S(2)}) collective-permute-start(f32[1,2,128]{2,1,0:T(2,128)S(1)} %fusion.153), channel_id=1, source_target_pairs={{0,16},{16,32},{32,48},{48,64},{64,80},{80,96},{96,112},{112,128},... | collective-permute-start | bytes 3080 | tf_op jit(solution)/shard_map/while/body/eval_jaxpr/ppermute | solution.py:17
  562.0 7.6 %collective-permute-start.17 = (f32[1,2,128]{2,1,0:T(2,128)S(1)}, f32[1,2,128]{2,1,0:T(2,128)S(1)}, u32[]{:S(2)}, u32[]{:S(2)}) collective-permute-start(f32[1,2,128]{2,1,0:T(2,128)S(1)} %broadcast_select_fusion.8), channel_id=1, source_target_pairs={{0,16},{16,32},{32,48},{48,64},{64,80},{80,96},{96,112},{112,128},... | collective-permute-start | bytes 3080 | tf_op jit(solution)/shard_map/while/body/eval_jaxpr/ppermute | solution.py:17
  579.8 7.6 %collective-permute-start.21 = (f32[1,2,128]{2,1,0:T(2,128)S(1)}, f32[1,2,128]{2,1,0:T(2,128)S(1)}, u32[]{:S(2)}, u32[]{:S(2)}) collective-permute-start(f32[1,2,128]{2,1,0:T(2,128)S(1)} %fusion.153), channel_id=1, source_target_pairs={{0,16},{16,32},{32,48},{48,64},{64,80},{80,96},{96,112},{112,128},... | collective-permute-start | bytes 3080 | tf_op jit(solution)/shard_map/while/body/eval_jaxpr/ppermute | solution.py:17
  597.5 7.6 %collective-permute-start.17 = (f32[1,2,128]{2,1,0:T(2,128)S(1)}, f32[1,2,128]{2,1,0:T(2,128)S(1)}, u32[]{:S(2)}, u32[]{:S(2)}) collective-permute-start(f32[1,2,128]{2,1,0:T(2,128)S(1)} %broadcast_select_fusion.8), channel_id=1, source_target_pairs={{0,16},{16,32},{32,48},{48,64},{64,80},{80,96},{96,112},{112,128},... | collective-permute-start | bytes 3080 | tf_op jit(solution)/shard_map/while/body/eval_jaxpr/ppermute | solution.py:17
  615.2 7.6 %collective-permute-start.21 = (f32[1,2,128]{2,1,0:T(2,128)S(1)}, f32[1,2,128]{2,1,0:T(2,128)S(1)}, u32[]{:S(2)}, u32[]{:S(2)}) collective-permute-start(f32[1,2,128]{2,1,0:T(2,128)S(1)} %fusion.153), channel_id=1, source_target_pairs={{0,16},{16,32},{32,48},{48,64},{64,80},{80,96},{96,112},{112,128},... | collective-permute-start | bytes 3080 | tf_op jit(solution)/shard_map/while/body/eval_jaxpr/ppermute | solution.py:17
  633.0 7.6 %collective-permute-start.17 = (f32[1,2,128]{2,1,0:T(2,128)S(1)}, f32[1,2,128]{2,1,0:T(2,128)S(1)}, u32[]{:S(2)}, u32[]{:S(2)}) collective-permute-start(f32[1,2,128]{2,1,0:T(2,128)S(1)} %broadcast_select_fusion.8), channel_id=1, source_target_pairs={{0,16},{16,32},{32,48},{48,64},{64,80},{80,96},{96,112},{112,128},... | collective-permute-start | bytes 3080 | tf_op jit(solution)/shard_map/while/body/eval_jaxpr/ppermute | solution.py:17
  650.7 7.6 %collective-permute-start.21 = (f32[1,2,128]{2,1,0:T(2,128)S(1)}, f32[1,2,128]{2,1,0:T(2,128)S(1)}, u32[]{:S(2)}, u32[]{:S(2)}) collective-permute-start(f32[1,2,128]{2,1,0:T(2,128)S(1)} %fusion.153), channel_id=1, source_target_pairs={{0,16},{16,32},{32,48},{48,64},{64,80},{80,96},{96,112},{112,128},... | collective-permute-start | bytes 3080 | tf_op jit(solution)/shard_map/while/body/eval_jaxpr/ppermute | solution.py:17
  668.4 7.6 %collective-permute-start.17 = (f32[1,2,128]{2,1,0:T(2,128)S(1)}, f32[1,2,128]{2,1,0:T(2,128)S(1)}, u32[]{:S(2)}, u32[]{:S(2)}) collective-permute-start(f32[1,2,128]{2,1,0:T(2,128)S(1)} %broadcast_select_fusion.8), channel_id=1, source_target_pairs={{0,16},{16,32},{32,48},{48,64},{64,80},{80,96},{96,112},{112,128},... | collective-permute-start | bytes 3080 | tf_op jit(solution)/shard_map/while/body/eval_jaxpr/ppermute | solution.py:17
  686.1 7.6 %collective-permute-start.21 = (f32[1,2,128]{2,1,0:T(2,128)S(1)}, f32[1,2,128]{2,1,0:T(2,128)S(1)}, u32[]{:S(2)}, u32[]{:S(2)}) collective-permute-start(f32[1,2,128]{2,1,0:T(2,128)S(1)} %fusion.153), channel_id=1, source_target_pairs={{0,16},{16,32},{32,48},{48,64},{64,80},{80,96},{96,112},{112,128},... | collective-permute-start | bytes 3080 | tf_op jit(solution)/shard_map/while/body/eval_jaxpr/ppermute | solution.py:17
  (98 other events, 558.0 us)
where the time goes:
time: 708 us; the launch traced here: 704 us
  starting transfers between devices  372 us (53%)
  waiting for transfers between devices  245 us (35%)
  local copies, waits for them, and re-layouts  62.4 us (9%)
  other arithmetic  20.3 us (3%)
    ppermute x68, waiting for transfers between devices, extended(): before = lax.ppermute(last, axis, up)  243 us
    ppermute x68, starting transfers between devices, extended(): before = lax.ppermute(last, axis, up)  205 us
    ppermute x68, starting transfers between devices, extended(): after = lax.ppermute(leading, axis, down)  154 us
    reshape x6, local copies, waits for them, and re-layouts, coarsen_face(): blocks = faces.reshape(size_x // 2, 2, size_y // 2, 2, size_z // 2, 2)  33.8 us
  transfers between devices with their start and end apart: 138, of which 66 were waited for; matrix products, arithmetic and copies ran while one was open for 7% of the time, Pallas kernels for 0%

commit v1 on v0

v1 whole, which is shorter than its diff:
```python
import jax
import jax.numpy as jnp
from jax import lax
from jax.experimental import pallas as pl
from jax.experimental.pallas import tpu as pltpu
from jax.sharding import PartitionSpec as P

F32 = jnp.float32
RHS, ALPHA, BX, BY, BZ = range(5)


def shifted(values, axis, name, steps):
    count = lax.axis_size(name)
    lead, last = max(0, -steps), min(count, count - steps)
    return lax.ppermute(values, name, [(i, i + steps) for i in range(lead, last)])


def call(kernel, outs, scratch=(), smem=()):
    def run(*args):
        specs = [
            pl.BlockSpec(memory_space=pltpu.SMEM if i in smem else pltpu.VMEM)
            for i in range(len(args))
        ]
        shapes = [jax.ShapeDtypeStruct(s, F32) for s in outs]
        return pl.pallas_call(
            kernel,
            out_shape=shapes,
            in_specs=specs,
            out_specs=[pl.BlockSpec(memory_space=pltpu.VMEM)] * len(outs),
            scratch_shapes=[pltpu.VMEM(s, F32) for s in scratch],
        )(*args)

    return run


def iotas(shape):
    return lax.broadcasted_iota(jnp.int32, shape, 0), lax.broadcasted_iota(jnp.int32, shape, 1)


def even_mask(shape):
    row, lane = iotas(shape)
    return ((row + lane) & 1) == 0


def half(x):
    return pltpu.roll(x, 4, 0)


def prev_row(x):
    return pltpu.roll(x, 1, 0)


def next_row(x):
    return pltpu.roll(x, x.shape[0] - 1, 0)


def prev_lane(x):
    return pltpu.roll(x, 1, 1)


def next_lane(x):
    return pltpu.roll(x, x.shape[1] - 1, 1)


def exact_dot(a, b):
    return jnp.dot(a, b, precision=lax.Precision.HIGHEST, preferred_element_type=F32)


def one_hot(shape, test):
    row, col = iotas(shape)
    return jnp.where(test(row, col), 1.0, 0.0).astype(F32)


def low_rows(shape):
    row, _ = iotas(shape)
    return (row & 7) < 4


S_R, S_B, WP, WO_R, WO_B, YM_R, YM_B, YP_R, YP_B, ZM_R, ZM_B, ZP_R, ZP_B, I_R, I_B, D_R, D_B = range(17)


def beside(co, src, p, red, q0):
    v = src[p + 1]
    before, after = src[p], src[p + 2]
    other = jnp.where(q0, before, after) if red else jnp.where(q0, after, before)
    wo, ym, yp, zm, zp = (
        (WO_R, YM_R, YP_R, ZM_R, ZP_R) if red else (WO_B, YM_B, YP_B, ZM_B, ZP_B)
    )
    total = co[WP, p] * v + co[wo, p] * other
    total = total + (co[ym, p] * prev_row(v) + co[yp, p] * next_row(v))
    return total + (co[zm, p] * prev_lane(v) + co[zp, p] * next_lane(v))


def relax(co, dst, src, pairs, red, q0):
    s, inv = (S_R, I_R) if red else (S_B, I_B)
    for p in pairs:
        dst[p + 1] = (co[s, p] + beside(co, src, p, red, q0)) * co[inv, p]


def first_red(co, dst, pairs):
    for p in pairs:
        dst[p + 1] = co[S_R, p] * co[I_R, p]


def residual(co, r, b, p, q0):
    red = co[S_R, p] - (co[D_R, p] * r[p + 1] - beside(co, b, p, True, q0))
    black = co[S_B, p] - (co[D_B, p] * b[p + 1] - beside(co, r, p, False, q0))
    return red, black


def put_faces(co, p, q0, bx, by, bz):
    b0, b1, b2 = bx
    wo_r, wo_b = jnp.where(q0, b0, b2), jnp.where(q0, b2, b0)
    y_r, y_b = jnp.where(q0, by[0], by[1]), jnp.where(q0, by[1], by[0])
    z_r, z_b = jnp.where(q0, bz[0], bz[1]), jnp.where(q0, bz[1], bz[0])
    yp_r, yp_b = next_row(y_b), next_row(y_r)
    row, lane = iotas(q0.shape)
    first, last = lane == 0, lane == q0.shape[1] - 1
    zp_r, zp_b = jnp.where(last, 0.0, next_lane(z_b)), jnp.where(last, 0.0, next_lane(z_r))
    co[WP, p], co[WO_R, p], co[WO_B, p] = b1, wo_r, wo_b
    co[YM_R, p], co[YM_B, p] = y_r, y_b
    co[ZM_R, p], co[ZM_B, p] = jnp.where(first, 0.0, z_r), jnp.where(first, 0.0, z_b)
    co[ZP_R, p], co[ZP_B, p] = zp_r, zp_b
    return (b1 + wo_r, b1 + wo_b), (y_r, y_b), (yp_r, yp_b), (z_r + zp_r, z_b + zp_b)


def pack_rows_kernel(n_extra, left, own, right, to_low, to_high):
    arrays, planes = own.shape[0], own.shape[1]
    keep = low_rows((8, own.shape[3]))
    for a in range(arrays):
        for k, block in enumerate((left, own, right)):
            for x in range(0, planes, 2):
                t = a * (3 * planes // 2) + (k * planes + x) // 2
                e0, e1 = block[a, x], block[a, x + 1]
                to_low[t] = jnp.where(keep, e0, half(e1))
                to_high[t] = jnp.where(keep, half(e1), e0)
    if n_extra:
        base = arrays * 3 * planes // 2
        for x in range(0, planes, 2):
            e0, e1 = next_row(own[BY, x]), next_row(own[BY, x + 1])
            to_low[base + x // 2] = jnp.where(keep, e0, half(e1))


def halo_tile(from_low, from_high, t, odd, keep):
    high, low = from_high[t], from_low[t]
    if odd:
        high, low = half(high), half(low)
    return jnp.where(keep, high, low)


def fine_setup(co, left, own, right, beyond, from_low, from_high, q0):
    keep = low_rows((8, own.shape[3]))
    q0t = q0[:8]
    blocks = (left, own, right)

    def plane(a, x):
        return jnp.concatenate(
            [blocks[x // 4][a, x % 4], halo_tile(from_low, from_high, a * 6 + x // 2, x % 2, keep)], 0
        )

    bx0 = plane(BX, 0)
    for p in range(6):
        e0, e1 = plane(RHS, 2 * p), plane(RHS, 2 * p + 1)
        co[S_R, p], co[S_B, p] = jnp.where(q0, e0, e1), jnp.where(q0, e1, e0)
        b1 = plane(BX, 2 * p + 1)
        if p < 5:
            b2 = plane(BX, 2 * p + 2)
        else:
            b2 = jnp.concatenate([beyond[...], jnp.zeros_like(beyond[...])], 0)
        by = plane(BY, 2 * p), plane(BY, 2 * p + 1)
        bz = plane(BZ, 2 * p), plane(BZ, 2 * p + 1)
        fx, fy, fyp, fz = put_faces(co, p, q0, (bx0, b1, b2), by, bz)
        bx0 = b2
        yp_r, yp_b = fyp
        if p in (2, 3):
            up = from_high[30 + p - 2]
            u0, u1 = up, half(up)
            up_r, up_b = jnp.where(q0t, u0, u1), jnp.where(q0t, u1, u0)
            yp_r = jnp.concatenate([yp_r[:8], jnp.where(keep, up_r, yp_r[8:])], 0)
            yp_b = jnp.concatenate([yp_b[:8], jnp.where(keep, up_b, yp_b[8:])], 0)
        co[YP_R, p], co[YP_B, p] = yp_r, yp_b
        e0, e1 = plane(ALPHA, 2 * p), plane(ALPHA, 2 * p + 1)
        a_r, a_b = jnp.where(q0, e0, e1), jnp.where(q0, e1, e0)
        d_r = a_r + ((fx[0] + fz[0]) + (fy[0] + yp_r))
        d_b = a_b + ((fx[1] + fz[1]) + (fy[1] + yp_b))
        co[D_R, p], co[D_B, p] = d_r, d_b
        co[I_R, p] = jnp.where(a_r > 0.0, 1.0 / jnp.where(a_r > 0.0, d_r, 1.0), 0.0)
        co[I_B, p] = jnp.where(a_b > 0.0, 1.0 / jnp.where(a_b > 0.0, d_b, 1.0), 0.0)


def clear_guards(r, b, n):
    for ref in (r, b):
        ref[0] = jnp.zeros_like(ref[0])
        ref[n + 1] = jnp.zeros_like(ref[n + 1])


def fine_first_kernel(left, own, right, beyond, from_low, from_high, red_out, co, r, b):
    q0 = even_mask(r.shape[1:])
    clear_guards(r, b, 6)
    fine_setup(co, left, own, right, beyond, from_low, from_high, q0)
    first_red(co, r, range(6))
    relax(co, b, r, range(6), False, q0)
    relax(co, r, b, range(1, 5), True, q0)
    relax(co, b, r, range(1, 5), False, q0)
    relax(co, r, b, range(2, 4), True, q0)
    red_out[0, 0] = r[3][:8]
    red_out[0, 1] = r[4][:8]


def fine_second_kernel(
    left, own, right, beyond, from_low, from_high,
    red_left, red_own, red_right, red_low, red_high,
    fine_out, mid_out, own_out, co, r, b,
):
    size_z = own.shape[3]
    mid_z = size_z // 2
    q0 = even_mask(r.shape[1:])
    keep = low_rows((8, size_z))
    clear_guards(r, b, 6)
    fine_setup(co, left, own, right, beyond, from_low, from_high, q0)
    reds = (red_left, red_own, red_right)
    for p in range(6):
        tile = halo_tile(red_low, red_high, p // 2, p % 2, keep)
        r[p + 1] = jnp.concatenate([reds[p // 2][0, p % 2], tile], 0)
    relax(co, b, r, range(6), False, q0)
    relax(co, r, b, range(1, 5), True, q0)
    relax(co, b, r, range(1, 5), False, q0)
    sums = []
    for p in (2, 3):
        red, black = residual(co, r, b, p, q0)
        sums.append((red + black)[:8])
        fine_out[0, p - 2] = r[p + 1][:8]
        fine_out[1, p - 2] = b[p + 1][:8]
    z_sum = one_hot((size_z, mid_z), lambda i, j: (i >> 1) == j)
    z_even = one_hot((size_z, mid_z), lambda i, j: i == 2 * j)
    y_sum = one_hot((8, 16), lambda i, j: (j >> 1) == i)
    y_even = one_hot((8, 16), lambda i, j: j == 2 * i)
    zeros8 = jnp.zeros((8, size_z), F32)
    alphas = [own[ALPHA, 2 * i] + own[ALPHA, 2 * i + 1] for i in range(2)]
    bys = [own[BY, 2 * i] + own[BY, 2 * i + 1] for i in range(2)]
    by_next = []
    for i in range(2):
        t = BY * 6 + 2 + i
        h = from_high[t]
        by_next.append(h + half(h))
    bzs = [own[BZ, 2 * i] + own[BZ, 2 * i + 1] for i in range(2)]
    bxs = [own[BX, 0], own[BX, 2], right[BX, 0]]
    stacked = jnp.concatenate([*sums, *alphas, *bys, *by_next, *bxs, zeros8], 0)
    along_z = exact_dot(stacked, z_sum)
    bz_z = exact_dot(jnp.concatenate(bzs, 0), z_even)
    source = exact_dot(y_sum, along_z[0:16]) * 0.125
    alpha = exact_dot(y_sum, along_z[16:32]) * 0.125
    y_lower = exact_dot(y_even, along_z[32:48]) * 0.0625
    y_next = one_hot((8, 16), lambda i, j: ((i & 3) < 3) & (j == 2 * i + 2))
    y_last = one_hot((8, 16), lambda i, j: ((i & 3) == 3) & (j == 8 * (i >> 2)))
    y_upper = (exact_dot(y_next, along_z[32:48]) + exact_dot(y_last, along_z[48:64])) * 0.0625
    x_lower = exact_dot(y_sum, along_z[64:80]) * 0.0625
    x_upper = exact_dot(y_sum, along_z[72:88]) * 0.0625
    z_lower = exact_dot(y_sum, bz_z) * 0.0625
    _, lane = iotas(z_lower.shape)
    z_upper = jnp.where(lane == mid_z - 1, 0.0, next_lane(z_lower))
    diagonal = alpha + ((x_lower + x_upper) + (y_lower + y_upper) + (z_lower + z_upper))
    mid_out[0] = source
    mid_out[1] = 1.0 / diagonal
    mid_out[2] = x_lower
    mid_out[3] = y_lower
    mid_out[4] = z_lower
    own_out[0] = diagonal
    own_out[1] = alpha


def mid_setup(co, cat, low, high, q0):
    size_z = q0.shape[1]
    keep = low_rows((8, size_z))
    zero = jnp.zeros((8, size_z), F32)

    def planes(p, a):
        c, h, w = cat[p, a], high[p, a], low[p, a]
        e0 = jnp.concatenate([jnp.where(keep, c, half(h)), jnp.where(keep, zero, half(w))], 0)
        e1 = jnp.concatenate([jnp.where(keep, half(c), h), jnp.where(keep, zero, w)], 0)
        return e0, e1

    b0, b1 = planes(0, 2)
    for p in range(5):
        e0, e1 = planes(p, 0)
        co[S_R, p], co[S_B, p] = jnp.where(q0, e0, e1), jnp.where(q0, e1, e0)
        e0, e1 = planes(p, 1)
        co[I_R, p], co[I_B, p] = jnp.where(q0, e0, e1), jnp.where(q0, e1, e0)
        n0, n1 = planes(p + 1, 2) if p < 4 else (jnp.zeros_like(b0), b1)
        _, _, fyp, _ = put_faces(co, p, q0, (b0, b1, n0), planes(p, 3), planes(p, 4))
        co[YP_R, p], co[YP_B, p] = fyp
        b0, b1 = n0, n1


def mid_first_kernel(cat, low, high, red_out, co, r, b):
    q0 = even_mask(r.shape[1:])
    clear_guards(r, b, 5)
    mid_setup(co, cat, low, high, q0)
    first_red(co, r, range(5))
    relax(co, b, r, range(5), False, q0)
    relax(co, r, b, range(1, 4), True, q0)
    relax(co, b, r, range(1, 4), False, q0)
    relax(co, r, b, range(2, 3), True, q0)
    red_out[0] = r[3][:8]


def mid_second_kernel(cat, low, high, reds, reds_low, reds_high, own, level_out, low_out, co, r, b):
    size_z = r.shape[2]
    low_z = size_z // 2
    q0 = even_mask(r.shape[1:])
    keep = low_rows((8, size_z))
    clear_guards(r, b, 5)
    mid_setup(co, cat, low, high, q0)
    for p in range(5):
        tile0 = jnp.where(keep, reds[p], half(reds_high[p]))
        tile1 = jnp.where(keep, 0.0, half(reds_low[p]))
        r[p + 1] = jnp.concatenate([tile0, tile1], 0)
    d0, d1 = own[0], half(own[0])
    d0, d1 = jnp.concatenate([d0, d0], 0), jnp.concatenate([d1, d1], 0)
    co[D_R, 2], co[D_B, 2] = jnp.where(q0, d0, d1), jnp.where(q0, d1, d0)
    relax(co, b, r, range(5), False, q0)
    relax(co, r, b, range(1, 4), True, q0)
    relax(co, b, r, range(1, 4), False, q0)
    red, black = residual(co, r, b, 2, q0)
    level_out[0] = r[3][:8]
    level_out[1] = b[3][:8]
    z_sum = one_hot((size_z, low_z), lambda i, j: (i >> 1) == j)
    z_even = one_hot((size_z, low_z), lambda i, j: i == 2 * j)
    res = (red + black)[:8]
    mine = cat[2]
    alpha, bx, by, bz = own[1], mine[2], mine[3], mine[4]
    along_z = exact_dot(jnp.concatenate([res, alpha, bx, by], 0), z_sum)
    bz_z = exact_dot(bz, z_even)

    def rows(out_row, test):
        return one_hot((16, 8), lambda i, j: ((i >> 1) == out_row) & test(i & 1, j))

    total = exact_dot(rows(0, lambda i, j: (j < 4) & ((j >> 1) == i)), along_z[0:8]) * 0.125
    total += exact_dot(rows(1, lambda i, j: ((j & 3) >> 1) == i), along_z[8:16]) * 0.125
    total += exact_dot(rows(2, lambda i, j: (j < 4) & ((j >> 1) == i)), along_z[16:24]) * 0.0625
    total += exact_dot(rows(3, lambda i, j: (j & 3) == 2 * i), along_z[24:32]) * 0.0625
    total += exact_dot(rows(4, lambda i, j: ((j & 3) >> 1) == i), bz_z) * 0.0625
    for j in range(low_out.shape[0]):
        low_out[j] = total


WINDOW = 40


def window_kernel(width, index, gathered, out):
    blocks, rows, size_z = gathered.shape
    size_y = 2 * blocks
    flat = gathered[...].reshape(blocks * rows, size_z)

    def test(i, j):
        k, y = i // size_y, i % size_y
        return j == (y // 2) * rows + 2 * k + y % 2

    planes = exact_dot(one_hot((5 * size_y, blocks * rows), test), flat)
    start = index[0] * width - 16
    planes = pltpu.roll(planes, lax.rem(2 * size_z - start, size_z), 1)
    _, lane = iotas(planes.shape)
    inside = (lane < WINDOW) & (lane + start >= 0) & (lane + start < size_z)
    planes = jnp.where(inside, planes, 0.0)
    parts = [planes[k * size_y : (k + 1) * size_y] for k in range(5)]
    tile0 = parts[0] + pltpu.roll(parts[1], WINDOW, 1) + pltpu.roll(parts[2], 2 * WINDOW, 1)
    tile1 = parts[3] + pltpu.roll(parts[4], WINDOW, 1)
    for g in range(out.shape[0]):
        out[g, :size_y] = tile0
        out[g, size_y:] = tile1


def coarse_kernel(width, sweeps, index, gathered, out, co, r, b):
    size_x, size_y = gathered.shape[0], gathered.shape[1] // 2
    lanes = gathered.shape[2]
    pairs = size_x // 2
    shape = (size_y, lanes)
    q0 = even_mask(shape)
    row, lane = iotas(shape)
    r[...] = jnp.zeros_like(r)
    b[...] = jnp.zeros_like(b)

    def setup(p, carry):
        x = 2 * p
        t0, t1 = gathered[x], gathered[x + 1]
        f0, g0, f1, g1 = t0[:size_y], t0[size_y:], t1[:size_y], t1[size_y:]
        after = gathered[jnp.minimum(x + 2, size_x - 1)][:size_y]
        after = jnp.where(x + 2 < size_x, after, 0.0)

        def at(tile, k):
            return jnp.where(lane < WINDOW, pltpu.roll(tile, (lanes - k * WINDOW) % lanes, 1) if k else tile, 0.0)

        s0, s1 = at(f0, 0), at(f1, 0)
        a0, a1 = at(f0, 1), at(f1, 1)
        co[S_R, p], co[S_B, p] = jnp.where(q0, s0, s1), jnp.where(q0, s1, s0)
        a_r, a_b = jnp.where(q0, a0, a1), jnp.where(q0, a1, a0)
        fx, fy, fyp, fz = put_faces(
            co, p, q0, (at(f0, 2), at(f1, 2), at(after, 2)), (at(g0, 0), at(g1, 0)), (at(g0, 1), at(g1, 1))
        )
        yp_r = jnp.where(row == size_y - 1, 0.0, fyp[0])
        yp_b = jnp.where(row == size_y - 1, 0.0, fyp[1])
        co[YP_R, p], co[YP_B, p] = yp_r, yp_b
        co[YM_R, p], co[YM_B, p] = jnp.where(row == 0, 0.0, fy[0]), jnp.where(row == 0, 0.0, fy[1])
        d_r = a_r + ((fx[0] + fz[0]) + (fy[0] + yp_r))
        d_b = a_b + ((fx[1] + fz[1]) + (fy[1] + yp_b))
        co[I_R, p] = jnp.where(a_r > 0.0, 1.0 / jnp.where(a_r > 0.0, d_r, 1.0), 0.0)
        co[I_B, p] = jnp.where(a_b > 0.0, 1.0 / jnp.where(a_b > 0.0, d_b, 1.0), 0.0)
        return carry

    lax.fori_loop(0, pairs, setup, 0)

    def sweep(step, carry):
        relax(co, r, b, range(pairs), True, q0)
        relax(co, b, r, range(pairs), False, q0)
        return carry

    lax.fori_loop(0, sweeps, sweep, 0)
    gx, gy = index[1], index[0]
    pair = gx // 2 + 1
    pick = ((row + lane + gx) & 1) == 0
    plane = jnp.where(pick, r[pair], b[pair])
    start = gy * width - 16
    plane = pltpu.roll(plane, lax.rem(start + lanes, lanes), 1)
    plane = jnp.where((lane >= gy * width) & (lane < (gy + 1) * width), plane, 0.0)
    for j in range(out.shape[0]):
        first = 8 * (2 * j // 8)
        out[j] = plane[first : first + 8]


def finish_kernel(index, pieces, level, fine, fine_out, coarse_out):
    total = pieces[0]
    for j in range(1, pieces.shape[0]):
        total = total + pieces[j]
    start = lax.rem(2 * index[0], 8)
    coarse_out[0] = exact_dot(one_hot((8, 8), lambda i, j: j == i + start), total)[:2]
    low_z, mid_z, size_z = pieces.shape[2], level.shape[2], fine.shape[3]
    up = exact_dot(one_hot((8, 8), lambda i, j: (j == start + (i >> 1)) & (i < 4)), total)
    up = exact_dot(up, one_hot((low_z, mid_z), lambda i, j: (j >> 1) == i))
    red, black = level[0] + up, level[1] + up
    q0 = even_mask((8, mid_z))
    mid = jnp.concatenate([jnp.where(q0, red, black), jnp.where(q0, black, red)], 0)
    wide = exact_dot(mid, one_hot((mid_z, size_z), lambda i, j: (j >> 1) == i))
    spread = one_hot((16, 16), lambda i, j: j == 8 * (i >> 3) + ((i & 7) >> 1))
    wide = exact_dot(spread, wide)
    q0 = even_mask((8, size_z))
    for i in range(2):
        add = wide[8 * i : 8 * i + 8]
        red, black = fine[0, i] + add, fine[1, i] + add
        fine_out[2 * i] = jnp.where(q0, red, black)
        fine_out[2 * i + 1] = jnp.where(q0, black, red)


def on_device(rhs, alpha, beta_x, beta_y, beta_z):
    size_z = rhs.shape[2]
    mid_z, low_z = size_z // 2, size_z // 4
    count_x, count_y = lax.axis_size("gx"), lax.axis_size("gy")
    index = jnp.stack([lax.axis_index("gy"), lax.axis_index("gx")]).astype(jnp.int32)
    own = jnp.stack([rhs, alpha, beta_x, beta_y, beta_z])
    beyond = shifted(beta_x[0], 0, "gx", -2)
    left, right = shifted(own, 1, "gx", 1), shifted(own, 1, "gx", -1)
    to_low, to_high = call(
        lambda *refs: pack_rows_kernel(2, *refs), [(32, 8, size_z), (30, 8, size_z)]
    )(left, own, right)
    from_high, from_low = shifted(to_low, 2, "gy", -1), shifted(to_high, 2, "gy", 1)
    fine_args = (left, own, right, beyond, from_low, from_high)
    scratch = [(17, 6, 16, size_z), (8, 16, size_z), (8, 16, size_z)]
    (red,) = call(fine_first_kernel, [(1, 2, 8, size_z)], scratch)(*fine_args)
    red_left, red_right = shifted(red, 1, "gx", 1), shifted(red, 1, "gx", -1)
    to_low, to_high = call(
        lambda *refs: pack_rows_kernel(0, *refs), [(3, 8, size_z), (3, 8, size_z)]
    )(red_left, red, red_right)
    red_high, red_low = shifted(to_low, 2, "gy", -1), shifted(to_high, 2, "gy", 1)
    fine, mid, mid_own = call(
        fine_second_kernel, [(2, 2, 8, size_z), (5, 8, mid_z), (2, 8, mid_z)], scratch
    )(*fine_args, red_left, red, red_right, red_low, red_high)

    cat = jnp.stack([shifted(mid, 0, "gx", 2), shifted(mid, 0, "gx", 1), mid, shifted(mid, 0, "gx", -1), shifted(mid, 0, "gx", -2)])
    mid_args = (cat, shifted(cat, 0, "gy", 1), shifted(cat, 0, "gy", -1))
    scratch = [(17, 5, 16, mid_z), (7, 16, mid_z), (7, 16, mid_z)]
    (red,) = call(mid_first_kernel, [(1, 8, mid_z)], scratch)(*mid_args)
    reds = jnp.concatenate([shifted(red, 0, "gx", 2), shifted(red, 0, "gx", 1), red, shifted(red, 0, "gx", -1), shifted(red, 0, "gx", -2)])
    level, low = call(
        mid_second_kernel, [(2, 8, mid_z), (count_y, 16, low_z)], scratch
    )(*mid_args, reds, shifted(reds, 0, "gy", 1), shifted(reds, 0, "gy", -1), mid_own)

    low = lax.all_to_all(low, "gy", 0, 0, tiled=True)
    size_y = 2 * count_y
    width = low_z // count_y
    (low,) = call(
        lambda *refs: window_kernel(width, *refs), [(count_x, 2 * size_y, low_z)], smem=(0,)
    )(index, low)
    low = lax.all_to_all(low, "gx", 0, 0, tiled=True)
    pairs = count_x // 2
    (pieces,) = call(
        lambda *refs: coarse_kernel(width, 8, *refs),
        [(count_y, 8, low_z)],
        [(17, pairs, size_y, low_z), (pairs + 2, size_y, low_z), (pairs + 2, size_y, low_z)],
        smem=(0,),
    )(index, low)
    pieces = lax.all_to_all(pieces, "gy", 0, 0, tiled=True)
    fine_solution, coarse = call(
        finish_kernel, [rhs.shape, (1, 2, low_z)], smem=(0,)
    )(index, pieces, level, fine)
    return fine_solution, coarse


def solution(mesh):
    placed = P("gx", "gy", None)
    return jax.shard_map(
        on_device,
        mesh=mesh,
        in_specs=(placed,) * 5,
        out_specs=(placed, placed),
        check_vma=False,
    )
```

time: 708 us -> 213 us (0.30)
  the two profiles are of different devices: /device:TPU:38 before, /device:TPU:1 now
where the time goes in v1:
time: 213 us; the launch traced here: 211 us
  starting transfers between devices  72.3 us (34%)
  blocking collectives  51.7 us (24%)
  waiting for transfers between devices  48.1 us (23%)
  Pallas kernels  27.4 us (13%)
  local copies, waits for them, and re-layouts  10.4 us (5%)
    ppermute x21, starting transfers between devices, shifted(): lax.ppermute(values, name, [(i, i + steps) for i in range(lead, last)])  63.1 us
    ppermute x21, waiting for transfers between devices, shifted(): lax.ppermute(values, name, [(i, i + steps) for i in range(lead, last)])  39.8 us
    all_to_all x1, blocking collectives, on_device(): low = lax.all_to_all(low, 'gx', 0, 0, tiled=True)  36.3 us
    pallas_call x9, Pallas kernels, run(): pl.pallas_call(kernel, out_shape=shapes, in_specs=specs, out_specs=[pl.Bl...  27.4 us
    all_to_all x1, blocking collectives, on_device(): pieces = lax.all_to_all(pieces, 'gy', 0, 0, tiled=True)  15.4 us
    unnamed x58, local copies, waits for them, and re-layouts  10.3 us
    all_to_all x1, starting transfers between devices, on_device(): low = lax.all_to_all(low, 'gy', 0, 0, tiled=True)  9.24 us
    all_to_all x1, waiting for transfers between devices, on_device(): low = lax.all_to_all(low, 'gy', 0, 0, tiled=True)  8.31 us
  transfers between devices with their start and end apart: 22, of which 13 were waited for; matrix products, arithmetic and copies ran while one was open for 0% of the time, Pallas kernels for 0%

profile of v1, /device:TPU:1, one launch (start us, length us, event | category | flops | bytes accessed | tf_op | source)
XLA Modules:
  0.0 211.4 jit_solution(9869182953433010993)
XLA Ops:
  0.6 0.9 bitcast_dynamic-update-slice_fusion.4
  2.4 0.8 copy-done.14
  3.2 0.8 copy-done.15
  4.1 4.8 %collective-permute-start = (f32[5,4,8,512]{3,2,1,0:T(8,128)S(1)}, f32[5,4,8,512]{3,2,1,0:T(8,128)S(1)}, u32[]{:S(2)}, u32[]{:S(2)}) collective-permute-start(f32[5,4,8,512]{3,2,1,0:T(8,128)S(1)} %bitcast_dynamic-update-slice_fusion.refs_1_.own), channel_id=1, source_target_pairs={{0,16},{16,32},{32,48},{48,64},{64,80},{80,96},{96,112},{112,128},... | collective-permute-start | bytes 983048 | tf_op jit(solution)/shard_map/ppermute | solution.py:15
  8.9 1.3 collective-permute-start.1
  10.2 2.7 %collective-permute-done.refs_0_.left = f32[5,4,8,512]{3,2,1,0:T(8,128)S(1)} collective-permute-done((f32[5,4,8,512]{3,2,1,0:T(8,128)S(1)}, f32[5,4,8,512]{3,2,1,0:T(8,128)S(1)}, u32[]{:S(2)}, u32[]{:S(2)}) %collective-permute-start) | collective-permute-done | bytes 327712 | tf_op jit(solution)/shard_map/ppermute | solution.py:15
  12.9 5.1 %collective-permute-done.1.refs_2_.right = f32[5,4,8,512]{3,2,1,0:T(8,128)S(1)} collective-permute-done((f32[5,4,8,512]{3,2,1,0:T(8,128)S(1)}, f32[5,4,8,512]{3,2,1,0:T(8,128)S(1)}, u32[]{:S(2)}, u32[]{:S(2)}) %collective-permute-start.1) | collective-permute-done | bytes 327712 | tf_op jit(solution)/shard_map/ppermute | solution.py:15
  18.7 2.2 %shard_map.68 = (f32[32,8,512]{2,1,0:T(8,128)}, f32[30,8,512]{2,1,0:T(8,128)}) custom-call(f32[5,4,8,512]{3,2,1,0:T(8,128)} %copy-done.1, f32[5,4,8,512]{3,2,1,0:T(8,128)} %copy-done, f32[5,4,8,512]{3,2,1,0:T(8,128)} %copy-done.2), custom_call_target="tpu_custom_call" | custom-call | tf_op jit(solution)/shard_map/pallas_call | solution.py:25
  20.9 5.4 %collective-permute-start.4 = (f32[32,8,512]{2,1,0:T(8,128)}, f32[32,8,512]{2,1,0:T(8,128)S(1)}, u32[]{:S(2)}, u32[]{:S(2)}) collective-permute-start(f32[32,8,512]{2,1,0:T(8,128)} %get-tuple-element.12), channel_id=1, source_target_pairs={{1,0},{2,1},{3,2},{4,3},{5,4},{6,5},{7,6},{8,7},{9,8},{10,9},{11,1... | collective-permute-start | bytes 1572872 | tf_op jit(solution)/shard_map/ppermute | solution.py:15
  26.4 3.1 %collective-permute-start.3 = (f32[30,8,512]{2,1,0:T(8,128)}, f32[30,8,512]{2,1,0:T(8,128)S(1)}, u32[]{:S(2)}, u32[]{:S(2)}) collective-permute-start(f32[30,8,512]{2,1,0:T(8,128)} %get-tuple-element.11), channel_id=1, source_target_pairs={{0,1},{1,2},{2,3},{3,4},{4,5},{5,6},{6,7},{7,8},{8,9},{9,10},{10,1... | collective-permute-start | bytes 1474568 | tf_op jit(solution)/shard_map/ppermute | solution.py:15
  29.5 1.3 collective-permute-start.2
  30.8 6.8 %collective-permute-done.2.beyond = f32[8,512]{1,0:T(8,128)S(1)} collective-permute-done((f32[8,512]{1,0:T(8,128)S(1)}, f32[8,512]{1,0:T(8,128)S(1)}, u32[]{:S(2)}, u32[]{:S(2)}) %collective-permute-start.2) | collective-permute-done | bytes 16416 | tf_op jit(solution)/shard_map/ppermute | solution.py:15
  39.3 2.8 %shard_map.69.refs_1_.red_own = f32[1,2,8,512]{3,2,1,0:T(8,128)} custom-call(f32[5,4,8,512]{3,2,1,0:T(8,128)} %copy-done.1, f32[5,4,8,512]{3,2,1,0:T(8,128)} %copy-done, f32[5,4,8,512]{3,2,1,0:T(8,128)} %copy-done.2, f32[8,512]{1,0:T(8,128)} %copy-done.12, f32[30,8,512]{2,1,0:T(8,128)} %copy-done.4, f32[32,8,512]{2,1,0:T(8,128)} %copy-done.3), custom_call_target="tpu_custom_call" | custom-call | tf_op jit(solution)/shard_map/pallas_call | solution.py:25
  42.1 4.6 %collective-permute-start.5 = (f32[1,2,8,512]{3,2,1,0:T(8,128)}, f32[1,2,8,512]{3,2,1,0:T(8,128)S(1)}, u32[]{:S(2)}, u32[]{:S(2)}) collective-permute-start(f32[1,2,8,512]{3,2,1,0:T(8,128)} %shard_map.69.refs_1_.red_own), channel_id=1, source_target_pairs={{0,16},{16,32},{32,48},{48,64},{64,80},{80,96},{96,112},{112,128},... | collective-permute-start | bytes 98312 | tf_op jit(solution)/shard_map/ppermute | solution.py:15
  46.7 1.3 collective-permute-start.6
  48.0 3.5 %collective-permute-done.6.refs_2_.red_right = f32[1,2,8,512]{3,2,1,0:T(8,128)S(1)} collective-permute-done((f32[1,2,8,512]{3,2,1,0:T(8,128)}, f32[1,2,8,512]{3,2,1,0:T(8,128)S(1)}, u32[]{:S(2)}, u32[]{:S(2)}) %collective-permute-start.6) | collective-permute-done | bytes 32800 | tf_op jit(solution)/shard_map/ppermute | solution.py:15
  52.1 1.4 shard_map.70
  53.6 4.7 %collective-permute-start.7 = (f32[3,8,512]{2,1,0:T(8,128)}, f32[3,8,512]{2,1,0:T(8,128)S(1)}, u32[]{:S(2)}, u32[]{:S(2)}) collective-permute-start(f32[3,8,512]{2,1,0:T(8,128)} %get-tuple-element.13), channel_id=1, source_target_pairs={{0,1},{1,2},{2,3},{3,4},{4,5},{5,6},{6,7},{7,8},{8,9},{9,10},{10,1... | collective-permute-start | bytes 147464 | tf_op jit(solution)/shard_map/ppermute | solution.py:15
  58.3 1.9 collective-permute-start.8
  60.2 3.7 %collective-permute-done.8.red_high = f32[3,8,512]{2,1,0:T(8,128)S(1)} collective-permute-done((f32[3,8,512]{2,1,0:T(8,128)}, f32[3,8,512]{2,1,0:T(8,128)S(1)}, u32[]{:S(2)}, u32[]{:S(2)}) %collective-permute-start.8) | collective-permute-done | bytes 49184 | tf_op jit(solution)/shard_map/ppermute | solution.py:15
  64.5 4.0 %shard_map.71 = (f32[2,2,8,512]{3,2,1,0:T(8,128)}, f32[5,8,256]{2,1,0:T(8,128)}, f32[2,8,256]{2,1,0:T(8,128)}) custom-call(f32[5,4,8,512]{3,2,1,0:T(8,128)} %copy-done.1, f32[5,4,8,512]{3,2,1,0:T(8,128)} %copy-done, f32[5,4,8,512]{3,2,1,0:T(8,128)} %copy-done.2, f32[8,512]{1,0:T(8,128)} %copy-done.12, f32[30,8,512]{2,1,0:T(8,128)} %copy-done.4, ...), custom_call_target="tpu_custom_call" | custom-call | tf_op jit(solution)/shard_map/pallas_call | solution.py:25
  68.5 5.9 %collective-permute-start.9 = (f32[5,8,256]{2,1,0:T(8,128)}, f32[5,8,256]{2,1,0:T(8,128)S(1)}, u32[]{:S(2)}, u32[]{:S(2)}) collective-permute-start(f32[5,8,256]{2,1,0:T(8,128)} %get-tuple-element.15), channel_id=1, source_target_pairs={{0,32},{16,48},{32,64},{48,80},{64,96},{80,112},{96,128},{112,144}... | collective-permute-start | bytes 122888 | tf_op jit(solution)/shard_map/ppermute | solution.py:15
  74.4 3.1 %collective-permute-start.10 = (f32[5,8,256]{2,1,0:T(8,128)}, f32[5,8,256]{2,1,0:T(8,128)S(1)}, u32[]{:S(2)}, u32[]{:S(2)}) collective-permute-start(f32[5,8,256]{2,1,0:T(8,128)} %get-tuple-element.15), channel_id=1, source_target_pairs={{0,16},{16,32},{32,48},{48,64},{64,80},{80,96},{96,112},{112,128},... | collective-permute-start | bytes 122888 | tf_op jit(solution)/shard_map/ppermute | solution.py:15
  77.5 1.3 collective-permute-start.11
  78.8 1.3 collective-permute-start.12
  80.9 1.5 collective-permute-done.11
  82.5 2.5 %collective-permute-done.12 = f32[5,8,256]{2,1,0:T(8,128)S(1)} collective-permute-done((f32[5,8,256]{2,1,0:T(8,128)}, f32[5,8,256]{2,1,0:T(8,128)S(1)}, u32[]{:S(2)}, u32[]{:S(2)}) %collective-permute-start.12) | collective-permute-done | bytes 40992 | tf_op jit(solution)/shard_map/ppermute | solution.py:15
  85.0 3.5 %collective-permute-start.13 = (f32[5,5,8,256]{3,2,1,0:T(8,128)S(1)}, f32[5,5,8,256]{3,2,1,0:T(8,128)S(1)}, u32[]{:S(2)}, u32[]{:S(2)}) collective-permute-start(f32[5,5,8,256]{3,2,1,0:T(8,128)S(1)} %bitcast_dynamic-update-slice_fusion.5.cat), channel_id=1, source_target_pairs={{0,1},{1,2},{2,3},{3,4},{4,5},{5,6},{6,7},{7,8},{8,9},{9,10},{10,1... | collective-permute-start | bytes 614408 | tf_op jit(solution)/shard_map/ppermute | solution.py:15
  88.5 1.9 collective-permute-start.14
  91.2 4.4 %collective-permute-done.14.high = f32[5,5,8,256]{3,2,1,0:T(8,128)S(1)} collective-permute-done((f32[5,5,8,256]{3,2,1,0:T(8,128)S(1)}, f32[5,5,8,256]{3,2,1,0:T(8,128)S(1)}, u32[]{:S(2)}, u32[]{:S(2)}) %collective-permute-start.14) | collective-permute-done | bytes 204832 | tf_op jit(solution)/shard_map/ppermute | solution.py:15
  96.2 2.0 shard_map.72
  98.3 6.6 %collective-permute-start.15 = (f32[1,8,256]{2,1,0:T(8,128)}, f32[1,8,256]{2,1,0:T(8,128)S(1)}, u32[]{:S(2)}, u32[]{:S(2)}) collective-permute-start(f32[1,8,256]{2,1,0:T(8,128)} %shard_map.72), channel_id=1, source_target_pairs={{0,32},{16,48},{32,64},{48,80},{64,96},{80,112},{96,128},{112,144}... | collective-permute-start | bytes 24584 | tf_op jit(solution)/shard_map/ppermute | solution.py:15
  104.8 3.1 %collective-permute-start.16 = (f32[1,8,256]{2,1,0:T(8,128)}, f32[1,8,256]{2,1,0:T(8,128)S(1)}, u32[]{:S(2)}, u32[]{:S(2)}) collective-permute-start(f32[1,8,256]{2,1,0:T(8,128)} %shard_map.72), channel_id=1, source_target_pairs={{0,16},{16,32},{32,48},{48,64},{64,80},{80,96},{96,112},{112,128},... | collective-permute-start | bytes 24584 | tf_op jit(solution)/shard_map/ppermute | solution.py:15
  107.9 1.3 collective-permute-start.17
  109.2 1.3 collective-permute-start.18
  111.2 2.6 %collective-permute-done.17 = f32[1,8,256]{2,1,0:T(8,128)S(1)} collective-permute-done((f32[1,8,256]{2,1,0:T(8,128)}, f32[1,8,256]{2,1,0:T(8,128)S(1)}, u32[]{:S(2)}, u32[]{:S(2)}) %collective-permute-start.17) | collective-permute-done | bytes 8224 | tf_op jit(solution)/shard_map/ppermute | solution.py:15
  113.9 2.8 %collective-permute-done.18 = f32[1,8,256]{2,1,0:T(8,128)S(1)} collective-permute-done((f32[1,8,256]{2,1,0:T(8,128)}, f32[1,8,256]{2,1,0:T(8,128)S(1)}, u32[]{:S(2)}, u32[]{:S(2)}) %collective-permute-start.18) | collective-permute-done | bytes 8224 | tf_op jit(solution)/shard_map/ppermute | solution.py:15
  116.7 3.4 %collective-permute-start.19 = (f32[5,8,256]{2,1,0:T(8,128)S(1)}, f32[5,8,256]{2,1,0:T(8,128)S(1)}, u32[]{:S(2)}, u32[]{:S(2)}) collective-permute-start(f32[5,8,256]{2,1,0:T(8,128)S(1)} %constant_dynamic-update-slice_fusion.reds), channel_id=1, source_target_pairs={{0,1},{1,2},{2,3},{3,4},{4,5},{5,6},{6,7},{7,8},{8,9},{9,10},{10,1... | collective-permute-start | bytes 122888 | tf_op jit(solution)/shard_map/ppermute | solution.py:15
  120.1 1.9 collective-permute-start.20
  122.1 3.4 %collective-permute-done.20.reds_high = f32[5,8,256]{2,1,0:T(8,128)S(1)} collective-permute-done((f32[5,8,256]{2,1,0:T(8,128)S(1)}, f32[5,8,256]{2,1,0:T(8,128)S(1)}, u32[]{:S(2)}, u32[]{:S(2)}) %collective-permute-start.20) | collective-permute-done | bytes 40992 | tf_op jit(solution)/shard_map/ppermute | solution.py:15
  126.1 2.5 %shard_map.73 = (f32[2,8,256]{2,1,0:T(8,128)}, f32[16,16,128]{2,1,0:T(8,128)}) custom-call(f32[5,5,8,256]{3,2,1,0:T(8,128)} %copy-done.5, f32[5,5,8,256]{3,2,1,0:T(8,128)} %copy-done.6, f32[5,5,8,256]{3,2,1,0:T(8,128)} %copy-done.7, f32[5,8,256]{2,1,0:T(8,128)} %copy-done.16, f32[5,8,256]{2,1,0:T(8,128)} %copy-done.19, f32[5,8,256]{2,1,0:T(8,128)} %copy-done.20, ...), custom_call_target="tpu_custom_call" | custom-call | tf_op jit(solution)/shard_map/pallas_call | solution.py:25
  128.6 9.2 %all-to-all-start = ((f32[16,16,128]{2,1,0:T(8,128)}), f32[16,16,128]{2,1,0:T(8,128)S(1)}, u32[]{:S(2)}, u32[]{:S(2)}) async-start(f32[16,16,128]{2,1,0:T(8,128)} %get-tuple-element.17), calls=%async_computation | async-start | bytes 262144 | tf_op jit(solution)/shard_map/all_to_all | solution.py:486
  138.4 8.3 %all-to-all-done.refs_1_ = f32[16,16,128]{2,1,0:T(8,128)S(1)} async-done(((f32[16,16,128]{2,1,0:T(8,128)}), f32[16,16,128]{2,1,0:T(8,128)S(1)}, u32[]{:S(2)}, u32[]{:S(2)}) %all-to-all-start) | async-done | bytes 131104 | tf_op jit(solution)/shard_map/all_to_all | solution.py:486
  147.4 2.5 %shard_map.74 = f32[32,64,128]{2,1,0:T(8,128)} custom-call(s32[2]{0:T(128)} %pad_add_fusion.refs_0_.index, f32[16,16,128]{2,1,0:T(8,128)} %copy-done.8), custom_call_target="tpu_custom_call" | custom-call | tf_op jit(solution)/shard_map/pallas_call | solution.py:25
  149.8 36.3 %all_to_all.15.refs_1_ = f32[32,64,128]{2,1,0:T(8,128)} all-to-all(f32[32,64,128]{2,1,0:T(8,128)} %shard_map.74), channel_id=1, replica_groups=mesh['gx'=32,'gy'=16] {'gx'}, dimensions={0} | all-to-all | bytes 2097152 | tf_op jit(solution)/shard_map/all_to_all | solution.py:492
  186.2 7.5 %shard_map.75 = f32[16,8,128]{2,1,0:T(8,128)} custom-call(s32[2]{0:T(128)} %pad_add_fusion.refs_0_.index, f32[32,64,128]{2,1,0:T(8,128)} %all_to_all.15.refs_1_), custom_call_target="tpu_custom_call" | custom-call | tf_op jit(solution)/shard_map/pallas_call | solution.py:25
  193.7 15.4 %all_to_all.16.pieces = f32[16,8,128]{2,1,0:T(8,128)} all-to-all(f32[16,8,128]{2,1,0:T(8,128)} %shard_map.75), channel_id=1, replica_groups=mesh['gx'=32,'gy'=16] {'gy'}, dimensions={0} | all-to-all | bytes 131072 | tf_op jit(solution)/shard_map/all_to_all | solution.py:500
  209.1 2.4 %shard_map.76 = (f32[4,8,512]{2,1,0:T(8,128)}, f32[1,2,128]{2,1,0:T(2,128)}) custom-call(s32[2]{0:T(128)} %pad_add_fusion.refs_0_.index, f32[16,8,128]{2,1,0:T(8,128)} %all_to_all.16.pieces, f32[2,8,256]{2,1,0:T(8,128)} %get-tuple-element.18.level, f32[2,2,8,512]{3,2,1,0:T(8,128)} %get-tuple-element.19.fine), custom_call_target="tpu_custom_call" | custom-call | tf_op jit(solution)/shard_map/pallas_call | solution.py:25
  (70 shorter events, 9.2 us)
Async XLA Ops:
  0.6 0.9 copy-start.13
  1.5 0.8 copy-start.11
  2.4 0.8 copy-start.14
  3.2 0.8 copy-start.15
  4.0 13.9 %copy-start = (f32[5,4,8,512]{3,2,1,0:T(8,128)}, f32[5,4,8,512]{3,2,1,0:T(8,128)S(1)}, u32[]{:S(2)}) copy-start(f32[5,4,8,512]{3,2,1,0:T(8,128)S(1)} %bitcast_dynamic-update-slice_fusion.refs_1_.own) | copy-start | bytes 983044
  4.1 8.8 %collective-permute-start = (f32[5,4,8,512]{3,2,1,0:T(8,128)S(1)}, f32[5,4,8,512]{3,2,1,0:T(8,128)S(1)}, u32[]{:S(2)}, u32[]{:S(2)}) collective-permute-start(f32[5,4,8,512]{3,2,1,0:T(8,128)S(1)} %bitcast_dynamic-update-slice_fusion.refs_1_.own), channel_id=1, source_target_pairs={{0,16},{16,32},{32,48},{48,64},{64,80},{80,96},{96,112},{112,128},... | collective-permute-start | bytes 983048 | tf_op jit(solution)/shard_map/ppermute | solution.py:15
  8.9 9.1 %collective-permute-start.1 = (f32[5,4,8,512]{3,2,1,0:T(8,128)S(1)}, f32[5,4,8,512]{3,2,1,0:T(8,128)S(1)}, u32[]{:S(2)}, u32[]{:S(2)}) collective-permute-start(f32[5,4,8,512]{3,2,1,0:T(8,128)S(1)} %bitcast_dynamic-update-slice_fusion.refs_1_.own), channel_id=1, source_target_pairs={{16,0},{32,16},{48,32},{64,48},{80,64},{96,80},{112,96},{128,112},... | collective-permute-start | bytes 983048 | tf_op jit(solution)/shard_map/ppermute | solution.py:15
  12.9 5.1 %copy-start.1 = (f32[5,4,8,512]{3,2,1,0:T(8,128)}, f32[5,4,8,512]{3,2,1,0:T(8,128)S(1)}, u32[]{:S(2)}) copy-start(f32[5,4,8,512]{3,2,1,0:T(8,128)S(1)} %collective-permute-done.refs_0_.left) | copy-start | bytes 983044
  18.0 0.7 copy-start.2
  20.9 16.7 %collective-permute-start.4 = (f32[32,8,512]{2,1,0:T(8,128)}, f32[32,8,512]{2,1,0:T(8,128)S(1)}, u32[]{:S(2)}, u32[]{:S(2)}) collective-permute-start(f32[32,8,512]{2,1,0:T(8,128)} %get-tuple-element.12), channel_id=1, source_target_pairs={{1,0},{2,1},{3,2},{4,3},{5,4},{6,5},{7,6},{8,7},{9,8},{10,9},{11,1... | collective-permute-start | bytes 1572872 | tf_op jit(solution)/shard_map/ppermute | solution.py:15
  26.4 11.3 %collective-permute-start.3 = (f32[30,8,512]{2,1,0:T(8,128)}, f32[30,8,512]{2,1,0:T(8,128)S(1)}, u32[]{:S(2)}, u32[]{:S(2)}) collective-permute-start(f32[30,8,512]{2,1,0:T(8,128)} %get-tuple-element.11), channel_id=1, source_target_pairs={{0,1},{1,2},{2,3},{3,4},{4,5},{5,6},{6,7},{7,8},{8,9},{9,10},{10,1... | collective-permute-start | bytes 1474568 | tf_op jit(solution)/shard_map/ppermute | solution.py:15
  29.5 8.1 %collective-permute-start.2 = (f32[8,512]{1,0:T(8,128)S(1)}, f32[8,512]{1,0:T(8,128)S(1)}, u32[]{:S(2)}, u32[]{:S(2)}) collective-permute-start(f32[8,512]{1,0:T(8,128)S(1)} %slice_bitcast_fusion), channel_id=1, source_target_pairs={{32,0},{48,16},{64,32},{80,48},{96,64},{112,80},{128,96},{144,112}... | collective-permute-start | bytes 49160 | tf_op jit(solution)/shard_map/ppermute | solution.py:15
  37.7 0.6 copy-start.12
  37.7 0.8 copy-start.4
  38.5 0.8 copy-start.3
  42.1 5.9 %collective-permute-start.5 = (f32[1,2,8,512]{3,2,1,0:T(8,128)}, f32[1,2,8,512]{3,2,1,0:T(8,128)S(1)}, u32[]{:S(2)}, u32[]{:S(2)}) collective-permute-start(f32[1,2,8,512]{3,2,1,0:T(8,128)} %shard_map.69.refs_1_.red_own), channel_id=1, source_target_pairs={{0,16},{16,32},{32,48},{48,64},{64,80},{80,96},{96,112},{112,128},... | collective-permute-start | bytes 98312 | tf_op jit(solution)/shard_map/ppermute | solution.py:15
  46.7 4.9 %collective-permute-start.6 = (f32[1,2,8,512]{3,2,1,0:T(8,128)}, f32[1,2,8,512]{3,2,1,0:T(8,128)S(1)}, u32[]{:S(2)}, u32[]{:S(2)}) collective-permute-start(f32[1,2,8,512]{3,2,1,0:T(8,128)} %shard_map.69.refs_1_.red_own), channel_id=1, source_target_pairs={{16,0},{32,16},{48,32},{64,48},{80,64},{96,80},{112,96},{128,112},... | collective-permute-start | bytes 98312 | tf_op jit(solution)/shard_map/ppermute | solution.py:15
  48.0 3.6 %copy-start.9 = (f32[1,2,8,512]{3,2,1,0:T(8,128)}, f32[1,2,8,512]{3,2,1,0:T(8,128)S(1)}, u32[]{:S(2)}) copy-start(f32[1,2,8,512]{3,2,1,0:T(8,128)S(1)} %collective-permute-done.5.refs_0_.red_left) | copy-start | bytes 98308
  51.5 0.6 copy-start.10
  53.6 6.6 %collective-permute-start.7 = (f32[3,8,512]{2,1,0:T(8,128)}, f32[3,8,512]{2,1,0:T(8,128)S(1)}, u32[]{:S(2)}, u32[]{:S(2)}) collective-permute-start(f32[3,8,512]{2,1,0:T(8,128)} %get-tuple-element.13), channel_id=1, source_target_pairs={{0,1},{1,2},{2,3},{3,4},{4,5},{5,6},{6,7},{7,8},{8,9},{9,10},{10,1... | collective-permute-start | bytes 147464 | tf_op jit(solution)/shard_map/ppermute | solution.py:15
  58.3 5.6 %collective-permute-start.8 = (f32[3,8,512]{2,1,0:T(8,128)}, f32[3,8,512]{2,1,0:T(8,128)S(1)}, u32[]{:S(2)}, u32[]{:S(2)}) collective-permute-start(f32[3,8,512]{2,1,0:T(8,128)} %get-tuple-element.14), channel_id=1, source_target_pairs={{1,0},{2,1},{3,2},{4,3},{5,4},{6,5},{7,6},{8,7},{9,8},{10,9},{11,1... | collective-permute-start | bytes 147464 | tf_op jit(solution)/shard_map/ppermute | solution.py:15
  60.2 3.7 %copy-start.17 = (f32[3,8,512]{2,1,0:T(8,128)}, f32[3,8,512]{2,1,0:T(8,128)S(1)}, u32[]{:S(2)}) copy-start(f32[3,8,512]{2,1,0:T(8,128)S(1)} %collective-permute-done.7.red_low) | copy-start | bytes 147460
  63.9 0.6 copy-start.18
  68.5 11.6 %collective-permute-start.9 = (f32[5,8,256]{2,1,0:T(8,128)}, f32[5,8,256]{2,1,0:T(8,128)S(1)}, u32[]{:S(2)}, u32[]{:S(2)}) collective-permute-start(f32[5,8,256]{2,1,0:T(8,128)} %get-tuple-element.15), channel_id=1, source_target_pairs={{0,32},{16,48},{32,64},{48,80},{64,96},{80,112},{96,128},{112,144}... | collective-permute-start | bytes 122888 | tf_op jit(solution)/shard_map/ppermute | solution.py:15
  74.4 5.7 %collective-permute-start.10 = (f32[5,8,256]{2,1,0:T(8,128)}, f32[5,8,256]{2,1,0:T(8,128)S(1)}, u32[]{:S(2)}, u32[]{:S(2)}) collective-permute-start(f32[5,8,256]{2,1,0:T(8,128)} %get-tuple-element.15), channel_id=1, source_target_pairs={{0,16},{16,32},{32,48},{48,64},{64,80},{80,96},{96,112},{112,128},... | collective-permute-start | bytes 122888 | tf_op jit(solution)/shard_map/ppermute | solution.py:15
  77.5 5.0 %collective-permute-start.11 = (f32[5,8,256]{2,1,0:T(8,128)}, f32[5,8,256]{2,1,0:T(8,128)S(1)}, u32[]{:S(2)}, u32[]{:S(2)}) collective-permute-start(f32[5,8,256]{2,1,0:T(8,128)} %get-tuple-element.15), channel_id=1, source_target_pairs={{16,0},{32,16},{48,32},{64,48},{80,64},{96,80},{112,96},{128,112},... | collective-permute-start | bytes 122888 | tf_op jit(solution)/shard_map/ppermute | solution.py:15
  78.8 6.1 %collective-permute-start.12 = (f32[5,8,256]{2,1,0:T(8,128)}, f32[5,8,256]{2,1,0:T(8,128)S(1)}, u32[]{:S(2)}, u32[]{:S(2)}) collective-permute-start(f32[5,8,256]{2,1,0:T(8,128)} %get-tuple-element.15), channel_id=1, source_target_pairs={{32,0},{48,16},{64,32},{80,48},{96,64},{112,80},{128,96},{144,112}... | collective-permute-start | bytes 122888 | tf_op jit(solution)/shard_map/ppermute | solution.py:15
  80.1 0.8 copy-start.21
  85.0 10.6 %copy-start.5 = (f32[5,5,8,256]{3,2,1,0:T(8,128)}, f32[5,5,8,256]{3,2,1,0:T(8,128)S(1)}, u32[]{:S(2)}) copy-start(f32[5,5,8,256]{3,2,1,0:T(8,128)S(1)} %bitcast_dynamic-update-slice_fusion.5.cat) | copy-start | bytes 614404
  85.0 6.2 %collective-permute-start.13 = (f32[5,5,8,256]{3,2,1,0:T(8,128)S(1)}, f32[5,5,8,256]{3,2,1,0:T(8,128)S(1)}, u32[]{:S(2)}, u32[]{:S(2)}) collective-permute-start(f32[5,5,8,256]{3,2,1,0:T(8,128)S(1)} %bitcast_dynamic-update-slice_fusion.5.cat), channel_id=1, source_target_pairs={{0,1},{1,2},{2,3},{3,4},{4,5},{5,6},{6,7},{7,8},{8,9},{9,10},{10,1... | collective-permute-start | bytes 614408 | tf_op jit(solution)/shard_map/ppermute | solution.py:15
  88.5 7.1 %collective-permute-start.14 = (f32[5,5,8,256]{3,2,1,0:T(8,128)S(1)}, f32[5,5,8,256]{3,2,1,0:T(8,128)S(1)}, u32[]{:S(2)}, u32[]{:S(2)}) collective-permute-start(f32[5,5,8,256]{3,2,1,0:T(8,128)S(1)} %bitcast_dynamic-update-slice_fusion.5.cat), channel_id=1, source_target_pairs={{1,0},{2,1},{3,2},{4,3},{5,4},{6,5},{7,6},{8,7},{9,8},{10,9},{11,1... | collective-permute-start | bytes 614408 | tf_op jit(solution)/shard_map/ppermute | solution.py:15
  91.2 4.4 %copy-start.6 = (f32[5,5,8,256]{3,2,1,0:T(8,128)}, f32[5,5,8,256]{3,2,1,0:T(8,128)S(1)}, u32[]{:S(2)}) copy-start(f32[5,5,8,256]{3,2,1,0:T(8,128)S(1)} %collective-permute-done.13.low) | copy-start | bytes 614404
  95.6 0.7 copy-start.7
  98.3 12.3 %collective-permute-start.15 = (f32[1,8,256]{2,1,0:T(8,128)}, f32[1,8,256]{2,1,0:T(8,128)S(1)}, u32[]{:S(2)}, u32[]{:S(2)}) collective-permute-start(f32[1,8,256]{2,1,0:T(8,128)} %shard_map.72), channel_id=1, source_target_pairs={{0,32},{16,48},{32,64},{48,80},{64,96},{80,112},{96,128},{112,144}... | collective-permute-start | bytes 24584 | tf_op jit(solution)/shard_map/ppermute | solution.py:15
  104.8 5.7 %collective-permute-start.16 = (f32[1,8,256]{2,1,0:T(8,128)}, f32[1,8,256]{2,1,0:T(8,128)S(1)}, u32[]{:S(2)}, u32[]{:S(2)}) collective-permute-start(f32[1,8,256]{2,1,0:T(8,128)} %shard_map.72), channel_id=1, source_target_pairs={{0,16},{16,32},{32,48},{48,64},{64,80},{80,96},{96,112},{112,128},... | collective-permute-start | bytes 24584 | tf_op jit(solution)/shard_map/ppermute | solution.py:15
  107.9 5.9 %collective-permute-start.17 = (f32[1,8,256]{2,1,0:T(8,128)}, f32[1,8,256]{2,1,0:T(8,128)S(1)}, u32[]{:S(2)}, u32[]{:S(2)}) collective-permute-start(f32[1,8,256]{2,1,0:T(8,128)} %shard_map.72), channel_id=1, source_target_pairs={{16,0},{32,16},{48,32},{64,48},{80,64},{96,80},{112,96},{128,112},... | collective-permute-start | bytes 24584 | tf_op jit(solution)/shard_map/ppermute | solution.py:15
  109.2 7.4 %collective-permute-start.18 = (f32[1,8,256]{2,1,0:T(8,128)}, f32[1,8,256]{2,1,0:T(8,128)S(1)}, u32[]{:S(2)}, u32[]{:S(2)}) collective-permute-start(f32[1,8,256]{2,1,0:T(8,128)} %shard_map.72), channel_id=1, source_target_pairs={{32,0},{48,16},{64,32},{80,48},{96,64},{112,80},{128,96},{144,112}... | collective-permute-start | bytes 24584 | tf_op jit(solution)/shard_map/ppermute | solution.py:15
  110.5 0.7 copy-start.22
  116.7 8.8 %copy-start.16 = (f32[5,8,256]{2,1,0:T(8,128)}, f32[5,8,256]{2,1,0:T(8,128)S(1)}, u32[]{:S(2)}) copy-start(f32[5,8,256]{2,1,0:T(8,128)S(1)} %constant_dynamic-update-slice_fusion.reds) | copy-start | bytes 122884
  116.7 5.4 %collective-permute-start.19 = (f32[5,8,256]{2,1,0:T(8,128)S(1)}, f32[5,8,256]{2,1,0:T(8,128)S(1)}, u32[]{:S(2)}, u32[]{:S(2)}) collective-permute-start(f32[5,8,256]{2,1,0:T(8,128)S(1)} %constant_dynamic-update-slice_fusion.reds), channel_id=1, source_target_pairs={{0,1},{1,2},{2,3},{3,4},{4,5},{5,6},{6,7},{7,8},{8,9},{9,10},{10,1... | collective-permute-start | bytes 122888 | tf_op jit(solution)/shard_map/ppermute | solution.py:15
  120.1 5.3 %collective-permute-start.20 = (f32[5,8,256]{2,1,0:T(8,128)S(1)}, f32[5,8,256]{2,1,0:T(8,128)S(1)}, u32[]{:S(2)}, u32[]{:S(2)}) collective-permute-start(f32[5,8,256]{2,1,0:T(8,128)S(1)} %constant_dynamic-update-slice_fusion.reds), channel_id=1, source_target_pairs={{1,0},{2,1},{3,2},{4,3},{5,4},{6,5},{7,6},{8,7},{9,8},{10,9},{11,1... | collective-permute-start | bytes 122888 | tf_op jit(solution)/shard_map/ppermute | solution.py:15
  122.1 3.4 %copy-start.19 = (f32[5,8,256]{2,1,0:T(8,128)}, f32[5,8,256]{2,1,0:T(8,128)S(1)}, u32[]{:S(2)}) copy-start(f32[5,8,256]{2,1,0:T(8,128)S(1)} %collective-permute-done.19.reds_low) | copy-start | bytes 122884
  125.4 0.6 copy-start.20
  128.6 18.1 %all-to-all-start = ((f32[16,16,128]{2,1,0:T(8,128)}), f32[16,16,128]{2,1,0:T(8,128)S(1)}, u32[]{:S(2)}, u32[]{:S(2)}) async-start(f32[16,16,128]{2,1,0:T(8,128)} %get-tuple-element.17), calls=%async_computation | async-start | bytes 262144 | tf_op jit(solution)/shard_map/all_to_all | solution.py:486
  146.7 0.7 copy-start.8

commit v2 on v1

--- a/solution.py
+++ b/solution.py
@@ -7,6 +7,8 @@
 
 F32 = jnp.float32
 RHS, ALPHA, BX, BY, BZ = range(5)
+VMEM_BYTES = 20 * 2**20
+RING = 8
 
 
 def shifted(values, axis, name, steps):
@@ -28,6 +30,7 @@
             in_specs=specs,
             out_specs=[pl.BlockSpec(memory_space=pltpu.VMEM)] * len(outs),
             scratch_shapes=[pltpu.VMEM(s, F32) for s in scratch],
+            compiler_params=pltpu.CompilerParams(vmem_limit_bytes=VMEM_BYTES),
         )(*args)
 
     return run
@@ -487,9 +490,13 @@
     size_y = 2 * count_y
     width = low_z // count_y
     (low,) = call(
-        lambda *refs: window_kernel(width, *refs), [(count_x, 2 * size_y, low_z)], smem=(0,)
+        lambda *refs: window_kernel(width, *refs), [(RING, 2 * size_y, low_z)], smem=(0,)
     )(index, low)
-    low = lax.all_to_all(low, "gx", 0, 0, tiled=True)
+    groups = count_x // RING
+    rings = [[RING * i + j for j in range(RING)] for i in range(groups)]
+    low = lax.all_to_all(low, "gx", 0, 0, tiled=True, axis_index_groups=rings)
+    low = jnp.broadcast_to(low[None], (groups, *low.shape)).reshape(-1, *low.shape[1:])
+    low = lax.all_to_all(low, "gx", 0, 0, tiled=True, axis_index_groups=[list(c) for c in zip(*rings)])
     pairs = count_x // 2
     (pieces,) = call(
         lambda *refs: coarse_kernel(width, 8, *refs),

time: 213 us -> 190 us (0.89)
  Pallas kernels: 27.4 us -> 13.6 us
  local copies, waits for them, and re-layouts: 10.4 us -> 3.53 us
    pallas_call x9, Pallas kernels: 27.4 us -> 13.6 us  [run(): pl.pallas_call(kernel, out_shape=shapes, in_specs=specs, out_specs=[pl.Bl...]
    unnamed x58 -> x20, local copies, waits for them, and re-layouts: 10.3 us -> 3.41 us
    all_to_all x1, blocking collectives: 15.4 us -> 12.1 us  [on_device(): pieces = lax.all_to_all(pieces, 'gy', 0, 0, tiled=True)]
    all_to_all x1 -> x2, blocking collectives: 36.3 us -> 37.6 us  [the longest x1 19.7 us: on_device(): low = lax.all_to_all(low, 'gx', 0, 0, tiled=True, axis_index_groups=rings)]
where the time goes in v2:
time: 190 us; the launch traced here: 189 us
  starting transfers between devices  71.6 us (38%)
  waiting for transfers between devices  49.7 us (26%)
  blocking collectives  49.7 us (26%)
  Pallas kernels  13.6 us (7%)
  local copies, waits for them, and re-layouts  3.53 us (2%)
    ppermute x21, starting transfers between devices, shifted(): lax.ppermute(values, name, [(i, i + steps) for i in range(lead, last)])  62.7 us
    ppermute x21, waiting for transfers between devices, shifted(): lax.ppermute(values, name, [(i, i + steps) for i in range(lead, last)])  40.9 us
    all_to_all x1, blocking collectives, on_device(): low = lax.all_to_all(low, 'gx', 0, 0, tiled=True, axis_index_groups=rings)  19.7 us
    all_to_all x1, blocking collectives, on_device(): lax.all_to_all(low, 'gx', 0, 0, tiled=True, axis_index_groups=[list(c) fo...  18 us
    pallas_call x9, Pallas kernels, run(): pl.pallas_call(kernel, out_shape=shapes, in_specs=specs, out_specs=[pl.Bl...  13.6 us
    all_to_all x1, blocking collectives, on_device(): pieces = lax.all_to_all(pieces, 'gy', 0, 0, tiled=True)  12.1 us
    all_to_all x1, starting transfers between devices, on_device(): low = lax.all_to_all(low, 'gy', 0, 0, tiled=True)  8.93 us
    all_to_all x1, waiting for transfers between devices, on_device(): low = lax.all_to_all(low, 'gy', 0, 0, tiled=True)  8.81 us
  transfers between devices with their start and end apart: 22, of which 13 were waited for; matrix products, arithmetic and copies ran while one was open for 0% of the time, Pallas kernels for 0%

profile of v2, /device:TPU:1, one launch (start us, length us, event | category | flops | bytes accessed | tf_op | source)
XLA Modules:
  0.0 189.2 jit_solution(17561836003909515803)
XLA Ops:
  0.6 0.9 bitcast_dynamic-update-slice_fusion.4
  1.5 0.8 copy-done
  2.4 0.8 copy-done.2
  3.2 0.8 copy-done.3
  4.0 4.8 %collective-permute-start = (f32[5,4,8,512]{3,2,1,0:T(8,128)S(1)}, f32[5,4,8,512]{3,2,1,0:T(8,128)S(1)}, u32[]{:S(2)}, u32[]{:S(2)}) collective-permute-start(f32[5,4,8,512]{3,2,1,0:T(8,128)S(1)} %bitcast_dynamic-update-slice_fusion.refs_1_.own), channel_id=1, source_target_pairs={{0,16},{16,32},{32,48},{48,64},{64,80},{80,96},{96,112},{112,128},... | collective-permute-start | bytes 983048 | tf_op jit(solution)/shard_map/ppermute | solution.py:17
  8.9 1.3 collective-permute-start.1
  10.2 2.7 %collective-permute-done.refs_0_.left = f32[5,4,8,512]{3,2,1,0:T(8,128)S(1)} collective-permute-done((f32[5,4,8,512]{3,2,1,0:T(8,128)S(1)}, f32[5,4,8,512]{3,2,1,0:T(8,128)S(1)}, u32[]{:S(2)}, u32[]{:S(2)}) %collective-permute-start) | collective-permute-done | bytes 327712 | tf_op jit(solution)/shard_map/ppermute | solution.py:17
  12.9 5.1 %collective-permute-done.1.refs_2_.right = f32[5,4,8,512]{3,2,1,0:T(8,128)S(1)} collective-permute-done((f32[5,4,8,512]{3,2,1,0:T(8,128)S(1)}, f32[5,4,8,512]{3,2,1,0:T(8,128)S(1)}, u32[]{:S(2)}, u32[]{:S(2)}) %collective-permute-start.1) | collective-permute-done | bytes 327712 | tf_op jit(solution)/shard_map/ppermute | solution.py:17
  18.0 5.5 %collective-permute-start.4 = (f32[32,8,512]{2,1,0:T(8,128)S(1)}, f32[32,8,512]{2,1,0:T(8,128)S(1)}, u32[]{:S(2)}, u32[]{:S(2)}) collective-permute-start(f32[32,8,512]{2,1,0:T(8,128)S(1)} %get-tuple-element.12), channel_id=1, source_target_pairs={{1,0},{2,1},{3,2},{4,3},{5,4},{6,5},{7,6},{8,7},{9,8},{10,9},{11,1... | collective-permute-start | bytes 1572872 | tf_op jit(solution)/shard_map/ppermute | solution.py:17
  23.5 3.1 %collective-permute-start.3 = (f32[30,8,512]{2,1,0:T(8,128)S(1)}, f32[30,8,512]{2,1,0:T(8,128)S(1)}, u32[]{:S(2)}, u32[]{:S(2)}) collective-permute-start(f32[30,8,512]{2,1,0:T(8,128)S(1)} %get-tuple-element.11), channel_id=1, source_target_pairs={{0,1},{1,2},{2,3},{3,4},{4,5},{5,6},{6,7},{7,8},{8,9},{9,10},{10,1... | collective-permute-start | bytes 1474568 | tf_op jit(solution)/shard_map/ppermute | solution.py:17
  26.6 1.3 collective-permute-start.2
  27.9 6.8 %collective-permute-done.2.beyond = f32[8,512]{1,0:T(8,128)S(1)} collective-permute-done((f32[8,512]{1,0:T(8,128)S(1)}, f32[8,512]{1,0:T(8,128)S(1)}, u32[]{:S(2)}, u32[]{:S(2)}) %collective-permute-start.2) | collective-permute-done | bytes 16416 | tf_op jit(solution)/shard_map/ppermute | solution.py:17
  34.8 0.7 shard_map.69.refs_1_.red_own
  35.5 4.6 %collective-permute-start.5 = (f32[1,2,8,512]{3,2,1,0:T(8,128)S(1)}, f32[1,2,8,512]{3,2,1,0:T(8,128)S(1)}, u32[]{:S(2)}, u32[]{:S(2)}) collective-permute-start(f32[1,2,8,512]{3,2,1,0:T(8,128)S(1)} %shard_map.69.refs_1_.red_own), channel_id=1, source_target_pairs={{0,16},{16,32},{32,48},{48,64},{64,80},{80,96},{96,112},{112,128},... | collective-permute-start | bytes 98312 | tf_op jit(solution)/shard_map/ppermute | solution.py:17
  40.1 1.3 collective-permute-start.6
  41.4 3.3 %collective-permute-done.6.refs_2_.red_right = f32[1,2,8,512]{3,2,1,0:T(8,128)S(1)} collective-permute-done((f32[1,2,8,512]{3,2,1,0:T(8,128)S(1)}, f32[1,2,8,512]{3,2,1,0:T(8,128)S(1)}, u32[]{:S(2)}, u32[]{:S(2)}) %collective-permute-start.6) | collective-permute-done | bytes 32800 | tf_op jit(solution)/shard_map/ppermute | solution.py:17
  44.8 4.7 %collective-permute-start.7 = (f32[3,8,512]{2,1,0:T(8,128)S(1)}, f32[3,8,512]{2,1,0:T(8,128)S(1)}, u32[]{:S(2)}, u32[]{:S(2)}) collective-permute-start(f32[3,8,512]{2,1,0:T(8,128)S(1)} %get-tuple-element.13), channel_id=1, source_target_pairs={{0,1},{1,2},{2,3},{3,4},{4,5},{5,6},{6,7},{7,8},{8,9},{9,10},{10,1... | collective-permute-start | bytes 147464 | tf_op jit(solution)/shard_map/ppermute | solution.py:17
  49.5 1.9 %collective-permute-start.8 = (f32[3,8,512]{2,1,0:T(8,128)S(1)}, f32[3,8,512]{2,1,0:T(8,128)S(1)}, u32[]{:S(2)}, u32[]{:S(2)}) collective-permute-start(f32[3,8,512]{2,1,0:T(8,128)S(1)} %get-tuple-element.14), channel_id=1, source_target_pairs={{1,0},{2,1},{3,2},{4,3},{5,4},{6,5},{7,6},{8,7},{9,8},{10,9},{11,1... | collective-permute-start | bytes 147464 | tf_op jit(solution)/shard_map/ppermute | solution.py:17
  51.4 3.5 %collective-permute-done.8.red_high = f32[3,8,512]{2,1,0:T(8,128)S(1)} collective-permute-done((f32[3,8,512]{2,1,0:T(8,128)S(1)}, f32[3,8,512]{2,1,0:T(8,128)S(1)}, u32[]{:S(2)}, u32[]{:S(2)}) %collective-permute-start.8) | collective-permute-done | bytes 49184 | tf_op jit(solution)/shard_map/ppermute | solution.py:17
  54.9 1.8 shard_map.71
  56.7 5.8 %collective-permute-start.9 = (f32[5,8,256]{2,1,0:T(8,128)S(1)}, f32[5,8,256]{2,1,0:T(8,128)S(1)}, u32[]{:S(2)}, u32[]{:S(2)}) collective-permute-start(f32[5,8,256]{2,1,0:T(8,128)S(1)} %get-tuple-element.15), channel_id=1, source_target_pairs={{0,32},{16,48},{32,64},{48,80},{64,96},{80,112},{96,128},{112,144}... | collective-permute-start | bytes 122888 | tf_op jit(solution)/shard_map/ppermute | solution.py:17
  62.5 3.1 %collective-permute-start.10 = (f32[5,8,256]{2,1,0:T(8,128)S(1)}, f32[5,8,256]{2,1,0:T(8,128)S(1)}, u32[]{:S(2)}, u32[]{:S(2)}) collective-permute-start(f32[5,8,256]{2,1,0:T(8,128)S(1)} %get-tuple-element.15), channel_id=1, source_target_pairs={{0,16},{16,32},{32,48},{48,64},{64,80},{80,96},{96,112},{112,128},... | collective-permute-start | bytes 122888 | tf_op jit(solution)/shard_map/ppermute | solution.py:17
  65.6 1.3 collective-permute-start.11
  66.9 1.3 collective-permute-start.12
  68.3 2.1 %collective-permute-done.11 = f32[5,8,256]{2,1,0:T(8,128)S(1)} collective-permute-done((f32[5,8,256]{2,1,0:T(8,128)S(1)}, f32[5,8,256]{2,1,0:T(8,128)S(1)}, u32[]{:S(2)}, u32[]{:S(2)}) %collective-permute-start.11) | collective-permute-done | bytes 40992 | tf_op jit(solution)/shard_map/ppermute | solution.py:17
  70.3 2.7 %collective-permute-done.12 = f32[5,8,256]{2,1,0:T(8,128)S(1)} collective-permute-done((f32[5,8,256]{2,1,0:T(8,128)S(1)}, f32[5,8,256]{2,1,0:T(8,128)S(1)}, u32[]{:S(2)}, u32[]{:S(2)}) %collective-permute-start.12) | collective-permute-done | bytes 40992 | tf_op jit(solution)/shard_map/ppermute | solution.py:17
  73.0 3.3 %collective-permute-start.13 = (f32[5,5,8,256]{3,2,1,0:T(8,128)S(1)}, f32[5,5,8,256]{3,2,1,0:T(8,128)S(1)}, u32[]{:S(2)}, u32[]{:S(2)}) collective-permute-start(f32[5,5,8,256]{3,2,1,0:T(8,128)S(1)} %bitcast_dynamic-update-slice_fusion.5.cat), channel_id=1, source_target_pairs={{0,1},{1,2},{2,3},{3,4},{4,5},{5,6},{6,7},{7,8},{8,9},{9,10},{10,1... | collective-permute-start | bytes 614408 | tf_op jit(solution)/shard_map/ppermute | solution.py:17
  76.3 1.9 %collective-permute-start.14 = (f32[5,5,8,256]{3,2,1,0:T(8,128)S(1)}, f32[5,5,8,256]{3,2,1,0:T(8,128)S(1)}, u32[]{:S(2)}, u32[]{:S(2)}) collective-permute-start(f32[5,5,8,256]{3,2,1,0:T(8,128)S(1)} %bitcast_dynamic-update-slice_fusion.5.cat), channel_id=1, source_target_pairs={{1,0},{2,1},{3,2},{4,3},{5,4},{6,5},{7,6},{8,7},{9,8},{10,9},{11,1... | collective-permute-start | bytes 614408 | tf_op jit(solution)/shard_map/ppermute | solution.py:17
  78.3 0.8 collective-permute-done.13.low
  79.0 4.4 %collective-permute-done.14.high = f32[5,5,8,256]{3,2,1,0:T(8,128)S(1)} collective-permute-done((f32[5,5,8,256]{3,2,1,0:T(8,128)S(1)}, f32[5,5,8,256]{3,2,1,0:T(8,128)S(1)}, u32[]{:S(2)}, u32[]{:S(2)}) %collective-permute-start.14) | collective-permute-done | bytes 204832 | tf_op jit(solution)/shard_map/ppermute | solution.py:17
  83.7 6.5 %collective-permute-start.15 = (f32[1,8,256]{2,1,0:T(8,128)S(1)}, f32[1,8,256]{2,1,0:T(8,128)S(1)}, u32[]{:S(2)}, u32[]{:S(2)}) collective-permute-start(f32[1,8,256]{2,1,0:T(8,128)S(1)} %shard_map.72), channel_id=1, source_target_pairs={{0,32},{16,48},{32,64},{48,80},{64,96},{80,112},{96,128},{112,144}... | collective-permute-start | bytes 24584 | tf_op jit(solution)/shard_map/ppermute | solution.py:17
  90.3 3.1 %collective-permute-start.16 = (f32[1,8,256]{2,1,0:T(8,128)S(1)}, f32[1,8,256]{2,1,0:T(8,128)S(1)}, u32[]{:S(2)}, u32[]{:S(2)}) collective-permute-start(f32[1,8,256]{2,1,0:T(8,128)S(1)} %shard_map.72), channel_id=1, source_target_pairs={{0,16},{16,32},{32,48},{48,64},{64,80},{80,96},{96,112},{112,128},... | collective-permute-start | bytes 24584 | tf_op jit(solution)/shard_map/ppermute | solution.py:17
  93.4 1.3 collective-permute-start.17
  94.7 1.3 collective-permute-start.18
  96.0 3.3 %collective-permute-done.17 = f32[1,8,256]{2,1,0:T(8,128)S(1)} collective-permute-done((f32[1,8,256]{2,1,0:T(8,128)S(1)}, f32[1,8,256]{2,1,0:T(8,128)S(1)}, u32[]{:S(2)}, u32[]{:S(2)}) %collective-permute-start.17) | collective-permute-done | bytes 8224 | tf_op jit(solution)/shard_map/ppermute | solution.py:17
  99.3 2.8 %collective-permute-done.18 = f32[1,8,256]{2,1,0:T(8,128)S(1)} collective-permute-done((f32[1,8,256]{2,1,0:T(8,128)S(1)}, f32[1,8,256]{2,1,0:T(8,128)S(1)}, u32[]{:S(2)}, u32[]{:S(2)}) %collective-permute-start.18) | collective-permute-done | bytes 8224 | tf_op jit(solution)/shard_map/ppermute | solution.py:17
  102.1 3.4 %collective-permute-start.19 = (f32[5,8,256]{2,1,0:T(8,128)S(1)}, f32[5,8,256]{2,1,0:T(8,128)S(1)}, u32[]{:S(2)}, u32[]{:S(2)}) collective-permute-start(f32[5,8,256]{2,1,0:T(8,128)S(1)} %constant_dynamic-update-slice_fusion.reds), channel_id=1, source_target_pairs={{0,1},{1,2},{2,3},{3,4},{4,5},{5,6},{6,7},{7,8},{8,9},{9,10},{10,1... | collective-permute-start | bytes 122888 | tf_op jit(solution)/shard_map/ppermute | solution.py:17
  105.6 1.9 %collective-permute-start.20 = (f32[5,8,256]{2,1,0:T(8,128)S(1)}, f32[5,8,256]{2,1,0:T(8,128)S(1)}, u32[]{:S(2)}, u32[]{:S(2)}) collective-permute-start(f32[5,8,256]{2,1,0:T(8,128)S(1)} %constant_dynamic-update-slice_fusion.reds), channel_id=1, source_target_pairs={{1,0},{2,1},{3,2},{4,3},{5,4},{6,5},{7,6},{8,7},{9,8},{10,9},{11,1... | collective-permute-start | bytes 122888 | tf_op jit(solution)/shard_map/ppermute | solution.py:17
  107.5 3.4 %collective-permute-done.20.reds_high = f32[5,8,256]{2,1,0:T(8,128)S(1)} collective-permute-done((f32[5,8,256]{2,1,0:T(8,128)S(1)}, f32[5,8,256]{2,1,0:T(8,128)S(1)}, u32[]{:S(2)}, u32[]{:S(2)}) %collective-permute-start.20) | collective-permute-done | bytes 40992 | tf_op jit(solution)/shard_map/ppermute | solution.py:17
  110.9 1.4 shard_map.73
  112.3 8.9 %all-to-all-start = ((f32[16,16,128]{2,1,0:T(8,128)}), f32[16,16,128]{2,1,0:T(8,128)S(1)}, u32[]{:S(2)}, u32[]{:S(2)}) async-start(f32[16,16,128]{2,1,0:T(8,128)} %get-tuple-element.17), calls=%async_computation | async-start | bytes 262144 | tf_op jit(solution)/shard_map/all_to_all | solution.py:489
  121.3 8.8 %all-to-all-done.refs_1_ = f32[16,16,128]{2,1,0:T(8,128)S(1)} async-done(((f32[16,16,128]{2,1,0:T(8,128)}), f32[16,16,128]{2,1,0:T(8,128)S(1)}, u32[]{:S(2)}, u32[]{:S(2)}) %all-to-all-start) | async-done | bytes 131104 | tf_op jit(solution)/shard_map/all_to_all | solution.py:489
  130.1 1.0 shard_map.74
  131.1 19.7 %all_to_all.20 = f32[8,64,128]{2,1,0:T(8,128)S(1)} all-to-all(f32[8,64,128]{2,1,0:T(8,128)S(1)} %shard_map.74), channel_id=1, replica_groups={{0,16,32,48,64,80,96,112},{128,144,160,176,192,208,224,240},{256,272,28..., dimensions={0} | all-to-all | bytes 524288 | tf_op jit(solution)/shard_map/all_to_all | solution.py:497
  150.9 18.0 %all_to_all.21.refs_1_ = f32[32,64,128]{2,1,0:T(8,128)S(1)} all-to-all(f32[32,64,128]{2,1,0:T(8,128)S(1)} %bitcast.25), channel_id=1, replica_groups={{0,128,256,384},{16,144,272,400},{32,160,288,416},{48,176,304,432},{64,..., dimensions={0} | all-to-all | bytes 2097152 | tf_op jit(solution)/shard_map/all_to_all | solution.py:499
  168.8 6.2 %shard_map.75 = f32[16,8,128]{2,1,0:T(8,128)S(1)} custom-call(s32[2]{0:T(128)S(1)} %pad_add_fusion.refs_0_.index, f32[32,64,128]{2,1,0:T(8,128)S(1)} %all_to_all.21.refs_1_), custom_call_target="tpu_custom_call" | custom-call | tf_op jit(solution)/shard_map/pallas_call | solution.py:27
  175.0 12.1 %all_to_all.22.pieces = f32[16,8,128]{2,1,0:T(8,128)S(1)} all-to-all(f32[16,8,128]{2,1,0:T(8,128)S(1)} %shard_map.75), channel_id=1, replica_groups=mesh['gx'=32,'gy'=16] {'gy'}, dimensions={0} | all-to-all | bytes 131072 | tf_op jit(solution)/shard_map/all_to_all | solution.py:507
  187.1 2.0 %shard_map.76 = (f32[4,8,512]{2,1,0:T(8,128)}, f32[1,2,128]{2,1,0:T(2,128)}) custom-call(s32[2]{0:T(128)S(1)} %pad_add_fusion.refs_0_.index, f32[16,8,128]{2,1,0:T(8,128)S(1)} %all_to_all.22.pieces, f32[2,8,256]{2,1,0:T(8,128)S(1)} %get-tuple-element.18.level, f32[2,2,8,512]{3,2,1,0:T(8,128)S(1)} %get-tuple-element.19.fine), custom_call_target="tpu_custom_call" | custom-call | tf_op jit(solution)/shard_map/pallas_call | solution.py:27
  (34 shorter events, 0.7 us)
Async XLA Ops:
  0.6 0.9 copy-start.1
  1.5 0.8 copy-start
  2.4 0.8 copy-start.2
  3.2 0.8 copy-start.3
  4.0 8.8 %collective-permute-start = (f32[5,4,8,512]{3,2,1,0:T(8,128)S(1)}, f32[5,4,8,512]{3,2,1,0:T(8,128)S(1)}, u32[]{:S(2)}, u32[]{:S(2)}) collective-permute-start(f32[5,4,8,512]{3,2,1,0:T(8,128)S(1)} %bitcast_dynamic-update-slice_fusion.refs_1_.own), channel_id=1, source_target_pairs={{0,16},{16,32},{32,48},{48,64},{64,80},{80,96},{96,112},{112,128},... | collective-permute-start | bytes 983048 | tf_op jit(solution)/shard_map/ppermute | solution.py:17
  8.9 9.1 %collective-permute-start.1 = (f32[5,4,8,512]{3,2,1,0:T(8,128)S(1)}, f32[5,4,8,512]{3,2,1,0:T(8,128)S(1)}, u32[]{:S(2)}, u32[]{:S(2)}) collective-permute-start(f32[5,4,8,512]{3,2,1,0:T(8,128)S(1)} %bitcast_dynamic-update-slice_fusion.refs_1_.own), channel_id=1, source_target_pairs={{16,0},{32,16},{48,32},{64,48},{80,64},{96,80},{112,96},{128,112},... | collective-permute-start | bytes 983048 | tf_op jit(solution)/shard_map/ppermute | solution.py:17
  18.0 16.7 %collective-permute-start.4 = (f32[32,8,512]{2,1,0:T(8,128)S(1)}, f32[32,8,512]{2,1,0:T(8,128)S(1)}, u32[]{:S(2)}, u32[]{:S(2)}) collective-permute-start(f32[32,8,512]{2,1,0:T(8,128)S(1)} %get-tuple-element.12), channel_id=1, source_target_pairs={{1,0},{2,1},{3,2},{4,3},{5,4},{6,5},{7,6},{8,7},{9,8},{10,9},{11,1... | collective-permute-start | bytes 1572872 | tf_op jit(solution)/shard_map/ppermute | solution.py:17
  23.5 11.3 %collective-permute-start.3 = (f32[30,8,512]{2,1,0:T(8,128)S(1)}, f32[30,8,512]{2,1,0:T(8,128)S(1)}, u32[]{:S(2)}, u32[]{:S(2)}) collective-permute-start(f32[30,8,512]{2,1,0:T(8,128)S(1)} %get-tuple-element.11), channel_id=1, source_target_pairs={{0,1},{1,2},{2,3},{3,4},{4,5},{5,6},{6,7},{7,8},{8,9},{9,10},{10,1... | collective-permute-start | bytes 1474568 | tf_op jit(solution)/shard_map/ppermute | solution.py:17
  26.6 8.1 %collective-permute-start.2 = (f32[8,512]{1,0:T(8,128)S(1)}, f32[8,512]{1,0:T(8,128)S(1)}, u32[]{:S(2)}, u32[]{:S(2)}) collective-permute-start(f32[8,512]{1,0:T(8,128)S(1)} %slice_bitcast_fusion), channel_id=1, source_target_pairs={{32,0},{48,16},{64,32},{80,48},{96,64},{112,80},{128,96},{144,112}... | collective-permute-start | bytes 49160 | tf_op jit(solution)/shard_map/ppermute | solution.py:17
  35.5 5.9 %collective-permute-start.5 = (f32[1,2,8,512]{3,2,1,0:T(8,128)S(1)}, f32[1,2,8,512]{3,2,1,0:T(8,128)S(1)}, u32[]{:S(2)}, u32[]{:S(2)}) collective-permute-start(f32[1,2,8,512]{3,2,1,0:T(8,128)S(1)} %shard_map.69.refs_1_.red_own), channel_id=1, source_target_pairs={{0,16},{16,32},{32,48},{48,64},{64,80},{80,96},{96,112},{112,128},... | collective-permute-start | bytes 98312 | tf_op jit(solution)/shard_map/ppermute | solution.py:17
  40.1 4.7 %collective-permute-start.6 = (f32[1,2,8,512]{3,2,1,0:T(8,128)S(1)}, f32[1,2,8,512]{3,2,1,0:T(8,128)S(1)}, u32[]{:S(2)}, u32[]{:S(2)}) collective-permute-start(f32[1,2,8,512]{3,2,1,0:T(8,128)S(1)} %shard_map.69.refs_1_.red_own), channel_id=1, source_target_pairs={{16,0},{32,16},{48,32},{64,48},{80,64},{96,80},{112,96},{128,112},... | collective-permute-start | bytes 98312 | tf_op jit(solution)/shard_map/ppermute | solution.py:17
  44.8 6.6 %collective-permute-start.7 = (f32[3,8,512]{2,1,0:T(8,128)S(1)}, f32[3,8,512]{2,1,0:T(8,128)S(1)}, u32[]{:S(2)}, u32[]{:S(2)}) collective-permute-start(f32[3,8,512]{2,1,0:T(8,128)S(1)} %get-tuple-element.13), channel_id=1, source_target_pairs={{0,1},{1,2},{2,3},{3,4},{4,5},{5,6},{6,7},{7,8},{8,9},{9,10},{10,1... | collective-permute-start | bytes 147464 | tf_op jit(solution)/shard_map/ppermute | solution.py:17
  49.5 5.4 %collective-permute-start.8 = (f32[3,8,512]{2,1,0:T(8,128)S(1)}, f32[3,8,512]{2,1,0:T(8,128)S(1)}, u32[]{:S(2)}, u32[]{:S(2)}) collective-permute-start(f32[3,8,512]{2,1,0:T(8,128)S(1)} %get-tuple-element.14), channel_id=1, source_target_pairs={{1,0},{2,1},{3,2},{4,3},{5,4},{6,5},{7,6},{8,7},{9,8},{10,9},{11,1... | collective-permute-start | bytes 147464 | tf_op jit(solution)/shard_map/ppermute | solution.py:17
  56.7 11.5 %collective-permute-start.9 = (f32[5,8,256]{2,1,0:T(8,128)S(1)}, f32[5,8,256]{2,1,0:T(8,128)S(1)}, u32[]{:S(2)}, u32[]{:S(2)}) collective-permute-start(f32[5,8,256]{2,1,0:T(8,128)S(1)} %get-tuple-element.15), channel_id=1, source_target_pairs={{0,32},{16,48},{32,64},{48,80},{64,96},{80,112},{96,128},{112,144}... | collective-permute-start | bytes 122888 | tf_op jit(solution)/shard_map/ppermute | solution.py:17
  62.5 5.7 %collective-permute-start.10 = (f32[5,8,256]{2,1,0:T(8,128)S(1)}, f32[5,8,256]{2,1,0:T(8,128)S(1)}, u32[]{:S(2)}, u32[]{:S(2)}) collective-permute-start(f32[5,8,256]{2,1,0:T(8,128)S(1)} %get-tuple-element.15), channel_id=1, source_target_pairs={{0,16},{16,32},{32,48},{48,64},{64,80},{80,96},{96,112},{112,128},... | collective-permute-start | bytes 122888 | tf_op jit(solution)/shard_map/ppermute | solution.py:17
  65.6 4.7 %collective-permute-start.11 = (f32[5,8,256]{2,1,0:T(8,128)S(1)}, f32[5,8,256]{2,1,0:T(8,128)S(1)}, u32[]{:S(2)}, u32[]{:S(2)}) collective-permute-start(f32[5,8,256]{2,1,0:T(8,128)S(1)} %get-tuple-element.15), channel_id=1, source_target_pairs={{16,0},{32,16},{48,32},{64,48},{80,64},{96,80},{112,96},{128,112},... | collective-permute-start | bytes 122888 | tf_op jit(solution)/shard_map/ppermute | solution.py:17
  66.9 6.1 %collective-permute-start.12 = (f32[5,8,256]{2,1,0:T(8,128)S(1)}, f32[5,8,256]{2,1,0:T(8,128)S(1)}, u32[]{:S(2)}, u32[]{:S(2)}) collective-permute-start(f32[5,8,256]{2,1,0:T(8,128)S(1)} %get-tuple-element.15), channel_id=1, source_target_pairs={{32,0},{48,16},{64,32},{80,48},{96,64},{112,80},{128,96},{144,112}... | collective-permute-start | bytes 122888 | tf_op jit(solution)/shard_map/ppermute | solution.py:17
  73.0 6.0 %collective-permute-start.13 = (f32[5,5,8,256]{3,2,1,0:T(8,128)S(1)}, f32[5,5,8,256]{3,2,1,0:T(8,128)S(1)}, u32[]{:S(2)}, u32[]{:S(2)}) collective-permute-start(f32[5,5,8,256]{3,2,1,0:T(8,128)S(1)} %bitcast_dynamic-update-slice_fusion.5.cat), channel_id=1, source_target_pairs={{0,1},{1,2},{2,3},{3,4},{4,5},{5,6},{6,7},{7,8},{8,9},{9,10},{10,1... | collective-permute-start | bytes 614408 | tf_op jit(solution)/shard_map/ppermute | solution.py:17
  76.3 7.1 %collective-permute-start.14 = (f32[5,5,8,256]{3,2,1,0:T(8,128)S(1)}, f32[5,5,8,256]{3,2,1,0:T(8,128)S(1)}, u32[]{:S(2)}, u32[]{:S(2)}) collective-permute-start(f32[5,5,8,256]{3,2,1,0:T(8,128)S(1)} %bitcast_dynamic-update-slice_fusion.5.cat), channel_id=1, source_target_pairs={{1,0},{2,1},{3,2},{4,3},{5,4},{6,5},{7,6},{8,7},{9,8},{10,9},{11,1... | collective-permute-start | bytes 614408 | tf_op jit(solution)/shard_map/ppermute | solution.py:17
  83.7 12.3 %collective-permute-start.15 = (f32[1,8,256]{2,1,0:T(8,128)S(1)}, f32[1,8,256]{2,1,0:T(8,128)S(1)}, u32[]{:S(2)}, u32[]{:S(2)}) collective-permute-start(f32[1,8,256]{2,1,0:T(8,128)S(1)} %shard_map.72), channel_id=1, source_target_pairs={{0,32},{16,48},{32,64},{48,80},{64,96},{80,112},{96,128},{112,144}... | collective-permute-start | bytes 24584 | tf_op jit(solution)/shard_map/ppermute | solution.py:17
  90.3 5.7 %collective-permute-start.16 = (f32[1,8,256]{2,1,0:T(8,128)S(1)}, f32[1,8,256]{2,1,0:T(8,128)S(1)}, u32[]{:S(2)}, u32[]{:S(2)}) collective-permute-start(f32[1,8,256]{2,1,0:T(8,128)S(1)} %shard_map.72), channel_id=1, source_target_pairs={{0,16},{16,32},{32,48},{48,64},{64,80},{80,96},{96,112},{112,128},... | collective-permute-start | bytes 24584 | tf_op jit(solution)/shard_map/ppermute | solution.py:17
  93.4 5.9 %collective-permute-start.17 = (f32[1,8,256]{2,1,0:T(8,128)S(1)}, f32[1,8,256]{2,1,0:T(8,128)S(1)}, u32[]{:S(2)}, u32[]{:S(2)}) collective-permute-start(f32[1,8,256]{2,1,0:T(8,128)S(1)} %shard_map.72), channel_id=1, source_target_pairs={{16,0},{32,16},{48,32},{64,48},{80,64},{96,80},{112,96},{128,112},... | collective-permute-start | bytes 24584 | tf_op jit(solution)/shard_map/ppermute | solution.py:17
  94.7 7.4 %collective-permute-start.18 = (f32[1,8,256]{2,1,0:T(8,128)S(1)}, f32[1,8,256]{2,1,0:T(8,128)S(1)}, u32[]{:S(2)}, u32[]{:S(2)}) collective-permute-start(f32[1,8,256]{2,1,0:T(8,128)S(1)} %shard_map.72), channel_id=1, source_target_pairs={{32,0},{48,16},{64,32},{80,48},{96,64},{112,80},{128,96},{144,112}... | collective-permute-start | bytes 24584 | tf_op jit(solution)/shard_map/ppermute | solution.py:17
  102.1 5.4 %collective-permute-start.19 = (f32[5,8,256]{2,1,0:T(8,128)S(1)}, f32[5,8,256]{2,1,0:T(8,128)S(1)}, u32[]{:S(2)}, u32[]{:S(2)}) collective-permute-start(f32[5,8,256]{2,1,0:T(8,128)S(1)} %constant_dynamic-update-slice_fusion.reds), channel_id=1, source_target_pairs={{0,1},{1,2},{2,3},{3,4},{4,5},{5,6},{6,7},{7,8},{8,9},{9,10},{10,1... | collective-permute-start | bytes 122888 | tf_op jit(solution)/shard_map/ppermute | solution.py:17
  105.6 5.3 %collective-permute-start.20 = (f32[5,8,256]{2,1,0:T(8,128)S(1)}, f32[5,8,256]{2,1,0:T(8,128)S(1)}, u32[]{:S(2)}, u32[]{:S(2)}) collective-permute-start(f32[5,8,256]{2,1,0:T(8,128)S(1)} %constant_dynamic-update-slice_fusion.reds), channel_id=1, source_target_pairs={{1,0},{2,1},{3,2},{4,3},{5,4},{6,5},{7,6},{8,7},{9,8},{10,9},{11,1... | collective-permute-start | bytes 122888 | tf_op jit(solution)/shard_map/ppermute | solution.py:17
  112.3 17.8 %all-to-all-start = ((f32[16,16,128]{2,1,0:T(8,128)}), f32[16,16,128]{2,1,0:T(8,128)S(1)}, u32[]{:S(2)}, u32[]{:S(2)}) async-start(f32[16,16,128]{2,1,0:T(8,128)} %get-tuple-element.17), calls=%async_computation | async-start | bytes 262144 | tf_op jit(solution)/shard_map/all_to_all | solution.py:489

commit v3 on v0

v3 whole, which is shorter than its diff:
```python
import jax
import jax.numpy as jnp
from jax import lax
from jax.experimental import pallas as pl
from jax.experimental.pallas import tpu as pltpu
from jax.sharding import PartitionSpec as P

F32 = jnp.float32
RHS, ALPHA, BX, BY, BZ = range(5)
VMEM_BYTES = 20 * 2**20
RING = 8


def shifted(values, axis, name, steps):
    count = lax.axis_size(name)
    lead, last = max(0, -steps), min(count, count - steps)
    return lax.ppermute(values, name, [(i, i + steps) for i in range(lead, last)])


def call(kernel, outs, scratch=(), smem=()):
    def run(*args):
        specs = [
            pl.BlockSpec(memory_space=pltpu.SMEM if i in smem else pltpu.VMEM)
            for i in range(len(args))
        ]
        shapes = [jax.ShapeDtypeStruct(s, F32) for s in outs]
        return pl.pallas_call(
            kernel,
            out_shape=shapes,
            in_specs=specs,
            out_specs=[pl.BlockSpec(memory_space=pltpu.VMEM)] * len(outs),
            scratch_shapes=[pltpu.VMEM(s, F32) for s in scratch],
            compiler_params=pltpu.CompilerParams(vmem_limit_bytes=VMEM_BYTES),
        )(*args)

    return run


def iotas(shape):
    return lax.broadcasted_iota(jnp.int32, shape, 0), lax.broadcasted_iota(jnp.int32, shape, 1)


def even_mask(shape):
    row, lane = iotas(shape)
    return ((row + lane) & 1) == 0


def half(x):
    return pltpu.roll(x, 4, 0)


def prev_row(x):
    return pltpu.roll(x, 1, 0)


def next_row(x):
    return pltpu.roll(x, x.shape[0] - 1, 0)


def prev_lane(x):
    return pltpu.roll(x, 1, 1)


def next_lane(x):
    return pltpu.roll(x, x.shape[1] - 1, 1)


def exact_dot(a, b):
    return jnp.dot(a, b, precision=lax.Precision.HIGHEST, preferred_element_type=F32)


def one_hot(shape, test):
    row, col = iotas(shape)
    return jnp.where(test(row, col), 1.0, 0.0).astype(F32)


def low_rows(shape):
    row, _ = iotas(shape)
    return (row & 7) < 4


def inverse_of(diagonal, cell):
    inside = cell > 0.0
    return jnp.where(inside, 1.0 / jnp.where(inside, diagonal, 1.0), 0.0)


def halves(q0, e0, e1):
    return jnp.where(q0, e0, e1), jnp.where(q0, e1, e0)


def clear_guards(r, b, n):
    for ref in (r, b):
        ref[0] = jnp.zeros_like(ref[0])
        ref[n + 1] = jnp.zeros_like(ref[n + 1])


S_R, S_B, WP, WO_R, WO_B, YM_R, YM_B, YP_R, YP_B, ZM_R, ZM_B, ZP_R, ZP_B, I_R, I_B, D_R, D_B = range(17)


def beside(co, src, p, red, q0):
    v = src[p + 1]
    before, after = src[p], src[p + 2]
    other = jnp.where(q0, before, after) if red else jnp.where(q0, after, before)
    wo, ym, yp, zm, zp = (
        (WO_R, YM_R, YP_R, ZM_R, ZP_R) if red else (WO_B, YM_B, YP_B, ZM_B, ZP_B)
    )
    total = co[WP, p] * v + co[wo, p] * other
    total = total + (co[ym, p] * prev_row(v) + co[yp, p] * next_row(v))
    return total + (co[zm, p] * prev_lane(v) + co[zp, p] * next_lane(v))


def relax(co, dst, src, pairs, red, q0):
    s, inv = (S_R, I_R) if red else (S_B, I_B)
    for p in pairs:
        dst[p + 1] = (co[s, p] + beside(co, src, p, red, q0)) * co[inv, p]


def first_red(co, dst, pairs):
    for p in pairs:
        dst[p + 1] = co[S_R, p] * co[I_R, p]


def residual(co, r, b, p, q0):
    red = co[S_R, p] - (co[D_R, p] * r[p + 1] - beside(co, b, p, True, q0))
    black = co[S_B, p] - (co[D_B, p] * b[p + 1] - beside(co, r, p, False, q0))
    return red, black


def put_faces(co, p, q0, bx, by, bz):
    b0, b1, b2 = bx
    wo_r, wo_b = halves(q0, b0, b2)
    y_r, y_b = halves(q0, *by)
    z_r, z_b = halves(q0, *bz)
    yp_r, yp_b = next_row(y_b), next_row(y_r)
    zp_r, zp_b = next_lane(z_b), next_lane(z_r)
    co[WP, p], co[WO_R, p], co[WO_B, p] = b1, wo_r, wo_b
    co[YM_R, p], co[YM_B, p], co[YP_R, p], co[YP_B, p] = y_r, y_b, yp_r, yp_b
    co[ZM_R, p], co[ZM_B, p], co[ZP_R, p], co[ZP_B, p] = z_r, z_b, zp_r, zp_b
    return (b1 + wo_r, b1 + wo_b), (y_r, y_b), (yp_r, yp_b), (z_r + zp_r, z_b + zp_b)


def smooth_cone(co, r, b, own, halo, q0):
    def pairs(reach):
        extra = min(halo, (reach + 1) // 2)
        return range(halo - extra, halo + own + extra)

    first_red(co, r, pairs(8))
    for step in range(2, 9):
        red = step % 2 == 1
        relax(co, r if red else b, b if red else r, pairs(9 - step), red, q0)


def to_windows_kernel(rhs, alpha, beta_x, beta_y, beta_z, out):
    _, lane = iotas((8, 128))
    zero = jnp.zeros((8, 128), F32)
    for a, ref in enumerate((rhs, alpha, beta_x, beta_y, beta_z)):
        for x in range(4):
            tiles = [ref[x, :, 128 * c : 128 * c + 128] for c in range(4)]
            up = [pltpu.roll(t, 32, 1) for t in tiles]
            down = [pltpu.roll(t, 96, 1) for t in tiles]
            for c in range(4):
                out[2 * c, a, x] = jnp.where(lane < 32, up[c - 1] if c else zero, up[c])
                out[2 * c + 1, a, x] = jnp.where(lane < 96, down[c], down[c + 1] if c < 3 else zero)


def x_messages_kernel(own, to_low, to_high, first_by):
    for s in range(2):
        for a in range(5):
            for x in range(4):
                t = (s * 5 + a) * 4 + x
                to_low[t] = own[s, a, x]
                to_high[t] = own[6 + s, a, x]
    to_low[40] = own[2, BX, 0]
    for x in range(32):
        first_by[x : x + 1] = own[x // 4, BY, x % 4][:1]


def y_message_kernel(low, own, high, out, beyond):
    for a in range(5):
        for x in range(4):
            for s in range(2):
                t = (s * 5 + a) * 4 + x
                out[s, a, x] = low[t]
                out[10 + s, a, x] = high[t]
            for s in range(8):
                out[2 + s, a, x] = own[s, a, x]
    beyond[...] = high[40]


def fine_kernel(mine, low, high, beyond_x, beyond_y, fine_out, mid_first, mid_last, own_out, co, r, b):
    q0 = even_mask((24, 128))
    row, lane = iotas((24, 128))
    clear_guards(r, b, 24)
    zero = jnp.zeros((8, 128), F32)

    def plane(a, x):
        return jnp.concatenate([ref[x // 4, a, x % 4] for ref in (mine, high, low)], 0)

    bx0 = plane(BX, 0)
    for p in range(24):
        x = 2 * p
        co[S_R, p], co[S_B, p] = halves(q0, plane(RHS, x), plane(RHS, x + 1))
        bx1 = plane(BX, x + 1)
        bx2 = plane(BX, x + 2) if p < 23 else jnp.concatenate([beyond_x[...], zero, zero], 0)
        by = plane(BY, x), plane(BY, x + 1)
        bz = plane(BZ, x), plane(BZ, x + 1)
        fx, fy, fyp, fz = put_faces(co, p, q0, (bx0, bx1, bx2), by, bz)
        bx0 = bx2
        yp_r, yp_b = fyp
        if 4 <= p < 20:
            e0, e1 = beyond_y[x - 8 : x - 7], beyond_y[x - 7 : x - 6]
            up_r, up_b = halves(q0[15:16], e0, e1)
            yp_r = jnp.where(row == 15, up_r, yp_r)
            yp_b = jnp.where(row == 15, up_b, yp_b)
            co[YP_R, p], co[YP_B, p] = yp_r, yp_b
        a_r, a_b = halves(q0, plane(ALPHA, x), plane(ALPHA, x + 1))
        d_r = a_r + ((fx[0] + fz[0]) + (fy[0] + yp_r))
        d_b = a_b + ((fx[1] + fz[1]) + (fy[1] + yp_b))
        co[D_R, p], co[D_B, p] = d_r, d_b
        co[I_R, p], co[I_B, p] = inverse_of(d_r, a_r), inverse_of(d_b, a_b)
    smooth_cone(co, r, b, 16, 4, q0)
    sums, alphas, bys, nexts, bxs, bzs = [], [], [], [], [], []
    for j in range(16):
        p = j + 4
        red, black = residual(co, r, b, p, q0)
        sums.append((red + black)[:8])
        fine_out[0, j] = r[p + 1][:8]
        fine_out[1, j] = b[p + 1][:8]
        s, x = (2 * p) // 4, (2 * p) % 4
        alphas.append(mine[s, ALPHA, x] + mine[s, ALPHA, x + 1])
        bys.append(mine[s, BY, x] + mine[s, BY, x + 1])
        nexts.append(high[s, BY, x] + high[s, BY, x + 1])
        bzs.append(mine[s, BZ, x] + mine[s, BZ, x + 1])
        bxs.append(mine[s, BX, x])
    bxs.append(mine[10, BX, 0])
    z_sum = one_hot((128, 128), lambda i, j: (i >> 1) == j)
    z_even = one_hot((128, 128), lambda i, j: i == 2 * j)
    y_sum = one_hot((64, 128), lambda i, j: (j >> 1) == i)
    y_even = one_hot((64, 128), lambda i, j: j == 2 * i)
    y_next = one_hot((64, 128), lambda i, j: ((i & 3) < 3) & (j == 2 * i + 2))
    y_last = one_hot((64, 128), lambda i, j: ((i & 3) == 3) & (j == 8 * (i >> 2)))
    along = exact_dot(jnp.concatenate(sums + alphas + bys + nexts + bxs, 0), z_sum)
    bz_z = exact_dot(jnp.concatenate(bzs, 0), z_even)
    source = exact_dot(y_sum, along[0:128]) * 0.125
    alpha = exact_dot(y_sum, along[128:256]) * 0.125
    y_lower = exact_dot(y_even, along[256:384]) * 0.0625
    y_upper = (exact_dot(y_next, along[256:384]) + exact_dot(y_last, along[384:512])) * 0.0625
    x_lower = exact_dot(y_sum, along[512:640]) * 0.0625
    x_upper = exact_dot(y_sum, along[520:648]) * 0.0625
    z_lower = exact_dot(y_sum, bz_z) * 0.0625
    z_upper = next_lane(z_lower)
    diagonal = alpha + ((x_lower + x_upper) + (y_lower + y_upper) + (z_lower + z_upper))
    arrays = (source, inverse_of(diagonal, alpha), x_lower, y_lower, z_lower)
    _, lane = iotas((8, 128))

    def tile(value, t):
        return jnp.where(lane < 64, value[16 * t : 16 * t + 8], pltpu.roll(value[16 * t + 8 : 16 * t + 16], 64, 1))

    for t in range(4):
        for a, value in enumerate(arrays):
            (mid_first if t < 2 else mid_last)[t % 2, a] = tile(value, t)
        own_out[t, 0] = tile(diagonal, t)
        own_out[t, 1] = tile(alpha, t)


def mid_message_kernel(low, first, last, high, near, far):
    tiles = [ref[s] for ref in (low, first, last, high) for s in range(2)]
    for s in range(8):
        near[s] = tiles[s]
        if 0 < s < 7:
            far[s - 1] = tiles[s]


def mid_kernel(mine, low1, high1, low2, high2, own, level_out, low_out, co, r, b):
    q0 = even_mask((24, 128))
    _, lane = iotas((8, 128))
    keep = low_rows((8, 128))
    zero = jnp.zeros((8, 128), F32)
    clear_guards(r, b, 16)

    def part(tile, p):
        return jnp.where(lane < 64, pltpu.roll(tile, 64, 1) if p % 2 else tile, 0.0)

    def planes(p, a):
        t = p // 2
        c, h1, w1 = part(mine[t, a], p), part(high1[t, a], p), part(low1[t, a], p)
        inner = 0 < t < 7
        h2 = part(high2[t - 1, a], p) if inner else zero
        w2 = part(low2[t - 1, a], p) if inner else zero
        e0 = [jnp.where(keep, c, half(h1)), jnp.where(keep, h2, 0.0), jnp.where(keep, w2, half(w1))]
        e1 = [jnp.where(keep, half(c), h1), jnp.where(keep, half(h2), 0.0), jnp.where(keep, half(w2), w1)]
        return jnp.concatenate(e0, 0), jnp.concatenate(e1, 0)

    bx0, bx1 = planes(0, 2)
    for p in range(16):
        co[S_R, p], co[S_B, p] = halves(q0, *planes(p, 0))
        co[I_R, p], co[I_B, p] = halves(q0, *planes(p, 1))
        n0, n1 = planes(p + 1, 2) if p < 15 else (jnp.zeros_like(bx0), bx1)
        put_faces(co, p, q0, (bx0, bx1, n0), planes(p, 3), planes(p, 4))
        bx0, bx1 = n0, n1
        if 4 <= p < 12:
            d = part(own[p // 2 - 2, 0], p)
            d = jnp.concatenate([d, d, d], 0), jnp.concatenate([half(d)] * 3, 0)
            co[D_R, p], co[D_B, p] = halves(q0, *d)
    smooth_cone(co, r, b, 8, 4, q0)
    sums = jnp.zeros((32, 128), F32)
    bz_z = zero
    for k in range(8):
        p = k + 4
        red, black = residual(co, r, b, p, q0)
        level_out[0, k] = r[p + 1][:8]
        level_out[1, k] = b[p + 1][:8]
        mid = [part(mine[p // 2, a], p) for a in (2, 3, 4)]
        stack = jnp.concatenate([(red + black)[:8], part(own[p // 2 - 2, 1], p), mid[0], mid[1]], 0)
        sums += exact_dot(stack, one_hot((128, 128), lambda i, j: ((i >> 1) == j - 16 * k + 8) & ((j >> 4) == k)))
        bz_z += exact_dot(mid[2], one_hot((128, 128), lambda i, j: (i == 2 * (j - 16 * k + 8)) & ((j >> 4) == k)))

    def rows(out_row, test):
        return one_hot((16, 8), lambda i, j: ((i >> 1) == out_row) & test(i & 1, j))

    total = exact_dot(rows(0, lambda i, j: (j < 4) & ((j >> 1) == i)), sums[0:8]) * 0.125
    total += exact_dot(rows(1, lambda i, j: ((j & 3) >> 1) == i), sums[8:16]) * 0.125
    total += exact_dot(rows(2, lambda i, j: (j < 4) & ((j >> 1) == i)), sums[16:24]) * 0.0625
    total += exact_dot(rows(3, lambda i, j: (j & 3) == 2 * i), sums[24:32]) * 0.0625
    total += exact_dot(rows(4, lambda i, j: ((j & 3) >> 1) == i), bz_z) * 0.0625
    for j in range(low_out.shape[0]):
        low_out[j] = total


def whole_y_kernel(gathered, out):
    flat = gathered[...].reshape(256, 128)

    def test(i, j):
        k, y = i >> 5, i & 31
        return j == (y >> 1) * 16 + 2 * k + (y & 1)

    out[...] = exact_dot(one_hot((160, 256), test), flat)


def copies_kernel(left, own, right, out):
    for g in range(out.shape[0]):
        for s, ref in enumerate((left, own, right)):
            out[g, s] = ref[...]


def coarse_kernel(sweeps, index, gathered, level, fine, out, co, r, b):
    shape = (32, 128)
    q0 = even_mask(shape)
    row, lane = iotas(shape)
    r[...] = jnp.zeros_like(r)
    b[...] = jnp.zeros_like(b)

    def plane(a, i):
        total = jnp.zeros(shape, F32)
        for side in range(2):
            x = i + 16 * side
            for s in range(3):
                target = 64 * side + 16 * s
                block = gathered[x // 8, s, 32 * a : 32 * a + 32]
                shift = (target - 16 * (x % 8)) % 128
                moved = pltpu.roll(block, shift, 1) if shift else block
                total = jnp.where((lane >> 4) == target // 16, moved, total)
        return total

    first_bx = plane(2, 0)
    bx0 = first_bx
    for p in range(8):
        x = 2 * p
        co[S_R, p], co[S_B, p] = halves(q0, plane(0, x), plane(0, x + 1))
        bx1 = plane(2, x + 1)
        bx2 = plane(2, x + 2) if p < 7 else jnp.where(lane < 64, pltpu.roll(first_bx, 64, 1), 0.0)
        by, bz = (plane(3, x), plane(3, x + 1)), (plane(4, x), plane(4, x + 1))
        fx, fy, fyp, fz = put_faces(co, p, q0, (bx0, bx1, bx2), by, bz)
        bx0 = bx2
        yp_r, yp_b = jnp.where(row == 31, 0.0, fyp[0]), jnp.where(row == 31, 0.0, fyp[1])
        co[YP_R, p], co[YP_B, p] = yp_r, yp_b
        co[YM_R, p], co[YM_B, p] = jnp.where(row == 0, 0.0, fy[0]), jnp.where(row == 0, 0.0, fy[1])
        a_r, a_b = halves(q0, plane(1, x), plane(1, x + 1))
        d_r = a_r + ((fx[0] + fz[0]) + (fy[0] + yp_r))
        d_b = a_b + ((fx[1] + fz[1]) + (fy[1] + yp_b))
        co[I_R, p], co[I_B, p] = inverse_of(d_r, a_r), inverse_of(d_b, a_b)

    def join(ref):
        ref[0] = jnp.where(lane < 64, 0.0, pltpu.roll(ref[8], 64, 1))
        ref[9] = jnp.where(lane < 64, pltpu.roll(ref[1], 64, 1), 0.0)

    def sweep(step, carry):
        relax(co, r, b, range(8), True, q0)
        join(r)
        relax(co, b, r, range(8), False, q0)
        join(b)
        return carry

    lax.fori_loop(0, sweeps, sweep, 0)

    gy, gx = index[0], index[1]
    ring, place = gx // RING, lax.rem(gx, RING)
    side, base = ring // 2, 4 * lax.rem(ring, 2)
    own = []
    for k in range(8):
        red, black = r[base + k // 2 + 1], b[base + k // 2 + 1]
        value = jnp.where(q0, red, black) if k % 2 == 0 else jnp.where(q0, black, red)
        value = pltpu.roll(value, lax.rem(32 - 2 * gy, 32), 0)
        own.append(pltpu.roll(value, 64 * side, 1)[:8])
    q0 = even_mask((8, 128))
    row, lane = iotas((8, 128))
    up = exact_dot(jnp.concatenate(own, 0), one_hot((128, 128), lambda i, j: (j >> 1) + 8 == i))
    spread = one_hot((64, 64), lambda i, j: ((i >> 3) == (j >> 3)) & (((i & 3) >> 1) == (j & 7)))
    up = exact_dot(spread, up)
    mid = []
    for k in range(8):
        add = up[8 * k : 8 * k + 8]
        mid.extend(halves(q0, level[0, k] + add, level[1, k] + add))
        mine = pltpu.roll(own[k], lax.rem(16 * place + 112, 128), 1)
        out[k, 2] = jnp.where(((lane >> 4) == place) & (row < 2), mine, 0.0)
    wide = exact_dot(jnp.concatenate(mid, 0), one_hot((128, 128), lambda i, j: (j >> 1) == i))
    spread = one_hot((128, 128), lambda i, j: ((i >> 3) == (j >> 3)) & (((i & 7) >> 1) == (j & 7)))
    wide = exact_dot(spread, wide)
    for j in range(16):
        add = wide[8 * j : 8 * j + 8]
        e0, e1 = halves(q0, fine[0, j] + add, fine[1, j] + add)
        out[j // 2, j % 2] = jnp.where(lane < 64, pltpu.roll(e0, 96, 1), pltpu.roll(e1, 32, 1))


def finish_kernel(pieces, fine_out, coarse_out):
    _, lane = iotas((8, 128))
    for t in range(2):
        for c in range(4):
            a, b = pieces[2 * c, t], pieces[2 * c + 1, t]
            span = slice(128 * c, 128 * c + 128)
            fine_out[2 * t, :, span] = jnp.where(lane < 64, a, pltpu.roll(b, 64, 1))
            fine_out[2 * t + 1, :, span] = jnp.where(lane < 64, pltpu.roll(a, 64, 1), b)
    total = pieces[0, 2]
    for j in range(1, RING):
        total = total + pieces[j, 2]
    coarse_out[0] = total[:2]


def in_rings(values, steps):
    count = lax.axis_size("gx")
    pairs = [(i, i + steps) for i in range(count) if 0 <= i % RING + steps < RING]
    return lax.ppermute(values, "gx", pairs)


def on_device(rhs, alpha, beta_x, beta_y, beta_z):
    count_x, count_y = lax.axis_size("gx"), lax.axis_size("gy")
    groups = count_x // RING
    rings = [[RING * i + j for j in range(RING)] for i in range(groups)]
    across = [list(c) for c in zip(*rings)]
    index = jnp.stack([lax.axis_index("gy"), lax.axis_index("gx")]).astype(jnp.int32)

    (own,) = call(to_windows_kernel, [(RING, 5, 4, 8, 128)])(rhs, alpha, beta_x, beta_y, beta_z)
    own = lax.all_to_all(own, "gx", 0, 0, tiled=True, axis_index_groups=rings)
    to_low, to_high, first_by = call(
        x_messages_kernel, [(41, 8, 128), (40, 8, 128), (32, 128)]
    )(own)
    low, high = shifted(to_high, 1, "gx", RING), shifted(to_low, 1, "gx", -RING)
    mine, beyond_x = call(
        y_message_kernel, [(12, 5, 4, 8, 128), (8, 128)]
    )(low, own, high)
    low, high = shifted(mine, 1, "gy", 1), shifted(mine, 1, "gy", -1)
    beyond_y = shifted(first_by, 0, "gy", -2)
    fine, mid_first, mid_last, mid_own = call(
        fine_kernel,
        [(2, 16, 8, 128), (2, 5, 8, 128), (2, 5, 8, 128), (4, 2, 8, 128)],
        [(17, 24, 24, 128), (26, 24, 128), (26, 24, 128)],
    )(mine, low, high, beyond_x, beyond_y)

    low, high = shifted(mid_last, 0, "gx", RING), shifted(mid_first, 0, "gx", -RING)
    near, far = call(
        mid_message_kernel, [(8, 5, 8, 128), (6, 5, 8, 128)]
    )(low, mid_first, mid_last, high)
    level, low = call(
        mid_kernel,
        [(2, 8, 8, 128), (count_y, 16, 128)],
        [(17, 16, 24, 128), (18, 24, 128), (18, 24, 128)],
    )(
        near, shifted(near, 0, "gy", 1), shifted(near, 0, "gy", -1),
        shifted(far, 0, "gy", 2), shifted(far, 0, "gy", -2), mid_own,
    )

    low = lax.all_to_all(low, "gy", 0, 0, tiled=True)
    (low,) = call(whole_y_kernel, [(160, 128)])(low)
    (low,) = call(copies_kernel, [(groups, 3, 160, 128)])(in_rings(low, 1), low, in_rings(low, -1))
    low = lax.all_to_all(low, "gx", 0, 0, tiled=True, axis_index_groups=across)
    (pieces,) = call(
        lambda *refs: coarse_kernel(8, *refs),
        [(RING, 3, 8, 128)],
        [(17, 8, 32, 128), (10, 32, 128), (10, 32, 128)],
        smem=(0,),
    )(index, low, level, fine)
    pieces = lax.all_to_all(pieces, "gx", 0, 0, tiled=True, axis_index_groups=rings)
    fine_solution, coarse = call(finish_kernel, [rhs.shape, (1, 2, 128)])(pieces)
    return fine_solution, coarse


def solution(mesh):
    placed = P("gx", "gy", None)
    return jax.shard_map(
        on_device,
        mesh=mesh,
        in_specs=(placed,) * 5,
        out_specs=(placed, placed),
        check_vma=False,
    )
```

time: 708 us -> 161 us (0.23)
  the two profiles are of different devices: /device:TPU:38 before, /device:TPU:1 now
where the time goes in v3:
time: 161 us; the launch traced here: 159 us
  blocking collectives  61.6 us (38%)
  starting transfers between devices  40.3 us (25%)
  waiting for transfers between devices  37.9 us (24%)
  Pallas kernels  14.4 us (9%)
  local copies, waits for them, and re-layouts  4.19 us (3%)
    ppermute x11, starting transfers between devices, shifted(): lax.ppermute(values, name, [(i, i + steps) for i in range(lead, last)])  32.8 us
    all_to_all x1, blocking collectives, on_device(): own = lax.all_to_all(own, 'gx', 0, 0, tiled=True, axis_index_groups=rings)  29.9 us
    all_to_all x1, blocking collectives, on_device(): low = lax.all_to_all(low, 'gy', 0, 0, tiled=True)  21.6 us
    ppermute x11, waiting for transfers between devices, shifted(): lax.ppermute(values, name, [(i, i + steps) for i in range(lead, last)])  20.3 us
    pallas_call x10, Pallas kernels, run(): pl.pallas_call(kernel, out_shape=shapes, in_specs=specs, out_specs=[pl.Bl...  14.4 us
    all_to_all x1, waiting for transfers between devices, on_device(): low = lax.all_to_all(low, 'gx', 0, 0, tiled=True, axis_index_groups=across)  13.1 us
    all_to_all x1, blocking collectives, on_device(): lax.all_to_all(pieces, 'gx', 0, 0, tiled=True, axis_index_groups=rings)  10.1 us
    ppermute x2, waiting for transfers between devices, in_rings(): return lax.ppermute(values, 'gx', pairs)  4.45 us
  transfers between devices with their start and end apart: 14, of which 10 were waited for; matrix products, arithmetic and copies ran while one was open for 0% of the time, Pallas kernels for 0%

profile of v3, /device:TPU:1, one launch (start us, length us, event | category | flops | bytes accessed | tf_op | source)
XLA Modules:
  0.0 159.2 jit_solution(1384361220782485302)
XLA Ops:
  0.6 0.0 copy-start
  0.6 0.8 copy-done
  1.5 0.0 copy-start.1
  1.5 0.8 copy-done.1
  2.3 0.0 copy-start.2
  2.3 0.8 copy-done.2
  3.2 0.8 copy-done.3
  4.0 0.8 copy-done.4
  4.8 0.2 shard_map.68
  5.1 29.9 %all_to_all.20.own = f32[8,5,4,8,128]{4,3,2,1,0:T(8,128)S(1)} all-to-all(f32[8,5,4,8,128]{4,3,2,1,0:T(8,128)S(1)} %shard_map.68), channel_id=1, replica_groups={{0,16,32,48,64,80,96,112},{128,144,160,176,192,208,224,240},{256,272,28..., dimensions={0} | all-to-all | bytes 1310720 | tf_op jit(solution)/shard_map/all_to_all | solution.py:453
  35.0 1.3 collective-permute-start.1
  36.3 4.0 %collective-permute-start = (f32[40,8,128]{2,1,0:T(8,128)S(1)}, f32[40,8,128]{2,1,0:T(8,128)S(1)}, u32[]{:S(2)}, u32[]{:S(2)}) collective-permute-start(f32[40,8,128]{2,1,0:T(8,128)S(1)} %get-tuple-element.15), channel_id=1, source_target_pairs={{0,128},{16,144},{32,160},{48,176},{64,192},{80,208},{96,224},{112... | collective-permute-start | bytes 491528 | tf_op jit(solution)/shard_map/ppermute | solution.py:17
  40.3 2.2 %collective-permute-done.low = f32[40,8,128]{2,1,0:T(8,128)S(1)} collective-permute-done((f32[40,8,128]{2,1,0:T(8,128)S(1)}, f32[40,8,128]{2,1,0:T(8,128)S(1)}, u32[]{:S(2)}, u32[]{:S(2)}) %collective-permute-start) | collective-permute-done | bytes 163872 | tf_op jit(solution)/shard_map/ppermute | solution.py:17
  42.5 0.0 collective-permute-done.1.high
  42.5 0.1 shard_map.70
  42.6 6.3 %collective-permute-start.2 = (f32[12,5,4,8,128]{4,3,2,1,0:T(8,128)S(1)}, f32[12,5,4,8,128]{4,3,2,1,0:T(8,128)S(1)}, u32[]{:S(2)}, u32[]{:S(2)}) collective-permute-start(f32[12,5,4,8,128]{4,3,2,1,0:T(8,128)S(1)} %get-tuple-element.17.mine), channel_id=1, source_target_pairs={{0,1},{1,2},{2,3},{3,4},{4,5},{5,6},{6,7},{7,8},{8,9},{9,10},{10,1... | collective-permute-start | bytes 2949128 | tf_op jit(solution)/shard_map/ppermute | solution.py:17
  48.9 1.9 %collective-permute-start.3 = (f32[12,5,4,8,128]{4,3,2,1,0:T(8,128)S(1)}, f32[12,5,4,8,128]{4,3,2,1,0:T(8,128)S(1)}, u32[]{:S(2)}, u32[]{:S(2)}) collective-permute-start(f32[12,5,4,8,128]{4,3,2,1,0:T(8,128)S(1)} %get-tuple-element.17.mine), channel_id=1, source_target_pairs={{1,0},{2,1},{3,2},{4,3},{5,4},{6,5},{7,6},{8,7},{9,8},{10,9},{11,1... | collective-permute-start | bytes 2949128 | tf_op jit(solution)/shard_map/ppermute | solution.py:17
  50.8 1.3 collective-permute-start.4
  52.1 3.4 %collective-permute-done.4.beyond_y = f32[32,128]{1,0:T(8,128)S(1)} collective-permute-done((f32[32,128]{1,0:T(8,128)S(1)}, f32[32,128]{1,0:T(8,128)S(1)}, u32[]{:S(2)}, u32[]{:S(2)}) %collective-permute-start.4) | collective-permute-done | bytes 16416 | tf_op jit(solution)/shard_map/ppermute | solution.py:17
  55.5 4.4 %collective-permute-done.2.low = f32[12,5,4,8,128]{4,3,2,1,0:T(8,128)S(1)} collective-permute-done((f32[12,5,4,8,128]{4,3,2,1,0:T(8,128)S(1)}, f32[12,5,4,8,128]{4,3,2,1,0:T(8,128)S(1)}, u32[]{:S(2)}, u32[]{:S(2)}) %collective-permute-start.2) | collective-permute-done | bytes 983072 | tf_op jit(solution)/shard_map/ppermute | solution.py:17
  59.9 4.6 %collective-permute-done.3.high = f32[12,5,4,8,128]{4,3,2,1,0:T(8,128)S(1)} collective-permute-done((f32[12,5,4,8,128]{4,3,2,1,0:T(8,128)S(1)}, f32[12,5,4,8,128]{4,3,2,1,0:T(8,128)S(1)}, u32[]{:S(2)}, u32[]{:S(2)}) %collective-permute-start.3) | collective-permute-done | bytes 983072 | tf_op jit(solution)/shard_map/ppermute | solution.py:17
  64.5 3.8 %shard_map.71 = (f32[2,16,8,128]{3,2,1,0:T(8,128)S(1)}, f32[2,5,8,128]{3,2,1,0:T(8,128)S(1)}, f32[2,5,8,128]{3,2,1,0:T(8,128)S(1)}, f32[4,2,8,128]{3,2,1,0:T(8,128)S(1)}) custom-call(f32[12,5,4,8,128]{4,3,2,1,0:T(8,128)S(1)} %get-tuple-element.17.mine, f32[12,5,4,8,128]{4,3,2,1,0:T(8,128)S(1)} %collective-permute-done.2.low, ...), custom_call_target="tpu_custom_call" | custom-call | tf_op jit(solution)/shard_map/pallas_call | solution.py:27
  68.3 4.1 %collective-permute-start.5 = (f32[2,5,8,128]{3,2,1,0:T(8,128)S(1)}, f32[2,5,8,128]{3,2,1,0:T(8,128)S(1)}, u32[]{:S(2)}, u32[]{:S(2)}) collective-permute-start(f32[2,5,8,128]{3,2,1,0:T(8,128)S(1)} %get-tuple-element.20.last), channel_id=1, source_target_pairs={{0,128},{16,144},{32,160},{48,176},{64,192},{80,208},{96,224},{112... | collective-permute-start | bytes 122888 | tf_op jit(solution)/shard_map/ppermute | solution.py:17
  72.4 1.3 collective-permute-start.6
  73.7 0.0 collective-permute-done.5.low
  73.7 3.4 %collective-permute-done.6.high = f32[2,5,8,128]{3,2,1,0:T(8,128)S(1)} collective-permute-done((f32[2,5,8,128]{3,2,1,0:T(8,128)S(1)}, f32[2,5,8,128]{3,2,1,0:T(8,128)S(1)}, u32[]{:S(2)}, u32[]{:S(2)}) %collective-permute-start.6) | collective-permute-done | bytes 40992 | tf_op jit(solution)/shard_map/ppermute | solution.py:17
  77.2 5.4 %collective-permute-start.7 = (f32[8,5,8,128]{3,2,1,0:T(8,128)S(1)}, f32[8,5,8,128]{3,2,1,0:T(8,128)S(1)}, u32[]{:S(2)}, u32[]{:S(2)}) collective-permute-start(f32[8,5,8,128]{3,2,1,0:T(8,128)S(1)} %get-tuple-element.22.mine), channel_id=1, source_target_pairs={{0,1},{1,2},{2,3},{3,4},{4,5},{5,6},{6,7},{7,8},{8,9},{9,10},{10,1... | collective-permute-start | bytes 491528 | tf_op jit(solution)/shard_map/ppermute | solution.py:17
  82.6 1.9 %collective-permute-start.8 = (f32[8,5,8,128]{3,2,1,0:T(8,128)S(1)}, f32[8,5,8,128]{3,2,1,0:T(8,128)S(1)}, u32[]{:S(2)}, u32[]{:S(2)}) collective-permute-start(f32[8,5,8,128]{3,2,1,0:T(8,128)S(1)} %get-tuple-element.22.mine), channel_id=1, source_target_pairs={{1,0},{2,1},{3,2},{4,3},{5,4},{6,5},{7,6},{8,7},{9,8},{10,9},{11,1... | collective-permute-start | bytes 491528 | tf_op jit(solution)/shard_map/ppermute | solution.py:17
  84.5 1.3 collective-permute-start.10
  85.8 4.0 %collective-permute-start.9 = (f32[6,5,8,128]{3,2,1,0:T(8,128)S(1)}, f32[6,5,8,128]{3,2,1,0:T(8,128)S(1)}, u32[]{:S(2)}, u32[]{:S(2)}) collective-permute-start(f32[6,5,8,128]{3,2,1,0:T(8,128)S(1)} %get-tuple-element.23), channel_id=1, source_target_pairs={{0,2},{1,3},{2,4},{3,5},{4,6},{5,7},{6,8},{7,9},{8,10},{9,11},{10,... | collective-permute-start | bytes 368648 | tf_op jit(solution)/shard_map/ppermute | solution.py:17
  89.8 1.9 %collective-permute-done.10.high2 = f32[6,5,8,128]{3,2,1,0:T(8,128)S(1)} collective-permute-done((f32[6,5,8,128]{3,2,1,0:T(8,128)S(1)}, f32[6,5,8,128]{3,2,1,0:T(8,128)S(1)}, u32[]{:S(2)}, u32[]{:S(2)}) %collective-permute-start.10) | collective-permute-done | bytes 122912 | tf_op jit(solution)/shard_map/ppermute | solution.py:17
  91.8 0.3 collective-permute-done.9.low2
  92.1 0.0 collective-permute-done.7.low1
  92.1 0.0 collective-permute-done.8.high1
  92.1 2.0 %shard_map.73 = (f32[2,8,8,128]{3,2,1,0:T(8,128)S(1)}, f32[16,16,128]{2,1,0:T(8,128)S(1)}) custom-call(f32[8,5,8,128]{3,2,1,0:T(8,128)S(1)} %get-tuple-element.22.mine, f32[8,5,8,128]{3,2,1,0:T(8,128)S(1)} %collective-permute-done.7.low1, f32[8,5,8,128]{3,2,1,0:T(8,128)S(1)} %collective-permute-done.8.high1, ...), custom_call_target="tpu_custom_call" | custom-call | tf_op jit(solution)/shard_map/pallas_call | solution.py:27
  94.1 21.6 %all_to_all.21.gathered = f32[16,16,128]{2,1,0:T(8,128)S(1)} all-to-all(f32[16,16,128]{2,1,0:T(8,128)S(1)} %get-tuple-element.25), channel_id=1, replica_groups=mesh['gx'=32,'gy'=16] {'gy'}, dimensions={0} | all-to-all | bytes 262144 | tf_op jit(solution)/shard_map/all_to_all | solution.py:482
  115.7 0.3 shard_map.74.own
  116.0 2.2 %collective-permute-start.11 = (f32[160,128]{1,0:T(8,128)S(1)}, f32[160,128]{1,0:T(8,128)S(1)}, u32[]{:S(2)}, u32[]{:S(2)}) collective-permute-start(f32[160,128]{1,0:T(8,128)S(1)} %shard_map.74.own), channel_id=1, source_target_pairs={{0,16},{16,32},{32,48},{48,64},{64,80},{80,96},{96,112},{128,144},... | collective-permute-start | bytes 245768 | tf_op jit(solution)/shard_map/ppermute | solution.py:442
  118.2 1.3 collective-permute-start.12
  119.5 0.6 collective-permute-done.11.left
  120.1 3.8 %collective-permute-done.12.right = f32[160,128]{1,0:T(8,128)S(1)} collective-permute-done((f32[160,128]{1,0:T(8,128)S(1)}, f32[160,128]{1,0:T(8,128)S(1)}, u32[]{:S(2)}, u32[]{:S(2)}) %collective-permute-start.12) | collective-permute-done | bytes 81952 | tf_op jit(solution)/shard_map/ppermute | solution.py:442
  123.9 1.0 shard_map.75
  125.0 4.0 %all-to-all-start.2 = ((f32[4,3,160,128]{3,2,1,0:T(8,128)}), f32[4,3,160,128]{3,2,1,0:T(8,128)S(1)}, u32[]{:S(2)}, u32[]{:S(2)}) async-start(f32[4,3,160,128]{3,2,1,0:T(8,128)} %shard_map.75), calls=%async_computation.2 | async-start | bytes 1966080 | tf_op jit(solution)/shard_map/all_to_all | solution.py:485
  129.0 0.1 pad_add_fusion.refs_0_
  129.1 13.1 %all-to-all-done.2.refs_1_ = f32[4,3,160,128]{3,2,1,0:T(8,128)S(1)} async-done(((f32[4,3,160,128]{3,2,1,0:T(8,128)}), f32[4,3,160,128]{3,2,1,0:T(8,128)S(1)}, u32[]{:S(2)}, u32[]{:S(2)}) %all-to-all-start.2) | async-done | bytes 983072 | tf_op jit(solution)/shard_map/all_to_all | solution.py:485
  142.2 6.1 %shard_map.76 = f32[8,3,8,128]{3,2,1,0:T(8,128)S(1)} custom-call(s32[2]{0:T(128)S(1)} %pad_add_fusion.refs_0_, f32[4,3,160,128]{3,2,1,0:T(8,128)S(1)} %all-to-all-done.2.refs_1_, f32[2,8,8,128]{3,2,1,0:T(8,128)S(1)} %get-tuple-element.26.refs_2_, f32[2,16,8,128]{3,2,1,0:T(8,128)S(1)} %get-tuple-element.27.refs_3_), custom_call_target="tpu_custom_call" | custom-call | tf_op jit(solution)/shard_map/pallas_call | solution.py:27
  148.4 10.1 %all_to_all.22.pieces = f32[8,3,8,128]{3,2,1,0:T(8,128)S(1)} all-to-all(f32[8,3,8,128]{3,2,1,0:T(8,128)S(1)} %shard_map.76), channel_id=1, replica_groups={{0,16,32,48,64,80,96,112},{128,144,160,176,192,208,224,240},{256,272,28..., dimensions={0} | all-to-all | bytes 196608 | tf_op jit(solution)/shard_map/all_to_all | solution.py:492
  158.5 0.7 shard_map.77
  (4 shorter events, 0.1 us)
Async XLA Ops:
  0.6 0.8 copy-start
  1.5 0.8 copy-start.1
  2.3 0.8 copy-start.2
  3.2 0.8 copy-start.3
  4.0 0.8 copy-start.4
  35.0 7.5 %collective-permute-start.1 = (f32[41,8,128]{2,1,0:T(8,128)S(1)}, f32[41,8,128]{2,1,0:T(8,128)S(1)}, u32[]{:S(2)}, u32[]{:S(2)}) collective-permute-start(f32[41,8,128]{2,1,0:T(8,128)S(1)} %get-tuple-element.16), channel_id=1, source_target_pairs={{128,0},{144,16},{160,32},{176,48},{192,64},{208,80},{224,96},{240... | collective-permute-start | bytes 503816 | tf_op jit(solution)/shard_map/ppermute | solution.py:17
  36.3 6.2 %collective-permute-start = (f32[40,8,128]{2,1,0:T(8,128)S(1)}, f32[40,8,128]{2,1,0:T(8,128)S(1)}, u32[]{:S(2)}, u32[]{:S(2)}) collective-permute-start(f32[40,8,128]{2,1,0:T(8,128)S(1)} %get-tuple-element.15), channel_id=1, source_target_pairs={{0,128},{16,144},{32,160},{48,176},{64,192},{80,208},{96,224},{112... | collective-permute-start | bytes 491528 | tf_op jit(solution)/shard_map/ppermute | solution.py:17
  42.6 17.3 %collective-permute-start.2 = (f32[12,5,4,8,128]{4,3,2,1,0:T(8,128)S(1)}, f32[12,5,4,8,128]{4,3,2,1,0:T(8,128)S(1)}, u32[]{:S(2)}, u32[]{:S(2)}) collective-permute-start(f32[12,5,4,8,128]{4,3,2,1,0:T(8,128)S(1)} %get-tuple-element.17.mine), channel_id=1, source_target_pairs={{0,1},{1,2},{2,3},{3,4},{4,5},{5,6},{6,7},{7,8},{8,9},{9,10},{10,1... | collective-permute-start | bytes 2949128 | tf_op jit(solution)/shard_map/ppermute | solution.py:17
  48.9 15.6 %collective-permute-start.3 = (f32[12,5,4,8,128]{4,3,2,1,0:T(8,128)S(1)}, f32[12,5,4,8,128]{4,3,2,1,0:T(8,128)S(1)}, u32[]{:S(2)}, u32[]{:S(2)}) collective-permute-start(f32[12,5,4,8,128]{4,3,2,1,0:T(8,128)S(1)} %get-tuple-element.17.mine), channel_id=1, source_target_pairs={{1,0},{2,1},{3,2},{4,3},{5,4},{6,5},{7,6},{8,7},{9,8},{10,9},{11,1... | collective-permute-start | bytes 2949128 | tf_op jit(solution)/shard_map/ppermute | solution.py:17
  50.8 4.7 %collective-permute-start.4 = (f32[32,128]{1,0:T(8,128)S(1)}, f32[32,128]{1,0:T(8,128)S(1)}, u32[]{:S(2)}, u32[]{:S(2)}) collective-permute-start(f32[32,128]{1,0:T(8,128)S(1)} %get-tuple-element.19), channel_id=1, source_target_pairs={{2,0},{3,1},{4,2},{5,3},{6,4},{7,5},{8,6},{9,7},{10,8},{11,9},{12,... | collective-permute-start | bytes 49160 | tf_op jit(solution)/shard_map/ppermute | solution.py:17
  68.3 5.4 %collective-permute-start.5 = (f32[2,5,8,128]{3,2,1,0:T(8,128)S(1)}, f32[2,5,8,128]{3,2,1,0:T(8,128)S(1)}, u32[]{:S(2)}, u32[]{:S(2)}) collective-permute-start(f32[2,5,8,128]{3,2,1,0:T(8,128)S(1)} %get-tuple-element.20.last), channel_id=1, source_target_pairs={{0,128},{16,144},{32,160},{48,176},{64,192},{80,208},{96,224},{112... | collective-permute-start | bytes 122888 | tf_op jit(solution)/shard_map/ppermute | solution.py:17
  72.4 4.7 %collective-permute-start.6 = (f32[2,5,8,128]{3,2,1,0:T(8,128)S(1)}, f32[2,5,8,128]{3,2,1,0:T(8,128)S(1)}, u32[]{:S(2)}, u32[]{:S(2)}) collective-permute-start(f32[2,5,8,128]{3,2,1,0:T(8,128)S(1)} %get-tuple-element.21.first), channel_id=1, source_target_pairs={{128,0},{144,16},{160,32},{176,48},{192,64},{208,80},{224,96},{240... | collective-permute-start | bytes 122888 | tf_op jit(solution)/shard_map/ppermute | solution.py:17
  77.2 14.9 %collective-permute-start.7 = (f32[8,5,8,128]{3,2,1,0:T(8,128)S(1)}, f32[8,5,8,128]{3,2,1,0:T(8,128)S(1)}, u32[]{:S(2)}, u32[]{:S(2)}) collective-permute-start(f32[8,5,8,128]{3,2,1,0:T(8,128)S(1)} %get-tuple-element.22.mine), channel_id=1, source_target_pairs={{0,1},{1,2},{2,3},{3,4},{4,5},{5,6},{6,7},{7,8},{8,9},{9,10},{10,1... | collective-permute-start | bytes 491528 | tf_op jit(solution)/shard_map/ppermute | solution.py:17
  82.6 9.5 %collective-permute-start.8 = (f32[8,5,8,128]{3,2,1,0:T(8,128)S(1)}, f32[8,5,8,128]{3,2,1,0:T(8,128)S(1)}, u32[]{:S(2)}, u32[]{:S(2)}) collective-permute-start(f32[8,5,8,128]{3,2,1,0:T(8,128)S(1)} %get-tuple-element.22.mine), channel_id=1, source_target_pairs={{1,0},{2,1},{3,2},{4,3},{5,4},{6,5},{7,6},{8,7},{9,8},{10,9},{11,1... | collective-permute-start | bytes 491528 | tf_op jit(solution)/shard_map/ppermute | solution.py:17
  84.5 7.2 %collective-permute-start.10 = (f32[6,5,8,128]{3,2,1,0:T(8,128)S(1)}, f32[6,5,8,128]{3,2,1,0:T(8,128)S(1)}, u32[]{:S(2)}, u32[]{:S(2)}) collective-permute-start(f32[6,5,8,128]{3,2,1,0:T(8,128)S(1)} %get-tuple-element.23), channel_id=1, source_target_pairs={{2,0},{3,1},{4,2},{5,3},{6,4},{7,5},{8,6},{9,7},{10,8},{11,9},{12,... | collective-permute-start | bytes 368648 | tf_op jit(solution)/shard_map/ppermute | solution.py:17
  85.8 6.3 %collective-permute-start.9 = (f32[6,5,8,128]{3,2,1,0:T(8,128)S(1)}, f32[6,5,8,128]{3,2,1,0:T(8,128)S(1)}, u32[]{:S(2)}, u32[]{:S(2)}) collective-permute-start(f32[6,5,8,128]{3,2,1,0:T(8,128)S(1)} %get-tuple-element.23), channel_id=1, source_target_pairs={{0,2},{1,3},{2,4},{3,5},{4,6},{5,7},{6,8},{7,9},{8,10},{9,11},{10,... | collective-permute-start | bytes 368648 | tf_op jit(solution)/shard_map/ppermute | solution.py:17
  116.0 4.1 %collective-permute-start.11 = (f32[160,128]{1,0:T(8,128)S(1)}, f32[160,128]{1,0:T(8,128)S(1)}, u32[]{:S(2)}, u32[]{:S(2)}) collective-permute-start(f32[160,128]{1,0:T(8,128)S(1)} %shard_map.74.own), channel_id=1, source_target_pairs={{0,16},{16,32},{32,48},{48,64},{64,80},{80,96},{96,112},{128,144},... | collective-permute-start | bytes 245768 | tf_op jit(solution)/shard_map/ppermute | solution.py:442
  118.2 5.7 %collective-permute-start.12 = (f32[160,128]{1,0:T(8,128)S(1)}, f32[160,128]{1,0:T(8,128)S(1)}, u32[]{:S(2)}, u32[]{:S(2)}) collective-permute-start(f32[160,128]{1,0:T(8,128)S(1)} %shard_map.74.own), channel_id=1, source_target_pairs={{16,0},{32,16},{48,32},{64,48},{80,64},{96,80},{112,96},{144,128},... | collective-permute-start | bytes 245768 | tf_op jit(solution)/shard_map/ppermute | solution.py:442
  125.0 17.2 %all-to-all-start.2 = ((f32[4,3,160,128]{3,2,1,0:T(8,128)}), f32[4,3,160,128]{3,2,1,0:T(8,128)S(1)}, u32[]{:S(2)}, u32[]{:S(2)}) async-start(f32[4,3,160,128]{3,2,1,0:T(8,128)} %shard_map.75), calls=%async_computation.2 | async-start | bytes 1966080 | tf_op jit(solution)/shard_map/all_to_all | solution.py:485

commit v4 on v3

--- a/solution.py
+++ b/solution.py
@@ -8,6 +8,7 @@
 F32 = jnp.float32
 RHS, ALPHA, BX, BY, BZ = range(5)
 VMEM_BYTES = 20 * 2**20
+ALL_VMEM = 62 * 2**20
 RING = 8
 
 
@@ -17,20 +18,18 @@
     return lax.ppermute(values, name, [(i, i + steps) for i in range(lead, last)])
 
 
-def call(kernel, outs, scratch=(), smem=()):
+def call(kernel, outs, scratch=(), copied=False):
     def run(*args):
-        specs = [
-            pl.BlockSpec(memory_space=pltpu.SMEM if i in smem else pltpu.VMEM)
-            for i in range(len(args))
-        ]
-        shapes = [jax.ShapeDtypeStruct(s, F32) for s in outs]
+        space = pltpu.HBM if copied else pltpu.VMEM
+        buffers = [pltpu.VMEM(a.shape, F32) for a in args] if copied else []
+        sems = [pltpu.SemaphoreType.DMA] * len(args) if copied else []
         return pl.pallas_call(
             kernel,
-            out_shape=shapes,
-            in_specs=specs,
+            out_shape=[jax.ShapeDtypeStruct(s, F32) for s in outs],
+            in_specs=[pl.BlockSpec(memory_space=space)] * len(args),
             out_specs=[pl.BlockSpec(memory_space=pltpu.VMEM)] * len(outs),
-            scratch_shapes=[pltpu.VMEM(s, F32) for s in scratch],
-            compiler_params=pltpu.CompilerParams(vmem_limit_bytes=VMEM_BYTES),
+            scratch_shapes=[pltpu.VMEM(s, F32) for s in scratch] + buffers + sems,
+            compiler_params=pltpu.CompilerParams(vmem_limit_bytes=ALL_VMEM if copied else VMEM_BYTES),
         )(*args)
 
     return run
@@ -150,10 +149,15 @@
         relax(co, r if red else b, b if red else r, pairs(9 - step), red, q0)
 
 
-def to_windows_kernel(rhs, alpha, beta_x, beta_y, beta_z, out):
+def to_windows_kernel(*refs):
+    args, out, buffers, sems = refs[:5], refs[5], refs[6:11], refs[11:]
+    copies = [pltpu.make_async_copy(*c) for c in zip(args, buffers, sems)]
+    for c in copies:
+        c.start()
     _, lane = iotas((8, 128))
     zero = jnp.zeros((8, 128), F32)
-    for a, ref in enumerate((rhs, alpha, beta_x, beta_y, beta_z)):
+    for a, ref in enumerate(buffers):
+        copies[a].wait()
         for x in range(4):
             tiles = [ref[x, :, 128 * c : 128 * c + 128] for c in range(4)]
             up = [pltpu.roll(t, 32, 1) for t in tiles]
@@ -163,45 +167,64 @@
                 out[2 * c + 1, a, x] = jnp.where(lane < 96, down[c], down[c + 1] if c < 3 else zero)
 
 
+def flat(s, a, x):
+    return (s * 5 + a) * 4 + x
+
+
 def x_messages_kernel(own, to_low, to_high, first_by):
-    for s in range(2):
-        for a in range(5):
-            for x in range(4):
-                t = (s * 5 + a) * 4 + x
-                to_low[t] = own[s, a, x]
-                to_high[t] = own[6 + s, a, x]
+    for a in range(5):
+        for x in range(4):
+            for s in range(2):
+                to_low[flat(s, a, x)] = own[s, a, x]
+                to_high[flat(s, a, x)] = own[6 + s, a, x]
     to_low[40] = own[2, BX, 0]
     for x in range(32):
         first_by[x : x + 1] = own[x // 4, BY, x % 4][:1]
 
 
-def y_message_kernel(low, own, high, out, beyond):
+def corner_messages_kernel(low, high, to_low, to_high):
+    keep = low_rows((8, 128))
     for a in range(5):
         for x in range(4):
-            for s in range(2):
-                t = (s * 5 + a) * 4 + x
-                out[s, a, x] = low[t]
-                out[10 + s, a, x] = high[t]
-            for s in range(8):
-                out[2 + s, a, x] = own[s, a, x]
-    beyond[...] = high[40]
-
-
-def fine_kernel(mine, low, high, beyond_x, beyond_y, fine_out, mid_first, mid_last, own_out, co, r, b):
+            for ref in (to_low, to_high):
+                ref[flat(0, a, x)] = low[flat(1, a, x)]
+                ref[flat(1, a, x)] = high[flat(0, a, x)]
+            outer_low, outer_high = low[flat(0, a, x)], high[flat(1, a, x)]
+            to_low[flat(2, a, x)] = jnp.where(keep, outer_low, half(outer_high))
+            to_high[flat(2, a, x)] = jnp.where(keep, half(outer_low), outer_high)
+
+
+def fine_kernel(
+    own, x_low, x_high, y_low, y_high, corner_low, corner_high, beyond_y,
+    fine_out, mid_first, mid_last, own_out, co, r, b,
+):
     q0 = even_mask((24, 128))
     row, lane = iotas((24, 128))
     clear_guards(r, b, 24)
     zero = jnp.zeros((8, 128), F32)
 
     def plane(a, x):
-        return jnp.concatenate([ref[x // 4, a, x % 4] for ref in (mine, high, low)], 0)
+        block, i = x // 4, x % 4
+        if 2 <= block < 10:
+            tiles = [ref[block - 2, a, i] for ref in (own, y_high, y_low)]
+        elif block in (1, 10):
+            side = int(block == 10)
+            tiles = [(x_high if side else x_low)[flat(1 - side, a, i)]]
+            tiles += [ref[flat(side, a, i)] for ref in (corner_high, corner_low)]
+        else:
+            up, down = corner_high[flat(2, a, i)], corner_low[flat(2, a, i)]
+            if block == 0:
+                tiles = [x_low[flat(0, a, i)], up, half(down)]
+            else:
+                tiles = [x_high[flat(1, a, i)], half(up), down]
+        return jnp.concatenate(tiles, 0)
 
     bx0 = plane(BX, 0)
     for p in range(24):
         x = 2 * p
         co[S_R, p], co[S_B, p] = halves(q0, plane(RHS, x), plane(RHS, x + 1))
         bx1 = plane(BX, x + 1)
-        bx2 = plane(BX, x + 2) if p < 23 else jnp.concatenate([beyond_x[...], zero, zero], 0)
+        bx2 = plane(BX, x + 2) if p < 23 else jnp.concatenate([x_high[40], zero, zero], 0)
         by = plane(BY, x), plane(BY, x + 1)
         bz = plane(BZ, x), plane(BZ, x + 1)
         fx, fy, fyp, fz = put_faces(co, p, q0, (bx0, bx1, bx2), by, bz)
@@ -226,13 +249,13 @@
         sums.append((red + black)[:8])
         fine_out[0, j] = r[p + 1][:8]
         fine_out[1, j] = b[p + 1][:8]
-        s, x = (2 * p) // 4, (2 * p) % 4
-        alphas.append(mine[s, ALPHA, x] + mine[s, ALPHA, x + 1])
-        bys.append(mine[s, BY, x] + mine[s, BY, x + 1])
-        nexts.append(high[s, BY, x] + high[s, BY, x + 1])
-        bzs.append(mine[s, BZ, x] + mine[s, BZ, x + 1])
-        bxs.append(mine[s, BX, x])
-    bxs.append(mine[10, BX, 0])
+        s, x = j // 2, 2 * (j % 2)
+        alphas.append(own[s, ALPHA, x] + own[s, ALPHA, x + 1])
+        bys.append(own[s, BY, x] + own[s, BY, x + 1])
+        nexts.append(y_high[s, BY, x] + y_high[s, BY, x + 1])
+        bzs.append(own[s, BZ, x] + own[s, BZ, x + 1])
+        bxs.append(own[s, BX, x])
+    bxs.append(x_high[flat(0, BX, 0)])
     z_sum = one_hot((128, 128), lambda i, j: (i >> 1) == j)
     z_even = one_hot((128, 128), lambda i, j: i == 2 * j)
     y_sum = one_hot((64, 128), lambda i, j: (j >> 1) == i)
@@ -343,7 +366,7 @@
             out[g, s] = ref[...]
 
 
-def coarse_kernel(sweeps, index, gathered, level, fine, out, co, r, b):
+def coarse_kernel(sweeps, gathered, level, fine, out, co, r, b):
     shape = (32, 128)
     q0 = even_mask(shape)
     row, lane = iotas(shape)
@@ -393,7 +416,7 @@
 
     lax.fori_loop(0, sweeps, sweep, 0)
 
-    gy, gx = index[0], index[1]
+    gy, gx = lax.axis_index("gy"), lax.axis_index("gx")
     ring, place = gx // RING, lax.rem(gx, RING)
     side, base = ring // 2, 4 * lax.rem(ring, 2)
     own = []
@@ -447,24 +470,24 @@
     groups = count_x // RING
     rings = [[RING * i + j for j in range(RING)] for i in range(groups)]
     across = [list(c) for c in zip(*rings)]
-    index = jnp.stack([lax.axis_index("gy"), lax.axis_index("gx")]).astype(jnp.int32)
-
-    (own,) = call(to_windows_kernel, [(RING, 5, 4, 8, 128)])(rhs, alpha, beta_x, beta_y, beta_z)
+
+    (own,) = call(to_windows_kernel, [(RING, 5, 4, 8, 128)], copied=True)(rhs, alpha, beta_x, beta_y, beta_z)
     own = lax.all_to_all(own, "gx", 0, 0, tiled=True, axis_index_groups=rings)
     to_low, to_high, first_by = call(
         x_messages_kernel, [(41, 8, 128), (40, 8, 128), (32, 128)]
     )(own)
-    low, high = shifted(to_high, 1, "gx", RING), shifted(to_low, 1, "gx", -RING)
-    mine, beyond_x = call(
-        y_message_kernel, [(12, 5, 4, 8, 128), (8, 128)]
-    )(low, own, high)
-    low, high = shifted(mine, 1, "gy", 1), shifted(mine, 1, "gy", -1)
+    y_low, y_high = shifted(own, 1, "gy", 1), shifted(own, 1, "gy", -1)
+    x_low, x_high = shifted(to_high, 1, "gx", RING), shifted(to_low, 1, "gx", -RING)
     beyond_y = shifted(first_by, 0, "gy", -2)
+    to_low, to_high = call(
+        corner_messages_kernel, [(60, 8, 128), (60, 8, 128)]
+    )(x_low, x_high)
+    corner_low, corner_high = shifted(to_high, 1, "gy", 1), shifted(to_low, 1, "gy", -1)
     fine, mid_first, mid_last, mid_own = call(
         fine_kernel,
         [(2, 16, 8, 128), (2, 5, 8, 128), (2, 5, 8, 128), (4, 2, 8, 128)],
         [(17, 24, 24, 128), (26, 24, 128), (26, 24, 128)],
-    )(mine, low, high, beyond_x, beyond_y)
+    )(own, x_low, x_high, y_low, y_high, corner_low, corner_high, beyond_y)
 
     low, high = shifted(mid_last, 0, "gx", RING), shifted(mid_first, 0, "gx", -RING)
     near, far = call(
@@ -487,8 +510,7 @@
         lambda *refs: coarse_kernel(8, *refs),
         [(RING, 3, 8, 128)],
         [(17, 8, 32, 128), (10, 32, 128), (10, 32, 128)],
-        smem=(0,),
-    )(index, low, level, fine)
+    )(low, level, fine)
     pieces = lax.all_to_all(pieces, "gx", 0, 0, tiled=True, axis_index_groups=rings)
     fine_solution, coarse = call(finish_kernel, [rhs.shape, (1, 2, 128)])(pieces)
     return fine_solution, coarse

time: 161 us -> 156 us (0.969)
  waiting for transfers between devices: 37.9 us -> 16.5 us
  blocking collectives: 61.6 us -> 79.6 us
  local copies, waits for them, and re-layouts: 4.19 us -> 0 us
  starting transfers between devices: 40.3 us -> 42.4 us
    all_to_all x0 -> x1, blocking collectives: none -> 17 us  [on_device(): low = lax.all_to_all(low, 'gx', 0, 0, tiled=True, axis_index_groups=across)]
    all_to_all x1 -> x0, waiting for transfers between devices: 13.1 us -> none  [on_device(): low = lax.all_to_all(low, 'gx', 0, 0, tiled=True, axis_index_groups=across)]
    ppermute x11 -> x13, waiting for transfers between devices: 20.3 us -> 14.9 us  [shifted(): lax.ppermute(values, name, [(i, i + steps) for i in range(lead, last)])]
    ppermute x11 -> x13, starting transfers between devices: 32.8 us -> 37.1 us  [shifted(): lax.ppermute(values, name, [(i, i + steps) for i in range(lead, last)])]
    unnamed x10 -> x0, local copies, waits for them, and re-layouts: 4.19 us -> none
    all_to_all x1 -> x0, starting transfers between devices: 4.03 us -> none  [on_device(): low = lax.all_to_all(low, 'gx', 0, 0, tiled=True, axis_index_groups=across)]
    all_to_all x1, blocking collectives: 10.1 us -> 13.1 us  [on_device(): lax.all_to_all(pieces, 'gx', 0, 0, tiled=True, axis_index_groups=rings)]
    ppermute x2, waiting for transfers between devices: 4.45 us -> 1.64 us  [in_rings(): return lax.ppermute(values, 'gx', pairs)]
  transfers between devices with their start and end apart: 14 -> 15, of which waited for: 10 -> 8; matrix products, arithmetic and copies ran while one was open for 0% -> 0% of each run, Pallas kernels for 0% -> 0%
where the time goes in v4:
time: 156 us; the launch traced here: 154 us
  blocking collectives  79.6 us (51%)
  starting transfers between devices  42.4 us (27%)
  waiting for transfers between devices  16.5 us (11%)
  Pallas kernels  14.8 us (9%)
    ppermute x13, starting transfers between devices, shifted(): lax.ppermute(values, name, [(i, i + steps) for i in range(lead, last)])  37.1 us
    all_to_all x1, blocking collectives, on_device(): own = lax.all_to_all(own, 'gx', 0, 0, tiled=True, axis_index_groups=rings)  30.1 us
    all_to_all x1, blocking collectives, on_device(): low = lax.all_to_all(low, 'gy', 0, 0, tiled=True)  19.4 us
    all_to_all x1, blocking collectives, on_device(): low = lax.all_to_all(low, 'gx', 0, 0, tiled=True, axis_index_groups=across)  17 us
    ppermute x13, waiting for transfers between devices, shifted(): lax.ppermute(values, name, [(i, i + steps) for i in range(lead, last)])  14.9 us
    pallas_call x10, Pallas kernels, run(): pl.pallas_call(kernel, out_shape=[jax.ShapeDtypeStruct(s, F32) for s in o...  14.8 us
    all_to_all x1, blocking collectives, on_device(): lax.all_to_all(pieces, 'gx', 0, 0, tiled=True, axis_index_groups=rings)  13.1 us
    ppermute x2, starting transfers between devices, in_rings(): return lax.ppermute(values, 'gx', pairs)  5.28 us
  transfers between devices with their start and end apart: 15, of which 8 were waited for; matrix products, arithmetic and copies ran while one was open for 0% of the time, Pallas kernels for 0%

profile of v4, /device:TPU:1, one launch (start us, length us, event | category | flops | bytes accessed | tf_op | source)
XLA Modules:
  0.0 154.2 jit_solution(13169612872330221233)
XLA Ops:
  0.6 2.2 %shard_map.68 = f32[8,5,4,8,128]{4,3,2,1,0:T(8,128)} custom-call(f32[4,8,512]{2,1,0:T(8,128)} %refs_0_.1, f32[4,8,512]{2,1,0:T(8,128)} %refs_1_.1, f32[4,8,512]{2,1,0:T(8,128)} %refs_2_.1, f32[4,8,512]{2,1,0:T(8,128)} %refs_3_.1, f32[4,8,512]{2,1,0:T(8,128)} %refs_4_.1), custom_call_target="tpu_custom_call" | custom-call | tf_op jit(solution)/shard_map/pallas_call | solution.py:26
  2.9 30.1 %all_to_all.20.own = f32[8,5,4,8,128]{4,3,2,1,0:T(8,128)S(1)} all-to-all(f32[8,5,4,8,128]{4,3,2,1,0:T(8,128)} %shard_map.68), channel_id=1, replica_groups={{0,16,32,48,64,80,96,112},{128,144,160,176,192,208,224,240},{256,272,28..., dimensions={0} | all-to-all | bytes 1310720 | tf_op jit(solution)/shard_map/all_to_all | solution.py:475
  33.0 3.9 %collective-permute-start.3 = (f32[8,5,4,8,128]{4,3,2,1,0:T(8,128)S(1)}, f32[8,5,4,8,128]{4,3,2,1,0:T(8,128)S(1)}, u32[]{:S(2)}, u32[]{:S(2)}) collective-permute-start(f32[8,5,4,8,128]{4,3,2,1,0:T(8,128)S(1)} %all_to_all.20.own), channel_id=1, source_target_pairs={{1,0},{2,1},{3,2},{4,3},{5,4},{6,5},{7,6},{8,7},{9,8},{10,9},{11,1... | collective-permute-start | bytes 1966088 | tf_op jit(solution)/shard_map/ppermute | solution.py:18
  36.9 3.1 %collective-permute-start.2 = (f32[8,5,4,8,128]{4,3,2,1,0:T(8,128)S(1)}, f32[8,5,4,8,128]{4,3,2,1,0:T(8,128)S(1)}, u32[]{:S(2)}, u32[]{:S(2)}) collective-permute-start(f32[8,5,4,8,128]{4,3,2,1,0:T(8,128)S(1)} %all_to_all.20.own), channel_id=1, source_target_pairs={{0,1},{1,2},{2,3},{3,4},{4,5},{5,6},{6,7},{7,8},{8,9},{9,10},{10,1... | collective-permute-start | bytes 1966088 | tf_op jit(solution)/shard_map/ppermute | solution.py:18
  40.1 1.3 collective-permute-start.1
  41.4 4.0 %collective-permute-start = (f32[40,8,128]{2,1,0:T(8,128)S(1)}, f32[40,8,128]{2,1,0:T(8,128)S(1)}, u32[]{:S(2)}, u32[]{:S(2)}) collective-permute-start(f32[40,8,128]{2,1,0:T(8,128)S(1)} %get-tuple-element.15), channel_id=1, source_target_pairs={{0,128},{16,144},{32,160},{48,176},{64,192},{80,208},{96,224},{112... | collective-permute-start | bytes 491528 | tf_op jit(solution)/shard_map/ppermute | solution.py:18
  45.4 3.9 %collective-permute-done.low.x_low = f32[40,8,128]{2,1,0:T(8,128)S(1)} collective-permute-done((f32[40,8,128]{2,1,0:T(8,128)S(1)}, f32[40,8,128]{2,1,0:T(8,128)S(1)}, u32[]{:S(2)}, u32[]{:S(2)}) %collective-permute-start) | collective-permute-done | bytes 163872 | tf_op jit(solution)/shard_map/ppermute | solution.py:18
  49.3 0.0 collective-permute-done.1.high.x_high
  49.3 3.6 %collective-permute-start.4 = (f32[60,8,128]{2,1,0:T(8,128)S(1)}, f32[60,8,128]{2,1,0:T(8,128)S(1)}, u32[]{:S(2)}, u32[]{:S(2)}) collective-permute-start(f32[60,8,128]{2,1,0:T(8,128)S(1)} %get-tuple-element.17), channel_id=1, source_target_pairs={{0,1},{1,2},{2,3},{3,4},{4,5},{5,6},{6,7},{7,8},{8,9},{9,10},{10,1... | collective-permute-start | bytes 737288 | tf_op jit(solution)/shard_map/ppermute | solution.py:18
  52.9 1.9 %collective-permute-start.5 = (f32[60,8,128]{2,1,0:T(8,128)S(1)}, f32[60,8,128]{2,1,0:T(8,128)S(1)}, u32[]{:S(2)}, u32[]{:S(2)}) collective-permute-start(f32[60,8,128]{2,1,0:T(8,128)S(1)} %get-tuple-element.18), channel_id=1, source_target_pairs={{1,0},{2,1},{3,2},{4,3},{5,4},{6,5},{7,6},{8,7},{9,8},{10,9},{11,1... | collective-permute-start | bytes 737288 | tf_op jit(solution)/shard_map/ppermute | solution.py:18
  54.8 1.3 collective-permute-start.6
  56.1 3.4 %collective-permute-done.6.beyond_y = f32[32,128]{1,0:T(8,128)S(1)} collective-permute-done((f32[32,128]{1,0:T(8,128)S(1)}, f32[32,128]{1,0:T(8,128)S(1)}, u32[]{:S(2)}, u32[]{:S(2)}) %collective-permute-start.6) | collective-permute-done | bytes 16416 | tf_op jit(solution)/shard_map/ppermute | solution.py:18
  59.5 0.0 collective-permute-done.4.corner_low
  59.5 1.1 collective-permute-done.5.corner_high
  60.6 0.0 collective-permute-done.3.y_high
  60.6 0.0 collective-permute-done.2.y_low
  60.6 3.8 %shard_map.71 = (f32[2,16,8,128]{3,2,1,0:T(8,128)S(1)}, f32[2,5,8,128]{3,2,1,0:T(8,128)S(1)}, f32[2,5,8,128]{3,2,1,0:T(8,128)S(1)}, f32[4,2,8,128]{3,2,1,0:T(8,128)S(1)}) custom-call(f32[8,5,4,8,128]{4,3,2,1,0:T(8,128)S(1)} %all_to_all.20.own, f32[40,8,128]{2,1,0:T(8,128)S(1)} %collective-permute-done.low.x_low, ...), custom_call_target="tpu_custom_call" | custom-call | tf_op jit(solution)/shard_map/pallas_call | solution.py:26
  64.4 4.1 %collective-permute-start.7 = (f32[2,5,8,128]{3,2,1,0:T(8,128)S(1)}, f32[2,5,8,128]{3,2,1,0:T(8,128)S(1)}, u32[]{:S(2)}, u32[]{:S(2)}) collective-permute-start(f32[2,5,8,128]{3,2,1,0:T(8,128)S(1)} %get-tuple-element.20.last), channel_id=1, source_target_pairs={{0,128},{16,144},{32,160},{48,176},{64,192},{80,208},{96,224},{112... | collective-permute-start | bytes 122888 | tf_op jit(solution)/shard_map/ppermute | solution.py:18
  68.5 1.3 collective-permute-start.8
  69.8 0.0 collective-permute-done.7.low
  69.8 3.4 %collective-permute-done.8.high = f32[2,5,8,128]{3,2,1,0:T(8,128)S(1)} collective-permute-done((f32[2,5,8,128]{3,2,1,0:T(8,128)S(1)}, f32[2,5,8,128]{3,2,1,0:T(8,128)S(1)}, u32[]{:S(2)}, u32[]{:S(2)}) %collective-permute-start.8) | collective-permute-done | bytes 40992 | tf_op jit(solution)/shard_map/ppermute | solution.py:18
  73.2 4.2 %collective-permute-start.10 = (f32[8,5,8,128]{3,2,1,0:T(8,128)S(1)}, f32[8,5,8,128]{3,2,1,0:T(8,128)S(1)}, u32[]{:S(2)}, u32[]{:S(2)}) collective-permute-start(f32[8,5,8,128]{3,2,1,0:T(8,128)S(1)} %get-tuple-element.22.mine), channel_id=1, source_target_pairs={{1,0},{2,1},{3,2},{4,3},{5,4},{6,5},{7,6},{8,7},{9,8},{10,9},{11,1... | collective-permute-start | bytes 491528 | tf_op jit(solution)/shard_map/ppermute | solution.py:18
  77.5 3.1 %collective-permute-start.9 = (f32[8,5,8,128]{3,2,1,0:T(8,128)S(1)}, f32[8,5,8,128]{3,2,1,0:T(8,128)S(1)}, u32[]{:S(2)}, u32[]{:S(2)}) collective-permute-start(f32[8,5,8,128]{3,2,1,0:T(8,128)S(1)} %get-tuple-element.22.mine), channel_id=1, source_target_pairs={{0,1},{1,2},{2,3},{3,4},{4,5},{5,6},{6,7},{7,8},{8,9},{9,10},{10,1... | collective-permute-start | bytes 491528 | tf_op jit(solution)/shard_map/ppermute | solution.py:18
  80.6 1.3 collective-permute-start.12
  81.9 4.0 %collective-permute-start.11 = (f32[6,5,8,128]{3,2,1,0:T(8,128)S(1)}, f32[6,5,8,128]{3,2,1,0:T(8,128)S(1)}, u32[]{:S(2)}, u32[]{:S(2)}) collective-permute-start(f32[6,5,8,128]{3,2,1,0:T(8,128)S(1)} %get-tuple-element.23), channel_id=1, source_target_pairs={{0,2},{1,3},{2,4},{3,5},{4,6},{5,7},{6,8},{7,9},{8,10},{9,11},{10,... | collective-permute-start | bytes 368648 | tf_op jit(solution)/shard_map/ppermute | solution.py:18
  85.9 1.5 collective-permute-done.12.high2
  87.4 1.6 %collective-permute-done.11.low2 = f32[6,5,8,128]{3,2,1,0:T(8,128)S(1)} collective-permute-done((f32[6,5,8,128]{3,2,1,0:T(8,128)S(1)}, f32[6,5,8,128]{3,2,1,0:T(8,128)S(1)}, u32[]{:S(2)}, u32[]{:S(2)}) %collective-permute-start.11) | collective-permute-done | bytes 122912 | tf_op jit(solution)/shard_map/ppermute | solution.py:18
  88.9 0.0 collective-permute-done.10.high1
  88.9 0.0 collective-permute-done.9.low1
  88.9 2.0 %shard_map.73 = (f32[2,8,8,128]{3,2,1,0:T(8,128)S(1)}, f32[16,16,128]{2,1,0:T(8,128)S(1)}) custom-call(f32[8,5,8,128]{3,2,1,0:T(8,128)S(1)} %get-tuple-element.22.mine, f32[8,5,8,128]{3,2,1,0:T(8,128)S(1)} %collective-permute-done.9.low1, f32[8,5,8,128]{3,2,1,0:T(8,128)S(1)} %collective-permute-done.10.high1, ...), custom_call_target="tpu_custom_call" | custom-call | tf_op jit(solution)/shard_map/pallas_call | solution.py:26
  91.0 19.4 %all_to_all.21.gathered = f32[16,16,128]{2,1,0:T(8,128)S(1)} all-to-all(f32[16,16,128]{2,1,0:T(8,128)S(1)} %get-tuple-element.25), channel_id=1, replica_groups=mesh['gx'=32,'gy'=16] {'gy'}, dimensions={0} | all-to-all | bytes 262144 | tf_op jit(solution)/shard_map/all_to_all | solution.py:505
  110.4 0.3 shard_map.74.own
  110.7 1.3 collective-permute-start.14
  112.0 4.0 %collective-permute-start.13 = (f32[160,128]{1,0:T(8,128)S(1)}, f32[160,128]{1,0:T(8,128)S(1)}, u32[]{:S(2)}, u32[]{:S(2)}) collective-permute-start(f32[160,128]{1,0:T(8,128)S(1)} %shard_map.74.own), channel_id=1, source_target_pairs={{0,16},{16,32},{32,48},{48,64},{64,80},{80,96},{96,112},{128,144},... | collective-permute-start | bytes 245768 | tf_op jit(solution)/shard_map/ppermute | solution.py:465
  116.0 0.7 collective-permute-done.14.right
  116.8 0.9 collective-permute-done.13.left
  117.7 0.1 shard_map.75
  117.7 17.0 %all_to_all.22.refs_0_ = f32[4,3,160,128]{3,2,1,0:T(8,128)S(1)} all-to-all(f32[4,3,160,128]{3,2,1,0:T(8,128)S(1)} %shard_map.75), channel_id=1, replica_groups={{0,128,256,384},{16,144,272,400},{32,160,288,416},{48,176,304,432},{64,..., dimensions={0} | all-to-all | bytes 1966080 | tf_op jit(solution)/shard_map/all_to_all | solution.py:508
  134.7 5.6 %shard_map.76 = f32[8,3,8,128]{3,2,1,0:T(8,128)S(1)} custom-call(f32[4,3,160,128]{3,2,1,0:T(8,128)S(1)} %all_to_all.22.refs_0_, f32[2,8,8,128]{3,2,1,0:T(8,128)S(1)} %get-tuple-element.26.refs_1_, f32[2,16,8,128]{3,2,1,0:T(8,128)S(1)} %get-tuple-element.27.refs_2_), custom_call_target="tpu_custom_call" | custom-call | tf_op jit(solution)/shard_map/pallas_call | solution.py:26
  140.3 13.1 %all_to_all.23.pieces = f32[8,3,8,128]{3,2,1,0:T(8,128)S(1)} all-to-all(f32[8,3,8,128]{3,2,1,0:T(8,128)S(1)} %shard_map.76), channel_id=1, replica_groups={{0,16,32,48,64,80,96,112},{128,144,160,176,192,208,224,240},{256,272,28..., dimensions={0} | all-to-all | bytes 196608 | tf_op jit(solution)/shard_map/all_to_all | solution.py:514
  153.4 0.7 shard_map.77
  (3 shorter events, 0.1 us)
Async XLA Ops:
  33.0 27.7 %collective-permute-start.3 = (f32[8,5,4,8,128]{4,3,2,1,0:T(8,128)S(1)}, f32[8,5,4,8,128]{4,3,2,1,0:T(8,128)S(1)}, u32[]{:S(2)}, u32[]{:S(2)}) collective-permute-start(f32[8,5,4,8,128]{4,3,2,1,0:T(8,128)S(1)} %all_to_all.20.own), channel_id=1, source_target_pairs={{1,0},{2,1},{3,2},{4,3},{5,4},{6,5},{7,6},{8,7},{9,8},{10,9},{11,1... | collective-permute-start | bytes 1966088 | tf_op jit(solution)/shard_map/ppermute | solution.py:18
  36.9 23.7 %collective-permute-start.2 = (f32[8,5,4,8,128]{4,3,2,1,0:T(8,128)S(1)}, f32[8,5,4,8,128]{4,3,2,1,0:T(8,128)S(1)}, u32[]{:S(2)}, u32[]{:S(2)}) collective-permute-start(f32[8,5,4,8,128]{4,3,2,1,0:T(8,128)S(1)} %all_to_all.20.own), channel_id=1, source_target_pairs={{0,1},{1,2},{2,3},{3,4},{4,5},{5,6},{6,7},{7,8},{8,9},{9,10},{10,1... | collective-permute-start | bytes 1966088 | tf_op jit(solution)/shard_map/ppermute | solution.py:18
  40.1 9.2 %collective-permute-start.1 = (f32[41,8,128]{2,1,0:T(8,128)S(1)}, f32[41,8,128]{2,1,0:T(8,128)S(1)}, u32[]{:S(2)}, u32[]{:S(2)}) collective-permute-start(f32[41,8,128]{2,1,0:T(8,128)S(1)} %get-tuple-element.16), channel_id=1, source_target_pairs={{128,0},{144,16},{160,32},{176,48},{192,64},{208,80},{224,96},{240... | collective-permute-start | bytes 503816 | tf_op jit(solution)/shard_map/ppermute | solution.py:18
  41.4 7.9 %collective-permute-start = (f32[40,8,128]{2,1,0:T(8,128)S(1)}, f32[40,8,128]{2,1,0:T(8,128)S(1)}, u32[]{:S(2)}, u32[]{:S(2)}) collective-permute-start(f32[40,8,128]{2,1,0:T(8,128)S(1)} %get-tuple-element.15), channel_id=1, source_target_pairs={{0,128},{16,144},{32,160},{48,176},{64,192},{80,208},{96,224},{112... | collective-permute-start | bytes 491528 | tf_op jit(solution)/shard_map/ppermute | solution.py:18
  49.3 10.2 %collective-permute-start.4 = (f32[60,8,128]{2,1,0:T(8,128)S(1)}, f32[60,8,128]{2,1,0:T(8,128)S(1)}, u32[]{:S(2)}, u32[]{:S(2)}) collective-permute-start(f32[60,8,128]{2,1,0:T(8,128)S(1)} %get-tuple-element.17), channel_id=1, source_target_pairs={{0,1},{1,2},{2,3},{3,4},{4,5},{5,6},{6,7},{7,8},{8,9},{9,10},{10,1... | collective-permute-start | bytes 737288 | tf_op jit(solution)/shard_map/ppermute | solution.py:18
  52.9 7.7 %collective-permute-start.5 = (f32[60,8,128]{2,1,0:T(8,128)S(1)}, f32[60,8,128]{2,1,0:T(8,128)S(1)}, u32[]{:S(2)}, u32[]{:S(2)}) collective-permute-start(f32[60,8,128]{2,1,0:T(8,128)S(1)} %get-tuple-element.18), channel_id=1, source_target_pairs={{1,0},{2,1},{3,2},{4,3},{5,4},{6,5},{7,6},{8,7},{9,8},{10,9},{11,1... | collective-permute-start | bytes 737288 | tf_op jit(solution)/shard_map/ppermute | solution.py:18
  54.8 4.7 %collective-permute-start.6 = (f32[32,128]{1,0:T(8,128)S(1)}, f32[32,128]{1,0:T(8,128)S(1)}, u32[]{:S(2)}, u32[]{:S(2)}) collective-permute-start(f32[32,128]{1,0:T(8,128)S(1)} %get-tuple-element.19), channel_id=1, source_target_pairs={{2,0},{3,1},{4,2},{5,3},{6,4},{7,5},{8,6},{9,7},{10,8},{11,9},{12,... | collective-permute-start | bytes 49160 | tf_op jit(solution)/shard_map/ppermute | solution.py:18
  64.4 5.4 %collective-permute-start.7 = (f32[2,5,8,128]{3,2,1,0:T(8,128)S(1)}, f32[2,5,8,128]{3,2,1,0:T(8,128)S(1)}, u32[]{:S(2)}, u32[]{:S(2)}) collective-permute-start(f32[2,5,8,128]{3,2,1,0:T(8,128)S(1)} %get-tuple-element.20.last), channel_id=1, source_target_pairs={{0,128},{16,144},{32,160},{48,176},{64,192},{80,208},{96,224},{112... | collective-permute-start | bytes 122888 | tf_op jit(solution)/shard_map/ppermute | solution.py:18
  68.5 4.7 %collective-permute-start.8 = (f32[2,5,8,128]{3,2,1,0:T(8,128)S(1)}, f32[2,5,8,128]{3,2,1,0:T(8,128)S(1)}, u32[]{:S(2)}, u32[]{:S(2)}) collective-permute-start(f32[2,5,8,128]{3,2,1,0:T(8,128)S(1)} %get-tuple-element.21.first), channel_id=1, source_target_pairs={{128,0},{144,16},{160,32},{176,48},{192,64},{208,80},{224,96},{240... | collective-permute-start | bytes 122888 | tf_op jit(solution)/shard_map/ppermute | solution.py:18
  73.2 15.7 %collective-permute-start.10 = (f32[8,5,8,128]{3,2,1,0:T(8,128)S(1)}, f32[8,5,8,128]{3,2,1,0:T(8,128)S(1)}, u32[]{:S(2)}, u32[]{:S(2)}) collective-permute-start(f32[8,5,8,128]{3,2,1,0:T(8,128)S(1)} %get-tuple-element.22.mine), channel_id=1, source_target_pairs={{1,0},{2,1},{3,2},{4,3},{5,4},{6,5},{7,6},{8,7},{9,8},{10,9},{11,1... | collective-permute-start | bytes 491528 | tf_op jit(solution)/shard_map/ppermute | solution.py:18
  77.5 11.5 %collective-permute-start.9 = (f32[8,5,8,128]{3,2,1,0:T(8,128)S(1)}, f32[8,5,8,128]{3,2,1,0:T(8,128)S(1)}, u32[]{:S(2)}, u32[]{:S(2)}) collective-permute-start(f32[8,5,8,128]{3,2,1,0:T(8,128)S(1)} %get-tuple-element.22.mine), channel_id=1, source_target_pairs={{0,1},{1,2},{2,3},{3,4},{4,5},{5,6},{6,7},{7,8},{8,9},{9,10},{10,1... | collective-permute-start | bytes 491528 | tf_op jit(solution)/shard_map/ppermute | solution.py:18
  80.6 6.8 %collective-permute-start.12 = (f32[6,5,8,128]{3,2,1,0:T(8,128)S(1)}, f32[6,5,8,128]{3,2,1,0:T(8,128)S(1)}, u32[]{:S(2)}, u32[]{:S(2)}) collective-permute-start(f32[6,5,8,128]{3,2,1,0:T(8,128)S(1)} %get-tuple-element.23), channel_id=1, source_target_pairs={{2,0},{3,1},{4,2},{5,3},{6,4},{7,5},{8,6},{9,7},{10,8},{11,9},{12,... | collective-permute-start | bytes 368648 | tf_op jit(solution)/shard_map/ppermute | solution.py:18
  81.9 7.1 %collective-permute-start.11 = (f32[6,5,8,128]{3,2,1,0:T(8,128)S(1)}, f32[6,5,8,128]{3,2,1,0:T(8,128)S(1)}, u32[]{:S(2)}, u32[]{:S(2)}) collective-permute-start(f32[6,5,8,128]{3,2,1,0:T(8,128)S(1)} %get-tuple-element.23), channel_id=1, source_target_pairs={{0,2},{1,3},{2,4},{3,5},{4,6},{5,7},{6,8},{7,9},{8,10},{9,11},{10,... | collective-permute-start | bytes 368648 | tf_op jit(solution)/shard_map/ppermute | solution.py:18
  110.7 6.0 %collective-permute-start.14 = (f32[160,128]{1,0:T(8,128)S(1)}, f32[160,128]{1,0:T(8,128)S(1)}, u32[]{:S(2)}, u32[]{:S(2)}) collective-permute-start(f32[160,128]{1,0:T(8,128)S(1)} %shard_map.74.own), channel_id=1, source_target_pairs={{16,0},{32,16},{48,32},{64,48},{80,64},{96,80},{112,96},{144,128},... | collective-permute-start | bytes 245768 | tf_op jit(solution)/shard_map/ppermute | solution.py:465
  112.0 5.6 %collective-permute-start.13 = (f32[160,128]{1,0:T(8,128)S(1)}, f32[160,128]{1,0:T(8,128)S(1)}, u32[]{:S(2)}, u32[]{:S(2)}) collective-permute-start(f32[160,128]{1,0:T(8,128)S(1)} %shard_map.74.own), channel_id=1, source_target_pairs={{0,16},{16,32},{32,48},{48,64},{64,80},{80,96},{96,112},{128,144},... | collective-permute-start | bytes 245768 | tf_op jit(solution)/shard_map/ppermute | solution.py:465

commit v5 on v4

--- a/solution.py
+++ b/solution.py
@@ -1,8 +1,10 @@
 import jax
 import jax.numpy as jnp
+import numpy as np
 from jax import lax
 from jax.experimental import pallas as pl
 from jax.experimental.pallas import tpu as pltpu
+from jax.sharding import Mesh
 from jax.sharding import PartitionSpec as P
 
 F32 = jnp.float32
@@ -12,7 +14,7 @@
 RING = 8
 
 
-def shifted(values, axis, name, steps):
+def shifted(values, name, steps):
     count = lax.axis_size(name)
     lead, last = max(0, -steps), min(count, count - steps)
     return lax.ppermute(values, name, [(i, i + steps) for i in range(lead, last)])
@@ -346,27 +348,20 @@
     total += exact_dot(rows(2, lambda i, j: (j < 4) & ((j >> 1) == i)), sums[16:24]) * 0.0625
     total += exact_dot(rows(3, lambda i, j: (j & 3) == 2 * i), sums[24:32]) * 0.0625
     total += exact_dot(rows(4, lambda i, j: ((j & 3) >> 1) == i), bz_z) * 0.0625
-    for j in range(low_out.shape[0]):
-        low_out[j] = total
+    for k in range(5):
+        mine = total[2 * k : 2 * k + 2]
+        for j in range(low_out.shape[0]):
+            low_out[j, k] = mine
 
 
 def whole_y_kernel(gathered, out):
-    flat = gathered[...].reshape(256, 128)
-
-    def test(i, j):
-        k, y = i >> 5, i & 31
-        return j == (y >> 1) * 16 + 2 * k + (y & 1)
-
-    out[...] = exact_dot(one_hot((160, 256), test), flat)
-
-
-def copies_kernel(left, own, right, out):
     for g in range(out.shape[0]):
-        for s, ref in enumerate((left, own, right)):
-            out[g, s] = ref[...]
-
-
-def coarse_kernel(sweeps, gathered, level, fine, out, co, r, b):
+        for j in range(16):
+            for k in range(5):
+                out[g, 32 * k + 2 * j : 32 * k + 2 * j + 2] = gathered[16 * g + j, k]
+
+
+def coarse_kernel(sweeps, low, own, high, level, fine, out, co, r, b):
     shape = (32, 128)
     q0 = even_mask(shape)
     row, lane = iotas(shape)
@@ -379,7 +374,7 @@
             x = i + 16 * side
             for s in range(3):
                 target = 64 * side + 16 * s
-                block = gathered[x // 8, s, 32 * a : 32 * a + 32]
+                block = (low, own, high)[s][x // 8, 32 * a : 32 * a + 32]
                 shift = (target - 16 * (x % 8)) % 128
                 moved = pltpu.roll(block, shift, 1) if shift else block
                 total = jnp.where((lane >> 4) == target // 16, moved, total)
@@ -416,25 +411,24 @@
 
     lax.fori_loop(0, sweeps, sweep, 0)
 
-    gy, gx = lax.axis_index("gy"), lax.axis_index("gx")
-    ring, place = gx // RING, lax.rem(gx, RING)
+    gy, ring, place = (lax.axis_index(name) for name in ("gy", "ring", "place"))
     side, base = ring // 2, 4 * lax.rem(ring, 2)
-    own = []
+    parts = []
     for k in range(8):
         red, black = r[base + k // 2 + 1], b[base + k // 2 + 1]
         value = jnp.where(q0, red, black) if k % 2 == 0 else jnp.where(q0, black, red)
         value = pltpu.roll(value, lax.rem(32 - 2 * gy, 32), 0)
-        own.append(pltpu.roll(value, 64 * side, 1)[:8])
+        parts.append(pltpu.roll(value, 64 * side, 1)[:8])
     q0 = even_mask((8, 128))
     row, lane = iotas((8, 128))
-    up = exact_dot(jnp.concatenate(own, 0), one_hot((128, 128), lambda i, j: (j >> 1) + 8 == i))
+    up = exact_dot(jnp.concatenate(parts, 0), one_hot((128, 128), lambda i, j: (j >> 1) + 8 == i))
     spread = one_hot((64, 64), lambda i, j: ((i >> 3) == (j >> 3)) & (((i & 3) >> 1) == (j & 7)))
     up = exact_dot(spread, up)
     mid = []
     for k in range(8):
         add = up[8 * k : 8 * k + 8]
         mid.extend(halves(q0, level[0, k] + add, level[1, k] + add))
-        mine = pltpu.roll(own[k], lax.rem(16 * place + 112, 128), 1)
+        mine = pltpu.roll(parts[k], lax.rem(16 * place + 112, 128), 1)
         out[k, 2] = jnp.where(((lane >> 4) == place) & (row < 2), mine, 0.0)
     wide = exact_dot(jnp.concatenate(mid, 0), one_hot((128, 128), lambda i, j: (j >> 1) == i))
     spread = one_hot((128, 128), lambda i, j: ((i >> 3) == (j >> 3)) & (((i & 7) >> 1) == (j & 7)))
@@ -459,68 +453,61 @@
     coarse_out[0] = total[:2]
 
 
-def in_rings(values, steps):
-    count = lax.axis_size("gx")
-    pairs = [(i, i + steps) for i in range(count) if 0 <= i % RING + steps < RING]
-    return lax.ppermute(values, "gx", pairs)
-
-
-def on_device(rhs, alpha, beta_x, beta_y, beta_z):
-    count_x, count_y = lax.axis_size("gx"), lax.axis_size("gy")
-    groups = count_x // RING
-    rings = [[RING * i + j for j in range(RING)] for i in range(groups)]
-    across = [list(c) for c in zip(*rings)]
+def cycle(rhs, alpha, beta_x, beta_y, beta_z):
+    rings, count_y = lax.axis_size("ring"), lax.axis_size("gy")
 
     (own,) = call(to_windows_kernel, [(RING, 5, 4, 8, 128)], copied=True)(rhs, alpha, beta_x, beta_y, beta_z)
-    own = lax.all_to_all(own, "gx", 0, 0, tiled=True, axis_index_groups=rings)
+    own = lax.all_to_all(own, "place", 0, 0, tiled=True)
     to_low, to_high, first_by = call(
         x_messages_kernel, [(41, 8, 128), (40, 8, 128), (32, 128)]
     )(own)
-    y_low, y_high = shifted(own, 1, "gy", 1), shifted(own, 1, "gy", -1)
-    x_low, x_high = shifted(to_high, 1, "gx", RING), shifted(to_low, 1, "gx", -RING)
-    beyond_y = shifted(first_by, 0, "gy", -2)
+    x_low, x_high = shifted(to_high, "ring", 1), shifted(to_low, "ring", -1)
+    y_low, y_high = shifted(own, "gy", 1), shifted(own, "gy", -1)
+    beyond_y = shifted(first_by, "gy", -2)
     to_low, to_high = call(
         corner_messages_kernel, [(60, 8, 128), (60, 8, 128)]
     )(x_low, x_high)
-    corner_low, corner_high = shifted(to_high, 1, "gy", 1), shifted(to_low, 1, "gy", -1)
+    corner_low = shifted(to_high, "gy", 1)
+    corner_high = shifted(to_low, "gy", -1)
     fine, mid_first, mid_last, mid_own = call(
         fine_kernel,
         [(2, 16, 8, 128), (2, 5, 8, 128), (2, 5, 8, 128), (4, 2, 8, 128)],
         [(17, 24, 24, 128), (26, 24, 128), (26, 24, 128)],
     )(own, x_low, x_high, y_low, y_high, corner_low, corner_high, beyond_y)
 
-    low, high = shifted(mid_last, 0, "gx", RING), shifted(mid_first, 0, "gx", -RING)
+    low, high = shifted(mid_last, "ring", 1), shifted(mid_first, "ring", -1)
     near, far = call(
         mid_message_kernel, [(8, 5, 8, 128), (6, 5, 8, 128)]
     )(low, mid_first, mid_last, high)
     level, low = call(
         mid_kernel,
-        [(2, 8, 8, 128), (count_y, 16, 128)],
+        [(2, 8, 8, 128), (rings * count_y, 5, 2, 128)],
         [(17, 16, 24, 128), (18, 24, 128), (18, 24, 128)],
     )(
-        near, shifted(near, 0, "gy", 1), shifted(near, 0, "gy", -1),
-        shifted(far, 0, "gy", 2), shifted(far, 0, "gy", -2), mid_own,
+        near, shifted(near, "gy", 1), shifted(near, "gy", -1),
+        shifted(far, "gy", 2), shifted(far, "gy", -2), mid_own,
     )
 
-    low = lax.all_to_all(low, "gy", 0, 0, tiled=True)
-    (low,) = call(whole_y_kernel, [(160, 128)])(low)
-    (low,) = call(copies_kernel, [(groups, 3, 160, 128)])(in_rings(low, 1), low, in_rings(low, -1))
-    low = lax.all_to_all(low, "gx", 0, 0, tiled=True, axis_index_groups=across)
+    low = lax.all_to_all(low, ("ring", "gy"), 0, 0, tiled=True)
+    (own,) = call(whole_y_kernel, [(rings, 160, 128)])(low)
     (pieces,) = call(
         lambda *refs: coarse_kernel(8, *refs),
         [(RING, 3, 8, 128)],
         [(17, 8, 32, 128), (10, 32, 128), (10, 32, 128)],
-    )(low, level, fine)
-    pieces = lax.all_to_all(pieces, "gx", 0, 0, tiled=True, axis_index_groups=rings)
+    )(shifted(own, "place", 1), own, shifted(own, "place", -1), level, fine)
+    pieces = lax.all_to_all(pieces, "place", 0, 0, tiled=True)
     fine_solution, coarse = call(finish_kernel, [rhs.shape, (1, 2, 128)])(pieces)
     return fine_solution, coarse
 
 
 def solution(mesh):
-    placed = P("gx", "gy", None)
+    count_x, count_y = mesh.devices.shape
+    devices = np.array(mesh.devices).reshape(count_x // RING, RING, count_y)
+    split = Mesh(devices, ("ring", "place", "gy"))
+    placed = P(("ring", "place"), "gy", None)
     return jax.shard_map(
-        on_device,
-        mesh=mesh,
+        cycle,
+        mesh=split,
         in_specs=(placed,) * 5,
         out_specs=(placed, placed),
         check_vma=False,

time: 156 us -> 151 us (0.968)
  blocking collectives: 79.6 us -> 70.1 us
  waiting for transfers between devices: 16.5 us -> 21.2 us
    all_to_all x4 -> x3, blocking collectives: 79.6 us -> 70.1 us  [the longest x1 30.1 us: cycle(): own = lax.all_to_all(own, 'place', 0, 0, tiled=True)]
    ppermute x13 -> x15, waiting for transfers between devices: 14.9 us -> 21.2 us  [shifted(): lax.ppermute(values, name, [(i, i + steps) for i in range(lead, last)])]
    ppermute x13 -> x15, starting transfers between devices: 37.1 us -> 42.4 us  [shifted(): lax.ppermute(values, name, [(i, i + steps) for i in range(lead, last)])]
    ppermute x2 -> x0, starting transfers between devices: 5.28 us -> none  [in_rings(): return lax.ppermute(values, 'gx', pairs)]
    ppermute x2 -> x0, waiting for transfers between devices: 1.64 us -> none  [in_rings(): return lax.ppermute(values, 'gx', pairs)]
    pallas_call x10 -> x9, Pallas kernels: 14.8 us -> 14.6 us  [run(): pl.pallas_call(kernel, out_shape=[jax.ShapeDtypeStruct(s, F32) for s in o...]
where the time goes in v5:
time: 151 us; the launch traced here: 149 us
  blocking collectives  70.1 us (46%)
  starting transfers between devices  42.4 us (28%)
  waiting for transfers between devices  21.2 us (14%)
  Pallas kernels  14.6 us (10%)
    ppermute x15, starting transfers between devices, shifted(): lax.ppermute(values, name, [(i, i + steps) for i in range(lead, last)])  42.4 us
    all_to_all x1, blocking collectives, cycle(): own = lax.all_to_all(own, 'place', 0, 0, tiled=True)  30.1 us
    all_to_all x1, blocking collectives, cycle(): low = lax.all_to_all(low, ('ring', 'gy'), 0, 0, tiled=True)  26.8 us
    ppermute x15, waiting for transfers between devices, shifted(): lax.ppermute(values, name, [(i, i + steps) for i in range(lead, last)])  21.2 us
    pallas_call x9, Pallas kernels, run(): pl.pallas_call(kernel, out_shape=[jax.ShapeDtypeStruct(s, F32) for s in o...  14.6 us
    all_to_all x1, blocking collectives, cycle(): pieces = lax.all_to_all(pieces, 'place', 0, 0, tiled=True)  13.2 us
  transfers between devices with their start and end apart: 15, of which 8 were waited for; matrix products, arithmetic and copies ran while one was open for 0% of the time, Pallas kernels for 0%

profile of v5, /device:TPU:1, one launch (start us, length us, event | category | flops | bytes accessed | tf_op | source)
XLA Modules:
  0.0 149.1 jit_solution(10062231440893415833)
XLA Ops:
  0.6 2.2 %shard_map.68 = f32[8,5,4,8,128]{4,3,2,1,0:T(8,128)} custom-call(f32[4,8,512]{2,1,0:T(8,128)} %refs_0_.1, f32[4,8,512]{2,1,0:T(8,128)} %refs_1_.1, f32[4,8,512]{2,1,0:T(8,128)} %refs_2_.1, f32[4,8,512]{2,1,0:T(8,128)} %refs_3_.1, f32[4,8,512]{2,1,0:T(8,128)} %refs_4_.1), custom_call_target="tpu_custom_call" | custom-call | tf_op jit(solution)/shard_map/pallas_call | solution.py:28
  2.9 30.1 %all_to_all.15.own = f32[8,5,4,8,128]{4,3,2,1,0:T(8,128)S(1)} all-to-all(f32[8,5,4,8,128]{4,3,2,1,0:T(8,128)} %shard_map.68), channel_id=1, replica_groups=mesh['ring'=4,'place'=8,'gy'=16] {'place'}, dimensions={0} | all-to-all | bytes 1310720 | tf_op jit(solution)/shard_map/all_to_all | solution.py:460
  33.0 3.9 %collective-permute-start.3 = (f32[8,5,4,8,128]{4,3,2,1,0:T(8,128)S(1)}, f32[8,5,4,8,128]{4,3,2,1,0:T(8,128)S(1)}, u32[]{:S(2)}, u32[]{:S(2)}) collective-permute-start(f32[8,5,4,8,128]{4,3,2,1,0:T(8,128)S(1)} %all_to_all.15.own), channel_id=1, source_target_pairs={{1,0},{2,1},{3,2},{4,3},{5,4},{6,5},{7,6},{8,7},{9,8},{10,9},{11,1... | collective-permute-start | bytes 1966088 | tf_op jit(solution)/shard_map/ppermute | solution.py:20
  36.9 3.1 %collective-permute-start.2 = (f32[8,5,4,8,128]{4,3,2,1,0:T(8,128)S(1)}, f32[8,5,4,8,128]{4,3,2,1,0:T(8,128)S(1)}, u32[]{:S(2)}, u32[]{:S(2)}) collective-permute-start(f32[8,5,4,8,128]{4,3,2,1,0:T(8,128)S(1)} %all_to_all.15.own), channel_id=1, source_target_pairs={{0,1},{1,2},{2,3},{3,4},{4,5},{5,6},{6,7},{7,8},{8,9},{9,10},{10,1... | collective-permute-start | bytes 1966088 | tf_op jit(solution)/shard_map/ppermute | solution.py:20
  40.1 1.3 collective-permute-start.1
  41.4 4.0 %collective-permute-start = (f32[40,8,128]{2,1,0:T(8,128)S(1)}, f32[40,8,128]{2,1,0:T(8,128)S(1)}, u32[]{:S(2)}, u32[]{:S(2)}) collective-permute-start(f32[40,8,128]{2,1,0:T(8,128)S(1)} %get-tuple-element.15), channel_id=1, source_target_pairs={{0,128},{128,256},{256,384},{1,129},{129,257},{257,385},{2,130},{1... | collective-permute-start | bytes 491528 | tf_op jit(solution)/shard_map/ppermute | solution.py:20
  45.4 3.9 %collective-permute-done.low.x_low = f32[40,8,128]{2,1,0:T(8,128)S(1)} collective-permute-done((f32[40,8,128]{2,1,0:T(8,128)S(1)}, f32[40,8,128]{2,1,0:T(8,128)S(1)}, u32[]{:S(2)}, u32[]{:S(2)}) %collective-permute-start) | collective-permute-done | bytes 163872 | tf_op jit(solution)/shard_map/ppermute | solution.py:20
  49.3 0.0 collective-permute-done.1.high.x_high
  49.3 3.6 %collective-permute-start.4 = (f32[60,8,128]{2,1,0:T(8,128)S(1)}, f32[60,8,128]{2,1,0:T(8,128)S(1)}, u32[]{:S(2)}, u32[]{:S(2)}) collective-permute-start(f32[60,8,128]{2,1,0:T(8,128)S(1)} %get-tuple-element.17), channel_id=1, source_target_pairs={{0,1},{1,2},{2,3},{3,4},{4,5},{5,6},{6,7},{7,8},{8,9},{9,10},{10,1... | collective-permute-start | bytes 737288 | tf_op jit(solution)/shard_map/ppermute | solution.py:20
  52.9 1.9 %collective-permute-start.5 = (f32[60,8,128]{2,1,0:T(8,128)S(1)}, f32[60,8,128]{2,1,0:T(8,128)S(1)}, u32[]{:S(2)}, u32[]{:S(2)}) collective-permute-start(f32[60,8,128]{2,1,0:T(8,128)S(1)} %get-tuple-element.18), channel_id=1, source_target_pairs={{1,0},{2,1},{3,2},{4,3},{5,4},{6,5},{7,6},{8,7},{9,8},{10,9},{11,1... | collective-permute-start | bytes 737288 | tf_op jit(solution)/shard_map/ppermute | solution.py:20
  54.8 1.3 collective-permute-start.6
  56.1 3.4 %collective-permute-done.6.beyond_y = f32[32,128]{1,0:T(8,128)S(1)} collective-permute-done((f32[32,128]{1,0:T(8,128)S(1)}, f32[32,128]{1,0:T(8,128)S(1)}, u32[]{:S(2)}, u32[]{:S(2)}) %collective-permute-start.6) | collective-permute-done | bytes 16416 | tf_op jit(solution)/shard_map/ppermute | solution.py:20
  59.5 0.0 collective-permute-done.4.corner_low
  59.5 1.1 collective-permute-done.5.corner_high
  60.6 0.0 collective-permute-done.3.y_high
  60.6 0.0 collective-permute-done.2.y_low
  60.6 3.8 %shard_map.71 = (f32[2,16,8,128]{3,2,1,0:T(8,128)S(1)}, f32[2,5,8,128]{3,2,1,0:T(8,128)S(1)}, f32[2,5,8,128]{3,2,1,0:T(8,128)S(1)}, f32[4,2,8,128]{3,2,1,0:T(8,128)S(1)}) custom-call(f32[8,5,4,8,128]{4,3,2,1,0:T(8,128)S(1)} %all_to_all.15.own, f32[40,8,128]{2,1,0:T(8,128)S(1)} %collective-permute-done.low.x_low, ...), custom_call_target="tpu_custom_call" | custom-call | tf_op jit(solution)/shard_map/pallas_call | solution.py:28
  64.4 4.1 %collective-permute-start.7 = (f32[2,5,8,128]{3,2,1,0:T(8,128)S(1)}, f32[2,5,8,128]{3,2,1,0:T(8,128)S(1)}, u32[]{:S(2)}, u32[]{:S(2)}) collective-permute-start(f32[2,5,8,128]{3,2,1,0:T(8,128)S(1)} %get-tuple-element.20.last), channel_id=1, source_target_pairs={{0,128},{128,256},{256,384},{1,129},{129,257},{257,385},{2,130},{1... | collective-permute-start | bytes 122888 | tf_op jit(solution)/shard_map/ppermute | solution.py:20
  68.5 1.3 collective-permute-start.8
  69.8 0.0 collective-permute-done.7.low
  69.8 3.4 %collective-permute-done.8.high = f32[2,5,8,128]{3,2,1,0:T(8,128)S(1)} collective-permute-done((f32[2,5,8,128]{3,2,1,0:T(8,128)S(1)}, f32[2,5,8,128]{3,2,1,0:T(8,128)S(1)}, u32[]{:S(2)}, u32[]{:S(2)}) %collective-permute-start.8) | collective-permute-done | bytes 40992 | tf_op jit(solution)/shard_map/ppermute | solution.py:20
  73.2 4.2 %collective-permute-start.10 = (f32[8,5,8,128]{3,2,1,0:T(8,128)S(1)}, f32[8,5,8,128]{3,2,1,0:T(8,128)S(1)}, u32[]{:S(2)}, u32[]{:S(2)}) collective-permute-start(f32[8,5,8,128]{3,2,1,0:T(8,128)S(1)} %get-tuple-element.22.mine), channel_id=1, source_target_pairs={{1,0},{2,1},{3,2},{4,3},{5,4},{6,5},{7,6},{8,7},{9,8},{10,9},{11,1... | collective-permute-start | bytes 491528 | tf_op jit(solution)/shard_map/ppermute | solution.py:20
  77.5 3.1 %collective-permute-start.9 = (f32[8,5,8,128]{3,2,1,0:T(8,128)S(1)}, f32[8,5,8,128]{3,2,1,0:T(8,128)S(1)}, u32[]{:S(2)}, u32[]{:S(2)}) collective-permute-start(f32[8,5,8,128]{3,2,1,0:T(8,128)S(1)} %get-tuple-element.22.mine), channel_id=1, source_target_pairs={{0,1},{1,2},{2,3},{3,4},{4,5},{5,6},{6,7},{7,8},{8,9},{9,10},{10,1... | collective-permute-start | bytes 491528 | tf_op jit(solution)/shard_map/ppermute | solution.py:20
  80.6 1.3 collective-permute-start.12
  81.9 4.0 %collective-permute-start.11 = (f32[6,5,8,128]{3,2,1,0:T(8,128)S(1)}, f32[6,5,8,128]{3,2,1,0:T(8,128)S(1)}, u32[]{:S(2)}, u32[]{:S(2)}) collective-permute-start(f32[6,5,8,128]{3,2,1,0:T(8,128)S(1)} %get-tuple-element.23), channel_id=1, source_target_pairs={{0,2},{1,3},{2,4},{3,5},{4,6},{5,7},{6,8},{7,9},{8,10},{9,11},{10,... | collective-permute-start | bytes 368648 | tf_op jit(solution)/shard_map/ppermute | solution.py:20
  85.9 1.5 %collective-permute-done.12.high2 = f32[6,5,8,128]{3,2,1,0:T(8,128)S(1)} collective-permute-done((f32[6,5,8,128]{3,2,1,0:T(8,128)S(1)}, f32[6,5,8,128]{3,2,1,0:T(8,128)S(1)}, u32[]{:S(2)}, u32[]{:S(2)}) %collective-permute-start.12) | collective-permute-done | bytes 122912 | tf_op jit(solution)/shard_map/ppermute | solution.py:20
  87.4 1.6 %collective-permute-done.11.low2 = f32[6,5,8,128]{3,2,1,0:T(8,128)S(1)} collective-permute-done((f32[6,5,8,128]{3,2,1,0:T(8,128)S(1)}, f32[6,5,8,128]{3,2,1,0:T(8,128)S(1)}, u32[]{:S(2)}, u32[]{:S(2)}) %collective-permute-start.11) | collective-permute-done | bytes 122912 | tf_op jit(solution)/shard_map/ppermute | solution.py:20
  88.9 0.0 collective-permute-done.10.high1
  88.9 0.0 collective-permute-done.9.low1
  88.9 2.0 %shard_map.73 = (f32[2,8,8,128]{3,2,1,0:T(8,128)S(1)}, f32[64,5,2,128]{3,2,1,0:T(2,128)S(1)}) custom-call(f32[8,5,8,128]{3,2,1,0:T(8,128)S(1)} %get-tuple-element.22.mine, f32[8,5,8,128]{3,2,1,0:T(8,128)S(1)} %collective-permute-done.9.low1, f32[8,5,8,128]{3,2,1,0:T(8,128)S(1)} %collective-permute-done.10.high1, ...), custom_call_target="tpu_custom_call" | custom-call | tf_op jit(solution)/shard_map/pallas_call | solution.py:28
  91.0 26.8 %all_to_all.16.gathered = f32[64,5,2,128]{3,2,1,0:T(2,128)S(1)} all-to-all(f32[64,5,2,128]{3,2,1,0:T(2,128)S(1)} %get-tuple-element.25), channel_id=1, replica_groups=mesh['ring'=4,'place'=8,'gy'=16] {'ring','gy'}, dimensions={0} | all-to-all | bytes 655360 | tf_op jit(solution)/shard_map/all_to_all | solution.py:491
  117.8 0.1 shard_map.74.refs_1_
  117.9 1.3 collective-permute-start.14
  119.2 4.0 %collective-permute-start.13 = (f32[4,160,128]{2,1,0:T(8,128)S(1)}, f32[4,160,128]{2,1,0:T(8,128)S(1)}, u32[]{:S(2)}, u32[]{:S(2)}) collective-permute-start(f32[4,160,128]{2,1,0:T(8,128)S(1)} %shard_map.74.refs_1_), channel_id=1, source_target_pairs={{0,16},{16,32},{32,48},{48,64},{64,80},{80,96},{96,112},{1,17},{17... | collective-permute-start | bytes 983048 | tf_op jit(solution)/shard_map/ppermute | solution.py:20
  123.3 5.4 %collective-permute-done.14.refs_2_ = f32[4,160,128]{2,1,0:T(8,128)S(1)} collective-permute-done((f32[4,160,128]{2,1,0:T(8,128)S(1)}, f32[4,160,128]{2,1,0:T(8,128)S(1)}, u32[]{:S(2)}, u32[]{:S(2)}) %collective-permute-start.14) | collective-permute-done | bytes 327712 | tf_op jit(solution)/shard_map/ppermute | solution.py:20
  128.7 0.9 collective-permute-done.13.refs_0_
  129.6 5.6 %shard_map.75 = f32[8,3,8,128]{3,2,1,0:T(8,128)S(1)} custom-call(f32[4,160,128]{2,1,0:T(8,128)S(1)} %collective-permute-done.13.refs_0_, f32[4,160,128]{2,1,0:T(8,128)S(1)} %shard_map.74.refs_1_, f32[4,160,128]{2,1,0:T(8,128)S(1)} %collective-permute-done.14.refs_2_, f32[2,8,8,128]{3,2,1,0:T(8,128)S(1)} %get-tuple-element.26.refs_3_, ...), custom_call_target="tpu_custom_call" | custom-call | tf_op jit(solution)/shard_map/pallas_call | solution.py:28
  135.2 13.2 %all_to_all.17.pieces = f32[8,3,8,128]{3,2,1,0:T(8,128)S(1)} all-to-all(f32[8,3,8,128]{3,2,1,0:T(8,128)S(1)} %shard_map.75), channel_id=1, replica_groups=mesh['ring'=4,'place'=8,'gy'=16] {'place'}, dimensions={0} | all-to-all | bytes 196608 | tf_op jit(solution)/shard_map/all_to_all | solution.py:498
  148.4 0.7 shard_map.76
  (3 shorter events, 0.1 us)
Async XLA Ops:
  33.0 27.7 %collective-permute-start.3 = (f32[8,5,4,8,128]{4,3,2,1,0:T(8,128)S(1)}, f32[8,5,4,8,128]{4,3,2,1,0:T(8,128)S(1)}, u32[]{:S(2)}, u32[]{:S(2)}) collective-permute-start(f32[8,5,4,8,128]{4,3,2,1,0:T(8,128)S(1)} %all_to_all.15.own), channel_id=1, source_target_pairs={{1,0},{2,1},{3,2},{4,3},{5,4},{6,5},{7,6},{8,7},{9,8},{10,9},{11,1... | collective-permute-start | bytes 1966088 | tf_op jit(solution)/shard_map/ppermute | solution.py:20
  36.9 23.7 %collective-permute-start.2 = (f32[8,5,4,8,128]{4,3,2,1,0:T(8,128)S(1)}, f32[8,5,4,8,128]{4,3,2,1,0:T(8,128)S(1)}, u32[]{:S(2)}, u32[]{:S(2)}) collective-permute-start(f32[8,5,4,8,128]{4,3,2,1,0:T(8,128)S(1)} %all_to_all.15.own), channel_id=1, source_target_pairs={{0,1},{1,2},{2,3},{3,4},{4,5},{5,6},{6,7},{7,8},{8,9},{9,10},{10,1... | collective-permute-start | bytes 1966088 | tf_op jit(solution)/shard_map/ppermute | solution.py:20
  40.1 9.2 %collective-permute-start.1 = (f32[41,8,128]{2,1,0:T(8,128)S(1)}, f32[41,8,128]{2,1,0:T(8,128)S(1)}, u32[]{:S(2)}, u32[]{:S(2)}) collective-permute-start(f32[41,8,128]{2,1,0:T(8,128)S(1)} %get-tuple-element.16), channel_id=1, source_target_pairs={{128,0},{256,128},{384,256},{129,1},{257,129},{385,257},{130,2},{2... | collective-permute-start | bytes 503816 | tf_op jit(solution)/shard_map/ppermute | solution.py:20
  41.4 7.9 %collective-permute-start = (f32[40,8,128]{2,1,0:T(8,128)S(1)}, f32[40,8,128]{2,1,0:T(8,128)S(1)}, u32[]{:S(2)}, u32[]{:S(2)}) collective-permute-start(f32[40,8,128]{2,1,0:T(8,128)S(1)} %get-tuple-element.15), channel_id=1, source_target_pairs={{0,128},{128,256},{256,384},{1,129},{129,257},{257,385},{2,130},{1... | collective-permute-start | bytes 491528 | tf_op jit(solution)/shard_map/ppermute | solution.py:20
  49.3 10.2 %collective-permute-start.4 = (f32[60,8,128]{2,1,0:T(8,128)S(1)}, f32[60,8,128]{2,1,0:T(8,128)S(1)}, u32[]{:S(2)}, u32[]{:S(2)}) collective-permute-start(f32[60,8,128]{2,1,0:T(8,128)S(1)} %get-tuple-element.17), channel_id=1, source_target_pairs={{0,1},{1,2},{2,3},{3,4},{4,5},{5,6},{6,7},{7,8},{8,9},{9,10},{10,1... | collective-permute-start | bytes 737288 | tf_op jit(solution)/shard_map/ppermute | solution.py:20
  52.9 7.7 %collective-permute-start.5 = (f32[60,8,128]{2,1,0:T(8,128)S(1)}, f32[60,8,128]{2,1,0:T(8,128)S(1)}, u32[]{:S(2)}, u32[]{:S(2)}) collective-permute-start(f32[60,8,128]{2,1,0:T(8,128)S(1)} %get-tuple-element.18), channel_id=1, source_target_pairs={{1,0},{2,1},{3,2},{4,3},{5,4},{6,5},{7,6},{8,7},{9,8},{10,9},{11,1... | collective-permute-start | bytes 737288 | tf_op jit(solution)/shard_map/ppermute | solution.py:20
  54.8 4.7 %collective-permute-start.6 = (f32[32,128]{1,0:T(8,128)S(1)}, f32[32,128]{1,0:T(8,128)S(1)}, u32[]{:S(2)}, u32[]{:S(2)}) collective-permute-start(f32[32,128]{1,0:T(8,128)S(1)} %get-tuple-element.19), channel_id=1, source_target_pairs={{2,0},{3,1},{4,2},{5,3},{6,4},{7,5},{8,6},{9,7},{10,8},{11,9},{12,... | collective-permute-start | bytes 49160 | tf_op jit(solution)/shard_map/ppermute | solution.py:20
  64.4 5.4 %collective-permute-start.7 = (f32[2,5,8,128]{3,2,1,0:T(8,128)S(1)}, f32[2,5,8,128]{3,2,1,0:T(8,128)S(1)}, u32[]{:S(2)}, u32[]{:S(2)}) collective-permute-start(f32[2,5,8,128]{3,2,1,0:T(8,128)S(1)} %get-tuple-element.20.last), channel_id=1, source_target_pairs={{0,128},{128,256},{256,384},{1,129},{129,257},{257,385},{2,130},{1... | collective-permute-start | bytes 122888 | tf_op jit(solution)/shard_map/ppermute | solution.py:20
  68.5 4.7 %collective-permute-start.8 = (f32[2,5,8,128]{3,2,1,0:T(8,128)S(1)}, f32[2,5,8,128]{3,2,1,0:T(8,128)S(1)}, u32[]{:S(2)}, u32[]{:S(2)}) collective-permute-start(f32[2,5,8,128]{3,2,1,0:T(8,128)S(1)} %get-tuple-element.21.first), channel_id=1, source_target_pairs={{128,0},{256,128},{384,256},{129,1},{257,129},{385,257},{130,2},{2... | collective-permute-start | bytes 122888 | tf_op jit(solution)/shard_map/ppermute | solution.py:20
  73.2 15.7 %collective-permute-start.10 = (f32[8,5,8,128]{3,2,1,0:T(8,128)S(1)}, f32[8,5,8,128]{3,2,1,0:T(8,128)S(1)}, u32[]{:S(2)}, u32[]{:S(2)}) collective-permute-start(f32[8,5,8,128]{3,2,1,0:T(8,128)S(1)} %get-tuple-element.22.mine), channel_id=1, source_target_pairs={{1,0},{2,1},{3,2},{4,3},{5,4},{6,5},{7,6},{8,7},{9,8},{10,9},{11,1... | collective-permute-start | bytes 491528 | tf_op jit(solution)/shard_map/ppermute | solution.py:20
  77.5 11.5 %collective-permute-start.9 = (f32[8,5,8,128]{3,2,1,0:T(8,128)S(1)}, f32[8,5,8,128]{3,2,1,0:T(8,128)S(1)}, u32[]{:S(2)}, u32[]{:S(2)}) collective-permute-start(f32[8,5,8,128]{3,2,1,0:T(8,128)S(1)} %get-tuple-element.22.mine), channel_id=1, source_target_pairs={{0,1},{1,2},{2,3},{3,4},{4,5},{5,6},{6,7},{7,8},{8,9},{9,10},{10,1... | collective-permute-start | bytes 491528 | tf_op jit(solution)/shard_map/ppermute | solution.py:20
  80.6 6.8 %collective-permute-start.12 = (f32[6,5,8,128]{3,2,1,0:T(8,128)S(1)}, f32[6,5,8,128]{3,2,1,0:T(8,128)S(1)}, u32[]{:S(2)}, u32[]{:S(2)}) collective-permute-start(f32[6,5,8,128]{3,2,1,0:T(8,128)S(1)} %get-tuple-element.23), channel_id=1, source_target_pairs={{2,0},{3,1},{4,2},{5,3},{6,4},{7,5},{8,6},{9,7},{10,8},{11,9},{12,... | collective-permute-start | bytes 368648 | tf_op jit(solution)/shard_map/ppermute | solution.py:20
  81.9 7.1 %collective-permute-start.11 = (f32[6,5,8,128]{3,2,1,0:T(8,128)S(1)}, f32[6,5,8,128]{3,2,1,0:T(8,128)S(1)}, u32[]{:S(2)}, u32[]{:S(2)}) collective-permute-start(f32[6,5,8,128]{3,2,1,0:T(8,128)S(1)} %get-tuple-element.23), channel_id=1, source_target_pairs={{0,2},{1,3},{2,4},{3,5},{4,6},{5,7},{6,8},{7,9},{8,10},{9,11},{10,... | collective-permute-start | bytes 368648 | tf_op jit(solution)/shard_map/ppermute | solution.py:20
  117.9 10.8 %collective-permute-start.14 = (f32[4,160,128]{2,1,0:T(8,128)S(1)}, f32[4,160,128]{2,1,0:T(8,128)S(1)}, u32[]{:S(2)}, u32[]{:S(2)}) collective-permute-start(f32[4,160,128]{2,1,0:T(8,128)S(1)} %shard_map.74.refs_1_), channel_id=1, source_target_pairs={{16,0},{32,16},{48,32},{64,48},{80,64},{96,80},{112,96},{17,1},{33... | collective-permute-start | bytes 983048 | tf_op jit(solution)/shard_map/ppermute | solution.py:20
  119.2 10.4 %collective-permute-start.13 = (f32[4,160,128]{2,1,0:T(8,128)S(1)}, f32[4,160,128]{2,1,0:T(8,128)S(1)}, u32[]{:S(2)}, u32[]{:S(2)}) collective-permute-start(f32[4,160,128]{2,1,0:T(8,128)S(1)} %shard_map.74.refs_1_), channel_id=1, source_target_pairs={{0,16},{16,32},{32,48},{48,64},{64,80},{80,96},{96,112},{1,17},{17... | collective-permute-start | bytes 983048 | tf_op jit(solution)/shard_map/ppermute | solution.py:20

commit v6 on v5

--- a/solution.py
+++ b/solution.py
@@ -198,7 +198,7 @@
 
 def fine_kernel(
     own, x_low, x_high, y_low, y_high, corner_low, corner_high, beyond_y,
-    fine_out, mid_first, mid_last, own_out, co, r, b,
+    fine_out, mid_out, mid_first, mid_last, own_out, co, r, b,
 ):
     q0 = even_mask((24, 128))
     row, lane = iotas((24, 128))
@@ -283,20 +283,25 @@
 
     for t in range(4):
         for a, value in enumerate(arrays):
-            (mid_first if t < 2 else mid_last)[t % 2, a] = tile(value, t)
+            mid_out[t, a] = tile(value, t)
+            (mid_first if t < 2 else mid_last)[t % 2, a] = mid_out[t, a]
         own_out[t, 0] = tile(diagonal, t)
         own_out[t, 1] = tile(alpha, t)
 
 
-def mid_message_kernel(low, first, last, high, near, far):
-    tiles = [ref[s] for ref in (low, first, last, high) for s in range(2)]
-    for s in range(8):
-        near[s] = tiles[s]
-        if 0 < s < 7:
-            far[s - 1] = tiles[s]
-
-
-def mid_kernel(mine, low1, high1, low2, high2, own, level_out, low_out, co, r, b):
+def mid_corners_kernel(low1, high1, low2, high2, to_low, to_high):
+    for out, first, inner in ((to_low, 0, 0), (to_high, 2, 3)):
+        for t in range(2):
+            out[t] = high1[first + t]
+            out[2 + t] = low1[first + t]
+        out[4] = high2[inner]
+        out[5] = low2[inner]
+
+
+def mid_kernel(
+    mine, x_low, x_high, low1, high1, low2, high2, corner_low, corner_high, own,
+    level_out, low_out, co, r, b,
+):
     q0 = even_mask((24, 128))
     _, lane = iotas((8, 128))
     keep = low_rows((8, 128))
@@ -306,12 +311,15 @@
     def part(tile, p):
         return jnp.where(lane < 64, pltpu.roll(tile, 64, 1) if p % 2 else tile, 0.0)
 
+    def tiles(t, a):
+        if 2 <= t < 6:
+            return [ref[t - 2, a] for ref in (mine, high1, low1, high2, low2)]
+        x, corner, s = (x_low, corner_low, t) if t < 2 else (x_high, corner_high, t - 6)
+        far = [corner[4, a], corner[5, a]] if t in (1, 6) else [zero, zero]
+        return [x[s, a], corner[s, a], corner[2 + s, a]] + far
+
     def planes(p, a):
-        t = p // 2
-        c, h1, w1 = part(mine[t, a], p), part(high1[t, a], p), part(low1[t, a], p)
-        inner = 0 < t < 7
-        h2 = part(high2[t - 1, a], p) if inner else zero
-        w2 = part(low2[t - 1, a], p) if inner else zero
+        c, h1, w1, h2, w2 = (part(value, p) for value in tiles(p // 2, a))
         e0 = [jnp.where(keep, c, half(h1)), jnp.where(keep, h2, 0.0), jnp.where(keep, w2, half(w1))]
         e1 = [jnp.where(keep, half(c), h1), jnp.where(keep, half(h2), 0.0), jnp.where(keep, half(w2), w1)]
         return jnp.concatenate(e0, 0), jnp.concatenate(e1, 0)
@@ -335,7 +343,7 @@
         red, black = residual(co, r, b, p, q0)
         level_out[0, k] = r[p + 1][:8]
         level_out[1, k] = b[p + 1][:8]
-        mid = [part(mine[p // 2, a], p) for a in (2, 3, 4)]
+        mid = [part(mine[p // 2 - 2, a], p) for a in (2, 3, 4)]
         stack = jnp.concatenate([(red + black)[:8], part(own[p // 2 - 2, 1], p), mid[0], mid[1]], 0)
         sums += exact_dot(stack, one_hot((128, 128), lambda i, j: ((i >> 1) == j - 16 * k + 8) & ((j >> 4) == k)))
         bz_z += exact_dot(mid[2], one_hot((128, 128), lambda i, j: (i == 2 * (j - 16 * k + 8)) & ((j >> 4) == k)))
@@ -361,24 +369,30 @@
                 out[g, 32 * k + 2 * j : 32 * k + 2 * j + 2] = gathered[16 * g + j, k]
 
 
-def coarse_kernel(sweeps, low, own, high, level, fine, out, co, r, b):
+def coarse_kernel(sweeps, low, own, high, level, fine, out, co, r, b, planes):
     shape = (32, 128)
     q0 = even_mask(shape)
     row, lane = iotas(shape)
     r[...] = jnp.zeros_like(r)
     b[...] = jnp.zeros_like(b)
 
+    place_of = lane >> 4
+    for a in range(5):
+        for g in range(2):
+            pieces = []
+            for side in range(2):
+                for s, ref in enumerate((low, own, high)):
+                    block = ref[g + 2 * side, 32 * a : 32 * a + 32]
+                    offset = 4 * side + s
+                    pieces.append((offset, pltpu.roll(block, 16 * offset, 1) if offset else block))
+            for k in range(8):
+                total = jnp.zeros(shape, F32)
+                for offset, piece in pieces:
+                    total = jnp.where(place_of == (k + offset) % 8, piece, total)
+                planes[a, 8 * g + k] = pltpu.roll(total, 128 - 16 * k, 1) if k else total
+
     def plane(a, i):
-        total = jnp.zeros(shape, F32)
-        for side in range(2):
-            x = i + 16 * side
-            for s in range(3):
-                target = 64 * side + 16 * s
-                block = (low, own, high)[s][x // 8, 32 * a : 32 * a + 32]
-                shift = (target - 16 * (x % 8)) % 128
-                moved = pltpu.roll(block, shift, 1) if shift else block
-                total = jnp.where((lane >> 4) == target // 16, moved, total)
-        return total
+        return planes[a, i]
 
     first_bx = plane(2, 0)
     bx0 = first_bx
@@ -469,31 +483,30 @@
     )(x_low, x_high)
     corner_low = shifted(to_high, "gy", 1)
     corner_high = shifted(to_low, "gy", -1)
-    fine, mid_first, mid_last, mid_own = call(
+    fine, mid, mid_first, mid_last, mid_own = call(
         fine_kernel,
-        [(2, 16, 8, 128), (2, 5, 8, 128), (2, 5, 8, 128), (4, 2, 8, 128)],
+        [(2, 16, 8, 128), (4, 5, 8, 128), (2, 5, 8, 128), (2, 5, 8, 128), (4, 2, 8, 128)],
         [(17, 24, 24, 128), (26, 24, 128), (26, 24, 128)],
     )(own, x_low, x_high, y_low, y_high, corner_low, corner_high, beyond_y)
 
-    low, high = shifted(mid_last, "ring", 1), shifted(mid_first, "ring", -1)
-    near, far = call(
-        mid_message_kernel, [(8, 5, 8, 128), (6, 5, 8, 128)]
-    )(low, mid_first, mid_last, high)
+    rows = [shifted(mid, "gy", steps) for steps in (1, -1, 2, -2)]
+    x_low = shifted(mid_last, "ring", 1)
+    x_high = shifted(mid_first, "ring", -1)
+    to_low, to_high = call(mid_corners_kernel, [(6, 5, 8, 128), (6, 5, 8, 128)])(*rows)
+    corner_low = shifted(to_high, "ring", 1)
+    corner_high = shifted(to_low, "ring", -1)
     level, low = call(
         mid_kernel,
         [(2, 8, 8, 128), (rings * count_y, 5, 2, 128)],
         [(17, 16, 24, 128), (18, 24, 128), (18, 24, 128)],
-    )(
-        near, shifted(near, "gy", 1), shifted(near, "gy", -1),
-        shifted(far, "gy", 2), shifted(far, "gy", -2), mid_own,
-    )
+    )(mid, x_low, x_high, *rows, corner_low, corner_high, mid_own)
 
     low = lax.all_to_all(low, ("ring", "gy"), 0, 0, tiled=True)
     (own,) = call(whole_y_kernel, [(rings, 160, 128)])(low)
     (pieces,) = call(
         lambda *refs: coarse_kernel(8, *refs),
         [(RING, 3, 8, 128)],
-        [(17, 8, 32, 128), (10, 32, 128), (10, 32, 128)],
+        [(17, 8, 32, 128), (10, 32, 128), (10, 32, 128), (5, 16, 32, 128)],
     )(shifted(own, "place", 1), own, shifted(own, "place", -1), level, fine)
     pieces = lax.all_to_all(pieces, "place", 0, 0, tiled=True)
     fine_solution, coarse = call(finish_kernel, [rhs.shape, (1, 2, 128)])(pieces)

time: 151 us -> 156 us (1.033)
  starting transfers between devices: 42.4 us -> 46.8 us
  blocking collectives: 70.1 us -> 72 us
    ppermute x15 -> x17, starting transfers between devices: 42.4 us -> 46.8 us  [shifted(): lax.ppermute(values, name, [(i, i + steps) for i in range(lead, last)])]
    all_to_all x1, blocking collectives: 26.8 us -> 28.7 us  [cycle(): low = lax.all_to_all(low, ('ring', 'gy'), 0, 0, tiled=True)]
    ppermute x15 -> x17, waiting for transfers between devices: 21.2 us -> 20.3 us  [shifted(): lax.ppermute(values, name, [(i, i + steps) for i in range(lead, last)])]
  transfers between devices with their start and end apart: 15 -> 17, of which waited for: 8 -> 8; matrix products, arithmetic and copies ran while one was open for 0% -> 0% of each run, Pallas kernels for 0% -> 0%
where the time goes in v6:
time: 156 us; the launch traced here: 153 us
  blocking collectives  72 us (46%)
  starting transfers between devices  46.8 us (30%)
  waiting for transfers between devices  20.3 us (13%)
  Pallas kernels  13.4 us (9%)
    ppermute x17, starting transfers between devices, shifted(): lax.ppermute(values, name, [(i, i + steps) for i in range(lead, last)])  46.8 us
    all_to_all x1, blocking collectives, cycle(): own = lax.all_to_all(own, 'place', 0, 0, tiled=True)  30.1 us
    all_to_all x1, blocking collectives, cycle(): low = lax.all_to_all(low, ('ring', 'gy'), 0, 0, tiled=True)  28.7 us
    ppermute x17, waiting for transfers between devices, shifted(): lax.ppermute(values, name, [(i, i + steps) for i in range(lead, last)])  20.3 us
    pallas_call x9, Pallas kernels, run(): pl.pallas_call(kernel, out_shape=[jax.ShapeDtypeStruct(s, F32) for s in o...  13.4 us
    all_to_all x1, blocking collectives, cycle(): pieces = lax.all_to_all(pieces, 'place', 0, 0, tiled=True)  13.2 us
  transfers between devices with their start and end apart: 17, of which 8 were waited for; matrix products, arithmetic and copies ran while one was open for 0% of the time, Pallas kernels for 0%

profile of v6, /device:TPU:1, one launch (start us, length us, event | category | flops | bytes accessed | tf_op | source)
XLA Modules:
  0.0 153.4 jit_solution(14497628529978983277)
XLA Ops:
  0.6 2.3 %shard_map.68 = f32[8,5,4,8,128]{4,3,2,1,0:T(8,128)} custom-call(f32[4,8,512]{2,1,0:T(8,128)} %refs_0_.1, f32[4,8,512]{2,1,0:T(8,128)} %refs_1_.1, f32[4,8,512]{2,1,0:T(8,128)} %refs_2_.1, f32[4,8,512]{2,1,0:T(8,128)} %refs_3_.1, f32[4,8,512]{2,1,0:T(8,128)} %refs_4_.1), custom_call_target="tpu_custom_call" | custom-call | tf_op jit(solution)/shard_map/pallas_call | solution.py:28
  2.9 30.1 %all_to_all.15.own = f32[8,5,4,8,128]{4,3,2,1,0:T(8,128)S(1)} all-to-all(f32[8,5,4,8,128]{4,3,2,1,0:T(8,128)} %shard_map.68), channel_id=1, replica_groups=mesh['ring'=4,'place'=8,'gy'=16] {'place'}, dimensions={0} | all-to-all | bytes 1310720 | tf_op jit(solution)/shard_map/all_to_all | solution.py:474
  33.0 3.9 %collective-permute-start.3 = (f32[8,5,4,8,128]{4,3,2,1,0:T(8,128)S(1)}, f32[8,5,4,8,128]{4,3,2,1,0:T(8,128)S(1)}, u32[]{:S(2)}, u32[]{:S(2)}) collective-permute-start(f32[8,5,4,8,128]{4,3,2,1,0:T(8,128)S(1)} %all_to_all.15.own), channel_id=1, source_target_pairs={{1,0},{2,1},{3,2},{4,3},{5,4},{6,5},{7,6},{8,7},{9,8},{10,9},{11,1... | collective-permute-start | bytes 1966088 | tf_op jit(solution)/shard_map/ppermute | solution.py:20
  36.9 3.1 %collective-permute-start.2 = (f32[8,5,4,8,128]{4,3,2,1,0:T(8,128)S(1)}, f32[8,5,4,8,128]{4,3,2,1,0:T(8,128)S(1)}, u32[]{:S(2)}, u32[]{:S(2)}) collective-permute-start(f32[8,5,4,8,128]{4,3,2,1,0:T(8,128)S(1)} %all_to_all.15.own), channel_id=1, source_target_pairs={{0,1},{1,2},{2,3},{3,4},{4,5},{5,6},{6,7},{7,8},{8,9},{9,10},{10,1... | collective-permute-start | bytes 1966088 | tf_op jit(solution)/shard_map/ppermute | solution.py:20
  40.1 1.3 collective-permute-start.1
  41.4 4.0 %collective-permute-start = (f32[40,8,128]{2,1,0:T(8,128)S(1)}, f32[40,8,128]{2,1,0:T(8,128)S(1)}, u32[]{:S(2)}, u32[]{:S(2)}) collective-permute-start(f32[40,8,128]{2,1,0:T(8,128)S(1)} %get-tuple-element.16), channel_id=1, source_target_pairs={{0,128},{128,256},{256,384},{1,129},{129,257},{257,385},{2,130},{1... | collective-permute-start | bytes 491528 | tf_op jit(solution)/shard_map/ppermute | solution.py:20
  45.4 3.9 %collective-permute-done.low.x_low = f32[40,8,128]{2,1,0:T(8,128)S(1)} collective-permute-done((f32[40,8,128]{2,1,0:T(8,128)S(1)}, f32[40,8,128]{2,1,0:T(8,128)S(1)}, u32[]{:S(2)}, u32[]{:S(2)}) %collective-permute-start) | collective-permute-done | bytes 163872 | tf_op jit(solution)/shard_map/ppermute | solution.py:20
  49.3 0.0 collective-permute-done.1.high.x_high
  49.3 3.6 %collective-permute-start.4 = (f32[60,8,128]{2,1,0:T(8,128)S(1)}, f32[60,8,128]{2,1,0:T(8,128)S(1)}, u32[]{:S(2)}, u32[]{:S(2)}) collective-permute-start(f32[60,8,128]{2,1,0:T(8,128)S(1)} %get-tuple-element.18), channel_id=1, source_target_pairs={{0,1},{1,2},{2,3},{3,4},{4,5},{5,6},{6,7},{7,8},{8,9},{9,10},{10,1... | collective-permute-start | bytes 737288 | tf_op jit(solution)/shard_map/ppermute | solution.py:20
  52.9 1.9 %collective-permute-start.5 = (f32[60,8,128]{2,1,0:T(8,128)S(1)}, f32[60,8,128]{2,1,0:T(8,128)S(1)}, u32[]{:S(2)}, u32[]{:S(2)}) collective-permute-start(f32[60,8,128]{2,1,0:T(8,128)S(1)} %get-tuple-element.19), channel_id=1, source_target_pairs={{1,0},{2,1},{3,2},{4,3},{5,4},{6,5},{7,6},{8,7},{9,8},{10,9},{11,1... | collective-permute-start | bytes 737288 | tf_op jit(solution)/shard_map/ppermute | solution.py:20
  54.8 1.3 collective-permute-start.6
  56.1 3.4 %collective-permute-done.6.beyond_y = f32[32,128]{1,0:T(8,128)S(1)} collective-permute-done((f32[32,128]{1,0:T(8,128)S(1)}, f32[32,128]{1,0:T(8,128)S(1)}, u32[]{:S(2)}, u32[]{:S(2)}) %collective-permute-start.6) | collective-permute-done | bytes 16416 | tf_op jit(solution)/shard_map/ppermute | solution.py:20
  59.5 0.0 collective-permute-done.4.corner_low
  59.5 1.1 collective-permute-done.5.corner_high
  60.6 0.0 collective-permute-done.3.y_high
  60.6 0.0 collective-permute-done.2.y_low
  60.6 3.8 %shard_map.71 = (f32[2,16,8,128]{3,2,1,0:T(8,128)S(1)}, f32[4,5,8,128]{3,2,1,0:T(8,128)S(1)}, f32[2,5,8,128]{3,2,1,0:T(8,128)S(1)}, f32[2,5,8,128]{3,2,1,0:T(8,128)S(1)}, f32[4,2,8,128]{3,2,1,0:T(8,128)S(1)}) custom-call(f32[8,5,4,8,128]{4,3,2,1,0:T(8,128)S(1)} %all_to_all.15.own, f32[40,8,128]{2,1,0:T(8,128)S(1)} %collective-permute-done.low.x_low, ...), custom_call_target="tpu_custom_call" | custom-call | tf_op jit(solution)/shard_map/pallas_call | solution.py:28
  64.4 1.3 collective-permute-start.12
  65.7 4.0 %collective-permute-start.11 = (f32[4,5,8,128]{3,2,1,0:T(8,128)S(1)}, f32[4,5,8,128]{3,2,1,0:T(8,128)S(1)}, u32[]{:S(2)}, u32[]{:S(2)}) collective-permute-start(f32[4,5,8,128]{3,2,1,0:T(8,128)S(1)} %get-tuple-element.21.mine), channel_id=1, source_target_pairs={{0,2},{1,3},{2,4},{3,5},{4,6},{5,7},{6,8},{7,9},{8,10},{9,11},{10,... | collective-permute-start | bytes 245768 | tf_op jit(solution)/shard_map/ppermute | solution.py:20
  69.7 3.4 %collective-permute-start.10 = (f32[4,5,8,128]{3,2,1,0:T(8,128)S(1)}, f32[4,5,8,128]{3,2,1,0:T(8,128)S(1)}, u32[]{:S(2)}, u32[]{:S(2)}) collective-permute-start(f32[4,5,8,128]{3,2,1,0:T(8,128)S(1)} %get-tuple-element.21.mine), channel_id=1, source_target_pairs={{1,0},{2,1},{3,2},{4,3},{5,4},{6,5},{7,6},{8,7},{9,8},{10,9},{11,1... | collective-permute-start | bytes 245768 | tf_op jit(solution)/shard_map/ppermute | solution.py:20
  73.0 3.1 %collective-permute-start.9 = (f32[4,5,8,128]{3,2,1,0:T(8,128)S(1)}, f32[4,5,8,128]{3,2,1,0:T(8,128)S(1)}, u32[]{:S(2)}, u32[]{:S(2)}) collective-permute-start(f32[4,5,8,128]{3,2,1,0:T(8,128)S(1)} %get-tuple-element.21.mine), channel_id=1, source_target_pairs={{0,1},{1,2},{2,3},{3,4},{4,5},{5,6},{6,7},{7,8},{8,9},{9,10},{10,1... | collective-permute-start | bytes 245768 | tf_op jit(solution)/shard_map/ppermute | solution.py:20
  76.2 0.0 collective-permute-done.12.high2
  76.2 0.0 collective-permute-done.11.low2
  76.2 0.2 collective-permute-done.10.high1
  76.3 1.3 collective-permute-done.9.low1
  77.6 4.1 %collective-permute-start.13 = (f32[6,5,8,128]{3,2,1,0:T(8,128)S(1)}, f32[6,5,8,128]{3,2,1,0:T(8,128)S(1)}, u32[]{:S(2)}, u32[]{:S(2)}) collective-permute-start(f32[6,5,8,128]{3,2,1,0:T(8,128)S(1)} %get-tuple-element.24), channel_id=1, source_target_pairs={{0,128},{128,256},{256,384},{1,129},{129,257},{257,385},{2,130},{1... | collective-permute-start | bytes 368648 | tf_op jit(solution)/shard_map/ppermute | solution.py:20
  81.7 1.3 collective-permute-start.14
  83.0 4.0 %collective-permute-start.7 = (f32[2,5,8,128]{3,2,1,0:T(8,128)S(1)}, f32[2,5,8,128]{3,2,1,0:T(8,128)S(1)}, u32[]{:S(2)}, u32[]{:S(2)}) collective-permute-start(f32[2,5,8,128]{3,2,1,0:T(8,128)S(1)} %get-tuple-element.22), channel_id=1, source_target_pairs={{0,128},{128,256},{256,384},{1,129},{129,257},{257,385},{2,130},{1... | collective-permute-start | bytes 122888 | tf_op jit(solution)/shard_map/ppermute | solution.py:20
  87.0 1.3 collective-permute-start.8
  88.3 0.0 collective-permute-done.7.x_low
  88.3 4.1 %collective-permute-done.8.x_high = f32[2,5,8,128]{3,2,1,0:T(8,128)S(1)} collective-permute-done((f32[2,5,8,128]{3,2,1,0:T(8,128)S(1)}, f32[2,5,8,128]{3,2,1,0:T(8,128)S(1)}, u32[]{:S(2)}, u32[]{:S(2)}) %collective-permute-start.8) | collective-permute-done | bytes 40992 | tf_op jit(solution)/shard_map/ppermute | solution.py:20
  92.5 0.0 collective-permute-done.13.corner_low
  92.5 0.0 collective-permute-done.14.corner_high
  92.5 2.1 %shard_map.73 = (f32[2,8,8,128]{3,2,1,0:T(8,128)S(1)}, f32[64,5,2,128]{3,2,1,0:T(2,128)S(1)}) custom-call(f32[4,5,8,128]{3,2,1,0:T(8,128)S(1)} %get-tuple-element.21.mine, f32[2,5,8,128]{3,2,1,0:T(8,128)S(1)} %collective-permute-done.7.x_low, f32[2,5,8,128]{3,2,1,0:T(8,128)S(1)} %collective-permute-done.8.x_high, ...), custom_call_target="tpu_custom_call" | custom-call | tf_op jit(solution)/shard_map/pallas_call | solution.py:28
  94.5 28.7 %all_to_all.16.gathered = f32[64,5,2,128]{3,2,1,0:T(2,128)S(1)} all-to-all(f32[64,5,2,128]{3,2,1,0:T(2,128)S(1)} %get-tuple-element.27), channel_id=1, replica_groups=mesh['ring'=4,'place'=8,'gy'=16] {'ring','gy'}, dimensions={0} | all-to-all | bytes 655360 | tf_op jit(solution)/shard_map/all_to_all | solution.py:504
  123.3 0.1 shard_map.74.refs_1_
  123.4 1.3 collective-permute-start.16
  124.7 4.0 %collective-permute-start.15 = (f32[4,160,128]{2,1,0:T(8,128)S(1)}, f32[4,160,128]{2,1,0:T(8,128)S(1)}, u32[]{:S(2)}, u32[]{:S(2)}) collective-permute-start(f32[4,160,128]{2,1,0:T(8,128)S(1)} %shard_map.74.refs_1_), channel_id=1, source_target_pairs={{0,16},{16,32},{32,48},{48,64},{64,80},{80,96},{96,112},{1,17},{17... | collective-permute-start | bytes 983048 | tf_op jit(solution)/shard_map/ppermute | solution.py:20
  128.7 5.4 %collective-permute-done.16.refs_2_ = f32[4,160,128]{2,1,0:T(8,128)S(1)} collective-permute-done((f32[4,160,128]{2,1,0:T(8,128)S(1)}, f32[4,160,128]{2,1,0:T(8,128)S(1)}, u32[]{:S(2)}, u32[]{:S(2)}) %collective-permute-start.16) | collective-permute-done | bytes 327712 | tf_op jit(solution)/shard_map/ppermute | solution.py:20
  134.2 0.9 collective-permute-done.15.refs_0_
  135.1 4.4 %shard_map.75 = f32[8,3,8,128]{3,2,1,0:T(8,128)S(1)} custom-call(f32[4,160,128]{2,1,0:T(8,128)S(1)} %collective-permute-done.15.refs_0_, f32[4,160,128]{2,1,0:T(8,128)S(1)} %shard_map.74.refs_1_, f32[4,160,128]{2,1,0:T(8,128)S(1)} %collective-permute-done.16.refs_2_, f32[2,8,8,128]{3,2,1,0:T(8,128)S(1)} %get-tuple-element.28.refs_3_, ...), custom_call_target="tpu_custom_call" | custom-call | tf_op jit(solution)/shard_map/pallas_call | solution.py:28
  139.5 13.2 %all_to_all.17.pieces = f32[8,3,8,128]{3,2,1,0:T(8,128)S(1)} all-to-all(f32[8,3,8,128]{3,2,1,0:T(8,128)S(1)} %shard_map.75), channel_id=1, replica_groups=mesh['ring'=4,'place'=8,'gy'=16] {'place'}, dimensions={0} | all-to-all | bytes 196608 | tf_op jit(solution)/shard_map/all_to_all | solution.py:511
  152.7 0.7 shard_map.76
  (3 shorter events, 0.1 us)
Async XLA Ops:
  33.0 27.7 %collective-permute-start.3 = (f32[8,5,4,8,128]{4,3,2,1,0:T(8,128)S(1)}, f32[8,5,4,8,128]{4,3,2,1,0:T(8,128)S(1)}, u32[]{:S(2)}, u32[]{:S(2)}) collective-permute-start(f32[8,5,4,8,128]{4,3,2,1,0:T(8,128)S(1)} %all_to_all.15.own), channel_id=1, source_target_pairs={{1,0},{2,1},{3,2},{4,3},{5,4},{6,5},{7,6},{8,7},{9,8},{10,9},{11,1... | collective-permute-start | bytes 1966088 | tf_op jit(solution)/shard_map/ppermute | solution.py:20
  36.9 23.7 %collective-permute-start.2 = (f32[8,5,4,8,128]{4,3,2,1,0:T(8,128)S(1)}, f32[8,5,4,8,128]{4,3,2,1,0:T(8,128)S(1)}, u32[]{:S(2)}, u32[]{:S(2)}) collective-permute-start(f32[8,5,4,8,128]{4,3,2,1,0:T(8,128)S(1)} %all_to_all.15.own), channel_id=1, source_target_pairs={{0,1},{1,2},{2,3},{3,4},{4,5},{5,6},{6,7},{7,8},{8,9},{9,10},{10,1... | collective-permute-start | bytes 1966088 | tf_op jit(solution)/shard_map/ppermute | solution.py:20
  40.1 9.2 %collective-permute-start.1 = (f32[41,8,128]{2,1,0:T(8,128)S(1)}, f32[41,8,128]{2,1,0:T(8,128)S(1)}, u32[]{:S(2)}, u32[]{:S(2)}) collective-permute-start(f32[41,8,128]{2,1,0:T(8,128)S(1)} %get-tuple-element.17), channel_id=1, source_target_pairs={{128,0},{256,128},{384,256},{129,1},{257,129},{385,257},{130,2},{2... | collective-permute-start | bytes 503816 | tf_op jit(solution)/shard_map/ppermute | solution.py:20
  41.4 7.9 %collective-permute-start = (f32[40,8,128]{2,1,0:T(8,128)S(1)}, f32[40,8,128]{2,1,0:T(8,128)S(1)}, u32[]{:S(2)}, u32[]{:S(2)}) collective-permute-start(f32[40,8,128]{2,1,0:T(8,128)S(1)} %get-tuple-element.16), channel_id=1, source_target_pairs={{0,128},{128,256},{256,384},{1,129},{129,257},{257,385},{2,130},{1... | collective-permute-start | bytes 491528 | tf_op jit(solution)/shard_map/ppermute | solution.py:20
  49.3 10.2 %collective-permute-start.4 = (f32[60,8,128]{2,1,0:T(8,128)S(1)}, f32[60,8,128]{2,1,0:T(8,128)S(1)}, u32[]{:S(2)}, u32[]{:S(2)}) collective-permute-start(f32[60,8,128]{2,1,0:T(8,128)S(1)} %get-tuple-element.18), channel_id=1, source_target_pairs={{0,1},{1,2},{2,3},{3,4},{4,5},{5,6},{6,7},{7,8},{8,9},{9,10},{10,1... | collective-permute-start | bytes 737288 | tf_op jit(solution)/shard_map/ppermute | solution.py:20
  52.9 7.7 %collective-permute-start.5 = (f32[60,8,128]{2,1,0:T(8,128)S(1)}, f32[60,8,128]{2,1,0:T(8,128)S(1)}, u32[]{:S(2)}, u32[]{:S(2)}) collective-permute-start(f32[60,8,128]{2,1,0:T(8,128)S(1)} %get-tuple-element.19), channel_id=1, source_target_pairs={{1,0},{2,1},{3,2},{4,3},{5,4},{6,5},{7,6},{8,7},{9,8},{10,9},{11,1... | collective-permute-start | bytes 737288 | tf_op jit(solution)/shard_map/ppermute | solution.py:20
  54.8 4.7 %collective-permute-start.6 = (f32[32,128]{1,0:T(8,128)S(1)}, f32[32,128]{1,0:T(8,128)S(1)}, u32[]{:S(2)}, u32[]{:S(2)}) collective-permute-start(f32[32,128]{1,0:T(8,128)S(1)} %get-tuple-element.20), channel_id=1, source_target_pairs={{2,0},{3,1},{4,2},{5,3},{6,4},{7,5},{8,6},{9,7},{10,8},{11,9},{12,... | collective-permute-start | bytes 49160 | tf_op jit(solution)/shard_map/ppermute | solution.py:20
  64.4 11.8 %collective-permute-start.12 = (f32[4,5,8,128]{3,2,1,0:T(8,128)S(1)}, f32[4,5,8,128]{3,2,1,0:T(8,128)S(1)}, u32[]{:S(2)}, u32[]{:S(2)}) collective-permute-start(f32[4,5,8,128]{3,2,1,0:T(8,128)S(1)} %get-tuple-element.21.mine), channel_id=1, source_target_pairs={{2,0},{3,1},{4,2},{5,3},{6,4},{7,5},{8,6},{9,7},{10,8},{11,9},{12,... | collective-permute-start | bytes 245768 | tf_op jit(solution)/shard_map/ppermute | solution.py:20
  65.7 10.5 %collective-permute-start.11 = (f32[4,5,8,128]{3,2,1,0:T(8,128)S(1)}, f32[4,5,8,128]{3,2,1,0:T(8,128)S(1)}, u32[]{:S(2)}, u32[]{:S(2)}) collective-permute-start(f32[4,5,8,128]{3,2,1,0:T(8,128)S(1)} %get-tuple-element.21.mine), channel_id=1, source_target_pairs={{0,2},{1,3},{2,4},{3,5},{4,6},{5,7},{6,8},{7,9},{8,10},{9,11},{10,... | collective-permute-start | bytes 245768 | tf_op jit(solution)/shard_map/ppermute | solution.py:20
  69.7 6.7 %collective-permute-start.10 = (f32[4,5,8,128]{3,2,1,0:T(8,128)S(1)}, f32[4,5,8,128]{3,2,1,0:T(8,128)S(1)}, u32[]{:S(2)}, u32[]{:S(2)}) collective-permute-start(f32[4,5,8,128]{3,2,1,0:T(8,128)S(1)} %get-tuple-element.21.mine), channel_id=1, source_target_pairs={{1,0},{2,1},{3,2},{4,3},{5,4},{6,5},{7,6},{8,7},{9,8},{10,9},{11,1... | collective-permute-start | bytes 245768 | tf_op jit(solution)/shard_map/ppermute | solution.py:20
  73.0 4.6 %collective-permute-start.9 = (f32[4,5,8,128]{3,2,1,0:T(8,128)S(1)}, f32[4,5,8,128]{3,2,1,0:T(8,128)S(1)}, u32[]{:S(2)}, u32[]{:S(2)}) collective-permute-start(f32[4,5,8,128]{3,2,1,0:T(8,128)S(1)} %get-tuple-element.21.mine), channel_id=1, source_target_pairs={{0,1},{1,2},{2,3},{3,4},{4,5},{5,6},{6,7},{7,8},{8,9},{9,10},{10,1... | collective-permute-start | bytes 245768 | tf_op jit(solution)/shard_map/ppermute | solution.py:20
  77.6 14.8 %collective-permute-start.13 = (f32[6,5,8,128]{3,2,1,0:T(8,128)S(1)}, f32[6,5,8,128]{3,2,1,0:T(8,128)S(1)}, u32[]{:S(2)}, u32[]{:S(2)}) collective-permute-start(f32[6,5,8,128]{3,2,1,0:T(8,128)S(1)} %get-tuple-element.24), channel_id=1, source_target_pairs={{0,128},{128,256},{256,384},{1,129},{129,257},{257,385},{2,130},{1... | collective-permute-start | bytes 368648 | tf_op jit(solution)/shard_map/ppermute | solution.py:20
  81.7 10.7 %collective-permute-start.14 = (f32[6,5,8,128]{3,2,1,0:T(8,128)S(1)}, f32[6,5,8,128]{3,2,1,0:T(8,128)S(1)}, u32[]{:S(2)}, u32[]{:S(2)}) collective-permute-start(f32[6,5,8,128]{3,2,1,0:T(8,128)S(1)} %get-tuple-element.25), channel_id=1, source_target_pairs={{128,0},{256,128},{384,256},{129,1},{257,129},{385,257},{130,2},{2... | collective-permute-start | bytes 368648 | tf_op jit(solution)/shard_map/ppermute | solution.py:20
  83.0 5.3 %collective-permute-start.7 = (f32[2,5,8,128]{3,2,1,0:T(8,128)S(1)}, f32[2,5,8,128]{3,2,1,0:T(8,128)S(1)}, u32[]{:S(2)}, u32[]{:S(2)}) collective-permute-start(f32[2,5,8,128]{3,2,1,0:T(8,128)S(1)} %get-tuple-element.22), channel_id=1, source_target_pairs={{0,128},{128,256},{256,384},{1,129},{129,257},{257,385},{2,130},{1... | collective-permute-start | bytes 122888 | tf_op jit(solution)/shard_map/ppermute | solution.py:20
  87.0 5.4 %collective-permute-start.8 = (f32[2,5,8,128]{3,2,1,0:T(8,128)S(1)}, f32[2,5,8,128]{3,2,1,0:T(8,128)S(1)}, u32[]{:S(2)}, u32[]{:S(2)}) collective-permute-start(f32[2,5,8,128]{3,2,1,0:T(8,128)S(1)} %get-tuple-element.23), channel_id=1, source_target_pairs={{128,0},{256,128},{384,256},{129,1},{257,129},{385,257},{130,2},{2... | collective-permute-start | bytes 122888 | tf_op jit(solution)/shard_map/ppermute | solution.py:20
  123.4 10.8 %collective-permute-start.16 = (f32[4,160,128]{2,1,0:T(8,128)S(1)}, f32[4,160,128]{2,1,0:T(8,128)S(1)}, u32[]{:S(2)}, u32[]{:S(2)}) collective-permute-start(f32[4,160,128]{2,1,0:T(8,128)S(1)} %shard_map.74.refs_1_), channel_id=1, source_target_pairs={{16,0},{32,16},{48,32},{64,48},{80,64},{96,80},{112,96},{17,1},{33... | collective-permute-start | bytes 983048 | tf_op jit(solution)/shard_map/ppermute | solution.py:20
  124.7 10.4 %collective-permute-start.15 = (f32[4,160,128]{2,1,0:T(8,128)S(1)}, f32[4,160,128]{2,1,0:T(8,128)S(1)}, u32[]{:S(2)}, u32[]{:S(2)}) collective-permute-start(f32[4,160,128]{2,1,0:T(8,128)S(1)} %shard_map.74.refs_1_), channel_id=1, source_target_pairs={{0,16},{16,32},{32,48},{48,64},{64,80},{80,96},{96,112},{1,17},{17... | collective-permute-start | bytes 983048 | tf_op jit(solution)/shard_map/ppermute | solution.py:20

commit v7 on v5

--- a/solution.py
+++ b/solution.py
@@ -361,24 +361,30 @@
                 out[g, 32 * k + 2 * j : 32 * k + 2 * j + 2] = gathered[16 * g + j, k]
 
 
-def coarse_kernel(sweeps, low, own, high, level, fine, out, co, r, b):
+def coarse_kernel(sweeps, low, own, high, level, fine, out, co, r, b, planes):
     shape = (32, 128)
     q0 = even_mask(shape)
     row, lane = iotas(shape)
     r[...] = jnp.zeros_like(r)
     b[...] = jnp.zeros_like(b)
 
+    place_of = lane >> 4
+    for a in range(5):
+        for g in range(2):
+            pieces = []
+            for side in range(2):
+                for s, ref in enumerate((low, own, high)):
+                    block = ref[g + 2 * side, 32 * a : 32 * a + 32]
+                    offset = 4 * side + s
+                    pieces.append((offset, pltpu.roll(block, 16 * offset, 1) if offset else block))
+            for k in range(8):
+                total = jnp.zeros(shape, F32)
+                for offset, piece in pieces:
+                    total = jnp.where(place_of == (k + offset) % 8, piece, total)
+                planes[a, 8 * g + k] = pltpu.roll(total, 128 - 16 * k, 1) if k else total
+
     def plane(a, i):
-        total = jnp.zeros(shape, F32)
-        for side in range(2):
-            x = i + 16 * side
-            for s in range(3):
-                target = 64 * side + 16 * s
-                block = (low, own, high)[s][x // 8, 32 * a : 32 * a + 32]
-                shift = (target - 16 * (x % 8)) % 128
-                moved = pltpu.roll(block, shift, 1) if shift else block
-                total = jnp.where((lane >> 4) == target // 16, moved, total)
-        return total
+        return planes[a, i]
 
     first_bx = plane(2, 0)
     bx0 = first_bx
@@ -493,7 +499,7 @@
     (pieces,) = call(
         lambda *refs: coarse_kernel(8, *refs),
         [(RING, 3, 8, 128)],
-        [(17, 8, 32, 128), (10, 32, 128), (10, 32, 128)],
+        [(17, 8, 32, 128), (10, 32, 128), (10, 32, 128), (5, 16, 32, 128)],
     )(shifted(own, "place", 1), own, shifted(own, "place", -1), level, fine)
     pieces = lax.all_to_all(pieces, "place", 0, 0, tiled=True)
     fine_solution, coarse = call(finish_kernel, [rhs.shape, (1, 2, 128)])(pieces)

time: 151 us -> 150 us (level)
  no operation moved by 1% of the time
where the time goes in v7:
time: 150 us; the launch traced here: 148 us
  blocking collectives  70.1 us (47%)
  starting transfers between devices  42.4 us (28%)
  waiting for transfers between devices  21.2 us (14%)
  Pallas kernels  13.4 us (9%)
    ppermute x15, starting transfers between devices, shifted(): lax.ppermute(values, name, [(i, i + steps) for i in range(lead, last)])  42.4 us
    all_to_all x1, blocking collectives, cycle(): own = lax.all_to_all(own, 'place', 0, 0, tiled=True)  30.1 us
    all_to_all x1, blocking collectives, cycle(): low = lax.all_to_all(low, ('ring', 'gy'), 0, 0, tiled=True)  26.8 us
    ppermute x15, waiting for transfers between devices, shifted(): lax.ppermute(values, name, [(i, i + steps) for i in range(lead, last)])  21.2 us
    pallas_call x9, Pallas kernels, run(): pl.pallas_call(kernel, out_shape=[jax.ShapeDtypeStruct(s, F32) for s in o...  13.4 us
    all_to_all x1, blocking collectives, cycle(): pieces = lax.all_to_all(pieces, 'place', 0, 0, tiled=True)  13.2 us
  transfers between devices with their start and end apart: 15, of which 8 were waited for; matrix products, arithmetic and copies ran while one was open for 0% of the time, Pallas kernels for 0%

profile of v7, /device:TPU:1, one launch (start us, length us, event | category | flops | bytes accessed | tf_op | source)
XLA Modules:
  0.0 147.9 jit_solution(3693165237984941216)
XLA Ops:
  0.6 2.2 %shard_map.68 = f32[8,5,4,8,128]{4,3,2,1,0:T(8,128)} custom-call(f32[4,8,512]{2,1,0:T(8,128)} %refs_0_.1, f32[4,8,512]{2,1,0:T(8,128)} %refs_1_.1, f32[4,8,512]{2,1,0:T(8,128)} %refs_2_.1, f32[4,8,512]{2,1,0:T(8,128)} %refs_3_.1, f32[4,8,512]{2,1,0:T(8,128)} %refs_4_.1), custom_call_target="tpu_custom_call" | custom-call | tf_op jit(solution)/shard_map/pallas_call | solution.py:28
  2.9 30.1 %all_to_all.15.own = f32[8,5,4,8,128]{4,3,2,1,0:T(8,128)S(1)} all-to-all(f32[8,5,4,8,128]{4,3,2,1,0:T(8,128)} %shard_map.68), channel_id=1, replica_groups=mesh['ring'=4,'place'=8,'gy'=16] {'place'}, dimensions={0} | all-to-all | bytes 1310720 | tf_op jit(solution)/shard_map/all_to_all | solution.py:466
  33.0 3.9 %collective-permute-start.3 = (f32[8,5,4,8,128]{4,3,2,1,0:T(8,128)S(1)}, f32[8,5,4,8,128]{4,3,2,1,0:T(8,128)S(1)}, u32[]{:S(2)}, u32[]{:S(2)}) collective-permute-start(f32[8,5,4,8,128]{4,3,2,1,0:T(8,128)S(1)} %all_to_all.15.own), channel_id=1, source_target_pairs={{1,0},{2,1},{3,2},{4,3},{5,4},{6,5},{7,6},{8,7},{9,8},{10,9},{11,1... | collective-permute-start | bytes 1966088 | tf_op jit(solution)/shard_map/ppermute | solution.py:20
  36.9 3.1 %collective-permute-start.2 = (f32[8,5,4,8,128]{4,3,2,1,0:T(8,128)S(1)}, f32[8,5,4,8,128]{4,3,2,1,0:T(8,128)S(1)}, u32[]{:S(2)}, u32[]{:S(2)}) collective-permute-start(f32[8,5,4,8,128]{4,3,2,1,0:T(8,128)S(1)} %all_to_all.15.own), channel_id=1, source_target_pairs={{0,1},{1,2},{2,3},{3,4},{4,5},{5,6},{6,7},{7,8},{8,9},{9,10},{10,1... | collective-permute-start | bytes 1966088 | tf_op jit(solution)/shard_map/ppermute | solution.py:20
  40.1 1.3 collective-permute-start.1
  41.4 4.0 %collective-permute-start = (f32[40,8,128]{2,1,0:T(8,128)S(1)}, f32[40,8,128]{2,1,0:T(8,128)S(1)}, u32[]{:S(2)}, u32[]{:S(2)}) collective-permute-start(f32[40,8,128]{2,1,0:T(8,128)S(1)} %get-tuple-element.15), channel_id=1, source_target_pairs={{0,128},{128,256},{256,384},{1,129},{129,257},{257,385},{2,130},{1... | collective-permute-start | bytes 491528 | tf_op jit(solution)/shard_map/ppermute | solution.py:20
  45.4 3.9 %collective-permute-done.low.x_low = f32[40,8,128]{2,1,0:T(8,128)S(1)} collective-permute-done((f32[40,8,128]{2,1,0:T(8,128)S(1)}, f32[40,8,128]{2,1,0:T(8,128)S(1)}, u32[]{:S(2)}, u32[]{:S(2)}) %collective-permute-start) | collective-permute-done | bytes 163872 | tf_op jit(solution)/shard_map/ppermute | solution.py:20
  49.3 0.0 collective-permute-done.1.high.x_high
  49.3 3.6 %collective-permute-start.4 = (f32[60,8,128]{2,1,0:T(8,128)S(1)}, f32[60,8,128]{2,1,0:T(8,128)S(1)}, u32[]{:S(2)}, u32[]{:S(2)}) collective-permute-start(f32[60,8,128]{2,1,0:T(8,128)S(1)} %get-tuple-element.17), channel_id=1, source_target_pairs={{0,1},{1,2},{2,3},{3,4},{4,5},{5,6},{6,7},{7,8},{8,9},{9,10},{10,1... | collective-permute-start | bytes 737288 | tf_op jit(solution)/shard_map/ppermute | solution.py:20
  52.9 1.9 %collective-permute-start.5 = (f32[60,8,128]{2,1,0:T(8,128)S(1)}, f32[60,8,128]{2,1,0:T(8,128)S(1)}, u32[]{:S(2)}, u32[]{:S(2)}) collective-permute-start(f32[60,8,128]{2,1,0:T(8,128)S(1)} %get-tuple-element.18), channel_id=1, source_target_pairs={{1,0},{2,1},{3,2},{4,3},{5,4},{6,5},{7,6},{8,7},{9,8},{10,9},{11,1... | collective-permute-start | bytes 737288 | tf_op jit(solution)/shard_map/ppermute | solution.py:20
  54.8 1.3 collective-permute-start.6
  56.1 3.4 %collective-permute-done.6.beyond_y = f32[32,128]{1,0:T(8,128)S(1)} collective-permute-done((f32[32,128]{1,0:T(8,128)S(1)}, f32[32,128]{1,0:T(8,128)S(1)}, u32[]{:S(2)}, u32[]{:S(2)}) %collective-permute-start.6) | collective-permute-done | bytes 16416 | tf_op jit(solution)/shard_map/ppermute | solution.py:20
  59.5 0.0 collective-permute-done.4.corner_low
  59.5 1.1 collective-permute-done.5.corner_high
  60.6 0.0 collective-permute-done.3.y_high
  60.6 0.0 collective-permute-done.2.y_low
  60.6 3.8 %shard_map.71 = (f32[2,16,8,128]{3,2,1,0:T(8,128)S(1)}, f32[2,5,8,128]{3,2,1,0:T(8,128)S(1)}, f32[2,5,8,128]{3,2,1,0:T(8,128)S(1)}, f32[4,2,8,128]{3,2,1,0:T(8,128)S(1)}) custom-call(f32[8,5,4,8,128]{4,3,2,1,0:T(8,128)S(1)} %all_to_all.15.own, f32[40,8,128]{2,1,0:T(8,128)S(1)} %collective-permute-done.low.x_low, ...), custom_call_target="tpu_custom_call" | custom-call | tf_op jit(solution)/shard_map/pallas_call | solution.py:28
  64.4 4.1 %collective-permute-start.7 = (f32[2,5,8,128]{3,2,1,0:T(8,128)S(1)}, f32[2,5,8,128]{3,2,1,0:T(8,128)S(1)}, u32[]{:S(2)}, u32[]{:S(2)}) collective-permute-start(f32[2,5,8,128]{3,2,1,0:T(8,128)S(1)} %get-tuple-element.20.last), channel_id=1, source_target_pairs={{0,128},{128,256},{256,384},{1,129},{129,257},{257,385},{2,130},{1... | collective-permute-start | bytes 122888 | tf_op jit(solution)/shard_map/ppermute | solution.py:20
  68.5 1.3 collective-permute-start.8
  69.8 0.0 collective-permute-done.7.low
  69.8 3.4 %collective-permute-done.8.high = f32[2,5,8,128]{3,2,1,0:T(8,128)S(1)} collective-permute-done((f32[2,5,8,128]{3,2,1,0:T(8,128)S(1)}, f32[2,5,8,128]{3,2,1,0:T(8,128)S(1)}, u32[]{:S(2)}, u32[]{:S(2)}) %collective-permute-start.8) | collective-permute-done | bytes 40992 | tf_op jit(solution)/shard_map/ppermute | solution.py:20
  73.2 4.2 %collective-permute-start.10 = (f32[8,5,8,128]{3,2,1,0:T(8,128)S(1)}, f32[8,5,8,128]{3,2,1,0:T(8,128)S(1)}, u32[]{:S(2)}, u32[]{:S(2)}) collective-permute-start(f32[8,5,8,128]{3,2,1,0:T(8,128)S(1)} %get-tuple-element.22.mine), channel_id=1, source_target_pairs={{1,0},{2,1},{3,2},{4,3},{5,4},{6,5},{7,6},{8,7},{9,8},{10,9},{11,1... | collective-permute-start | bytes 491528 | tf_op jit(solution)/shard_map/ppermute | solution.py:20
  77.5 3.1 %collective-permute-start.9 = (f32[8,5,8,128]{3,2,1,0:T(8,128)S(1)}, f32[8,5,8,128]{3,2,1,0:T(8,128)S(1)}, u32[]{:S(2)}, u32[]{:S(2)}) collective-permute-start(f32[8,5,8,128]{3,2,1,0:T(8,128)S(1)} %get-tuple-element.22.mine), channel_id=1, source_target_pairs={{0,1},{1,2},{2,3},{3,4},{4,5},{5,6},{6,7},{7,8},{8,9},{9,10},{10,1... | collective-permute-start | bytes 491528 | tf_op jit(solution)/shard_map/ppermute | solution.py:20
  80.6 1.3 collective-permute-start.12
  81.9 4.0 %collective-permute-start.11 = (f32[6,5,8,128]{3,2,1,0:T(8,128)S(1)}, f32[6,5,8,128]{3,2,1,0:T(8,128)S(1)}, u32[]{:S(2)}, u32[]{:S(2)}) collective-permute-start(f32[6,5,8,128]{3,2,1,0:T(8,128)S(1)} %get-tuple-element.23), channel_id=1, source_target_pairs={{0,2},{1,3},{2,4},{3,5},{4,6},{5,7},{6,8},{7,9},{8,10},{9,11},{10,... | collective-permute-start | bytes 368648 | tf_op jit(solution)/shard_map/ppermute | solution.py:20
  85.9 1.5 %collective-permute-done.12.high2 = f32[6,5,8,128]{3,2,1,0:T(8,128)S(1)} collective-permute-done((f32[6,5,8,128]{3,2,1,0:T(8,128)S(1)}, f32[6,5,8,128]{3,2,1,0:T(8,128)S(1)}, u32[]{:S(2)}, u32[]{:S(2)}) %collective-permute-start.12) | collective-permute-done | bytes 122912 | tf_op jit(solution)/shard_map/ppermute | solution.py:20
  87.4 1.6 %collective-permute-done.11.low2 = f32[6,5,8,128]{3,2,1,0:T(8,128)S(1)} collective-permute-done((f32[6,5,8,128]{3,2,1,0:T(8,128)S(1)}, f32[6,5,8,128]{3,2,1,0:T(8,128)S(1)}, u32[]{:S(2)}, u32[]{:S(2)}) %collective-permute-start.11) | collective-permute-done | bytes 122912 | tf_op jit(solution)/shard_map/ppermute | solution.py:20
  88.9 0.0 collective-permute-done.10.high1
  88.9 0.0 collective-permute-done.9.low1
  88.9 2.0 %shard_map.73 = (f32[2,8,8,128]{3,2,1,0:T(8,128)S(1)}, f32[64,5,2,128]{3,2,1,0:T(2,128)S(1)}) custom-call(f32[8,5,8,128]{3,2,1,0:T(8,128)S(1)} %get-tuple-element.22.mine, f32[8,5,8,128]{3,2,1,0:T(8,128)S(1)} %collective-permute-done.9.low1, f32[8,5,8,128]{3,2,1,0:T(8,128)S(1)} %collective-permute-done.10.high1, ...), custom_call_target="tpu_custom_call" | custom-call | tf_op jit(solution)/shard_map/pallas_call | solution.py:28
  91.0 26.8 %all_to_all.16.gathered = f32[64,5,2,128]{3,2,1,0:T(2,128)S(1)} all-to-all(f32[64,5,2,128]{3,2,1,0:T(2,128)S(1)} %get-tuple-element.25), channel_id=1, replica_groups=mesh['ring'=4,'place'=8,'gy'=16] {'ring','gy'}, dimensions={0} | all-to-all | bytes 655360 | tf_op jit(solution)/shard_map/all_to_all | solution.py:497
  117.8 0.1 shard_map.74.refs_1_
  117.9 1.3 collective-permute-start.14
  119.2 4.0 %collective-permute-start.13 = (f32[4,160,128]{2,1,0:T(8,128)S(1)}, f32[4,160,128]{2,1,0:T(8,128)S(1)}, u32[]{:S(2)}, u32[]{:S(2)}) collective-permute-start(f32[4,160,128]{2,1,0:T(8,128)S(1)} %shard_map.74.refs_1_), channel_id=1, source_target_pairs={{0,16},{16,32},{32,48},{48,64},{64,80},{80,96},{96,112},{1,17},{17... | collective-permute-start | bytes 983048 | tf_op jit(solution)/shard_map/ppermute | solution.py:20
  123.3 5.4 %collective-permute-done.14.refs_2_ = f32[4,160,128]{2,1,0:T(8,128)S(1)} collective-permute-done((f32[4,160,128]{2,1,0:T(8,128)S(1)}, f32[4,160,128]{2,1,0:T(8,128)S(1)}, u32[]{:S(2)}, u32[]{:S(2)}) %collective-permute-start.14) | collective-permute-done | bytes 327712 | tf_op jit(solution)/shard_map/ppermute | solution.py:20
  128.7 0.9 collective-permute-done.13.refs_0_
  129.6 4.4 %shard_map.75 = f32[8,3,8,128]{3,2,1,0:T(8,128)S(1)} custom-call(f32[4,160,128]{2,1,0:T(8,128)S(1)} %collective-permute-done.13.refs_0_, f32[4,160,128]{2,1,0:T(8,128)S(1)} %shard_map.74.refs_1_, f32[4,160,128]{2,1,0:T(8,128)S(1)} %collective-permute-done.14.refs_2_, f32[2,8,8,128]{3,2,1,0:T(8,128)S(1)} %get-tuple-element.26.refs_3_, ...), custom_call_target="tpu_custom_call" | custom-call | tf_op jit(solution)/shard_map/pallas_call | solution.py:28
  134.0 13.2 %all_to_all.17.pieces = f32[8,3,8,128]{3,2,1,0:T(8,128)S(1)} all-to-all(f32[8,3,8,128]{3,2,1,0:T(8,128)S(1)} %shard_map.75), channel_id=1, replica_groups=mesh['ring'=4,'place'=8,'gy'=16] {'place'}, dimensions={0} | all-to-all | bytes 196608 | tf_op jit(solution)/shard_map/all_to_all | solution.py:504
  147.2 0.7 shard_map.76
  (3 shorter events, 0.1 us)
Async XLA Ops:
  33.0 27.7 %collective-permute-start.3 = (f32[8,5,4,8,128]{4,3,2,1,0:T(8,128)S(1)}, f32[8,5,4,8,128]{4,3,2,1,0:T(8,128)S(1)}, u32[]{:S(2)}, u32[]{:S(2)}) collective-permute-start(f32[8,5,4,8,128]{4,3,2,1,0:T(8,128)S(1)} %all_to_all.15.own), channel_id=1, source_target_pairs={{1,0},{2,1},{3,2},{4,3},{5,4},{6,5},{7,6},{8,7},{9,8},{10,9},{11,1... | collective-permute-start | bytes 1966088 | tf_op jit(solution)/shard_map/ppermute | solution.py:20
  36.9 23.7 %collective-permute-start.2 = (f32[8,5,4,8,128]{4,3,2,1,0:T(8,128)S(1)}, f32[8,5,4,8,128]{4,3,2,1,0:T(8,128)S(1)}, u32[]{:S(2)}, u32[]{:S(2)}) collective-permute-start(f32[8,5,4,8,128]{4,3,2,1,0:T(8,128)S(1)} %all_to_all.15.own), channel_id=1, source_target_pairs={{0,1},{1,2},{2,3},{3,4},{4,5},{5,6},{6,7},{7,8},{8,9},{9,10},{10,1... | collective-permute-start | bytes 1966088 | tf_op jit(solution)/shard_map/ppermute | solution.py:20
  40.1 9.2 %collective-permute-start.1 = (f32[41,8,128]{2,1,0:T(8,128)S(1)}, f32[41,8,128]{2,1,0:T(8,128)S(1)}, u32[]{:S(2)}, u32[]{:S(2)}) collective-permute-start(f32[41,8,128]{2,1,0:T(8,128)S(1)} %get-tuple-element.16), channel_id=1, source_target_pairs={{128,0},{256,128},{384,256},{129,1},{257,129},{385,257},{130,2},{2... | collective-permute-start | bytes 503816 | tf_op jit(solution)/shard_map/ppermute | solution.py:20
  41.4 7.9 %collective-permute-start = (f32[40,8,128]{2,1,0:T(8,128)S(1)}, f32[40,8,128]{2,1,0:T(8,128)S(1)}, u32[]{:S(2)}, u32[]{:S(2)}) collective-permute-start(f32[40,8,128]{2,1,0:T(8,128)S(1)} %get-tuple-element.15), channel_id=1, source_target_pairs={{0,128},{128,256},{256,384},{1,129},{129,257},{257,385},{2,130},{1... | collective-permute-start | bytes 491528 | tf_op jit(solution)/shard_map/ppermute | solution.py:20
  49.3 10.2 %collective-permute-start.4 = (f32[60,8,128]{2,1,0:T(8,128)S(1)}, f32[60,8,128]{2,1,0:T(8,128)S(1)}, u32[]{:S(2)}, u32[]{:S(2)}) collective-permute-start(f32[60,8,128]{2,1,0:T(8,128)S(1)} %get-tuple-element.17), channel_id=1, source_target_pairs={{0,1},{1,2},{2,3},{3,4},{4,5},{5,6},{6,7},{7,8},{8,9},{9,10},{10,1... | collective-permute-start | bytes 737288 | tf_op jit(solution)/shard_map/ppermute | solution.py:20
  52.9 7.7 %collective-permute-start.5 = (f32[60,8,128]{2,1,0:T(8,128)S(1)}, f32[60,8,128]{2,1,0:T(8,128)S(1)}, u32[]{:S(2)}, u32[]{:S(2)}) collective-permute-start(f32[60,8,128]{2,1,0:T(8,128)S(1)} %get-tuple-element.18), channel_id=1, source_target_pairs={{1,0},{2,1},{3,2},{4,3},{5,4},{6,5},{7,6},{8,7},{9,8},{10,9},{11,1... | collective-permute-start | bytes 737288 | tf_op jit(solution)/shard_map/ppermute | solution.py:20
  54.8 4.7 %collective-permute-start.6 = (f32[32,128]{1,0:T(8,128)S(1)}, f32[32,128]{1,0:T(8,128)S(1)}, u32[]{:S(2)}, u32[]{:S(2)}) collective-permute-start(f32[32,128]{1,0:T(8,128)S(1)} %get-tuple-element.19), channel_id=1, source_target_pairs={{2,0},{3,1},{4,2},{5,3},{6,4},{7,5},{8,6},{9,7},{10,8},{11,9},{12,... | collective-permute-start | bytes 49160 | tf_op jit(solution)/shard_map/ppermute | solution.py:20
  64.4 5.4 %collective-permute-start.7 = (f32[2,5,8,128]{3,2,1,0:T(8,128)S(1)}, f32[2,5,8,128]{3,2,1,0:T(8,128)S(1)}, u32[]{:S(2)}, u32[]{:S(2)}) collective-permute-start(f32[2,5,8,128]{3,2,1,0:T(8,128)S(1)} %get-tuple-element.20.last), channel_id=1, source_target_pairs={{0,128},{128,256},{256,384},{1,129},{129,257},{257,385},{2,130},{1... | collective-permute-start | bytes 122888 | tf_op jit(solution)/shard_map/ppermute | solution.py:20
  68.5 4.7 %collective-permute-start.8 = (f32[2,5,8,128]{3,2,1,0:T(8,128)S(1)}, f32[2,5,8,128]{3,2,1,0:T(8,128)S(1)}, u32[]{:S(2)}, u32[]{:S(2)}) collective-permute-start(f32[2,5,8,128]{3,2,1,0:T(8,128)S(1)} %get-tuple-element.21.first), channel_id=1, source_target_pairs={{128,0},{256,128},{384,256},{129,1},{257,129},{385,257},{130,2},{2... | collective-permute-start | bytes 122888 | tf_op jit(solution)/shard_map/ppermute | solution.py:20
  73.2 15.7 %collective-permute-start.10 = (f32[8,5,8,128]{3,2,1,0:T(8,128)S(1)}, f32[8,5,8,128]{3,2,1,0:T(8,128)S(1)}, u32[]{:S(2)}, u32[]{:S(2)}) collective-permute-start(f32[8,5,8,128]{3,2,1,0:T(8,128)S(1)} %get-tuple-element.22.mine), channel_id=1, source_target_pairs={{1,0},{2,1},{3,2},{4,3},{5,4},{6,5},{7,6},{8,7},{9,8},{10,9},{11,1... | collective-permute-start | bytes 491528 | tf_op jit(solution)/shard_map/ppermute | solution.py:20
  77.5 11.5 %collective-permute-start.9 = (f32[8,5,8,128]{3,2,1,0:T(8,128)S(1)}, f32[8,5,8,128]{3,2,1,0:T(8,128)S(1)}, u32[]{:S(2)}, u32[]{:S(2)}) collective-permute-start(f32[8,5,8,128]{3,2,1,0:T(8,128)S(1)} %get-tuple-element.22.mine), channel_id=1, source_target_pairs={{0,1},{1,2},{2,3},{3,4},{4,5},{5,6},{6,7},{7,8},{8,9},{9,10},{10,1... | collective-permute-start | bytes 491528 | tf_op jit(solution)/shard_map/ppermute | solution.py:20
  80.6 6.8 %collective-permute-start.12 = (f32[6,5,8,128]{3,2,1,0:T(8,128)S(1)}, f32[6,5,8,128]{3,2,1,0:T(8,128)S(1)}, u32[]{:S(2)}, u32[]{:S(2)}) collective-permute-start(f32[6,5,8,128]{3,2,1,0:T(8,128)S(1)} %get-tuple-element.23), channel_id=1, source_target_pairs={{2,0},{3,1},{4,2},{5,3},{6,4},{7,5},{8,6},{9,7},{10,8},{11,9},{12,... | collective-permute-start | bytes 368648 | tf_op jit(solution)/shard_map/ppermute | solution.py:20
  81.9 7.1 %collective-permute-start.11 = (f32[6,5,8,128]{3,2,1,0:T(8,128)S(1)}, f32[6,5,8,128]{3,2,1,0:T(8,128)S(1)}, u32[]{:S(2)}, u32[]{:S(2)}) collective-permute-start(f32[6,5,8,128]{3,2,1,0:T(8,128)S(1)} %get-tuple-element.23), channel_id=1, source_target_pairs={{0,2},{1,3},{2,4},{3,5},{4,6},{5,7},{6,8},{7,9},{8,10},{9,11},{10,... | collective-permute-start | bytes 368648 | tf_op jit(solution)/shard_map/ppermute | solution.py:20
  117.9 10.8 %collective-permute-start.14 = (f32[4,160,128]{2,1,0:T(8,128)S(1)}, f32[4,160,128]{2,1,0:T(8,128)S(1)}, u32[]{:S(2)}, u32[]{:S(2)}) collective-permute-start(f32[4,160,128]{2,1,0:T(8,128)S(1)} %shard_map.74.refs_1_), channel_id=1, source_target_pairs={{16,0},{32,16},{48,32},{64,48},{80,64},{96,80},{112,96},{17,1},{33... | collective-permute-start | bytes 983048 | tf_op jit(solution)/shard_map/ppermute | solution.py:20
  119.2 10.4 %collective-permute-start.13 = (f32[4,160,128]{2,1,0:T(8,128)S(1)}, f32[4,160,128]{2,1,0:T(8,128)S(1)}, u32[]{:S(2)}, u32[]{:S(2)}) collective-permute-start(f32[4,160,128]{2,1,0:T(8,128)S(1)} %shard_map.74.refs_1_), channel_id=1, source_target_pairs={{0,16},{16,32},{32,48},{48,64},{64,80},{80,96},{96,112},{1,17},{17... | collective-permute-start | bytes 983048 | tf_op jit(solution)/shard_map/ppermute | solution.py:20

commit v8 on v7

--- a/solution.py
+++ b/solution.py
@@ -66,13 +66,29 @@
     return pltpu.roll(x, x.shape[1] - 1, 1)
 
 
-def exact_dot(a, b):
-    return jnp.dot(a, b, precision=lax.Precision.HIGHEST, preferred_element_type=F32)
+def pick(values, chooser):
+    parts, rest = [], values
+    for _ in range(3):
+        part = rest.astype(jnp.bfloat16)
+        parts.append(part)
+        rest = rest - part.astype(F32)
+    total = jnp.dot(jnp.concatenate(parts, 0), chooser, preferred_element_type=F32)
+    n = values.shape[0]
+    return (total[2 * n :] + total[n : 2 * n]) + total[:n]
+
+
+def pick_rows(chooser, values):
+    parts, rest = [], values
+    for _ in range(3):
+        part = rest.astype(jnp.bfloat16)
+        parts.append(jnp.dot(chooser, part, preferred_element_type=F32))
+        rest = rest - part.astype(F32)
+    return (parts[2] + parts[1]) + parts[0]
 
 
 def one_hot(shape, test):
     row, col = iotas(shape)
-    return jnp.where(test(row, col), 1.0, 0.0).astype(F32)
+    return jnp.where(test(row, col), 1.0, 0.0).astype(jnp.bfloat16)
 
 
 def low_rows(shape):
@@ -197,11 +213,11 @@
 
 
 def fine_kernel(
-    own, x_low, x_high, y_low, y_high, corner_low, corner_high, beyond_y,
-    fine_out, mid_first, mid_last, own_out, co, r, b,
+    own, x_low, x_high, y_low, y_high, corner_low, corner_high, beyond_y, mid_coefs,
+    fine_out, mid_first, mid_last, co, r, b,
 ):
     q0 = even_mask((24, 128))
-    row, lane = iotas((24, 128))
+    row, _ = iotas((24, 128))
     clear_guards(r, b, 24)
     zero = jnp.zeros((8, 128), F32)
 
@@ -244,13 +260,34 @@
         co[D_R, p], co[D_B, p] = d_r, d_b
         co[I_R, p], co[I_B, p] = inverse_of(d_r, a_r), inverse_of(d_b, a_b)
     smooth_cone(co, r, b, 16, 4, q0)
-    sums, alphas, bys, nexts, bxs, bzs = [], [], [], [], [], []
+    sums = []
     for j in range(16):
         p = j + 4
         red, black = residual(co, r, b, p, q0)
         sums.append((red + black)[:8])
         fine_out[0, j] = r[p + 1][:8]
         fine_out[1, j] = b[p + 1][:8]
+    along = pick(jnp.concatenate(sums, 0), one_hot((128, 128), lambda i, j: (i >> 1) == j))
+    source = pick_rows(one_hot((64, 128), lambda i, j: (j >> 1) == i), along) * 0.125
+    for t in range(4):
+        out = mid_first if t < 2 else mid_last
+        out[t % 2, 0] = mid_tile(source, t)
+        for a in range(4):
+            out[t % 2, a + 1] = mid_coefs[t, a]
+
+
+def mid_tile(value, t):
+    _, lane = iotas((8, 128))
+    return jnp.where(lane < 64, value[16 * t : 16 * t + 8], pltpu.roll(value[16 * t + 8 : 16 * t + 16], 64, 1))
+
+
+def low_rows_of(out_row, test):
+    return one_hot((16, 8), lambda i, j: ((i >> 1) == out_row) & test(i & 1, j))
+
+
+def coefficients_kernel(own, x_high, y_high, mid_coefs, mid_own, low_out):
+    alphas, bys, nexts, bxs, bzs = [], [], [], [], []
+    for j in range(16):
         s, x = j // 2, 2 * (j % 2)
         alphas.append(own[s, ALPHA, x] + own[s, ALPHA, x + 1])
         bys.append(own[s, BY, x] + own[s, BY, x + 1])
@@ -258,34 +295,44 @@
         bzs.append(own[s, BZ, x] + own[s, BZ, x + 1])
         bxs.append(own[s, BX, x])
     bxs.append(x_high[flat(0, BX, 0)])
-    z_sum = one_hot((128, 128), lambda i, j: (i >> 1) == j)
-    z_even = one_hot((128, 128), lambda i, j: i == 2 * j)
+    along = pick(
+        jnp.concatenate(alphas + bys + nexts + bxs, 0), one_hot((128, 128), lambda i, j: (i >> 1) == j)
+    )
+    bz_z = pick(jnp.concatenate(bzs, 0), one_hot((128, 128), lambda i, j: i == 2 * j))
     y_sum = one_hot((64, 128), lambda i, j: (j >> 1) == i)
     y_even = one_hot((64, 128), lambda i, j: j == 2 * i)
     y_next = one_hot((64, 128), lambda i, j: ((i & 3) < 3) & (j == 2 * i + 2))
     y_last = one_hot((64, 128), lambda i, j: ((i & 3) == 3) & (j == 8 * (i >> 2)))
-    along = exact_dot(jnp.concatenate(sums + alphas + bys + nexts + bxs, 0), z_sum)
-    bz_z = exact_dot(jnp.concatenate(bzs, 0), z_even)
-    source = exact_dot(y_sum, along[0:128]) * 0.125
-    alpha = exact_dot(y_sum, along[128:256]) * 0.125
-    y_lower = exact_dot(y_even, along[256:384]) * 0.0625
-    y_upper = (exact_dot(y_next, along[256:384]) + exact_dot(y_last, along[384:512])) * 0.0625
-    x_lower = exact_dot(y_sum, along[512:640]) * 0.0625
-    x_upper = exact_dot(y_sum, along[520:648]) * 0.0625
-    z_lower = exact_dot(y_sum, bz_z) * 0.0625
-    z_upper = next_lane(z_lower)
-    diagonal = alpha + ((x_lower + x_upper) + (y_lower + y_upper) + (z_lower + z_upper))
-    arrays = (source, inverse_of(diagonal, alpha), x_lower, y_lower, z_lower)
-    _, lane = iotas((8, 128))
-
-    def tile(value, t):
-        return jnp.where(lane < 64, value[16 * t : 16 * t + 8], pltpu.roll(value[16 * t + 8 : 16 * t + 16], 64, 1))
-
+    alpha = pick_rows(y_sum, along[0:128]) * 0.125
+    y_lower = pick_rows(y_even, along[128:256]) * 0.0625
+    y_upper = (pick_rows(y_next, along[128:256]) + pick_rows(y_last, along[256:384])) * 0.0625
+    x_lower = pick_rows(y_sum, along[384:512]) * 0.0625
+    x_upper = pick_rows(y_sum, along[392:520]) * 0.0625
+    z_lower = pick_rows(y_sum, bz_z) * 0.0625
+    diagonal = alpha + ((x_lower + x_upper) + (y_lower + y_upper) + (z_lower + next_lane(z_lower)))
+    sums = jnp.zeros((24, 128), F32)
+    low_bz = jnp.zeros((8, 128), F32)
     for t in range(4):
-        for a, value in enumerate(arrays):
-            (mid_first if t < 2 else mid_last)[t % 2, a] = tile(value, t)
-        own_out[t, 0] = tile(diagonal, t)
-        own_out[t, 1] = tile(alpha, t)
+        for a, value in enumerate((inverse_of(diagonal, alpha), x_lower, y_lower, z_lower)):
+            mid_coefs[t, a] = mid_tile(value, t)
+        mid_own[t] = mid_tile(diagonal, t)
+        stack = jnp.concatenate([mid_tile(alpha, t), mid_coefs[t, 1], mid_coefs[t, 2]], 0)
+
+        def chooser(test):
+            def to(i, j):
+                k = 2 * t + (i >> 6)
+                return ((j >> 4) == k) & test(i & 63, j - 16 * k + 8)
+
+            return one_hot((128, 128), to)
+
+        sums += pick(stack, chooser(lambda i, j: (i >> 1) == j))
+        low_bz += pick(mid_coefs[t, 3], chooser(lambda i, j: i == 2 * j))
+    total = pick_rows(low_rows_of(0, lambda i, j: ((j & 3) >> 1) == i), sums[0:8]) * 0.125
+    total += pick_rows(low_rows_of(1, lambda i, j: (j < 4) & ((j >> 1) == i)), sums[8:16]) * 0.0625
+    total += pick_rows(low_rows_of(2, lambda i, j: (j & 3) == 2 * i), sums[16:24]) * 0.0625
+    total += pick_rows(low_rows_of(3, lambda i, j: ((j & 3) >> 1) == i), low_bz) * 0.0625
+    for k in range(4):
+        low_out[k] = total[2 * k : 2 * k + 2]
 
 
 def mid_message_kernel(low, first, last, high, near, far):
@@ -296,7 +343,7 @@
             far[s - 1] = tiles[s]
 
 
-def mid_kernel(mine, low1, high1, low2, high2, own, level_out, low_out, co, r, b):
+def mid_kernel(mine, low1, high1, low2, high2, own, low_coefs, level_out, low_out, co, r, b):
     q0 = even_mask((24, 128))
     _, lane = iotas((8, 128))
     keep = low_rows((8, 128))
@@ -324,34 +371,27 @@
         put_faces(co, p, q0, (bx0, bx1, n0), planes(p, 3), planes(p, 4))
         bx0, bx1 = n0, n1
         if 4 <= p < 12:
-            d = part(own[p // 2 - 2, 0], p)
+            d = part(own[p // 2 - 2], p)
             d = jnp.concatenate([d, d, d], 0), jnp.concatenate([half(d)] * 3, 0)
             co[D_R, p], co[D_B, p] = halves(q0, *d)
     smooth_cone(co, r, b, 8, 4, q0)
-    sums = jnp.zeros((32, 128), F32)
-    bz_z = zero
+    sums = []
     for k in range(8):
-        p = k + 4
-        red, black = residual(co, r, b, p, q0)
-        level_out[0, k] = r[p + 1][:8]
-        level_out[1, k] = b[p + 1][:8]
-        mid = [part(mine[p // 2, a], p) for a in (2, 3, 4)]
-        stack = jnp.concatenate([(red + black)[:8], part(own[p // 2 - 2, 1], p), mid[0], mid[1]], 0)
-        sums += exact_dot(stack, one_hot((128, 128), lambda i, j: ((i >> 1) == j - 16 * k + 8) & ((j >> 4) == k)))
-        bz_z += exact_dot(mid[2], one_hot((128, 128), lambda i, j: (i == 2 * (j - 16 * k + 8)) & ((j >> 4) == k)))
-
-    def rows(out_row, test):
-        return one_hot((16, 8), lambda i, j: ((i >> 1) == out_row) & test(i & 1, j))
-
-    total = exact_dot(rows(0, lambda i, j: (j < 4) & ((j >> 1) == i)), sums[0:8]) * 0.125
-    total += exact_dot(rows(1, lambda i, j: ((j & 3) >> 1) == i), sums[8:16]) * 0.125
-    total += exact_dot(rows(2, lambda i, j: (j < 4) & ((j >> 1) == i)), sums[16:24]) * 0.0625
-    total += exact_dot(rows(3, lambda i, j: (j & 3) == 2 * i), sums[24:32]) * 0.0625
-    total += exact_dot(rows(4, lambda i, j: ((j & 3) >> 1) == i), bz_z) * 0.0625
-    for k in range(5):
-        mine = total[2 * k : 2 * k + 2]
-        for j in range(low_out.shape[0]):
-            low_out[j, k] = mine
+        red, black = residual(co, r, b, k + 4, q0)
+        level_out[0, k] = r[k + 5][:8]
+        level_out[1, k] = b[k + 5][:8]
+        sums.append((red + black)[:8])
+    along = pick(jnp.concatenate(sums, 0), one_hot((128, 128), lambda i, j: (i >> 1) == j))
+    total = zero
+    for k in range(8):
+        moved = pltpu.roll(along[8 * k : 8 * k + 8], (16 * k - 8) % 128, 1)
+        total = jnp.where((lane >> 4) == k, moved, total)
+    source = pick_rows(low_rows_of(0, lambda i, j: (j < 4) & ((j >> 1) == i)), total)[:2] * 0.125
+    coefs = [low_coefs[k] for k in range(4)]
+    for j in range(low_out.shape[0]):
+        low_out[j, 0] = source
+        for k in range(4):
+            low_out[j, k + 1] = coefs[k]
 
 
 def whole_y_kernel(gathered, out):
@@ -427,18 +467,18 @@
         parts.append(pltpu.roll(value, 64 * side, 1)[:8])
     q0 = even_mask((8, 128))
     row, lane = iotas((8, 128))
-    up = exact_dot(jnp.concatenate(parts, 0), one_hot((128, 128), lambda i, j: (j >> 1) + 8 == i))
+    up = pick(jnp.concatenate(parts, 0), one_hot((128, 128), lambda i, j: (j >> 1) + 8 == i))
     spread = one_hot((64, 64), lambda i, j: ((i >> 3) == (j >> 3)) & (((i & 3) >> 1) == (j & 7)))
-    up = exact_dot(spread, up)
+    up = pick_rows(spread, up)
     mid = []
     for k in range(8):
         add = up[8 * k : 8 * k + 8]
         mid.extend(halves(q0, level[0, k] + add, level[1, k] + add))
         mine = pltpu.roll(parts[k], lax.rem(16 * place + 112, 128), 1)
         out[k, 2] = jnp.where(((lane >> 4) == place) & (row < 2), mine, 0.0)
-    wide = exact_dot(jnp.concatenate(mid, 0), one_hot((128, 128), lambda i, j: (j >> 1) == i))
+    wide = pick(jnp.concatenate(mid, 0), one_hot((128, 128), lambda i, j: (j >> 1) == i))
     spread = one_hot((128, 128), lambda i, j: ((i >> 3) == (j >> 3)) & (((i & 7) >> 1) == (j & 7)))
-    wide = exact_dot(spread, wide)
+    wide = pick_rows(spread, wide)
     for j in range(16):
         add = wide[8 * j : 8 * j + 8]
         e0, e1 = halves(q0, fine[0, j] + add, fine[1, j] + add)
@@ -475,11 +515,14 @@
     )(x_low, x_high)
     corner_low = shifted(to_high, "gy", 1)
     corner_high = shifted(to_low, "gy", -1)
-    fine, mid_first, mid_last, mid_own = call(
+    mid_coefs, mid_own, low_coefs = call(
+        coefficients_kernel, [(4, 4, 8, 128), (4, 8, 128), (4, 2, 128)]
+    )(own, x_high, y_high)
+    fine, mid_first, mid_last = call(
         fine_kernel,
-        [(2, 16, 8, 128), (2, 5, 8, 128), (2, 5, 8, 128), (4, 2, 8, 128)],
+        [(2, 16, 8, 128), (2, 5, 8, 128), (2, 5, 8, 128)],
         [(17, 24, 24, 128), (26, 24, 128), (26, 24, 128)],
-    )(own, x_low, x_high, y_low, y_high, corner_low, corner_high, beyond_y)
+    )(own, x_low, x_high, y_low, y_high, corner_low, corner_high, beyond_y, mid_coefs)
 
     low, high = shifted(mid_last, "ring", 1), shifted(mid_first, "ring", -1)
     near, far = call(
@@ -491,7 +534,7 @@
         [(17, 16, 24, 128), (18, 24, 128), (18, 24, 128)],
     )(
         near, shifted(near, "gy", 1), shifted(near, "gy", -1),
-        shifted(far, "gy", 2), shifted(far, "gy", -2), mid_own,
+        shifted(far, "gy", 2), shifted(far, "gy", -2), mid_own, low_coefs,
     )
 
     low = lax.all_to_all(low, ("ring", "gy"), 0, 0, tiled=True)

time: 150 us -> 148 us (0.987)
    pallas_call x9 -> x10, Pallas kernels: 13.4 us -> 12.3 us  [run(): pl.pallas_call(kernel, out_shape=[jax.ShapeDtypeStruct(s, F32) for s in o...]
  transfers between devices with their start and end apart: 15 -> 15, of which waited for: 8 -> 8; matrix products, arithmetic and copies ran while one was open for 0% -> 0% of each run, Pallas kernels for 0% -> 1%
where the time goes in v8:
time: 148 us; the launch traced here: 146 us
  blocking collectives  70.1 us (47%)
  starting transfers between devices  42.4 us (29%)
  waiting for transfers between devices  20.3 us (14%)
  Pallas kernels  12.3 us (8%)
    ppermute x15, starting transfers between devices, shifted(): lax.ppermute(values, name, [(i, i + steps) for i in range(lead, last)])  42.4 us
    all_to_all x1, blocking collectives, cycle(): own = lax.all_to_all(own, 'place', 0, 0, tiled=True)  30.1 us
    all_to_all x1, blocking collectives, cycle(): low = lax.all_to_all(low, ('ring', 'gy'), 0, 0, tiled=True)  26.8 us
    ppermute x15, waiting for transfers between devices, shifted(): lax.ppermute(values, name, [(i, i + steps) for i in range(lead, last)])  20.3 us
    all_to_all x1, blocking collectives, cycle(): pieces = lax.all_to_all(pieces, 'place', 0, 0, tiled=True)  13.2 us
    pallas_call x10, Pallas kernels, run(): pl.pallas_call(kernel, out_shape=[jax.ShapeDtypeStruct(s, F32) for s in o...  12.3 us
  transfers between devices with their start and end apart: 15, of which 8 were waited for; matrix products, arithmetic and copies ran while one was open for 0% of the time, Pallas kernels for 1%

profile of v8, /device:TPU:1, one launch (start us, length us, event | category | flops | bytes accessed | tf_op | source)
XLA Modules:
  0.0 145.9 jit_solution(4547124701578078028)
XLA Ops:
  0.6 2.2 %shard_map.68 = f32[8,5,4,8,128]{4,3,2,1,0:T(8,128)} custom-call(f32[4,8,512]{2,1,0:T(8,128)} %refs_0_.1, f32[4,8,512]{2,1,0:T(8,128)} %refs_1_.1, f32[4,8,512]{2,1,0:T(8,128)} %refs_2_.1, f32[4,8,512]{2,1,0:T(8,128)} %refs_3_.1, f32[4,8,512]{2,1,0:T(8,128)} %refs_4_.1), custom_call_target="tpu_custom_call" | custom-call | tf_op jit(solution)/shard_map/pallas_call | solution.py:28
  2.9 30.1 %all_to_all.15.own = f32[8,5,4,8,128]{4,3,2,1,0:T(8,128)S(1)} all-to-all(f32[8,5,4,8,128]{4,3,2,1,0:T(8,128)} %shard_map.68), channel_id=1, replica_groups=mesh['ring'=4,'place'=8,'gy'=16] {'place'}, dimensions={0} | all-to-all | bytes 1310720 | tf_op jit(solution)/shard_map/all_to_all | solution.py:506
  32.9 3.9 %collective-permute-start.3 = (f32[8,5,4,8,128]{4,3,2,1,0:T(8,128)S(1)}, f32[8,5,4,8,128]{4,3,2,1,0:T(8,128)S(1)}, u32[]{:S(2)}, u32[]{:S(2)}) collective-permute-start(f32[8,5,4,8,128]{4,3,2,1,0:T(8,128)S(1)} %all_to_all.15.own), channel_id=1, source_target_pairs={{1,0},{2,1},{3,2},{4,3},{5,4},{6,5},{7,6},{8,7},{9,8},{10,9},{11,1... | collective-permute-start | bytes 1966088 | tf_op jit(solution)/shard_map/ppermute | solution.py:20
  36.9 3.1 %collective-permute-start.2 = (f32[8,5,4,8,128]{4,3,2,1,0:T(8,128)S(1)}, f32[8,5,4,8,128]{4,3,2,1,0:T(8,128)S(1)}, u32[]{:S(2)}, u32[]{:S(2)}) collective-permute-start(f32[8,5,4,8,128]{4,3,2,1,0:T(8,128)S(1)} %all_to_all.15.own), channel_id=1, source_target_pairs={{0,1},{1,2},{2,3},{3,4},{4,5},{5,6},{6,7},{7,8},{8,9},{9,10},{10,1... | collective-permute-start | bytes 1966088 | tf_op jit(solution)/shard_map/ppermute | solution.py:20
  40.1 1.3 collective-permute-start.1
  41.4 4.0 %collective-permute-start = (f32[40,8,128]{2,1,0:T(8,128)S(1)}, f32[40,8,128]{2,1,0:T(8,128)S(1)}, u32[]{:S(2)}, u32[]{:S(2)}) collective-permute-start(f32[40,8,128]{2,1,0:T(8,128)S(1)} %get-tuple-element.17), channel_id=1, source_target_pairs={{0,128},{128,256},{256,384},{1,129},{129,257},{257,385},{2,130},{1... | collective-permute-start | bytes 491528 | tf_op jit(solution)/shard_map/ppermute | solution.py:20
  45.4 3.9 %collective-permute-done.low.x_low = f32[40,8,128]{2,1,0:T(8,128)S(1)} collective-permute-done((f32[40,8,128]{2,1,0:T(8,128)S(1)}, f32[40,8,128]{2,1,0:T(8,128)S(1)}, u32[]{:S(2)}, u32[]{:S(2)}) %collective-permute-start) | collective-permute-done | bytes 163872 | tf_op jit(solution)/shard_map/ppermute | solution.py:20
  49.3 0.0 collective-permute-done.1.high.x_high
  49.3 3.6 %collective-permute-start.4 = (f32[60,8,128]{2,1,0:T(8,128)S(1)}, f32[60,8,128]{2,1,0:T(8,128)S(1)}, u32[]{:S(2)}, u32[]{:S(2)}) collective-permute-start(f32[60,8,128]{2,1,0:T(8,128)S(1)} %get-tuple-element.19), channel_id=1, source_target_pairs={{0,1},{1,2},{2,3},{3,4},{4,5},{5,6},{6,7},{7,8},{8,9},{9,10},{10,1... | collective-permute-start | bytes 737288 | tf_op jit(solution)/shard_map/ppermute | solution.py:20
  52.9 1.9 %collective-permute-start.5 = (f32[60,8,128]{2,1,0:T(8,128)S(1)}, f32[60,8,128]{2,1,0:T(8,128)S(1)}, u32[]{:S(2)}, u32[]{:S(2)}) collective-permute-start(f32[60,8,128]{2,1,0:T(8,128)S(1)} %get-tuple-element.20), channel_id=1, source_target_pairs={{1,0},{2,1},{3,2},{4,3},{5,4},{6,5},{7,6},{8,7},{9,8},{10,9},{11,1... | collective-permute-start | bytes 737288 | tf_op jit(solution)/shard_map/ppermute | solution.py:20
  54.8 1.3 collective-permute-start.6
  56.1 0.0 collective-permute-done.3.y_high
  56.1 0.9 shard_map.71
  57.1 2.4 %collective-permute-done.6.beyond_y = f32[32,128]{1,0:T(8,128)S(1)} collective-permute-done((f32[32,128]{1,0:T(8,128)S(1)}, f32[32,128]{1,0:T(8,128)S(1)}, u32[]{:S(2)}, u32[]{:S(2)}) %collective-permute-start.6) | collective-permute-done | bytes 16416 | tf_op jit(solution)/shard_map/ppermute | solution.py:20
  59.5 0.0 collective-permute-done.4.corner_low
  59.5 1.1 collective-permute-done.5.corner_high
  60.6 0.0 collective-permute-done.2.y_low
  60.6 2.1 %shard_map.72 = (f32[2,16,8,128]{3,2,1,0:T(8,128)S(1)}, f32[2,5,8,128]{3,2,1,0:T(8,128)S(1)}, f32[2,5,8,128]{3,2,1,0:T(8,128)S(1)}) custom-call(f32[8,5,4,8,128]{4,3,2,1,0:T(8,128)S(1)} %all_to_all.15.own, f32[40,8,128]{2,1,0:T(8,128)S(1)} %collective-permute-done.low.x_low, f32[41,8,128]{2,1,0:T(8,128)S(1)} %collective-permute-done.1.high.x_high, ...), custom_call_target="tpu_custom_call" | custom-call | tf_op jit(solution)/shard_map/pallas_call | solution.py:28
  62.7 4.1 %collective-permute-start.7 = (f32[2,5,8,128]{3,2,1,0:T(8,128)S(1)}, f32[2,5,8,128]{3,2,1,0:T(8,128)S(1)}, u32[]{:S(2)}, u32[]{:S(2)}) collective-permute-start(f32[2,5,8,128]{3,2,1,0:T(8,128)S(1)} %get-tuple-element.23.last), channel_id=1, source_target_pairs={{0,128},{128,256},{256,384},{1,129},{129,257},{257,385},{2,130},{1... | collective-permute-start | bytes 122888 | tf_op jit(solution)/shard_map/ppermute | solution.py:20
  66.8 1.3 collective-permute-start.8
  68.1 0.0 collective-permute-done.7.low
  68.2 3.4 %collective-permute-done.8.high = f32[2,5,8,128]{3,2,1,0:T(8,128)S(1)} collective-permute-done((f32[2,5,8,128]{3,2,1,0:T(8,128)S(1)}, f32[2,5,8,128]{3,2,1,0:T(8,128)S(1)}, u32[]{:S(2)}, u32[]{:S(2)}) %collective-permute-start.8) | collective-permute-done | bytes 40992 | tf_op jit(solution)/shard_map/ppermute | solution.py:20
  71.6 4.2 %collective-permute-start.10 = (f32[8,5,8,128]{3,2,1,0:T(8,128)S(1)}, f32[8,5,8,128]{3,2,1,0:T(8,128)S(1)}, u32[]{:S(2)}, u32[]{:S(2)}) collective-permute-start(f32[8,5,8,128]{3,2,1,0:T(8,128)S(1)} %get-tuple-element.25.mine), channel_id=1, source_target_pairs={{1,0},{2,1},{3,2},{4,3},{5,4},{6,5},{7,6},{8,7},{9,8},{10,9},{11,1... | collective-permute-start | bytes 491528 | tf_op jit(solution)/shard_map/ppermute | solution.py:20
  75.8 3.1 %collective-permute-start.9 = (f32[8,5,8,128]{3,2,1,0:T(8,128)S(1)}, f32[8,5,8,128]{3,2,1,0:T(8,128)S(1)}, u32[]{:S(2)}, u32[]{:S(2)}) collective-permute-start(f32[8,5,8,128]{3,2,1,0:T(8,128)S(1)} %get-tuple-element.25.mine), channel_id=1, source_target_pairs={{0,1},{1,2},{2,3},{3,4},{4,5},{5,6},{6,7},{7,8},{8,9},{9,10},{10,1... | collective-permute-start | bytes 491528 | tf_op jit(solution)/shard_map/ppermute | solution.py:20
  78.9 1.3 collective-permute-start.12
  80.2 4.0 %collective-permute-start.11 = (f32[6,5,8,128]{3,2,1,0:T(8,128)S(1)}, f32[6,5,8,128]{3,2,1,0:T(8,128)S(1)}, u32[]{:S(2)}, u32[]{:S(2)}) collective-permute-start(f32[6,5,8,128]{3,2,1,0:T(8,128)S(1)} %get-tuple-element.26), channel_id=1, source_target_pairs={{0,2},{1,3},{2,4},{3,5},{4,6},{5,7},{6,8},{7,9},{8,10},{9,11},{10,... | collective-permute-start | bytes 368648 | tf_op jit(solution)/shard_map/ppermute | solution.py:20
  84.2 1.5 %collective-permute-done.12.high2 = f32[6,5,8,128]{3,2,1,0:T(8,128)S(1)} collective-permute-done((f32[6,5,8,128]{3,2,1,0:T(8,128)S(1)}, f32[6,5,8,128]{3,2,1,0:T(8,128)S(1)}, u32[]{:S(2)}, u32[]{:S(2)}) %collective-permute-start.12) | collective-permute-done | bytes 122912 | tf_op jit(solution)/shard_map/ppermute | solution.py:20
  85.7 1.6 %collective-permute-done.11.low2 = f32[6,5,8,128]{3,2,1,0:T(8,128)S(1)} collective-permute-done((f32[6,5,8,128]{3,2,1,0:T(8,128)S(1)}, f32[6,5,8,128]{3,2,1,0:T(8,128)S(1)}, u32[]{:S(2)}, u32[]{:S(2)}) %collective-permute-start.11) | collective-permute-done | bytes 122912 | tf_op jit(solution)/shard_map/ppermute | solution.py:20
  87.3 0.0 collective-permute-done.10.high1
  87.3 0.0 collective-permute-done.9.low1
  87.3 1.8 %shard_map.74 = (f32[2,8,8,128]{3,2,1,0:T(8,128)S(1)}, f32[64,5,2,128]{3,2,1,0:T(2,128)S(1)}) custom-call(f32[8,5,8,128]{3,2,1,0:T(8,128)S(1)} %get-tuple-element.25.mine, f32[8,5,8,128]{3,2,1,0:T(8,128)S(1)} %collective-permute-done.9.low1, f32[8,5,8,128]{3,2,1,0:T(8,128)S(1)} %collective-permute-done.10.high1, ...), custom_call_target="tpu_custom_call" | custom-call | tf_op jit(solution)/shard_map/pallas_call | solution.py:28
  89.1 26.8 %all_to_all.16.gathered = f32[64,5,2,128]{3,2,1,0:T(2,128)S(1)} all-to-all(f32[64,5,2,128]{3,2,1,0:T(2,128)S(1)} %get-tuple-element.29), channel_id=1, replica_groups=mesh['ring'=4,'place'=8,'gy'=16] {'ring','gy'}, dimensions={0} | all-to-all | bytes 655360 | tf_op jit(solution)/shard_map/all_to_all | solution.py:540
  115.9 0.1 shard_map.75.refs_1_
  116.1 1.3 collective-permute-start.14
  117.4 4.0 %collective-permute-start.13 = (f32[4,160,128]{2,1,0:T(8,128)S(1)}, f32[4,160,128]{2,1,0:T(8,128)S(1)}, u32[]{:S(2)}, u32[]{:S(2)}) collective-permute-start(f32[4,160,128]{2,1,0:T(8,128)S(1)} %shard_map.75.refs_1_), channel_id=1, source_target_pairs={{0,16},{16,32},{32,48},{48,64},{64,80},{80,96},{96,112},{1,17},{17... | collective-permute-start | bytes 983048 | tf_op jit(solution)/shard_map/ppermute | solution.py:20
  121.4 5.4 %collective-permute-done.14.refs_2_ = f32[4,160,128]{2,1,0:T(8,128)S(1)} collective-permute-done((f32[4,160,128]{2,1,0:T(8,128)S(1)}, f32[4,160,128]{2,1,0:T(8,128)S(1)}, u32[]{:S(2)}, u32[]{:S(2)}) %collective-permute-start.14) | collective-permute-done | bytes 327712 | tf_op jit(solution)/shard_map/ppermute | solution.py:20
  126.8 0.9 collective-permute-done.13.refs_0_
  127.7 4.2 %shard_map.76 = f32[8,3,8,128]{3,2,1,0:T(8,128)S(1)} custom-call(f32[4,160,128]{2,1,0:T(8,128)S(1)} %collective-permute-done.13.refs_0_, f32[4,160,128]{2,1,0:T(8,128)S(1)} %shard_map.75.refs_1_, f32[4,160,128]{2,1,0:T(8,128)S(1)} %collective-permute-done.14.refs_2_, f32[2,8,8,128]{3,2,1,0:T(8,128)S(1)} %get-tuple-element.30.refs_3_, ...), custom_call_target="tpu_custom_call" | custom-call | tf_op jit(solution)/shard_map/pallas_call | solution.py:28
  132.0 13.2 %all_to_all.17.pieces = f32[8,3,8,128]{3,2,1,0:T(8,128)S(1)} all-to-all(f32[8,3,8,128]{3,2,1,0:T(8,128)S(1)} %shard_map.76), channel_id=1, replica_groups=mesh['ring'=4,'place'=8,'gy'=16] {'place'}, dimensions={0} | all-to-all | bytes 196608 | tf_op jit(solution)/shard_map/all_to_all | solution.py:547
  145.2 0.7 shard_map.77
  (3 shorter events, 0.1 us)
Async XLA Ops:
  32.9 23.2 %collective-permute-start.3 = (f32[8,5,4,8,128]{4,3,2,1,0:T(8,128)S(1)}, f32[8,5,4,8,128]{4,3,2,1,0:T(8,128)S(1)}, u32[]{:S(2)}, u32[]{:S(2)}) collective-permute-start(f32[8,5,4,8,128]{4,3,2,1,0:T(8,128)S(1)} %all_to_all.15.own), channel_id=1, source_target_pairs={{1,0},{2,1},{3,2},{4,3},{5,4},{6,5},{7,6},{8,7},{9,8},{10,9},{11,1... | collective-permute-start | bytes 1966088 | tf_op jit(solution)/shard_map/ppermute | solution.py:20
  36.9 23.7 %collective-permute-start.2 = (f32[8,5,4,8,128]{4,3,2,1,0:T(8,128)S(1)}, f32[8,5,4,8,128]{4,3,2,1,0:T(8,128)S(1)}, u32[]{:S(2)}, u32[]{:S(2)}) collective-permute-start(f32[8,5,4,8,128]{4,3,2,1,0:T(8,128)S(1)} %all_to_all.15.own), channel_id=1, source_target_pairs={{0,1},{1,2},{2,3},{3,4},{4,5},{5,6},{6,7},{7,8},{8,9},{9,10},{10,1... | collective-permute-start | bytes 1966088 | tf_op jit(solution)/shard_map/ppermute | solution.py:20
  40.1 9.2 %collective-permute-start.1 = (f32[41,8,128]{2,1,0:T(8,128)S(1)}, f32[41,8,128]{2,1,0:T(8,128)S(1)}, u32[]{:S(2)}, u32[]{:S(2)}) collective-permute-start(f32[41,8,128]{2,1,0:T(8,128)S(1)} %get-tuple-element.18), channel_id=1, source_target_pairs={{128,0},{256,128},{384,256},{129,1},{257,129},{385,257},{130,2},{2... | collective-permute-start | bytes 503816 | tf_op jit(solution)/shard_map/ppermute | solution.py:20
  41.4 7.9 %collective-permute-start = (f32[40,8,128]{2,1,0:T(8,128)S(1)}, f32[40,8,128]{2,1,0:T(8,128)S(1)}, u32[]{:S(2)}, u32[]{:S(2)}) collective-permute-start(f32[40,8,128]{2,1,0:T(8,128)S(1)} %get-tuple-element.17), channel_id=1, source_target_pairs={{0,128},{128,256},{256,384},{1,129},{129,257},{257,385},{2,130},{1... | collective-permute-start | bytes 491528 | tf_op jit(solution)/shard_map/ppermute | solution.py:20
  49.3 10.2 %collective-permute-start.4 = (f32[60,8,128]{2,1,0:T(8,128)S(1)}, f32[60,8,128]{2,1,0:T(8,128)S(1)}, u32[]{:S(2)}, u32[]{:S(2)}) collective-permute-start(f32[60,8,128]{2,1,0:T(8,128)S(1)} %get-tuple-element.19), channel_id=1, source_target_pairs={{0,1},{1,2},{2,3},{3,4},{4,5},{5,6},{6,7},{7,8},{8,9},{9,10},{10,1... | collective-permute-start | bytes 737288 | tf_op jit(solution)/shard_map/ppermute | solution.py:20
  52.9 7.7 %collective-permute-start.5 = (f32[60,8,128]{2,1,0:T(8,128)S(1)}, f32[60,8,128]{2,1,0:T(8,128)S(1)}, u32[]{:S(2)}, u32[]{:S(2)}) collective-permute-start(f32[60,8,128]{2,1,0:T(8,128)S(1)} %get-tuple-element.20), channel_id=1, source_target_pairs={{1,0},{2,1},{3,2},{4,3},{5,4},{6,5},{7,6},{8,7},{9,8},{10,9},{11,1... | collective-permute-start | bytes 737288 | tf_op jit(solution)/shard_map/ppermute | solution.py:20
  54.8 4.7 %collective-permute-start.6 = (f32[32,128]{1,0:T(8,128)S(1)}, f32[32,128]{1,0:T(8,128)S(1)}, u32[]{:S(2)}, u32[]{:S(2)}) collective-permute-start(f32[32,128]{1,0:T(8,128)S(1)} %get-tuple-element.21), channel_id=1, source_target_pairs={{2,0},{3,1},{4,2},{5,3},{6,4},{7,5},{8,6},{9,7},{10,8},{11,9},{12,... | collective-permute-start | bytes 49160 | tf_op jit(solution)/shard_map/ppermute | solution.py:20
  62.7 5.4 %collective-permute-start.7 = (f32[2,5,8,128]{3,2,1,0:T(8,128)S(1)}, f32[2,5,8,128]{3,2,1,0:T(8,128)S(1)}, u32[]{:S(2)}, u32[]{:S(2)}) collective-permute-start(f32[2,5,8,128]{3,2,1,0:T(8,128)S(1)} %get-tuple-element.23.last), channel_id=1, source_target_pairs={{0,128},{128,256},{256,384},{1,129},{129,257},{257,385},{2,130},{1... | collective-permute-start | bytes 122888 | tf_op jit(solution)/shard_map/ppermute | solution.py:20
  66.8 4.7 %collective-permute-start.8 = (f32[2,5,8,128]{3,2,1,0:T(8,128)S(1)}, f32[2,5,8,128]{3,2,1,0:T(8,128)S(1)}, u32[]{:S(2)}, u32[]{:S(2)}) collective-permute-start(f32[2,5,8,128]{3,2,1,0:T(8,128)S(1)} %get-tuple-element.24.first), channel_id=1, source_target_pairs={{128,0},{256,128},{384,256},{129,1},{257,129},{385,257},{130,2},{2... | collective-permute-start | bytes 122888 | tf_op jit(solution)/shard_map/ppermute | solution.py:20
  71.6 15.7 %collective-permute-start.10 = (f32[8,5,8,128]{3,2,1,0:T(8,128)S(1)}, f32[8,5,8,128]{3,2,1,0:T(8,128)S(1)}, u32[]{:S(2)}, u32[]{:S(2)}) collective-permute-start(f32[8,5,8,128]{3,2,1,0:T(8,128)S(1)} %get-tuple-element.25.mine), channel_id=1, source_target_pairs={{1,0},{2,1},{3,2},{4,3},{5,4},{6,5},{7,6},{8,7},{9,8},{10,9},{11,1... | collective-permute-start | bytes 491528 | tf_op jit(solution)/shard_map/ppermute | solution.py:20
  75.8 11.5 %collective-permute-start.9 = (f32[8,5,8,128]{3,2,1,0:T(8,128)S(1)}, f32[8,5,8,128]{3,2,1,0:T(8,128)S(1)}, u32[]{:S(2)}, u32[]{:S(2)}) collective-permute-start(f32[8,5,8,128]{3,2,1,0:T(8,128)S(1)} %get-tuple-element.25.mine), channel_id=1, source_target_pairs={{0,1},{1,2},{2,3},{3,4},{4,5},{5,6},{6,7},{7,8},{8,9},{9,10},{10,1... | collective-permute-start | bytes 491528 | tf_op jit(solution)/shard_map/ppermute | solution.py:20
  78.9 6.8 %collective-permute-start.12 = (f32[6,5,8,128]{3,2,1,0:T(8,128)S(1)}, f32[6,5,8,128]{3,2,1,0:T(8,128)S(1)}, u32[]{:S(2)}, u32[]{:S(2)}) collective-permute-start(f32[6,5,8,128]{3,2,1,0:T(8,128)S(1)} %get-tuple-element.26), channel_id=1, source_target_pairs={{2,0},{3,1},{4,2},{5,3},{6,4},{7,5},{8,6},{9,7},{10,8},{11,9},{12,... | collective-permute-start | bytes 368648 | tf_op jit(solution)/shard_map/ppermute | solution.py:20
  80.2 7.1 %collective-permute-start.11 = (f32[6,5,8,128]{3,2,1,0:T(8,128)S(1)}, f32[6,5,8,128]{3,2,1,0:T(8,128)S(1)}, u32[]{:S(2)}, u32[]{:S(2)}) collective-permute-start(f32[6,5,8,128]{3,2,1,0:T(8,128)S(1)} %get-tuple-element.26), channel_id=1, source_target_pairs={{0,2},{1,3},{2,4},{3,5},{4,6},{5,7},{6,8},{7,9},{8,10},{9,11},{10,... | collective-permute-start | bytes 368648 | tf_op jit(solution)/shard_map/ppermute | solution.py:20
  116.1 10.8 %collective-permute-start.14 = (f32[4,160,128]{2,1,0:T(8,128)S(1)}, f32[4,160,128]{2,1,0:T(8,128)S(1)}, u32[]{:S(2)}, u32[]{:S(2)}) collective-permute-start(f32[4,160,128]{2,1,0:T(8,128)S(1)} %shard_map.75.refs_1_), channel_id=1, source_target_pairs={{16,0},{32,16},{48,32},{64,48},{80,64},{96,80},{112,96},{17,1},{33... | collective-permute-start | bytes 983048 | tf_op jit(solution)/shard_map/ppermute | solution.py:20
  117.4 10.4 %collective-permute-start.13 = (f32[4,160,128]{2,1,0:T(8,128)S(1)}, f32[4,160,128]{2,1,0:T(8,128)S(1)}, u32[]{:S(2)}, u32[]{:S(2)}) collective-permute-start(f32[4,160,128]{2,1,0:T(8,128)S(1)} %shard_map.75.refs_1_), channel_id=1, source_target_pairs={{0,16},{16,32},{32,48},{48,64},{64,80},{80,96},{96,112},{1,17},{17... | collective-permute-start | bytes 983048 | tf_op jit(solution)/shard_map/ppermute | solution.py:20

commit v9 on v8

--- a/solution.py
+++ b/solution.py
@@ -335,19 +335,31 @@
         low_out[k] = total[2 * k : 2 * k + 2]
 
 
-def mid_message_kernel(low, first, last, high, near, far):
-    tiles = [ref[s] for ref in (low, first, last, high) for s in range(2)]
+def mid_message_kernel(low, first, last, high, out):
+    for n, ref in enumerate((low, first, last, high)):
+        for s in range(2):
+            out[2 * n + s] = ref[s]
+
+
+def chip_message_kernel(other, own, out):
     for s in range(8):
-        near[s] = tiles[s]
-        if 0 < s < 7:
-            far[s - 1] = tiles[s]
-
-
-def mid_kernel(mine, low1, high1, low2, high2, own, low_coefs, level_out, low_out, co, r, b):
+        out[s] = other[s]
+    for s in range(6):
+        out[8 + s] = own[s + 1]
+
+
+def inner_tiles_kernel(values, out):
+    for s in range(6):
+        out[s] = values[s + 1]
+
+
+def mid_kernel(mine, beside, across, beyond, own, low_coefs, level_out, low_out, co, r, b):
+    upper = lax.rem(lax.axis_index("gy"), 2) == 1
     q0 = even_mask((24, 128))
     _, lane = iotas((8, 128))
     keep = low_rows((8, 128))
     zero = jnp.zeros((8, 128), F32)
+    lower_core = lane < jnp.where(upper, 0, 128)
     clear_guards(r, b, 16)
 
     def part(tile, p):
@@ -355,10 +367,13 @@
 
     def planes(p, a):
         t = p // 2
-        c, h1, w1 = part(mine[t, a], p), part(high1[t, a], p), part(low1[t, a], p)
-        inner = 0 < t < 7
-        h2 = part(high2[t - 1, a], p) if inner else zero
-        w2 = part(low2[t - 1, a], p) if inner else zero
+        c = part(mine[t, a], p)
+        near = part(beside[t, a], p), part(across[t, a], p)
+        h1, w1 = halves(lower_core, *near)
+        h2, w2 = zero, zero
+        if 0 < t < 7:
+            far = part(beyond[t - 1, a], p), part(across[t + 7, a], p)
+            h2, w2 = halves(lower_core, *far)
         e0 = [jnp.where(keep, c, half(h1)), jnp.where(keep, h2, 0.0), jnp.where(keep, w2, half(w1))]
         e1 = [jnp.where(keep, half(c), h1), jnp.where(keep, half(h2), 0.0), jnp.where(keep, half(w2), w1)]
         return jnp.concatenate(e0, 0), jnp.concatenate(e1, 0)
@@ -525,17 +540,19 @@
     )(own, x_low, x_high, y_low, y_high, corner_low, corner_high, beyond_y, mid_coefs)
 
     low, high = shifted(mid_last, "ring", 1), shifted(mid_first, "ring", -1)
-    near, far = call(
-        mid_message_kernel, [(8, 5, 8, 128), (6, 5, 8, 128)]
-    )(low, mid_first, mid_last, high)
+    (mid,) = call(mid_message_kernel, [(8, 5, 8, 128)])(low, mid_first, mid_last, high)
+    cores = [(i, i ^ 1) for i in range(count_y)]
+    chips = [(i, i + 2 - 4 * (i % 2)) for i in range(count_y) if 0 <= i + 2 - 4 * (i % 2) < count_y]
+    beside = lax.ppermute(mid, "gy", cores)
+    (message,) = call(chip_message_kernel, [(14, 5, 8, 128)])(beside, mid)
+    across = lax.ppermute(message, "gy", chips)
+    (inner,) = call(inner_tiles_kernel, [(6, 5, 8, 128)])(across)
+    beyond = lax.ppermute(inner, "gy", cores)
     level, low = call(
         mid_kernel,
         [(2, 8, 8, 128), (rings * count_y, 5, 2, 128)],
         [(17, 16, 24, 128), (18, 24, 128), (18, 24, 128)],
-    )(
-        near, shifted(near, "gy", 1), shifted(near, "gy", -1),
-        shifted(far, "gy", 2), shifted(far, "gy", -2), mid_own, low_coefs,
-    )
+    )(mid, beside, across, beyond, mid_own, low_coefs)
 
     low = lax.all_to_all(low, ("ring", "gy"), 0, 0, tiled=True)
     (own,) = call(whole_y_kernel, [(rings, 160, 128)])(low)

time: 148 us -> 147 us (level)
  waiting for transfers between devices: 20.3 us -> 25.2 us
  starting transfers between devices: 42.4 us -> 37.9 us
    ppermute x15 -> x11, starting transfers between devices: 42.4 us -> 29.8 us  [shifted(): lax.ppermute(values, name, [(i, i + steps) for i in range(lead, last)])]
    ppermute x0 -> x3, waiting for transfers between devices: none -> 8.04 us  [the longest x1 6.08 us: cycle(): across = lax.ppermute(message, 'gy', chips)]
    ppermute x0 -> x3, starting transfers between devices: none -> 8.03 us  [the longest x1 4.21 us: cycle(): beside = lax.ppermute(mid, 'gy', cores)]
    ppermute x15 -> x11, waiting for transfers between devices: 20.3 us -> 17.2 us  [shifted(): lax.ppermute(values, name, [(i, i + steps) for i in range(lead, last)])]
    pallas_call x10 -> x12, Pallas kernels: 12.3 us -> 12.3 us  [run(): pl.pallas_call(kernel, out_shape=[jax.ShapeDtypeStruct(s, F32) for s in o...]
  transfers between devices with their start and end apart: 15 -> 14, of which waited for: 8 -> 9; matrix products, arithmetic and copies ran while one was open for 0% -> 0% of each run, Pallas kernels for 1% -> 1%
where the time goes in v9:
time: 147 us; the launch traced here: 145 us
  blocking collectives  68.8 us (47%)
  starting transfers between devices  37.9 us (26%)
  waiting for transfers between devices  25.2 us (17%)
  Pallas kernels  12.3 us (8%)
    all_to_all x1, blocking collectives, cycle(): own = lax.all_to_all(own, 'place', 0, 0, tiled=True)  30.1 us
    ppermute x11, starting transfers between devices, shifted(): lax.ppermute(values, name, [(i, i + steps) for i in range(lead, last)])  29.8 us
    all_to_all x1, blocking collectives, cycle(): low = lax.all_to_all(low, ('ring', 'gy'), 0, 0, tiled=True)  25.5 us
    ppermute x11, waiting for transfers between devices, shifted(): lax.ppermute(values, name, [(i, i + steps) for i in range(lead, last)])  17.2 us
    all_to_all x1, blocking collectives, cycle(): pieces = lax.all_to_all(pieces, 'place', 0, 0, tiled=True)  13.2 us
    pallas_call x12, Pallas kernels, run(): pl.pallas_call(kernel, out_shape=[jax.ShapeDtypeStruct(s, F32) for s in o...  12.3 us
    ppermute x1, waiting for transfers between devices, cycle(): across = lax.ppermute(message, 'gy', chips)  6.08 us
    ppermute x1, starting transfers between devices, cycle(): beside = lax.ppermute(mid, 'gy', cores)  4.21 us
  transfers between devices with their start and end apart: 14, of which 9 were waited for; matrix products, arithmetic and copies ran while one was open for 0% of the time, Pallas kernels for 1%

profile of v9, /device:TPU:1, one launch (start us, length us, event | category | flops | bytes accessed | tf_op | source)
XLA Modules:
  0.0 145.0 jit_solution(17678824439771263920)
XLA Ops:
  0.6 2.2 %shard_map.68 = f32[8,5,4,8,128]{4,3,2,1,0:T(8,128)} custom-call(f32[4,8,512]{2,1,0:T(8,128)} %refs_0_.1, f32[4,8,512]{2,1,0:T(8,128)} %refs_1_.1, f32[4,8,512]{2,1,0:T(8,128)} %refs_2_.1, f32[4,8,512]{2,1,0:T(8,128)} %refs_3_.1, f32[4,8,512]{2,1,0:T(8,128)} %refs_4_.1), custom_call_target="tpu_custom_call" | custom-call | tf_op jit(solution)/shard_map/pallas_call | solution.py:28
  2.9 30.1 %all_to_all.15.own = f32[8,5,4,8,128]{4,3,2,1,0:T(8,128)S(1)} all-to-all(f32[8,5,4,8,128]{4,3,2,1,0:T(8,128)} %shard_map.68), channel_id=1, replica_groups=mesh['ring'=4,'place'=8,'gy'=16] {'place'}, dimensions={0} | all-to-all | bytes 1310720 | tf_op jit(solution)/shard_map/all_to_all | solution.py:521
  32.9 3.9 %collective-permute-start.3 = (f32[8,5,4,8,128]{4,3,2,1,0:T(8,128)S(1)}, f32[8,5,4,8,128]{4,3,2,1,0:T(8,128)S(1)}, u32[]{:S(2)}, u32[]{:S(2)}) collective-permute-start(f32[8,5,4,8,128]{4,3,2,1,0:T(8,128)S(1)} %all_to_all.15.own), channel_id=1, source_target_pairs={{1,0},{2,1},{3,2},{4,3},{5,4},{6,5},{7,6},{8,7},{9,8},{10,9},{11,1... | collective-permute-start | bytes 1966088 | tf_op jit(solution)/shard_map/ppermute | solution.py:20
  36.9 3.1 %collective-permute-start.2 = (f32[8,5,4,8,128]{4,3,2,1,0:T(8,128)S(1)}, f32[8,5,4,8,128]{4,3,2,1,0:T(8,128)S(1)}, u32[]{:S(2)}, u32[]{:S(2)}) collective-permute-start(f32[8,5,4,8,128]{4,3,2,1,0:T(8,128)S(1)} %all_to_all.15.own), channel_id=1, source_target_pairs={{0,1},{1,2},{2,3},{3,4},{4,5},{5,6},{6,7},{7,8},{8,9},{9,10},{10,1... | collective-permute-start | bytes 1966088 | tf_op jit(solution)/shard_map/ppermute | solution.py:20
  40.0 1.3 collective-permute-start.1
  41.3 4.0 %collective-permute-start = (f32[40,8,128]{2,1,0:T(8,128)S(1)}, f32[40,8,128]{2,1,0:T(8,128)S(1)}, u32[]{:S(2)}, u32[]{:S(2)}) collective-permute-start(f32[40,8,128]{2,1,0:T(8,128)S(1)} %get-tuple-element.15), channel_id=1, source_target_pairs={{0,128},{128,256},{256,384},{1,129},{129,257},{257,385},{2,130},{1... | collective-permute-start | bytes 491528 | tf_op jit(solution)/shard_map/ppermute | solution.py:20
  45.3 3.9 %collective-permute-done.low.x_low = f32[40,8,128]{2,1,0:T(8,128)S(1)} collective-permute-done((f32[40,8,128]{2,1,0:T(8,128)S(1)}, f32[40,8,128]{2,1,0:T(8,128)S(1)}, u32[]{:S(2)}, u32[]{:S(2)}) %collective-permute-start) | collective-permute-done | bytes 163872 | tf_op jit(solution)/shard_map/ppermute | solution.py:20
  49.2 0.0 collective-permute-done.1.high.x_high
  49.3 3.6 %collective-permute-start.4 = (f32[60,8,128]{2,1,0:T(8,128)S(1)}, f32[60,8,128]{2,1,0:T(8,128)S(1)}, u32[]{:S(2)}, u32[]{:S(2)}) collective-permute-start(f32[60,8,128]{2,1,0:T(8,128)S(1)} %get-tuple-element.17), channel_id=1, source_target_pairs={{0,1},{1,2},{2,3},{3,4},{4,5},{5,6},{6,7},{7,8},{8,9},{9,10},{10,1... | collective-permute-start | bytes 737288 | tf_op jit(solution)/shard_map/ppermute | solution.py:20
  52.9 1.9 %collective-permute-start.5 = (f32[60,8,128]{2,1,0:T(8,128)S(1)}, f32[60,8,128]{2,1,0:T(8,128)S(1)}, u32[]{:S(2)}, u32[]{:S(2)}) collective-permute-start(f32[60,8,128]{2,1,0:T(8,128)S(1)} %get-tuple-element.18), channel_id=1, source_target_pairs={{1,0},{2,1},{3,2},{4,3},{5,4},{6,5},{7,6},{8,7},{9,8},{10,9},{11,1... | collective-permute-start | bytes 737288 | tf_op jit(solution)/shard_map/ppermute | solution.py:20
  54.8 1.3 collective-permute-start.6
  56.1 0.0 collective-permute-done.3.y_high
  56.1 0.9 shard_map.71
  57.1 2.4 %collective-permute-done.6.beyond_y = f32[32,128]{1,0:T(8,128)S(1)} collective-permute-done((f32[32,128]{1,0:T(8,128)S(1)}, f32[32,128]{1,0:T(8,128)S(1)}, u32[]{:S(2)}, u32[]{:S(2)}) %collective-permute-start.6) | collective-permute-done | bytes 16416 | tf_op jit(solution)/shard_map/ppermute | solution.py:20
  59.5 0.0 collective-permute-done.4.corner_low
  59.5 1.1 collective-permute-done.5.corner_high
  60.6 0.0 collective-permute-done.2.y_low
  60.6 2.1 %shard_map.72 = (f32[2,16,8,128]{3,2,1,0:T(8,128)S(1)}, f32[2,5,8,128]{3,2,1,0:T(8,128)S(1)}, f32[2,5,8,128]{3,2,1,0:T(8,128)S(1)}) custom-call(f32[8,5,4,8,128]{4,3,2,1,0:T(8,128)S(1)} %all_to_all.15.own, f32[40,8,128]{2,1,0:T(8,128)S(1)} %collective-permute-done.low.x_low, f32[41,8,128]{2,1,0:T(8,128)S(1)} %collective-permute-done.1.high.x_high, ...), custom_call_target="tpu_custom_call" | custom-call | tf_op jit(solution)/shard_map/pallas_call | solution.py:28
  62.7 4.1 %collective-permute-start.7 = (f32[2,5,8,128]{3,2,1,0:T(8,128)S(1)}, f32[2,5,8,128]{3,2,1,0:T(8,128)S(1)}, u32[]{:S(2)}, u32[]{:S(2)}) collective-permute-start(f32[2,5,8,128]{3,2,1,0:T(8,128)S(1)} %get-tuple-element.21.last), channel_id=1, source_target_pairs={{0,128},{128,256},{256,384},{1,129},{129,257},{257,385},{2,130},{1... | collective-permute-start | bytes 122888 | tf_op jit(solution)/shard_map/ppermute | solution.py:20
  66.8 1.3 collective-permute-start.8
  68.1 0.0 collective-permute-done.7.low
  68.1 3.4 %collective-permute-done.8.high = f32[2,5,8,128]{3,2,1,0:T(8,128)S(1)} collective-permute-done((f32[2,5,8,128]{3,2,1,0:T(8,128)S(1)}, f32[2,5,8,128]{3,2,1,0:T(8,128)S(1)}, u32[]{:S(2)}, u32[]{:S(2)}) %collective-permute-start.8) | collective-permute-done | bytes 40992 | tf_op jit(solution)/shard_map/ppermute | solution.py:20
  71.6 4.2 %collective-permute-start.9 = (f32[8,5,8,128]{3,2,1,0:T(8,128)S(1)}, f32[8,5,8,128]{3,2,1,0:T(8,128)S(1)}, u32[]{:S(2)}, u32[]{:S(2)}) collective-permute-start(f32[8,5,8,128]{3,2,1,0:T(8,128)S(1)} %shard_map.73.own.mine), channel_id=1, source_target_pairs={{0,1},{1,0},{2,3},{3,2},{4,5},{5,4},{6,7},{7,6},{8,9},{9,8},{10,11... | collective-permute-start | bytes 491528 | tf_op jit(solution)/shard_map/ppermute | solution.py:546
  75.8 1.0 collective-permute-done.9.other.beside
  76.8 1.3 collective-permute-start.10
  78.1 6.1 %collective-permute-done.10.values.across = f32[14,5,8,128]{3,2,1,0:T(8,128)S(1)} collective-permute-done((f32[14,5,8,128]{3,2,1,0:T(8,128)S(1)}, f32[14,5,8,128]{3,2,1,0:T(8,128)S(1)}, u32[]{:S(2)}, u32[]{:S(2)}) %collective-permute-start.10) | collective-permute-done | bytes 286752 | tf_op jit(solution)/shard_map/ppermute | solution.py:548
  84.2 2.5 %collective-permute-start.11 = (f32[6,5,8,128]{3,2,1,0:T(8,128)S(1)}, f32[6,5,8,128]{3,2,1,0:T(8,128)S(1)}, u32[]{:S(2)}, u32[]{:S(2)}) collective-permute-start(f32[6,5,8,128]{3,2,1,0:T(8,128)S(1)} %shard_map.75), channel_id=1, source_target_pairs={{0,1},{1,0},{2,3},{3,2},{4,5},{5,4},{6,7},{7,6},{8,9},{9,8},{10,11... | collective-permute-start | bytes 368648 | tf_op jit(solution)/shard_map/ppermute | solution.py:550
  86.7 1.0 collective-permute-done.11.beyond
  87.7 1.8 %shard_map.76 = (f32[2,8,8,128]{3,2,1,0:T(8,128)S(1)}, f32[64,5,2,128]{3,2,1,0:T(2,128)S(1)}) custom-call(f32[8,5,8,128]{3,2,1,0:T(8,128)S(1)} %shard_map.73.own.mine, f32[8,5,8,128]{3,2,1,0:T(8,128)S(1)} %collective-permute-done.9.other.beside, f32[14,5,8,128]{3,2,1,0:T(8,128)S(1)} %collective-permute-done.10.values.across, ...), custom_call_target="tpu_custom_call" | custom-call | tf_op jit(solution)/shard_map/pallas_call | solution.py:28
  89.5 25.5 %all_to_all.16.gathered = f32[64,5,2,128]{3,2,1,0:T(2,128)S(1)} all-to-all(f32[64,5,2,128]{3,2,1,0:T(2,128)S(1)} %get-tuple-element.25), channel_id=1, replica_groups=mesh['ring'=4,'place'=8,'gy'=16] {'ring','gy'}, dimensions={0} | all-to-all | bytes 655360 | tf_op jit(solution)/shard_map/all_to_all | solution.py:557
  115.0 0.1 shard_map.77.refs_1_
  115.1 1.3 collective-permute-start.13
  116.4 4.0 %collective-permute-start.12 = (f32[4,160,128]{2,1,0:T(8,128)S(1)}, f32[4,160,128]{2,1,0:T(8,128)S(1)}, u32[]{:S(2)}, u32[]{:S(2)}) collective-permute-start(f32[4,160,128]{2,1,0:T(8,128)S(1)} %shard_map.77.refs_1_), channel_id=1, source_target_pairs={{0,16},{16,32},{32,48},{48,64},{64,80},{80,96},{96,112},{1,17},{17... | collective-permute-start | bytes 983048 | tf_op jit(solution)/shard_map/ppermute | solution.py:20
  120.5 5.4 %collective-permute-done.13.refs_2_ = f32[4,160,128]{2,1,0:T(8,128)S(1)} collective-permute-done((f32[4,160,128]{2,1,0:T(8,128)S(1)}, f32[4,160,128]{2,1,0:T(8,128)S(1)}, u32[]{:S(2)}, u32[]{:S(2)}) %collective-permute-start.13) | collective-permute-done | bytes 327712 | tf_op jit(solution)/shard_map/ppermute | solution.py:20
  125.9 0.9 collective-permute-done.12.refs_0_
  126.8 4.2 %shard_map.78 = f32[8,3,8,128]{3,2,1,0:T(8,128)S(1)} custom-call(f32[4,160,128]{2,1,0:T(8,128)S(1)} %collective-permute-done.12.refs_0_, f32[4,160,128]{2,1,0:T(8,128)S(1)} %shard_map.77.refs_1_, f32[4,160,128]{2,1,0:T(8,128)S(1)} %collective-permute-done.13.refs_2_, f32[2,8,8,128]{3,2,1,0:T(8,128)S(1)} %get-tuple-element.26.refs_3_, ...), custom_call_target="tpu_custom_call" | custom-call | tf_op jit(solution)/shard_map/pallas_call | solution.py:28
  131.1 13.2 %all_to_all.17.pieces = f32[8,3,8,128]{3,2,1,0:T(8,128)S(1)} all-to-all(f32[8,3,8,128]{3,2,1,0:T(8,128)S(1)} %shard_map.78), channel_id=1, replica_groups=mesh['ring'=4,'place'=8,'gy'=16] {'place'}, dimensions={0} | all-to-all | bytes 196608 | tf_op jit(solution)/shard_map/all_to_all | solution.py:564
  144.2 0.7 shard_map.79
  (5 shorter events, 0.1 us)
Async XLA Ops:
  32.9 23.2 %collective-permute-start.3 = (f32[8,5,4,8,128]{4,3,2,1,0:T(8,128)S(1)}, f32[8,5,4,8,128]{4,3,2,1,0:T(8,128)S(1)}, u32[]{:S(2)}, u32[]{:S(2)}) collective-permute-start(f32[8,5,4,8,128]{4,3,2,1,0:T(8,128)S(1)} %all_to_all.15.own), channel_id=1, source_target_pairs={{1,0},{2,1},{3,2},{4,3},{5,4},{6,5},{7,6},{8,7},{9,8},{10,9},{11,1... | collective-permute-start | bytes 1966088 | tf_op jit(solution)/shard_map/ppermute | solution.py:20
  36.9 23.7 %collective-permute-start.2 = (f32[8,5,4,8,128]{4,3,2,1,0:T(8,128)S(1)}, f32[8,5,4,8,128]{4,3,2,1,0:T(8,128)S(1)}, u32[]{:S(2)}, u32[]{:S(2)}) collective-permute-start(f32[8,5,4,8,128]{4,3,2,1,0:T(8,128)S(1)} %all_to_all.15.own), channel_id=1, source_target_pairs={{0,1},{1,2},{2,3},{3,4},{4,5},{5,6},{6,7},{7,8},{8,9},{9,10},{10,1... | collective-permute-start | bytes 1966088 | tf_op jit(solution)/shard_map/ppermute | solution.py:20
  40.0 9.2 %collective-permute-start.1 = (f32[41,8,128]{2,1,0:T(8,128)S(1)}, f32[41,8,128]{2,1,0:T(8,128)S(1)}, u32[]{:S(2)}, u32[]{:S(2)}) collective-permute-start(f32[41,8,128]{2,1,0:T(8,128)S(1)} %get-tuple-element.16), channel_id=1, source_target_pairs={{128,0},{256,128},{384,256},{129,1},{257,129},{385,257},{130,2},{2... | collective-permute-start | bytes 503816 | tf_op jit(solution)/shard_map/ppermute | solution.py:20
  41.3 7.9 %collective-permute-start = (f32[40,8,128]{2,1,0:T(8,128)S(1)}, f32[40,8,128]{2,1,0:T(8,128)S(1)}, u32[]{:S(2)}, u32[]{:S(2)}) collective-permute-start(f32[40,8,128]{2,1,0:T(8,128)S(1)} %get-tuple-element.15), channel_id=1, source_target_pairs={{0,128},{128,256},{256,384},{1,129},{129,257},{257,385},{2,130},{1... | collective-permute-start | bytes 491528 | tf_op jit(solution)/shard_map/ppermute | solution.py:20
  49.3 10.2 %collective-permute-start.4 = (f32[60,8,128]{2,1,0:T(8,128)S(1)}, f32[60,8,128]{2,1,0:T(8,128)S(1)}, u32[]{:S(2)}, u32[]{:S(2)}) collective-permute-start(f32[60,8,128]{2,1,0:T(8,128)S(1)} %get-tuple-element.17), channel_id=1, source_target_pairs={{0,1},{1,2},{2,3},{3,4},{4,5},{5,6},{6,7},{7,8},{8,9},{9,10},{10,1... | collective-permute-start | bytes 737288 | tf_op jit(solution)/shard_map/ppermute | solution.py:20
  52.9 7.7 %collective-permute-start.5 = (f32[60,8,128]{2,1,0:T(8,128)S(1)}, f32[60,8,128]{2,1,0:T(8,128)S(1)}, u32[]{:S(2)}, u32[]{:S(2)}) collective-permute-start(f32[60,8,128]{2,1,0:T(8,128)S(1)} %get-tuple-element.18), channel_id=1, source_target_pairs={{1,0},{2,1},{3,2},{4,3},{5,4},{6,5},{7,6},{8,7},{9,8},{10,9},{11,1... | collective-permute-start | bytes 737288 | tf_op jit(solution)/shard_map/ppermute | solution.py:20
  54.8 4.7 %collective-permute-start.6 = (f32[32,128]{1,0:T(8,128)S(1)}, f32[32,128]{1,0:T(8,128)S(1)}, u32[]{:S(2)}, u32[]{:S(2)}) collective-permute-start(f32[32,128]{1,0:T(8,128)S(1)} %get-tuple-element.19), channel_id=1, source_target_pairs={{2,0},{3,1},{4,2},{5,3},{6,4},{7,5},{8,6},{9,7},{10,8},{11,9},{12,... | collective-permute-start | bytes 49160 | tf_op jit(solution)/shard_map/ppermute | solution.py:20
  62.7 5.4 %collective-permute-start.7 = (f32[2,5,8,128]{3,2,1,0:T(8,128)S(1)}, f32[2,5,8,128]{3,2,1,0:T(8,128)S(1)}, u32[]{:S(2)}, u32[]{:S(2)}) collective-permute-start(f32[2,5,8,128]{3,2,1,0:T(8,128)S(1)} %get-tuple-element.21.last), channel_id=1, source_target_pairs={{0,128},{128,256},{256,384},{1,129},{129,257},{257,385},{2,130},{1... | collective-permute-start | bytes 122888 | tf_op jit(solution)/shard_map/ppermute | solution.py:20
  66.8 4.7 %collective-permute-start.8 = (f32[2,5,8,128]{3,2,1,0:T(8,128)S(1)}, f32[2,5,8,128]{3,2,1,0:T(8,128)S(1)}, u32[]{:S(2)}, u32[]{:S(2)}) collective-permute-start(f32[2,5,8,128]{3,2,1,0:T(8,128)S(1)} %get-tuple-element.22.first), channel_id=1, source_target_pairs={{128,0},{256,128},{384,256},{129,1},{257,129},{385,257},{130,2},{2... | collective-permute-start | bytes 122888 | tf_op jit(solution)/shard_map/ppermute | solution.py:20
  71.6 5.2 %collective-permute-start.9 = (f32[8,5,8,128]{3,2,1,0:T(8,128)S(1)}, f32[8,5,8,128]{3,2,1,0:T(8,128)S(1)}, u32[]{:S(2)}, u32[]{:S(2)}) collective-permute-start(f32[8,5,8,128]{3,2,1,0:T(8,128)S(1)} %shard_map.73.own.mine), channel_id=1, source_target_pairs={{0,1},{1,0},{2,3},{3,2},{4,5},{5,4},{6,7},{7,6},{8,9},{9,8},{10,11... | collective-permute-start | bytes 491528 | tf_op jit(solution)/shard_map/ppermute | solution.py:546
  76.8 7.4 %collective-permute-start.10 = (f32[14,5,8,128]{3,2,1,0:T(8,128)S(1)}, f32[14,5,8,128]{3,2,1,0:T(8,128)S(1)}, u32[]{:S(2)}, u32[]{:S(2)}) collective-permute-start(f32[14,5,8,128]{3,2,1,0:T(8,128)S(1)} %shard_map.74), channel_id=1, source_target_pairs={{0,2},{2,4},{3,1},{4,6},{5,3},{6,8},{7,5},{8,10},{9,7},{10,12},{11... | collective-permute-start | bytes 860168 | tf_op jit(solution)/shard_map/ppermute | solution.py:548
  84.2 3.5 %collective-permute-start.11 = (f32[6,5,8,128]{3,2,1,0:T(8,128)S(1)}, f32[6,5,8,128]{3,2,1,0:T(8,128)S(1)}, u32[]{:S(2)}, u32[]{:S(2)}) collective-permute-start(f32[6,5,8,128]{3,2,1,0:T(8,128)S(1)} %shard_map.75), channel_id=1, source_target_pairs={{0,1},{1,0},{2,3},{3,2},{4,5},{5,4},{6,7},{7,6},{8,9},{9,8},{10,11... | collective-permute-start | bytes 368648 | tf_op jit(solution)/shard_map/ppermute | solution.py:550
  115.1 10.8 %collective-permute-start.13 = (f32[4,160,128]{2,1,0:T(8,128)S(1)}, f32[4,160,128]{2,1,0:T(8,128)S(1)}, u32[]{:S(2)}, u32[]{:S(2)}) collective-permute-start(f32[4,160,128]{2,1,0:T(8,128)S(1)} %shard_map.77.refs_1_), channel_id=1, source_target_pairs={{16,0},{32,16},{48,32},{64,48},{80,64},{96,80},{112,96},{17,1},{33... | collective-permute-start | bytes 983048 | tf_op jit(solution)/shard_map/ppermute | solution.py:20
  116.4 10.4 %collective-permute-start.12 = (f32[4,160,128]{2,1,0:T(8,128)S(1)}, f32[4,160,128]{2,1,0:T(8,128)S(1)}, u32[]{:S(2)}, u32[]{:S(2)}) collective-permute-start(f32[4,160,128]{2,1,0:T(8,128)S(1)} %shard_map.77.refs_1_), channel_id=1, source_target_pairs={{0,16},{16,32},{32,48},{48,64},{64,80},{80,96},{96,112},{1,17},{17... | collective-permute-start | bytes 983048 | tf_op jit(solution)/shard_map/ppermute | solution.py:20

commit v10 on v9

--- a/solution.py
+++ b/solution.py
@@ -335,22 +335,19 @@
         low_out[k] = total[2 * k : 2 * k + 2]
 
 
-def mid_message_kernel(low, first, last, high, out):
-    for n, ref in enumerate((low, first, last, high)):
-        for s in range(2):
-            out[2 * n + s] = ref[s]
-
-
-def chip_message_kernel(other, own, out):
+def mid_message_kernel(low, first, last, high, out, inner):
+    tiles = [ref[s] for ref in (low, first, last, high) for s in range(2)]
+    for s in range(8):
+        out[s] = tiles[s]
+        if 0 < s < 7:
+            inner[s - 1] = tiles[s]
+
+
+def chip_message_kernel(other, inner, out):
     for s in range(8):
         out[s] = other[s]
     for s in range(6):
-        out[8 + s] = own[s + 1]
-
-
-def inner_tiles_kernel(values, out):
-    for s in range(6):
-        out[s] = values[s + 1]
+        out[8 + s] = inner[s]
 
 
 def mid_kernel(mine, beside, across, beyond, own, low_coefs, level_out, low_out, co, r, b):
@@ -540,14 +537,15 @@
     )(own, x_low, x_high, y_low, y_high, corner_low, corner_high, beyond_y, mid_coefs)
 
     low, high = shifted(mid_last, "ring", 1), shifted(mid_first, "ring", -1)
-    (mid,) = call(mid_message_kernel, [(8, 5, 8, 128)])(low, mid_first, mid_last, high)
+    mid, inner = call(mid_message_kernel, [(8, 5, 8, 128), (6, 5, 8, 128)])(low, mid_first, mid_last, high)
     cores = [(i, i ^ 1) for i in range(count_y)]
-    chips = [(i, i + 2 - 4 * (i % 2)) for i in range(count_y) if 0 <= i + 2 - 4 * (i % 2) < count_y]
+    outward = [(i, i + 2 - 4 * (i % 2)) for i in range(count_y)]
+    inward = [(j, i) for i, j in outward]
+    chips, far = ([(i, j) for i, j in p if min(i, j) >= 0 and max(i, j) < count_y] for p in (outward, inward))
     beside = lax.ppermute(mid, "gy", cores)
-    (message,) = call(chip_message_kernel, [(14, 5, 8, 128)])(beside, mid)
+    beyond = lax.ppermute(inner, "gy", far)
+    (message,) = call(chip_message_kernel, [(14, 5, 8, 128)])(beside, inner)
     across = lax.ppermute(message, "gy", chips)
-    (inner,) = call(inner_tiles_kernel, [(6, 5, 8, 128)])(across)
-    beyond = lax.ppermute(inner, "gy", cores)
     level, low = call(
         mid_kernel,
         [(2, 8, 8, 128), (rings * count_y, 5, 2, 128)],

time: 147 us -> 145 us (0.986)
  waiting for transfers between devices: 25.2 us -> 21.3 us
    ppermute x1, waiting for transfers between devices: 6.08 us -> 0.01 us  [cycle(): across = lax.ppermute(message, 'gy', chips)]
    ppermute x1, waiting for transfers between devices: 0.95 us -> 3.11 us  [cycle(): beyond = lax.ppermute(inner, 'gy', far)]
    ppermute x1, starting transfers between devices: 2.52 us -> 3.99 us  [cycle(): beyond = lax.ppermute(inner, 'gy', far)]
    pallas_call x12 -> x11, Pallas kernels: 12.3 us -> 12.3 us  [run(): pl.pallas_call(kernel, out_shape=[jax.ShapeDtypeStruct(s, F32) for s in o...]
  transfers between devices with their start and end apart: 14 -> 14, of which waited for: 9 -> 8; matrix products, arithmetic and copies ran while one was open for 0% -> 0% of each run, Pallas kernels for 1% -> 1%
where the time goes in v10:
time: 145 us; the launch traced here: 143 us
  blocking collectives  68.7 us (47%)
  starting transfers between devices  39.3 us (27%)
  waiting for transfers between devices  21.3 us (15%)
  Pallas kernels  12.3 us (8%)
    all_to_all x1, blocking collectives, cycle(): own = lax.all_to_all(own, 'place', 0, 0, tiled=True)  30.1 us
    ppermute x11, starting transfers between devices, shifted(): lax.ppermute(values, name, [(i, i + steps) for i in range(lead, last)])  29.8 us
    all_to_all x1, blocking collectives, cycle(): low = lax.all_to_all(low, ('ring', 'gy'), 0, 0, tiled=True)  25.5 us
    ppermute x11, waiting for transfers between devices, shifted(): lax.ppermute(values, name, [(i, i + steps) for i in range(lead, last)])  17.2 us
    all_to_all x1, blocking collectives, cycle(): pieces = lax.all_to_all(pieces, 'place', 0, 0, tiled=True)  13.2 us
    pallas_call x11, Pallas kernels, run(): pl.pallas_call(kernel, out_shape=[jax.ShapeDtypeStruct(s, F32) for s in o...  12.3 us
    ppermute x1, starting transfers between devices, cycle(): beside = lax.ppermute(mid, 'gy', cores)  4.21 us
    ppermute x1, starting transfers between devices, cycle(): beyond = lax.ppermute(inner, 'gy', far)  3.99 us
  transfers between devices with their start and end apart: 14, of which 8 were waited for; matrix products, arithmetic and copies ran while one was open for 0% of the time, Pallas kernels for 1%

profile of v10, /device:TPU:1, one launch (start us, length us, event | category | flops | bytes accessed | tf_op | source)
XLA Modules:
  0.0 142.5 jit_solution(13540451229179260735)
XLA Ops:
  0.6 2.2 %shard_map.68 = f32[8,5,4,8,128]{4,3,2,1,0:T(8,128)} custom-call(f32[4,8,512]{2,1,0:T(8,128)} %refs_0_.1, f32[4,8,512]{2,1,0:T(8,128)} %refs_1_.1, f32[4,8,512]{2,1,0:T(8,128)} %refs_2_.1, f32[4,8,512]{2,1,0:T(8,128)} %refs_3_.1, f32[4,8,512]{2,1,0:T(8,128)} %refs_4_.1), custom_call_target="tpu_custom_call" | custom-call | tf_op jit(solution)/shard_map/pallas_call | solution.py:28
  2.9 30.1 %all_to_all.15.own = f32[8,5,4,8,128]{4,3,2,1,0:T(8,128)S(1)} all-to-all(f32[8,5,4,8,128]{4,3,2,1,0:T(8,128)} %shard_map.68), channel_id=1, replica_groups=mesh['ring'=4,'place'=8,'gy'=16] {'place'}, dimensions={0} | all-to-all | bytes 1310720 | tf_op jit(solution)/shard_map/all_to_all | solution.py:518
  33.0 3.9 %collective-permute-start.3 = (f32[8,5,4,8,128]{4,3,2,1,0:T(8,128)S(1)}, f32[8,5,4,8,128]{4,3,2,1,0:T(8,128)S(1)}, u32[]{:S(2)}, u32[]{:S(2)}) collective-permute-start(f32[8,5,4,8,128]{4,3,2,1,0:T(8,128)S(1)} %all_to_all.15.own), channel_id=1, source_target_pairs={{1,0},{2,1},{3,2},{4,3},{5,4},{6,5},{7,6},{8,7},{9,8},{10,9},{11,1... | collective-permute-start | bytes 1966088 | tf_op jit(solution)/shard_map/ppermute | solution.py:20
  36.9 3.1 %collective-permute-start.2 = (f32[8,5,4,8,128]{4,3,2,1,0:T(8,128)S(1)}, f32[8,5,4,8,128]{4,3,2,1,0:T(8,128)S(1)}, u32[]{:S(2)}, u32[]{:S(2)}) collective-permute-start(f32[8,5,4,8,128]{4,3,2,1,0:T(8,128)S(1)} %all_to_all.15.own), channel_id=1, source_target_pairs={{0,1},{1,2},{2,3},{3,4},{4,5},{5,6},{6,7},{7,8},{8,9},{9,10},{10,1... | collective-permute-start | bytes 1966088 | tf_op jit(solution)/shard_map/ppermute | solution.py:20
  40.1 1.3 collective-permute-start.1
  41.4 4.0 %collective-permute-start = (f32[40,8,128]{2,1,0:T(8,128)S(1)}, f32[40,8,128]{2,1,0:T(8,128)S(1)}, u32[]{:S(2)}, u32[]{:S(2)}) collective-permute-start(f32[40,8,128]{2,1,0:T(8,128)S(1)} %get-tuple-element.17), channel_id=1, source_target_pairs={{0,128},{128,256},{256,384},{1,129},{129,257},{257,385},{2,130},{1... | collective-permute-start | bytes 491528 | tf_op jit(solution)/shard_map/ppermute | solution.py:20
  45.4 3.9 %collective-permute-done.low.x_low = f32[40,8,128]{2,1,0:T(8,128)S(1)} collective-permute-done((f32[40,8,128]{2,1,0:T(8,128)S(1)}, f32[40,8,128]{2,1,0:T(8,128)S(1)}, u32[]{:S(2)}, u32[]{:S(2)}) %collective-permute-start) | collective-permute-done | bytes 163872 | tf_op jit(solution)/shard_map/ppermute | solution.py:20
  49.3 0.0 collective-permute-done.1.high.x_high
  49.3 3.6 %collective-permute-start.4 = (f32[60,8,128]{2,1,0:T(8,128)S(1)}, f32[60,8,128]{2,1,0:T(8,128)S(1)}, u32[]{:S(2)}, u32[]{:S(2)}) collective-permute-start(f32[60,8,128]{2,1,0:T(8,128)S(1)} %get-tuple-element.19), channel_id=1, source_target_pairs={{0,1},{1,2},{2,3},{3,4},{4,5},{5,6},{6,7},{7,8},{8,9},{9,10},{10,1... | collective-permute-start | bytes 737288 | tf_op jit(solution)/shard_map/ppermute | solution.py:20
  52.9 1.9 %collective-permute-start.5 = (f32[60,8,128]{2,1,0:T(8,128)S(1)}, f32[60,8,128]{2,1,0:T(8,128)S(1)}, u32[]{:S(2)}, u32[]{:S(2)}) collective-permute-start(f32[60,8,128]{2,1,0:T(8,128)S(1)} %get-tuple-element.20), channel_id=1, source_target_pairs={{1,0},{2,1},{3,2},{4,3},{5,4},{6,5},{7,6},{8,7},{9,8},{10,9},{11,1... | collective-permute-start | bytes 737288 | tf_op jit(solution)/shard_map/ppermute | solution.py:20
  54.8 1.3 collective-permute-start.6
  56.1 0.0 collective-permute-done.3.y_high
  56.1 0.9 shard_map.71
  57.1 2.4 %collective-permute-done.6.beyond_y = f32[32,128]{1,0:T(8,128)S(1)} collective-permute-done((f32[32,128]{1,0:T(8,128)S(1)}, f32[32,128]{1,0:T(8,128)S(1)}, u32[]{:S(2)}, u32[]{:S(2)}) %collective-permute-start.6) | collective-permute-done | bytes 16416 | tf_op jit(solution)/shard_map/ppermute | solution.py:20
  59.5 0.0 collective-permute-done.4.corner_low
  59.5 1.1 collective-permute-done.5.corner_high
  60.6 0.0 collective-permute-done.2.y_low
  60.6 2.1 %shard_map.72 = (f32[2,16,8,128]{3,2,1,0:T(8,128)S(1)}, f32[2,5,8,128]{3,2,1,0:T(8,128)S(1)}, f32[2,5,8,128]{3,2,1,0:T(8,128)S(1)}) custom-call(f32[8,5,4,8,128]{4,3,2,1,0:T(8,128)S(1)} %all_to_all.15.own, f32[40,8,128]{2,1,0:T(8,128)S(1)} %collective-permute-done.low.x_low, f32[41,8,128]{2,1,0:T(8,128)S(1)} %collective-permute-done.1.high.x_high, ...), custom_call_target="tpu_custom_call" | custom-call | tf_op jit(solution)/shard_map/pallas_call | solution.py:28
  62.7 4.1 %collective-permute-start.7 = (f32[2,5,8,128]{3,2,1,0:T(8,128)S(1)}, f32[2,5,8,128]{3,2,1,0:T(8,128)S(1)}, u32[]{:S(2)}, u32[]{:S(2)}) collective-permute-start(f32[2,5,8,128]{3,2,1,0:T(8,128)S(1)} %get-tuple-element.23.last), channel_id=1, source_target_pairs={{0,128},{128,256},{256,384},{1,129},{129,257},{257,385},{2,130},{1... | collective-permute-start | bytes 122888 | tf_op jit(solution)/shard_map/ppermute | solution.py:20
  66.8 1.3 collective-permute-start.8
  68.1 0.0 collective-permute-done.7.low
  68.2 3.4 %collective-permute-done.8.high = f32[2,5,8,128]{3,2,1,0:T(8,128)S(1)} collective-permute-done((f32[2,5,8,128]{3,2,1,0:T(8,128)S(1)}, f32[2,5,8,128]{3,2,1,0:T(8,128)S(1)}, u32[]{:S(2)}, u32[]{:S(2)}) %collective-permute-start.8) | collective-permute-done | bytes 40992 | tf_op jit(solution)/shard_map/ppermute | solution.py:20
  71.6 4.2 %collective-permute-start.9 = (f32[8,5,8,128]{3,2,1,0:T(8,128)S(1)}, f32[8,5,8,128]{3,2,1,0:T(8,128)S(1)}, u32[]{:S(2)}, u32[]{:S(2)}) collective-permute-start(f32[8,5,8,128]{3,2,1,0:T(8,128)S(1)} %get-tuple-element.25.mine), channel_id=1, source_target_pairs={{0,1},{1,0},{2,3},{3,2},{4,5},{5,4},{6,7},{7,6},{8,9},{9,8},{10,11... | collective-permute-start | bytes 491528 | tf_op jit(solution)/shard_map/ppermute | solution.py:545
  75.8 1.0 collective-permute-done.9.other.beside
  76.9 1.3 collective-permute-start.10
  78.2 4.0 %collective-permute-start.11 = (f32[6,5,8,128]{3,2,1,0:T(8,128)S(1)}, f32[6,5,8,128]{3,2,1,0:T(8,128)S(1)}, u32[]{:S(2)}, u32[]{:S(2)}) collective-permute-start(f32[6,5,8,128]{3,2,1,0:T(8,128)S(1)} %get-tuple-element.26.inner), channel_id=1, source_target_pairs={{2,0},{4,2},{1,3},{6,4},{3,5},{8,6},{5,7},{10,8},{7,9},{12,10},{9,... | collective-permute-start | bytes 368648 | tf_op jit(solution)/shard_map/ppermute | solution.py:546
  82.2 3.1 %collective-permute-done.11.beyond = f32[6,5,8,128]{3,2,1,0:T(8,128)S(1)} collective-permute-done((f32[6,5,8,128]{3,2,1,0:T(8,128)S(1)}, f32[6,5,8,128]{3,2,1,0:T(8,128)S(1)}, u32[]{:S(2)}, u32[]{:S(2)}) %collective-permute-start.11) | collective-permute-done | bytes 122912 | tf_op jit(solution)/shard_map/ppermute | solution.py:546
  85.3 0.0 collective-permute-done.10.across
  85.3 1.8 %shard_map.75 = (f32[2,8,8,128]{3,2,1,0:T(8,128)S(1)}, f32[64,5,2,128]{3,2,1,0:T(2,128)S(1)}) custom-call(f32[8,5,8,128]{3,2,1,0:T(8,128)S(1)} %get-tuple-element.25.mine, f32[8,5,8,128]{3,2,1,0:T(8,128)S(1)} %collective-permute-done.9.other.beside, f32[14,5,8,128]{3,2,1,0:T(8,128)S(1)} %collective-permute-done.10.across, ...), custom_call_target="tpu_custom_call" | custom-call | tf_op jit(solution)/shard_map/pallas_call | solution.py:28
  87.1 25.5 %all_to_all.16.gathered = f32[64,5,2,128]{3,2,1,0:T(2,128)S(1)} all-to-all(f32[64,5,2,128]{3,2,1,0:T(2,128)S(1)} %get-tuple-element.29), channel_id=1, replica_groups=mesh['ring'=4,'place'=8,'gy'=16] {'ring','gy'}, dimensions={0} | all-to-all | bytes 655360 | tf_op jit(solution)/shard_map/all_to_all | solution.py:555
  112.6 0.1 shard_map.76.refs_1_
  112.7 1.3 collective-permute-start.13
  114.0 4.0 %collective-permute-start.12 = (f32[4,160,128]{2,1,0:T(8,128)S(1)}, f32[4,160,128]{2,1,0:T(8,128)S(1)}, u32[]{:S(2)}, u32[]{:S(2)}) collective-permute-start(f32[4,160,128]{2,1,0:T(8,128)S(1)} %shard_map.76.refs_1_), channel_id=1, source_target_pairs={{0,16},{16,32},{32,48},{48,64},{64,80},{80,96},{96,112},{1,17},{17... | collective-permute-start | bytes 983048 | tf_op jit(solution)/shard_map/ppermute | solution.py:20
  118.0 5.4 %collective-permute-done.13.refs_2_ = f32[4,160,128]{2,1,0:T(8,128)S(1)} collective-permute-done((f32[4,160,128]{2,1,0:T(8,128)S(1)}, f32[4,160,128]{2,1,0:T(8,128)S(1)}, u32[]{:S(2)}, u32[]{:S(2)}) %collective-permute-start.13) | collective-permute-done | bytes 327712 | tf_op jit(solution)/shard_map/ppermute | solution.py:20
  123.5 0.9 collective-permute-done.12.refs_0_
  124.4 4.2 %shard_map.77 = f32[8,3,8,128]{3,2,1,0:T(8,128)S(1)} custom-call(f32[4,160,128]{2,1,0:T(8,128)S(1)} %collective-permute-done.12.refs_0_, f32[4,160,128]{2,1,0:T(8,128)S(1)} %shard_map.76.refs_1_, f32[4,160,128]{2,1,0:T(8,128)S(1)} %collective-permute-done.13.refs_2_, f32[2,8,8,128]{3,2,1,0:T(8,128)S(1)} %get-tuple-element.30.refs_3_, ...), custom_call_target="tpu_custom_call" | custom-call | tf_op jit(solution)/shard_map/pallas_call | solution.py:28
  128.6 13.2 %all_to_all.17.pieces = f32[8,3,8,128]{3,2,1,0:T(8,128)S(1)} all-to-all(f32[8,3,8,128]{3,2,1,0:T(8,128)S(1)} %shard_map.77), channel_id=1, replica_groups=mesh['ring'=4,'place'=8,'gy'=16] {'place'}, dimensions={0} | all-to-all | bytes 196608 | tf_op jit(solution)/shard_map/all_to_all | solution.py:562
  141.8 0.7 shard_map.78
  (4 shorter events, 0.1 us)
Async XLA Ops:
  33.0 23.2 %collective-permute-start.3 = (f32[8,5,4,8,128]{4,3,2,1,0:T(8,128)S(1)}, f32[8,5,4,8,128]{4,3,2,1,0:T(8,128)S(1)}, u32[]{:S(2)}, u32[]{:S(2)}) collective-permute-start(f32[8,5,4,8,128]{4,3,2,1,0:T(8,128)S(1)} %all_to_all.15.own), channel_id=1, source_target_pairs={{1,0},{2,1},{3,2},{4,3},{5,4},{6,5},{7,6},{8,7},{9,8},{10,9},{11,1... | collective-permute-start | bytes 1966088 | tf_op jit(solution)/shard_map/ppermute | solution.py:20
  36.9 23.7 %collective-permute-start.2 = (f32[8,5,4,8,128]{4,3,2,1,0:T(8,128)S(1)}, f32[8,5,4,8,128]{4,3,2,1,0:T(8,128)S(1)}, u32[]{:S(2)}, u32[]{:S(2)}) collective-permute-start(f32[8,5,4,8,128]{4,3,2,1,0:T(8,128)S(1)} %all_to_all.15.own), channel_id=1, source_target_pairs={{0,1},{1,2},{2,3},{3,4},{4,5},{5,6},{6,7},{7,8},{8,9},{9,10},{10,1... | collective-permute-start | bytes 1966088 | tf_op jit(solution)/shard_map/ppermute | solution.py:20
  40.1 9.2 %collective-permute-start.1 = (f32[41,8,128]{2,1,0:T(8,128)S(1)}, f32[41,8,128]{2,1,0:T(8,128)S(1)}, u32[]{:S(2)}, u32[]{:S(2)}) collective-permute-start(f32[41,8,128]{2,1,0:T(8,128)S(1)} %get-tuple-element.18), channel_id=1, source_target_pairs={{128,0},{256,128},{384,256},{129,1},{257,129},{385,257},{130,2},{2... | collective-permute-start | bytes 503816 | tf_op jit(solution)/shard_map/ppermute | solution.py:20
  41.4 7.9 %collective-permute-start = (f32[40,8,128]{2,1,0:T(8,128)S(1)}, f32[40,8,128]{2,1,0:T(8,128)S(1)}, u32[]{:S(2)}, u32[]{:S(2)}) collective-permute-start(f32[40,8,128]{2,1,0:T(8,128)S(1)} %get-tuple-element.17), channel_id=1, source_target_pairs={{0,128},{128,256},{256,384},{1,129},{129,257},{257,385},{2,130},{1... | collective-permute-start | bytes 491528 | tf_op jit(solution)/shard_map/ppermute | solution.py:20
  49.3 10.2 %collective-permute-start.4 = (f32[60,8,128]{2,1,0:T(8,128)S(1)}, f32[60,8,128]{2,1,0:T(8,128)S(1)}, u32[]{:S(2)}, u32[]{:S(2)}) collective-permute-start(f32[60,8,128]{2,1,0:T(8,128)S(1)} %get-tuple-element.19), channel_id=1, source_target_pairs={{0,1},{1,2},{2,3},{3,4},{4,5},{5,6},{6,7},{7,8},{8,9},{9,10},{10,1... | collective-permute-start | bytes 737288 | tf_op jit(solution)/shard_map/ppermute | solution.py:20
  52.9 7.7 %collective-permute-start.5 = (f32[60,8,128]{2,1,0:T(8,128)S(1)}, f32[60,8,128]{2,1,0:T(8,128)S(1)}, u32[]{:S(2)}, u32[]{:S(2)}) collective-permute-start(f32[60,8,128]{2,1,0:T(8,128)S(1)} %get-tuple-element.20), channel_id=1, source_target_pairs={{1,0},{2,1},{3,2},{4,3},{5,4},{6,5},{7,6},{8,7},{9,8},{10,9},{11,1... | collective-permute-start | bytes 737288 | tf_op jit(solution)/shard_map/ppermute | solution.py:20
  54.8 4.7 %collective-permute-start.6 = (f32[32,128]{1,0:T(8,128)S(1)}, f32[32,128]{1,0:T(8,128)S(1)}, u32[]{:S(2)}, u32[]{:S(2)}) collective-permute-start(f32[32,128]{1,0:T(8,128)S(1)} %get-tuple-element.21), channel_id=1, source_target_pairs={{2,0},{3,1},{4,2},{5,3},{6,4},{7,5},{8,6},{9,7},{10,8},{11,9},{12,... | collective-permute-start | bytes 49160 | tf_op jit(solution)/shard_map/ppermute | solution.py:20
  62.7 5.4 %collective-permute-start.7 = (f32[2,5,8,128]{3,2,1,0:T(8,128)S(1)}, f32[2,5,8,128]{3,2,1,0:T(8,128)S(1)}, u32[]{:S(2)}, u32[]{:S(2)}) collective-permute-start(f32[2,5,8,128]{3,2,1,0:T(8,128)S(1)} %get-tuple-element.23.last), channel_id=1, source_target_pairs={{0,128},{128,256},{256,384},{1,129},{129,257},{257,385},{2,130},{1... | collective-permute-start | bytes 122888 | tf_op jit(solution)/shard_map/ppermute | solution.py:20
  66.8 4.7 %collective-permute-start.8 = (f32[2,5,8,128]{3,2,1,0:T(8,128)S(1)}, f32[2,5,8,128]{3,2,1,0:T(8,128)S(1)}, u32[]{:S(2)}, u32[]{:S(2)}) collective-permute-start(f32[2,5,8,128]{3,2,1,0:T(8,128)S(1)} %get-tuple-element.24.first), channel_id=1, source_target_pairs={{128,0},{256,128},{384,256},{129,1},{257,129},{385,257},{130,2},{2... | collective-permute-start | bytes 122888 | tf_op jit(solution)/shard_map/ppermute | solution.py:20
  71.6 5.2 %collective-permute-start.9 = (f32[8,5,8,128]{3,2,1,0:T(8,128)S(1)}, f32[8,5,8,128]{3,2,1,0:T(8,128)S(1)}, u32[]{:S(2)}, u32[]{:S(2)}) collective-permute-start(f32[8,5,8,128]{3,2,1,0:T(8,128)S(1)} %get-tuple-element.25.mine), channel_id=1, source_target_pairs={{0,1},{1,0},{2,3},{3,2},{4,5},{5,4},{6,7},{7,6},{8,9},{9,8},{10,11... | collective-permute-start | bytes 491528 | tf_op jit(solution)/shard_map/ppermute | solution.py:545
  76.9 8.4 %collective-permute-start.10 = (f32[14,5,8,128]{3,2,1,0:T(8,128)S(1)}, f32[14,5,8,128]{3,2,1,0:T(8,128)S(1)}, u32[]{:S(2)}, u32[]{:S(2)}) collective-permute-start(f32[14,5,8,128]{3,2,1,0:T(8,128)S(1)} %shard_map.74), channel_id=1, source_target_pairs={{0,2},{2,4},{3,1},{4,6},{5,3},{6,8},{7,5},{8,10},{9,7},{10,12},{11... | collective-permute-start | bytes 860168 | tf_op jit(solution)/shard_map/ppermute | solution.py:548
  78.2 7.1 %collective-permute-start.11 = (f32[6,5,8,128]{3,2,1,0:T(8,128)S(1)}, f32[6,5,8,128]{3,2,1,0:T(8,128)S(1)}, u32[]{:S(2)}, u32[]{:S(2)}) collective-permute-start(f32[6,5,8,128]{3,2,1,0:T(8,128)S(1)} %get-tuple-element.26.inner), channel_id=1, source_target_pairs={{2,0},{4,2},{1,3},{6,4},{3,5},{8,6},{5,7},{10,8},{7,9},{12,10},{9,... | collective-permute-start | bytes 368648 | tf_op jit(solution)/shard_map/ppermute | solution.py:546
  112.7 10.8 %collective-permute-start.13 = (f32[4,160,128]{2,1,0:T(8,128)S(1)}, f32[4,160,128]{2,1,0:T(8,128)S(1)}, u32[]{:S(2)}, u32[]{:S(2)}) collective-permute-start(f32[4,160,128]{2,1,0:T(8,128)S(1)} %shard_map.76.refs_1_), channel_id=1, source_target_pairs={{16,0},{32,16},{48,32},{64,48},{80,64},{96,80},{112,96},{17,1},{33... | collective-permute-start | bytes 983048 | tf_op jit(solution)/shard_map/ppermute | solution.py:20
  114.0 10.4 %collective-permute-start.12 = (f32[4,160,128]{2,1,0:T(8,128)S(1)}, f32[4,160,128]{2,1,0:T(8,128)S(1)}, u32[]{:S(2)}, u32[]{:S(2)}) collective-permute-start(f32[4,160,128]{2,1,0:T(8,128)S(1)} %shard_map.76.refs_1_), channel_id=1, source_target_pairs={{0,16},{16,32},{32,48},{48,64},{64,80},{80,96},{96,112},{1,17},{17... | collective-permute-start | bytes 983048 | tf_op jit(solution)/shard_map/ppermute | solution.py:20

commit v11 on v10

--- a/solution.py
+++ b/solution.py
@@ -24,12 +24,12 @@
     def run(*args):
         space = pltpu.HBM if copied else pltpu.VMEM
         buffers = [pltpu.VMEM(a.shape, F32) for a in args] if copied else []
-        sems = [pltpu.SemaphoreType.DMA] * len(args) if copied else []
+        sems = [pltpu.SemaphoreType.DMA] * (2 * len(args)) if copied else []
         return pl.pallas_call(
             kernel,
             out_shape=[jax.ShapeDtypeStruct(s, F32) for s in outs],
             in_specs=[pl.BlockSpec(memory_space=space)] * len(args),
-            out_specs=[pl.BlockSpec(memory_space=pltpu.VMEM)] * len(outs),
+            out_specs=[pl.BlockSpec(memory_space=space)] * len(outs),
             scratch_shapes=[pltpu.VMEM(s, F32) for s in scratch] + buffers + sems,
             compiler_params=pltpu.CompilerParams(vmem_limit_bytes=ALL_VMEM if copied else VMEM_BYTES),
         )(*args)
@@ -168,8 +168,9 @@
 
 
 def to_windows_kernel(*refs):
-    args, out, buffers, sems = refs[:5], refs[5], refs[6:11], refs[11:]
-    copies = [pltpu.make_async_copy(*c) for c in zip(args, buffers, sems)]
+    args, result, out, buffers, sems = refs[:5], refs[5], refs[6], refs[7:12], refs[12:]
+    copies = [pltpu.make_async_copy(*c) for c in zip(args, buffers, sems[:5])]
+    sends = [pltpu.make_async_copy(out.at[:, a], result.at[:, a], sems[5 + a]) for a in range(5)]
     for c in copies:
         c.start()
     _, lane = iotas((8, 128))
@@ -183,6 +184,9 @@
             for c in range(4):
                 out[2 * c, a, x] = jnp.where(lane < 32, up[c - 1] if c else zero, up[c])
                 out[2 * c + 1, a, x] = jnp.where(lane < 96, down[c], down[c + 1] if c < 3 else zero)
+        sends[a].start()
+    for c in sends:
+        c.wait()
 
 
 def flat(s, a, x):
@@ -461,13 +465,16 @@
         ref[9] = jnp.where(lane < 64, pltpu.roll(ref[1], 64, 1), 0.0)
 
     def sweep(step, carry):
+        relax(co, b, r, range(8), False, q0)
+        join(b)
         relax(co, r, b, range(8), True, q0)
         join(r)
-        relax(co, b, r, range(8), False, q0)
-        join(b)
         return carry
 
-    lax.fori_loop(0, sweeps, sweep, 0)
+    first_red(co, r, range(8))
+    join(r)
+    lax.fori_loop(1, sweeps, sweep, 0)
+    relax(co, b, r, range(8), False, q0)
 
     gy, ring, place = (lax.axis_index(name) for name in ("gy", "ring", "place"))
     side, base = ring // 2, 4 * lax.rem(ring, 2)
@@ -514,7 +521,7 @@
 def cycle(rhs, alpha, beta_x, beta_y, beta_z):
     rings, count_y = lax.axis_size("ring"), lax.axis_size("gy")
 
-    (own,) = call(to_windows_kernel, [(RING, 5, 4, 8, 128)], copied=True)(rhs, alpha, beta_x, beta_y, beta_z)
+    (own,) = call(to_windows_kernel, [(RING, 5, 4, 8, 128)], [(RING, 5, 4, 8, 128)], copied=True)(rhs, alpha, beta_x, beta_y, beta_z)
     own = lax.all_to_all(own, "place", 0, 0, tiled=True)
     to_low, to_high, first_by = call(
         x_messages_kernel, [(41, 8, 128), (40, 8, 128), (32, 128)]

time: 145 us -> 144 us (level)
  no operation moved by 1% of the time
where the time goes in v11:
time: 144 us; the launch traced here: 142 us
  blocking collectives  68.7 us (48%)
  starting transfers between devices  39.3 us (27%)
  waiting for transfers between devices  21.3 us (15%)
  Pallas kernels  12 us (8%)
    all_to_all x1, blocking collectives, cycle(): own = lax.all_to_all(own, 'place', 0, 0, tiled=True)  30.1 us
    ppermute x11, starting transfers between devices, shifted(): lax.ppermute(values, name, [(i, i + steps) for i in range(lead, last)])  29.8 us
    all_to_all x1, blocking collectives, cycle(): low = lax.all_to_all(low, ('ring', 'gy'), 0, 0, tiled=True)  25.5 us
    ppermute x11, waiting for transfers between devices, shifted(): lax.ppermute(values, name, [(i, i + steps) for i in range(lead, last)])  17.2 us
    all_to_all x1, blocking collectives, cycle(): pieces = lax.all_to_all(pieces, 'place', 0, 0, tiled=True)  13.2 us
    pallas_call x11, Pallas kernels, run(): pl.pallas_call(kernel, out_shape=[jax.ShapeDtypeStruct(s, F32) for s in o...  12 us
    ppermute x1, starting transfers between devices, cycle(): beside = lax.ppermute(mid, 'gy', cores)  4.21 us
    ppermute x1, starting transfers between devices, cycle(): beyond = lax.ppermute(inner, 'gy', far)  3.99 us
  transfers between devices with their start and end apart: 14, of which 8 were waited for; matrix products, arithmetic and copies ran while one was open for 0% of the time, Pallas kernels for 1%

profile of v11, /device:TPU:1, one launch (start us, length us, event | category | flops | bytes accessed | tf_op | source)
XLA Modules:
  0.0 142.2 jit_solution(9146862799690367058)
XLA Ops:
  0.6 2.1 %shard_map.68 = f32[8,5,4,8,128]{4,3,2,1,0:T(8,128)} custom-call(f32[4,8,512]{2,1,0:T(8,128)} %refs_0_.1, f32[4,8,512]{2,1,0:T(8,128)} %refs_1_.1, f32[4,8,512]{2,1,0:T(8,128)} %refs_2_.1, f32[4,8,512]{2,1,0:T(8,128)} %refs_3_.1, f32[4,8,512]{2,1,0:T(8,128)} %refs_4_.1), custom_call_target="tpu_custom_call" | custom-call | tf_op jit(solution)/shard_map/pallas_call | solution.py:28
  2.7 30.1 %all_to_all.15.own = f32[8,5,4,8,128]{4,3,2,1,0:T(8,128)S(1)} all-to-all(f32[8,5,4,8,128]{4,3,2,1,0:T(8,128)} %shard_map.68), channel_id=1, replica_groups=mesh['ring'=4,'place'=8,'gy'=16] {'place'}, dimensions={0} | all-to-all | bytes 1310720 | tf_op jit(solution)/shard_map/all_to_all | solution.py:525
  32.8 3.9 %collective-permute-start.3 = (f32[8,5,4,8,128]{4,3,2,1,0:T(8,128)S(1)}, f32[8,5,4,8,128]{4,3,2,1,0:T(8,128)S(1)}, u32[]{:S(2)}, u32[]{:S(2)}) collective-permute-start(f32[8,5,4,8,128]{4,3,2,1,0:T(8,128)S(1)} %all_to_all.15.own), channel_id=1, source_target_pairs={{1,0},{2,1},{3,2},{4,3},{5,4},{6,5},{7,6},{8,7},{9,8},{10,9},{11,1... | collective-permute-start | bytes 1966088 | tf_op jit(solution)/shard_map/ppermute | solution.py:20
  36.8 3.1 %collective-permute-start.2 = (f32[8,5,4,8,128]{4,3,2,1,0:T(8,128)S(1)}, f32[8,5,4,8,128]{4,3,2,1,0:T(8,128)S(1)}, u32[]{:S(2)}, u32[]{:S(2)}) collective-permute-start(f32[8,5,4,8,128]{4,3,2,1,0:T(8,128)S(1)} %all_to_all.15.own), channel_id=1, source_target_pairs={{0,1},{1,2},{2,3},{3,4},{4,5},{5,6},{6,7},{7,8},{8,9},{9,10},{10,1... | collective-permute-start | bytes 1966088 | tf_op jit(solution)/shard_map/ppermute | solution.py:20
  39.9 1.3 collective-permute-start.1
  41.2 4.0 %collective-permute-start = (f32[40,8,128]{2,1,0:T(8,128)S(1)}, f32[40,8,128]{2,1,0:T(8,128)S(1)}, u32[]{:S(2)}, u32[]{:S(2)}) collective-permute-start(f32[40,8,128]{2,1,0:T(8,128)S(1)} %get-tuple-element.17), channel_id=1, source_target_pairs={{0,128},{128,256},{256,384},{1,129},{129,257},{257,385},{2,130},{1... | collective-permute-start | bytes 491528 | tf_op jit(solution)/shard_map/ppermute | solution.py:20
  45.2 3.9 %collective-permute-done.low.x_low = f32[40,8,128]{2,1,0:T(8,128)S(1)} collective-permute-done((f32[40,8,128]{2,1,0:T(8,128)S(1)}, f32[40,8,128]{2,1,0:T(8,128)S(1)}, u32[]{:S(2)}, u32[]{:S(2)}) %collective-permute-start) | collective-permute-done | bytes 163872 | tf_op jit(solution)/shard_map/ppermute | solution.py:20
  49.1 0.0 collective-permute-done.1.high.x_high
  49.2 3.6 %collective-permute-start.4 = (f32[60,8,128]{2,1,0:T(8,128)S(1)}, f32[60,8,128]{2,1,0:T(8,128)S(1)}, u32[]{:S(2)}, u32[]{:S(2)}) collective-permute-start(f32[60,8,128]{2,1,0:T(8,128)S(1)} %get-tuple-element.19), channel_id=1, source_target_pairs={{0,1},{1,2},{2,3},{3,4},{4,5},{5,6},{6,7},{7,8},{8,9},{9,10},{10,1... | collective-permute-start | bytes 737288 | tf_op jit(solution)/shard_map/ppermute | solution.py:20
  52.8 1.9 %collective-permute-start.5 = (f32[60,8,128]{2,1,0:T(8,128)S(1)}, f32[60,8,128]{2,1,0:T(8,128)S(1)}, u32[]{:S(2)}, u32[]{:S(2)}) collective-permute-start(f32[60,8,128]{2,1,0:T(8,128)S(1)} %get-tuple-element.20), channel_id=1, source_target_pairs={{1,0},{2,1},{3,2},{4,3},{5,4},{6,5},{7,6},{8,7},{9,8},{10,9},{11,1... | collective-permute-start | bytes 737288 | tf_op jit(solution)/shard_map/ppermute | solution.py:20
  54.7 1.3 collective-permute-start.6
  56.0 0.0 collective-permute-done.3.y_high
  56.0 0.9 shard_map.71
  57.0 2.4 %collective-permute-done.6.beyond_y = f32[32,128]{1,0:T(8,128)S(1)} collective-permute-done((f32[32,128]{1,0:T(8,128)S(1)}, f32[32,128]{1,0:T(8,128)S(1)}, u32[]{:S(2)}, u32[]{:S(2)}) %collective-permute-start.6) | collective-permute-done | bytes 16416 | tf_op jit(solution)/shard_map/ppermute | solution.py:20
  59.4 0.0 collective-permute-done.4.corner_low
  59.4 1.1 collective-permute-done.5.corner_high
  60.5 0.0 collective-permute-done.2.y_low
  60.5 2.1 %shard_map.72 = (f32[2,16,8,128]{3,2,1,0:T(8,128)S(1)}, f32[2,5,8,128]{3,2,1,0:T(8,128)S(1)}, f32[2,5,8,128]{3,2,1,0:T(8,128)S(1)}) custom-call(f32[8,5,4,8,128]{4,3,2,1,0:T(8,128)S(1)} %all_to_all.15.own, f32[40,8,128]{2,1,0:T(8,128)S(1)} %collective-permute-done.low.x_low, f32[41,8,128]{2,1,0:T(8,128)S(1)} %collective-permute-done.1.high.x_high, ...), custom_call_target="tpu_custom_call" | custom-call | tf_op jit(solution)/shard_map/pallas_call | solution.py:28
  62.6 4.1 %collective-permute-start.7 = (f32[2,5,8,128]{3,2,1,0:T(8,128)S(1)}, f32[2,5,8,128]{3,2,1,0:T(8,128)S(1)}, u32[]{:S(2)}, u32[]{:S(2)}) collective-permute-start(f32[2,5,8,128]{3,2,1,0:T(8,128)S(1)} %get-tuple-element.23.last), channel_id=1, source_target_pairs={{0,128},{128,256},{256,384},{1,129},{129,257},{257,385},{2,130},{1... | collective-permute-start | bytes 122888 | tf_op jit(solution)/shard_map/ppermute | solution.py:20
  66.7 1.3 collective-permute-start.8
  68.0 0.0 collective-permute-done.7.low
  68.0 3.4 %collective-permute-done.8.high = f32[2,5,8,128]{3,2,1,0:T(8,128)S(1)} collective-permute-done((f32[2,5,8,128]{3,2,1,0:T(8,128)S(1)}, f32[2,5,8,128]{3,2,1,0:T(8,128)S(1)}, u32[]{:S(2)}, u32[]{:S(2)}) %collective-permute-start.8) | collective-permute-done | bytes 40992 | tf_op jit(solution)/shard_map/ppermute | solution.py:20
  71.5 4.2 %collective-permute-start.9 = (f32[8,5,8,128]{3,2,1,0:T(8,128)S(1)}, f32[8,5,8,128]{3,2,1,0:T(8,128)S(1)}, u32[]{:S(2)}, u32[]{:S(2)}) collective-permute-start(f32[8,5,8,128]{3,2,1,0:T(8,128)S(1)} %get-tuple-element.25.mine), channel_id=1, source_target_pairs={{0,1},{1,0},{2,3},{3,2},{4,5},{5,4},{6,7},{7,6},{8,9},{9,8},{10,11... | collective-permute-start | bytes 491528 | tf_op jit(solution)/shard_map/ppermute | solution.py:552
  75.7 1.0 collective-permute-done.9.other.beside
  76.7 1.3 collective-permute-start.10
  78.0 4.0 %collective-permute-start.11 = (f32[6,5,8,128]{3,2,1,0:T(8,128)S(1)}, f32[6,5,8,128]{3,2,1,0:T(8,128)S(1)}, u32[]{:S(2)}, u32[]{:S(2)}) collective-permute-start(f32[6,5,8,128]{3,2,1,0:T(8,128)S(1)} %get-tuple-element.26.inner), channel_id=1, source_target_pairs={{2,0},{4,2},{1,3},{6,4},{3,5},{8,6},{5,7},{10,8},{7,9},{12,10},{9,... | collective-permute-start | bytes 368648 | tf_op jit(solution)/shard_map/ppermute | solution.py:553
  82.0 3.1 %collective-permute-done.11.beyond = f32[6,5,8,128]{3,2,1,0:T(8,128)S(1)} collective-permute-done((f32[6,5,8,128]{3,2,1,0:T(8,128)S(1)}, f32[6,5,8,128]{3,2,1,0:T(8,128)S(1)}, u32[]{:S(2)}, u32[]{:S(2)}) %collective-permute-start.11) | collective-permute-done | bytes 122912 | tf_op jit(solution)/shard_map/ppermute | solution.py:553
  85.1 0.0 collective-permute-done.10.across
  85.2 1.8 %shard_map.75 = (f32[2,8,8,128]{3,2,1,0:T(8,128)S(1)}, f32[64,5,2,128]{3,2,1,0:T(2,128)S(1)}) custom-call(f32[8,5,8,128]{3,2,1,0:T(8,128)S(1)} %get-tuple-element.25.mine, f32[8,5,8,128]{3,2,1,0:T(8,128)S(1)} %collective-permute-done.9.other.beside, f32[14,5,8,128]{3,2,1,0:T(8,128)S(1)} %collective-permute-done.10.across, ...), custom_call_target="tpu_custom_call" | custom-call | tf_op jit(solution)/shard_map/pallas_call | solution.py:28
  87.0 25.5 %all_to_all.16.gathered = f32[64,5,2,128]{3,2,1,0:T(2,128)S(1)} all-to-all(f32[64,5,2,128]{3,2,1,0:T(2,128)S(1)} %get-tuple-element.29), channel_id=1, replica_groups=mesh['ring'=4,'place'=8,'gy'=16] {'ring','gy'}, dimensions={0} | all-to-all | bytes 655360 | tf_op jit(solution)/shard_map/all_to_all | solution.py:562
  112.5 0.1 shard_map.76.refs_1_
  112.6 1.3 collective-permute-start.13
  113.9 4.0 %collective-permute-start.12 = (f32[4,160,128]{2,1,0:T(8,128)S(1)}, f32[4,160,128]{2,1,0:T(8,128)S(1)}, u32[]{:S(2)}, u32[]{:S(2)}) collective-permute-start(f32[4,160,128]{2,1,0:T(8,128)S(1)} %shard_map.76.refs_1_), channel_id=1, source_target_pairs={{0,16},{16,32},{32,48},{48,64},{64,80},{80,96},{96,112},{1,17},{17... | collective-permute-start | bytes 983048 | tf_op jit(solution)/shard_map/ppermute | solution.py:20
  117.9 5.4 %collective-permute-done.13.refs_2_ = f32[4,160,128]{2,1,0:T(8,128)S(1)} collective-permute-done((f32[4,160,128]{2,1,0:T(8,128)S(1)}, f32[4,160,128]{2,1,0:T(8,128)S(1)}, u32[]{:S(2)}, u32[]{:S(2)}) %collective-permute-start.13) | collective-permute-done | bytes 327712 | tf_op jit(solution)/shard_map/ppermute | solution.py:20
  123.3 0.9 collective-permute-done.12.refs_0_
  124.2 4.0 %shard_map.77 = f32[8,3,8,128]{3,2,1,0:T(8,128)S(1)} custom-call(f32[4,160,128]{2,1,0:T(8,128)S(1)} %collective-permute-done.12.refs_0_, f32[4,160,128]{2,1,0:T(8,128)S(1)} %shard_map.76.refs_1_, f32[4,160,128]{2,1,0:T(8,128)S(1)} %collective-permute-done.13.refs_2_, f32[2,8,8,128]{3,2,1,0:T(8,128)S(1)} %get-tuple-element.30.refs_3_, ...), custom_call_target="tpu_custom_call" | custom-call | tf_op jit(solution)/shard_map/pallas_call | solution.py:28
  128.3 13.2 %all_to_all.17.pieces = f32[8,3,8,128]{3,2,1,0:T(8,128)S(1)} all-to-all(f32[8,3,8,128]{3,2,1,0:T(8,128)S(1)} %shard_map.77), channel_id=1, replica_groups=mesh['ring'=4,'place'=8,'gy'=16] {'place'}, dimensions={0} | all-to-all | bytes 196608 | tf_op jit(solution)/shard_map/all_to_all | solution.py:569
  141.5 0.7 shard_map.78
  (4 shorter events, 0.1 us)
Async XLA Ops:
  32.8 23.2 %collective-permute-start.3 = (f32[8,5,4,8,128]{4,3,2,1,0:T(8,128)S(1)}, f32[8,5,4,8,128]{4,3,2,1,0:T(8,128)S(1)}, u32[]{:S(2)}, u32[]{:S(2)}) collective-permute-start(f32[8,5,4,8,128]{4,3,2,1,0:T(8,128)S(1)} %all_to_all.15.own), channel_id=1, source_target_pairs={{1,0},{2,1},{3,2},{4,3},{5,4},{6,5},{7,6},{8,7},{9,8},{10,9},{11,1... | collective-permute-start | bytes 1966088 | tf_op jit(solution)/shard_map/ppermute | solution.py:20
  36.8 23.7 %collective-permute-start.2 = (f32[8,5,4,8,128]{4,3,2,1,0:T(8,128)S(1)}, f32[8,5,4,8,128]{4,3,2,1,0:T(8,128)S(1)}, u32[]{:S(2)}, u32[]{:S(2)}) collective-permute-start(f32[8,5,4,8,128]{4,3,2,1,0:T(8,128)S(1)} %all_to_all.15.own), channel_id=1, source_target_pairs={{0,1},{1,2},{2,3},{3,4},{4,5},{5,6},{6,7},{7,8},{8,9},{9,10},{10,1... | collective-permute-start | bytes 1966088 | tf_op jit(solution)/shard_map/ppermute | solution.py:20
  39.9 9.2 %collective-permute-start.1 = (f32[41,8,128]{2,1,0:T(8,128)S(1)}, f32[41,8,128]{2,1,0:T(8,128)S(1)}, u32[]{:S(2)}, u32[]{:S(2)}) collective-permute-start(f32[41,8,128]{2,1,0:T(8,128)S(1)} %get-tuple-element.18), channel_id=1, source_target_pairs={{128,0},{256,128},{384,256},{129,1},{257,129},{385,257},{130,2},{2... | collective-permute-start | bytes 503816 | tf_op jit(solution)/shard_map/ppermute | solution.py:20
  41.2 7.9 %collective-permute-start = (f32[40,8,128]{2,1,0:T(8,128)S(1)}, f32[40,8,128]{2,1,0:T(8,128)S(1)}, u32[]{:S(2)}, u32[]{:S(2)}) collective-permute-start(f32[40,8,128]{2,1,0:T(8,128)S(1)} %get-tuple-element.17), channel_id=1, source_target_pairs={{0,128},{128,256},{256,384},{1,129},{129,257},{257,385},{2,130},{1... | collective-permute-start | bytes 491528 | tf_op jit(solution)/shard_map/ppermute | solution.py:20
  49.2 10.2 %collective-permute-start.4 = (f32[60,8,128]{2,1,0:T(8,128)S(1)}, f32[60,8,128]{2,1,0:T(8,128)S(1)}, u32[]{:S(2)}, u32[]{:S(2)}) collective-permute-start(f32[60,8,128]{2,1,0:T(8,128)S(1)} %get-tuple-element.19), channel_id=1, source_target_pairs={{0,1},{1,2},{2,3},{3,4},{4,5},{5,6},{6,7},{7,8},{8,9},{9,10},{10,1... | collective-permute-start | bytes 737288 | tf_op jit(solution)/shard_map/ppermute | solution.py:20
  52.8 7.7 %collective-permute-start.5 = (f32[60,8,128]{2,1,0:T(8,128)S(1)}, f32[60,8,128]{2,1,0:T(8,128)S(1)}, u32[]{:S(2)}, u32[]{:S(2)}) collective-permute-start(f32[60,8,128]{2,1,0:T(8,128)S(1)} %get-tuple-element.20), channel_id=1, source_target_pairs={{1,0},{2,1},{3,2},{4,3},{5,4},{6,5},{7,6},{8,7},{9,8},{10,9},{11,1... | collective-permute-start | bytes 737288 | tf_op jit(solution)/shard_map/ppermute | solution.py:20
  54.7 4.7 %collective-permute-start.6 = (f32[32,128]{1,0:T(8,128)S(1)}, f32[32,128]{1,0:T(8,128)S(1)}, u32[]{:S(2)}, u32[]{:S(2)}) collective-permute-start(f32[32,128]{1,0:T(8,128)S(1)} %get-tuple-element.21), channel_id=1, source_target_pairs={{2,0},{3,1},{4,2},{5,3},{6,4},{7,5},{8,6},{9,7},{10,8},{11,9},{12,... | collective-permute-start | bytes 49160 | tf_op jit(solution)/shard_map/ppermute | solution.py:20
  62.6 5.4 %collective-permute-start.7 = (f32[2,5,8,128]{3,2,1,0:T(8,128)S(1)}, f32[2,5,8,128]{3,2,1,0:T(8,128)S(1)}, u32[]{:S(2)}, u32[]{:S(2)}) collective-permute-start(f32[2,5,8,128]{3,2,1,0:T(8,128)S(1)} %get-tuple-element.23.last), channel_id=1, source_target_pairs={{0,128},{128,256},{256,384},{1,129},{129,257},{257,385},{2,130},{1... | collective-permute-start | bytes 122888 | tf_op jit(solution)/shard_map/ppermute | solution.py:20
  66.7 4.7 %collective-permute-start.8 = (f32[2,5,8,128]{3,2,1,0:T(8,128)S(1)}, f32[2,5,8,128]{3,2,1,0:T(8,128)S(1)}, u32[]{:S(2)}, u32[]{:S(2)}) collective-permute-start(f32[2,5,8,128]{3,2,1,0:T(8,128)S(1)} %get-tuple-element.24.first), channel_id=1, source_target_pairs={{128,0},{256,128},{384,256},{129,1},{257,129},{385,257},{130,2},{2... | collective-permute-start | bytes 122888 | tf_op jit(solution)/shard_map/ppermute | solution.py:20
  71.5 5.2 %collective-permute-start.9 = (f32[8,5,8,128]{3,2,1,0:T(8,128)S(1)}, f32[8,5,8,128]{3,2,1,0:T(8,128)S(1)}, u32[]{:S(2)}, u32[]{:S(2)}) collective-permute-start(f32[8,5,8,128]{3,2,1,0:T(8,128)S(1)} %get-tuple-element.25.mine), channel_id=1, source_target_pairs={{0,1},{1,0},{2,3},{3,2},{4,5},{5,4},{6,7},{7,6},{8,9},{9,8},{10,11... | collective-permute-start | bytes 491528 | tf_op jit(solution)/shard_map/ppermute | solution.py:552
  76.7 8.4 %collective-permute-start.10 = (f32[14,5,8,128]{3,2,1,0:T(8,128)S(1)}, f32[14,5,8,128]{3,2,1,0:T(8,128)S(1)}, u32[]{:S(2)}, u32[]{:S(2)}) collective-permute-start(f32[14,5,8,128]{3,2,1,0:T(8,128)S(1)} %shard_map.74), channel_id=1, source_target_pairs={{0,2},{2,4},{3,1},{4,6},{5,3},{6,8},{7,5},{8,10},{9,7},{10,12},{11... | collective-permute-start | bytes 860168 | tf_op jit(solution)/shard_map/ppermute | solution.py:555
  78.0 7.1 %collective-permute-start.11 = (f32[6,5,8,128]{3,2,1,0:T(8,128)S(1)}, f32[6,5,8,128]{3,2,1,0:T(8,128)S(1)}, u32[]{:S(2)}, u32[]{:S(2)}) collective-permute-start(f32[6,5,8,128]{3,2,1,0:T(8,128)S(1)} %get-tuple-element.26.inner), channel_id=1, source_target_pairs={{2,0},{4,2},{1,3},{6,4},{3,5},{8,6},{5,7},{10,8},{7,9},{12,10},{9,... | collective-permute-start | bytes 368648 | tf_op jit(solution)/shard_map/ppermute | solution.py:553
  112.6 10.8 %collective-permute-start.13 = (f32[4,160,128]{2,1,0:T(8,128)S(1)}, f32[4,160,128]{2,1,0:T(8,128)S(1)}, u32[]{:S(2)}, u32[]{:S(2)}) collective-permute-start(f32[4,160,128]{2,1,0:T(8,128)S(1)} %shard_map.76.refs_1_), channel_id=1, source_target_pairs={{16,0},{32,16},{48,32},{64,48},{80,64},{96,80},{112,96},{17,1},{33... | collective-permute-start | bytes 983048 | tf_op jit(solution)/shard_map/ppermute | solution.py:20
  113.9 10.4 %collective-permute-start.12 = (f32[4,160,128]{2,1,0:T(8,128)S(1)}, f32[4,160,128]{2,1,0:T(8,128)S(1)}, u32[]{:S(2)}, u32[]{:S(2)}) collective-permute-start(f32[4,160,128]{2,1,0:T(8,128)S(1)} %shard_map.76.refs_1_), channel_id=1, source_target_pairs={{0,16},{16,32},{32,48},{48,64},{64,80},{80,96},{96,112},{1,17},{17... | collective-permute-start | bytes 983048 | tf_op jit(solution)/shard_map/ppermute | solution.py:20
